TPU v7x, 32 devices: a whole 2x2x4 slice. The times are simulated.
32 devices in a mesh: land: 4 (over z), rows: 8 (over y, x, core).
Axes of the slice: x: 2, y: 2, z: 4, core: 2. Of those that a mesh axis runs over, the one named last changes fastest.
Arguments:
- embeddings: bfloat16 [32768, 768], P(('land', 'rows')), may hold values from -8 to 8
- landmarks: bfloat16 [1024, 768], P('land'), may hold values from -8 to 8
Outputs:
- factor: float32 [1024, 1024], replicated
All inputs are finite; a program needn't handle non-finite values.
Results may differ from a plain program's by a relative error of at most 0.0003.
Values may be sent and summed in bfloat16 or wider, within the bound.
No kernel may reach another device: no remote copies, remote signals or barrier semaphores. Data moves between devices by JAX's collectives and lax.ppermute only.
A program may use at most 64 MiB of HBM per device.

v0:
```python
import math

import jax
import jax.numpy as jnp
from jax import lax
from jax.sharding import PartitionSpec as P

LAYERS = 6


SCALE_SQ = 1.0 / 32.0
RIDGE = 0.1


def squares_mean(points):
    wide = points.astype(jnp.float32)
    return jnp.sum(wide * wide, axis=1, keepdims=True) / points.shape[1] + 1e-06


def nngp_kernel(left, left_q, right, right_q):
    kernel = (
        lax.dot_general(left, right, (((1,), (1,)), ((), ())), preferred_element_type=jnp.float32)
        / left.shape[1]
    )
    q_left = left_q
    q_right = right_q
    for layer in range(LAYERS):
        scale = jnp.sqrt(q_left * q_right)
        cosine = jnp.clip(kernel / scale, -1.0, 1.0)
        branch = (
            scale
            / math.pi
            * (
                jnp.sqrt(jnp.maximum(1.0 - cosine * cosine, 0.0))
                + (math.pi - jnp.arccos(cosine)) * cosine
            )
        )
        kernel = kernel + SCALE_SQ * branch
        q_left = q_left * (1.0 + SCALE_SQ)
        q_right = q_right * (1.0 + SCALE_SQ)
    return kernel


def shards(embeddings, landmarks):
    all_points = embeddings.shape[0] * lax.axis_size("land") * lax.axis_size("rows")
    gathered = lax.all_gather(landmarks, "land", axis=0, tiled=True)
    land_q = squares_mean(gathered)
    cross = nngp_kernel(embeddings, squares_mean(embeddings), gathered, land_q.T).astype(
        jnp.bfloat16
    )
    local_gram = (
        lax.dot_general(cross, cross, (((0,), (0,)), ((), ())), preferred_element_type=jnp.float32)
        / all_points
    )
    share = gathered.shape[0] // (lax.axis_size("land") * lax.axis_size("rows"))
    position = (lax.axis_index("land") * lax.axis_size("rows") + lax.axis_index("rows")) * share
    own_marks = lax.dynamic_slice_in_dim(gathered, position, share, 0)
    own_q = lax.dynamic_slice_in_dim(land_q, position, share, 0)
    ridge_rows = RIDGE * nngp_kernel(own_marks, own_q, gathered, land_q.T)
    current = lax.dynamic_slice_in_dim(local_gram, position, share, 0)
    contribution = lax.dynamic_update_slice_in_dim(local_gram, current + ridge_rows, position, 0)
    total = lax.psum(contribution, ("land", "rows"))
    return jnp.linalg.cholesky(total).T


def solution(mesh):
    in_specs = (P(("land", "rows"), None), P("land", None))
    out_specs = P()
    return jax.shard_map(shards, mesh=mesh, in_specs=in_specs, out_specs=out_specs, check_vma=False)
```

profile of v0, /device:TPU:0, one launch (start us, length us, event | category | flops | bytes accessed | tf_op | source)
XLA Modules:
  0.0 517.8 jit_solution(11428233393149090244)
XLA Ops:
  6.5 0.7 all-gather.2.cloned.1.call-update
  7.3 1.8 multiply_reduce_fusion.1
  9.1 39.6 %all-gather.2.cloned.1.call-done = bf16[1024,768]{1,0:T(8,128)(2,1)} async-done(((bf16[256,768]{1,0:T(8,128)(2,1)}), bf16[1024,768]{1,0:T(8,128)(2,1)}) %all-gather.2.cloned.1.call-update) | async-done | bytes 1572880 | tf_op jit(solution)/shard_map/all_gather | solution.py:46
  48.8 1.8 multiply_reduce_fusion
  50.6 76.7 %add_convert_fusion.clone.6 = bf16[1024,1024]{1,0:T(8,128)(2,1)S(1)} fusion(bf16[1024,768]{1,0:T(8,128)(2,1)} %param.2, bf16[1024,768]{1,0:T(8,128)(2,1)} %all-gather.2.cloned.1.call-done, f32[1024]{0:T(1024)S(1)} %get-tuple-element.40, f32[1024]{0:T(1024)S(1)} %get-tuple-element.34, f32[1024]{0:T(1024)S(1)} %get-tuple-element.39, ...), kind=kOutput, calls=%fused_computation.3.clone.clone.clone.2 | convolution fusion | flops 1713373184 | bytes 5292032 | tf_op jit(solution)/shard_map/dot_general | solution.py:22
  127.3 2.4 convolution_multiply_fusion
  129.8 2.0 copy-done.1
  131.8 9.1 %multiply_add_fusion = f32[32,1024]{0,1:T(8,128)S(1)} fusion(bf16[1024,768]{1,0:T(8,128)(2,1)S(1)} %copy-done.2, f32[1024,1024]{0,1:T(8,128)S(1)} %convolution_multiply_fusion, s32[]{:T(128)S(6)} %select_n.10, f32[1024]{0:T(1024)S(1)} %get-tuple-element.40, f32[32]{0:T(128)S(1)} %get-tuple-element.44, f32[1024]{0:T(1024)S(1)} %get-tuple-element.39, ...), kind=kOutput, calls=%fused_computation.27 | convolution fusion | flops 53575680 | bytes 2306048 | tf_op jit(solution)/shard_map/dot_general | solution.py:22
  140.9 3.5 dynamic_update_slice.3
  144.4 141.3 %all-reduce.3.cloned.1.call-done = f32[1024,1024]{0,1:T(8,128)} async-done(((f32[1024,1024]{0,1:T(8,128)}), f32[1024,1024]{0,1:T(8,128)}) %all-reduce.3.cloned.1.call-update) | async-done | bytes 4194320 | tf_op jit(solution)/shard_map/psum | solution.py:62
  285.7 5.5 %copy.10 = f32[1024,1024]{1,0:T(8,128)} copy(f32[1024,1024]{0,1:T(8,128)} %all-reduce.3.cloned.1.call-done) | data formatting | bytes 8388608 | tf_op jit(solution)/shard_map/psum | solution.py:62
  291.2 4.4 fusion
  295.6 1.9 copy-done
  297.5 11.7 %cholesky.222 = f32[128,128]{1,0:T(8,128)S(1)} custom-call(f32[128,128]{1,0:T(8,128)S(1)} %cholesky.577), custom_call_target="Cholesky" | custom-call | tf_op jit(solution)/shard_map/jit(cholesky)/cholesky | solution.py:63
  309.3 9.8 %custom-call.59 = f32[1,128,128]{1,2,0:T(8,128)S(1)} custom-call(f32[1,128,128]{2,1,0:T(8,128)S(1)} %get-tuple-element.28), custom_call_target="InvertDiagBlocksLowerTriangular" | custom-call | tf_op jit(solution)/shard_map/jit(cholesky)/cholesky | solution.py:63
  319.1 2.5 cholesky.254
  321.6 2.3 constant_dynamic-update-slice_fusion.6
  323.9 1.5 convolution_subtract_fusion
  325.5 11.9 %cholesky.243 = f32[128,128]{1,0:T(8,128)S(1)} custom-call(f32[128,128]{1,0:T(8,128)S(1)} %cholesky.581), custom_call_target="Cholesky" | custom-call | tf_op jit(solution)/shard_map/jit(cholesky)/cholesky | solution.py:63
  338.0 9.8 %custom-call.60 = f32[1,128,128]{1,2,0:T(8,128)S(1)} custom-call(f32[1,128,128]{2,1,0:T(8,128)S(1)} %get-tuple-element.25), custom_call_target="InvertDiagBlocksLowerTriangular" | custom-call | tf_op jit(solution)/shard_map/jit(cholesky)/cholesky | solution.py:63
  347.9 1.2 convolution_dynamic-update-slice_fusion
  349.1 2.1 convolution_subtract_fusion.1
  351.2 11.7 %cholesky.466 = f32[128,128]{1,0:T(8,128)S(1)} custom-call(f32[128,128]{1,0:T(8,128)S(1)} %cholesky.586), custom_call_target="Cholesky" | custom-call | tf_op jit(solution)/shard_map/jit(cholesky)/cholesky | solution.py:63
  364.2 9.8 %custom-call.61 = f32[1,128,128]{1,2,0:T(8,128)S(1)} custom-call(f32[1,128,128]{2,1,0:T(8,128)S(1)} %get-tuple-element.22), custom_call_target="InvertDiagBlocksLowerTriangular" | custom-call | tf_op jit(solution)/shard_map/jit(cholesky)/cholesky | solution.py:63
  374.0 1.1 convolution_dynamic-update-slice_fusion.1
  375.1 2.3 convolution_subtract_fusion.2
  377.5 12.1 %cholesky.485 = f32[128,128]{1,0:T(8,128)S(1)} custom-call(f32[128,128]{1,0:T(8,128)S(1)} %cholesky.591), custom_call_target="Cholesky" | custom-call | tf_op jit(solution)/shard_map/jit(cholesky)/cholesky | solution.py:63
  390.2 0.7 compare_reduce_fusion.4
  390.9 9.8 %custom-call.62 = f32[1,128,128]{1,2,0:T(8,128)S(1)} custom-call(f32[1,128,128]{2,1,0:T(8,128)S(1)} %get-tuple-element.19), custom_call_target="InvertDiagBlocksLowerTriangular" | custom-call | tf_op jit(solution)/shard_map/jit(cholesky)/cholesky | solution.py:63
  400.7 1.1 convolution_dynamic-update-slice_fusion.2
  401.8 2.3 convolution_subtract_fusion.3
  404.1 11.7 %cholesky.504 = f32[128,128]{1,0:T(8,128)S(1)} custom-call(f32[128,128]{1,0:T(8,128)S(1)} %cholesky.596), custom_call_target="Cholesky" | custom-call | tf_op jit(solution)/shard_map/jit(cholesky)/cholesky | solution.py:63
  416.5 0.7 compare_reduce_fusion.3
  417.2 10.0 %custom-call.63 = f32[1,128,128]{1,2,0:T(8,128)S(1)} custom-call(f32[1,128,128]{2,1,0:T(8,128)S(1)} %get-tuple-element.16), custom_call_target="InvertDiagBlocksLowerTriangular" | custom-call | tf_op jit(solution)/shard_map/jit(cholesky)/cholesky | solution.py:63
  427.2 1.0 convolution_dynamic-update-slice_fusion.3
  428.1 2.3 convolution_subtract_fusion.4
  430.4 11.7 %cholesky.524 = f32[128,128]{1,0:T(8,128)S(1)} custom-call(f32[128,128]{1,0:T(8,128)S(1)} %cholesky.601), custom_call_target="Cholesky" | custom-call | tf_op jit(solution)/shard_map/jit(cholesky)/cholesky | solution.py:63
  443.4 9.8 %custom-call.64 = f32[1,128,128]{1,2,0:T(8,128)S(1)} custom-call(f32[1,128,128]{2,1,0:T(8,128)S(1)} %get-tuple-element.13), custom_call_target="InvertDiagBlocksLowerTriangular" | custom-call | tf_op jit(solution)/shard_map/jit(cholesky)/cholesky | solution.py:63
  453.2 0.9 convolution_dynamic-update-slice_fusion.4
  454.2 2.1 convolution_subtract_fusion.5
  456.3 11.9 %cholesky.544 = f32[128,128]{1,0:T(8,128)S(1)} custom-call(f32[128,128]{1,0:T(8,128)S(1)} %cholesky.606), custom_call_target="Cholesky" | custom-call | tf_op jit(solution)/shard_map/jit(cholesky)/cholesky | solution.py:63
  469.4 9.8 %custom-call.65 = f32[1,128,128]{1,2,0:T(8,128)S(1)} custom-call(f32[1,128,128]{2,1,0:T(8,128)S(1)} %get-tuple-element.10), custom_call_target="InvertDiagBlocksLowerTriangular" | custom-call | tf_op jit(solution)/shard_map/jit(cholesky)/cholesky | solution.py:63
  479.2 0.8 convolution_dynamic-update-slice_fusion.5
  480.1 1.8 convolution_subtract_fusion.6
  481.9 11.7 %cholesky.562 = f32[128,128]{1,0:T(8,128)S(1)} custom-call(f32[128,128]{1,0:T(8,128)S(1)} %convolution_subtract_fusion.6), custom_call_target="Cholesky" | custom-call | tf_op jit(solution)/shard_map/jit(cholesky)/cholesky | solution.py:63
  494.2 0.7 compare_reduce_fusion
  500.5 4.8 select_bitcast_fusion
  505.3 5.3 %copy.11 = f32[1024,1024]{1,0:T(8,128)} copy(f32[1024,1024]{0,1:T(8,128)} %select_bitcast_fusion) | data formatting | bytes 8388608 | tf_op jit(solution)/shard_map/transpose | solution.py:63
  (30 shorter events, 7.3 us)
Async XLA Ops:
  6.5 42.2 %all-gather.2.cloned.1.call-start = ((), (), s32[]{:S(2)}) async-start(), calls=%async_computation | async-start | bytes 1966080 | tf_op jit(solution)/shard_map/all_gather | solution.py:46
  7.3 278.4 %all-reduce.3.cloned.1.call-start = ((), (), s32[]{:S(2)}) async-start(), calls=%async_computation.1 | async-start | bytes 8388608 | tf_op jit(solution)/shard_map/psum | solution.py:62
  127.3 4.4 copy-start.2
  129.7 2.0 copy-start.1
  295.6 1.9 copy-start
Sparse Core Ops, SparseCore 0:
  8.9 39.7 all-gather.1
  144.5 141.1 all-reduce.2
where the time goes:
time: 518 us
  other arithmetic  185 us (36%)
  waiting for transfers between devices  182 us (35%)
  matrix products  111 us (21%)
  local copies, waits for them, and re-layouts  20.8 us (4%)
  between operations  18.9 us (4%)
    another operation x30, other arithmetic, shards(): return jnp.linalg.cholesky(total).T  172 us
    psum x1, waiting for transfers between devices, shards(): total = lax.psum(contribution, ('land', 'rows'))  141 us
    dot_general x2, matrix products, nngp_kernel(): lax.dot_general(left, right, (((1,), (1,)), ((), ())), preferred_element_...  85.8 us
    all_gather x1, waiting for transfers between devices, shards(): gathered = lax.all_gather(landmarks, 'land', axis=0, tiled=True)  39.6 us
    another operation x14, matrix products, shards(): return jnp.linalg.cholesky(total).T  22.9 us
  transfers between devices with their start and end apart: 2, of which 2 were waited for; matrix products, arithmetic and copies ran while one was open for 0% of the time, Pallas kernels for 0%

commit v1 on v0

v1 whole, which is shorter than its diff:
```python
import functools
import math

import jax
import jax.numpy as jnp
from jax import lax
from jax.experimental import pallas as pl
from jax.experimental.pallas import tpu as pltpu
from jax.sharding import PartitionSpec as P

LAYERS = 6
SCALE_SQ = 1.0 / 32.0
RIDGE = 0.1
EPS = 1e-06
HI = lax.Precision.HIGHEST
B = 128
W = 16
TINY = 1e-30

ARC = (0.9428362797873839, 0.04684592969277604, 0.008663018923508323, 1.324670644556325e-05, 0.0016412996811995852)
KEEP = 1.0 / (1.0 + SCALE_SQ)
ARC = tuple(c * SCALE_SQ * KEEP / math.pi for c in ARC)
GROWTH = (1.0 + SCALE_SQ) ** LAYERS


def recursion(c):
    for _ in range(LAYERS):
        w = jnp.maximum(1.0 - jnp.abs(c), TINY)
        t = (w * w) * lax.rsqrt(w)
        poly = ARC[4]
        for a in ARC[3::-1]:
            poly = poly * w + a
        c = jnp.maximum(c, KEEP * c) + t * poly
    return c


def squares(x):
    wide = x.astype(jnp.float32)
    wide = wide * wide
    hi = wide.astype(jnp.bfloat16)
    return hi, (wide - hi.astype(jnp.float32)).astype(jnp.bfloat16)


def nt(a, b):
    return lax.dot_general(a, b, (((1,), (1,)), ((), ())), preferred_element_type=jnp.float32)


def squares_mean_column(x):
    ones = jnp.ones((B, x.shape[1]), jnp.bfloat16)
    hi, lo = squares(x)
    return (nt(hi, ones) + nt(lo, ones)) / x.shape[1] + EPS


def squares_mean_row(x):
    ones = jnp.ones((8, x.shape[1]), jnp.bfloat16)
    hi, lo = squares(x)
    return (nt(ones, hi) + nt(ones, lo)) / x.shape[1] + EPS


def spread(column, lanes):
    return jnp.concatenate([column] * (lanes // B), axis=1)


def gram_kernel(all_points, chunk, pos_ref, emb_ref, marks_ref, own_ref, out_ref, k_ref, x_ref, vq_ref, ridge_ref):
    n, e = marks_ref.shape
    m = emb_ref.shape[0]
    share = own_ref.shape[0]
    uq = squares_mean_row(emb_ref[...])
    u_inv = lax.rsqrt(uq)
    u_root = uq * u_inv
    vq_ref[...] = squares_mean_column(marks_ref[...])

    def block(j, _):
        row = pl.multiple_of(j * B, B)
        k_ref[...] = nt(marks_ref[pl.ds(row, B), :], emb_ref[...])

        def part(i, _):
            r = pl.multiple_of(i * chunk, chunk)
            vq = vq_ref[pl.ds(row + r, chunk), :]
            v_inv = lax.rsqrt(vq)
            v_root = vq * v_inv
            up = jnp.concatenate([u_inv] * (chunk // 8), axis=0)
            ur = jnp.concatenate([u_root] * (chunk // 8), axis=0)
            c = k_ref[pl.ds(r, chunk), :] * up * spread(v_inv * (1.0 / e), m)
            c = recursion(c)
            x_ref[pl.ds(row + r, chunk), :] = (c * ur * spread(v_root * GROWTH, m)).astype(jnp.bfloat16)
            return 0

        lax.fori_loop(0, B // chunk, part, 0)
        return 0

    lax.fori_loop(0, n // B, block, 0)

    oq = squares_mean_column(own_ref[...])
    vr = squares_mean_row(marks_ref[...])
    o_inv, v_inv = lax.rsqrt(oq), lax.rsqrt(vr)
    k_own = nt(own_ref[...], marks_ref[...])
    for i in range(share // 8):
        oi = o_inv[8 * i : 8 * i + 8]
        c = recursion(k_own[8 * i : 8 * i + 8] * v_inv * spread(oi * (1.0 / e), n))
        root = oq[8 * i : 8 * i + 8] * oi
        ridge_ref[8 * i : 8 * i + 8, :] = c * (vr * v_inv) * spread(root * (RIDGE * GROWTH), n)

    pos = pos_ref[0]
    row_block = pos // B
    offset = pos % B
    for j in range(n // B):
        start = j * (j + 1) // 2 * B
        out_ref[start : start + (j + 1) * B, :] = nt(
            x_ref[: (j + 1) * B, :], x_ref[j * B : (j + 1) * B, :]
        ) * (1.0 / all_points)

        @pl.when(row_block <= j)
        def _():
            at = pl.ds(pl.multiple_of(start + row_block * B + offset, share), share)
            out_ref[at, :] = out_ref[at, :] + ridge_ref[:, j * B : (j + 1) * B]


def local_normal(position, embeddings, gathered, own, all_points):
    n = gathered.shape[0]
    nb = n // B
    vmem = pl.BlockSpec(memory_space=pltpu.VMEM)
    return pl.pallas_call(
        functools.partial(gram_kernel, all_points, 16),
        out_shape=jax.ShapeDtypeStruct((nb * (nb + 1) // 2 * B, B), jnp.float32),
        in_specs=[pl.BlockSpec(memory_space=pltpu.SMEM), vmem, vmem, vmem],
        out_specs=vmem,
        scratch_shapes=[
            pltpu.VMEM((B, embeddings.shape[0]), jnp.float32),
            pltpu.VMEM((n, embeddings.shape[0]), jnp.bfloat16),
            pltpu.VMEM((n, B), jnp.float32),
            pltpu.VMEM((own.shape[0], n), jnp.float32),
        ],
        compiler_params=pltpu.CompilerParams(vmem_limit_bytes=40 << 20),
        name="gram",
    )(position.reshape(1), embeddings, gathered, own)


def factor_block(d):
    rows8 = lax.broadcasted_iota(jnp.int32, (8, 128), 0)
    eye = (lax.broadcasted_iota(jnp.int32, (B, B), 0) == lax.broadcasted_iota(jnp.int32, (B, B), 1)).astype(jnp.float32)
    n = B // W
    g = W // 8
    left = [d[8 * i:8 * i + 8] for i in range(B // 8)]
    right = [eye[8 * i:8 * i + 8] for i in range(B // 8)]
    for p in range(n):
        base = p * g
        last = p == n - 1
        groups = list(range(base, base + (g if last else 2 * g)))
        col = [[None] * len(groups) for _ in range(W)]
        for i in range(W):
            for t, r in enumerate(groups):
                if t < g and t < i // 8:
                    continue
                lane = p * W + i
                col[i][t] = jnp.broadcast_to(left[r][:, lane:lane + 1], (8, 128))
        diag = [jnp.ones((8, 128), jnp.float32) for _ in range(g)]
        for j in range(W):
            tj, sj = j // 8, j % 8
            pivot = jnp.broadcast_to(col[j][tj][sj:sj + 1], (8, 128))
            diag[tj] = jnp.where(rows8 == sj, pivot, diag[tj])
            inv = 1.0 / pivot
            coefs = {}
            for i in range(j + 1, W):
                coefs[i] = jnp.broadcast_to(col[j][i // 8][i % 8:i % 8 + 1], (8, 128))
            scaled = [None] * len(groups)
            for t in range(len(groups)):
                if col[j][t] is None:
                    continue
                scaled[t] = col[j][t] * inv
            for i in range(j + 1, W):
                for t in range(len(groups)):
                    if col[i][t] is None:
                        continue
                    if i == j + 1:
                        col[i][t] = col[i][t] - (col[j][t] * coefs[i]) * inv
                    else:
                        col[i][t] = col[i][t] - scaled[t] * coefs[i]
            rl = jnp.broadcast_to(left[base + tj][sj:sj + 1], (8, 128))
            rr = jnp.broadcast_to(right[base + tj][sj:sj + 1], (8, 128))
            for t, r in enumerate(groups):
                if scaled[t] is None:
                    continue
                c = scaled[t]
                if t == tj:
                    if sj == 7:
                        continue
                    c = jnp.where(rows8 > sj, c, 0.0)
                left[r] = left[r] - c * rl
                right[r] = right[r] - c * rr
        for t in range(g):
            s = lax.rsqrt(diag[t])
            left[base + t] = left[base + t] * s
            right[base + t] = right[base + t] * s
        rest = (n - p - 2) * W
        if rest > 0:
            ul = jnp.concatenate(left[base:base + g], 0)
            ur = jnp.concatenate(right[base:base + g], 0)
            u = jnp.concatenate([ul, ur], 1)
            lo_row = (p + 2) * W
            upd = lax.dot_general(ul, u, (((0,), (0,)), ((), ())), preferred_element_type=jnp.float32, precision=HI)
            for r in range(lo_row // 8, B // 8):
                left[r] = left[r] - upd[8 * r:8 * r + 8, :128]
                right[r] = right[r] - upd[8 * r:8 * r + 8, 128:]
    u = jnp.concatenate(left, 0)
    w = jnp.concatenate(right, 0)
    tri = lax.broadcasted_iota(jnp.int32, (B, B), 0) <= lax.broadcasted_iota(jnp.int32, (B, B), 1)
    return jnp.where(tri, u, 0.0), w

def chol_kernel(a_ref, o_ref, s_ref, w_ref):
    n = o_ref.shape[0] // B
    o_ref[...] = jnp.zeros_like(o_ref)
    def step(k, _):
        for i in range(n):
            @pl.when(k == i)
            def _():
                blk = jnp.concatenate([a_ref[(j * (j + 1) // 2 + i) * B:(j * (j + 1) // 2 + i + 1) * B, :] for j in range(i, n)], 1)
                if i:
                    l = o_ref[:i * B, i * B:(i + 1) * B]
                    r = o_ref[:i * B, i * B:]
                    blk = blk - lax.dot_general(l, r, (((0,), (0,)), ((), ())), preferred_element_type=jnp.float32, precision=HI)
                s_ref[:, :(n - i) * B] = blk
        u, w = factor_block(s_ref[:, :B])
        s_ref[:, :B] = u
        w_ref[...] = w
        for i in range(n):
            @pl.when(k == i)
            def _():
                o_ref[i * B:(i + 1) * B, i * B:(i + 1) * B] = s_ref[:, :B]
                if i < n - 1:
                    o_ref[i * B:(i + 1) * B, (i + 1) * B:] = lax.dot_general(w_ref[...], s_ref[:, B:(n - i) * B], (((1,), (0,)), ((), ())), preferred_element_type=jnp.float32, precision=HI)
        return 0
    lax.fori_loop(0, n, step, 0)


def cholesky_upper(packed, n):
    vmem = pl.BlockSpec(memory_space=pltpu.VMEM)
    return pl.pallas_call(
        chol_kernel,
        out_shape=jax.ShapeDtypeStruct((n, n), jnp.float32),
        in_specs=[vmem],
        out_specs=vmem,
        scratch_shapes=[pltpu.VMEM((B, n), jnp.float32), pltpu.VMEM((B, B), jnp.float32)],
        compiler_params=pltpu.CompilerParams(vmem_limit_bytes=40 << 20),
        name="chol",
    )(packed)


def bits_of(axis):
    return range(lax.axis_size(axis).bit_length() - 1)


def swap(x, axis, bit):
    return lax.ppermute(x, axis, [(i, i ^ (1 << bit)) for i in range(lax.axis_size(axis))])


def my_bit(axis, bit):
    return (lax.axis_index(axis) >> bit) & 1


def all_reduce(x):
    stages = [(axis, bit) for axis in ("rows", "land") for bit in bits_of(axis)]
    for axis, bit in stages:
        half = x.shape[0] // 2
        mine = my_bit(axis, bit)
        send = lax.dynamic_slice_in_dim(x, (1 - mine) * half, half, 0)
        keep = lax.dynamic_slice_in_dim(x, mine * half, half, 0)
        x = keep + swap(send, axis, bit)
    for axis, bit in stages[::-1]:
        other = swap(x, axis, bit)
        first = my_bit(axis, bit) == 0
        x = jnp.concatenate([jnp.where(first, x, other), jnp.where(first, other, x)], 0)
    return x


def gather_marks(landmarks):
    rows = lax.axis_size("rows")
    share = landmarks.shape[0] // rows
    x = lax.dynamic_slice_in_dim(landmarks, lax.axis_index("rows") * share, share, 0)
    x = x.reshape(1, 1, share, landmarks.shape[1])
    for dim, axis in ((0, "land"), (1, "rows")):
        for bit in bits_of(axis) if axis == "land" else list(bits_of(axis)):
            other = swap(x, axis, bit)
            first = my_bit(axis, bit) == 0
            x = jnp.concatenate([jnp.where(first, x, other), jnp.where(first, other, x)], dim)
    return x.reshape(-1, landmarks.shape[1])


def shards(embeddings, landmarks):
    land, rows = lax.axis_size("land"), lax.axis_size("rows")
    n = landmarks.shape[0] * land
    share = n // (land * rows)
    position = (lax.axis_index("land") * rows + lax.axis_index("rows")) * share
    own = lax.dynamic_slice_in_dim(landmarks, lax.axis_index("rows") * share, share, 0)
    gathered = gather_marks(landmarks)
    packed = local_normal(position, embeddings, gathered, own, embeddings.shape[0] * land * rows)
    return cholesky_upper(all_reduce(packed), n)


def solution(mesh):
    in_specs = (P(("land", "rows"), None), P("land", None))
    return jax.shard_map(shards, mesh=mesh, in_specs=in_specs, out_specs=P(), check_vma=False)
```

time: 518 us -> 187 us (0.36)
  other arithmetic: 185 us -> 3.44 us
  matrix products: 111 us -> 0 us
  waiting for transfers between devices: 182 us -> 82.7 us
  Pallas kernels: 0 us -> 68.2 us
  starting transfers between devices: 0.04 us -> 29.2 us
  between operations: 18.9 us -> 0.24 us
  local copies, waits for them, and re-layouts: 20.8 us -> 3.06 us
    another operation x30 -> x0, other arithmetic: 172 us -> none  [shards(): return jnp.linalg.cholesky(total).T]
    psum x1 -> x0, waiting for transfers between devices: 141 us -> none  [shards(): total = lax.psum(contribution, ('land', 'rows'))]
    dot_general x3 -> x0, matrix products: 88.2 us -> none  [the longest x2 85.8 us: nngp_kernel(): lax.dot_general(left, right, (((1,), (1,)), ((), ())), preferred_element_...]
    ppermute x0 -> x15, waiting for transfers between devices: none -> 82.7 us  [swap(): lax.ppermute(x, axis, [(i, i ^ 1 << bit) for i in range(lax.axis_size(axi...]
    pallas_call x0 -> x2, Pallas kernels: none -> 68.2 us  [the longest x1 35.7 us: cholesky_upper(): pl.pallas_call(chol_kernel, out_shape=jax.ShapeDtypeStruct((n, n), jnp.fl...]
    all_gather x1 -> x0, waiting for transfers between devices: 39.6 us -> none  [shards(): gathered = lax.all_gather(landmarks, 'land', axis=0, tiled=True)]
    ppermute x0 -> x15, starting transfers between devices: none -> 29.2 us  [swap(): lax.ppermute(x, axis, [(i, i ^ 1 << bit) for i in range(lax.axis_size(axi...]
    another operation x14 -> x0, matrix products: 22.9 us -> none  [shards(): return jnp.linalg.cholesky(total).T]
  transfers between devices with their start and end apart: 2 -> 15, of which waited for: 2 -> 15; matrix products, arithmetic and copies ran while one was open for 0% -> 0% of each run, Pallas kernels for 0% -> 0%
where the time goes in v1:
time: 187 us
  waiting for transfers between devices  82.7 us (44%)
  Pallas kernels  68.2 us (36%)
  starting transfers between devices  29.2 us (16%)
  other arithmetic  3.44 us (2%)
  local copies, waits for them, and re-layouts  3.06 us (2%)
    ppermute x15, waiting for transfers between devices, swap(): lax.ppermute(x, axis, [(i, i ^ 1 << bit) for i in range(lax.axis_size(axi...  82.7 us
    pallas_call x1, Pallas kernels, cholesky_upper(): pl.pallas_call(chol_kernel, out_shape=jax.ShapeDtypeStruct((n, n), jnp.fl...  35.7 us
    pallas_call x1, Pallas kernels, local_normal(): pl.pallas_call(functools.partial(gram_kernel, all_points, 16), out_shape=...  32.5 us
    ppermute x15, starting transfers between devices, swap(): lax.ppermute(x, axis, [(i, i ^ 1 << bit) for i in range(lax.axis_size(axi...  29.2 us
  transfers between devices with their start and end apart: 15, of which 15 were waited for; matrix products, arithmetic and copies ran while one was open for 0% of the time, Pallas kernels for 0%

profile of v1, /device:TPU:0, one launch (start us, length us, event | category | flops | bytes accessed | tf_op | source)
XLA Modules:
  0.0 186.8 jit_solution(14629520613136416903)
XLA Ops:
  0.0 0.8 fusion
  0.8 3.0 %collective-permute-start = (bf16[1,1,32,768]{3,2,1,0:T(8,128)(2,1)S(1)}, bf16[1,1,32,768]{3,2,1,0:T(8,128)(2,1)S(1)}, u32[]{:S(2)}, u32[]{:S(2)}) collective-permute-start(bf16[1,1,32,768]{3,2,1,0:T(8,128)(2,1)S(1)} %fusion), channel_id=1, source_target_pairs={{0,8},{8,0},{16,24},{24,16},{1,9},{9,1},{17,25},{25,17},{2,10},{10... | collective-permute-start | bytes 147464 | tf_op jit(solution)/shard_map/ppermute | solution.py:254
  3.8 2.1 %collective-permute-done = bf16[1,1,32,768]{3,2,1,0:T(8,128)(2,1)S(1)} collective-permute-done((bf16[1,1,32,768]{3,2,1,0:T(8,128)(2,1)S(1)}, bf16[1,1,32,768]{3,2,1,0:T(8,128)(2,1)S(1)}, u32[]{:S(2)}, u32[]{:S(2)}) %collective-permute-start) | collective-permute-done | bytes 49184 | tf_op jit(solution)/shard_map/ppermute | solution.py:254
  5.9 0.8 broadcast_select_fusion.17
  6.7 3.1 %collective-permute-start.1 = (bf16[2,1,32,768]{3,2,1,0:T(8,128)(2,1)S(1)}, bf16[2,1,32,768]{3,2,1,0:T(8,128)(2,1)S(1)}, u32[]{:S(2)}, u32[]{:S(2)}) collective-permute-start(bf16[2,1,32,768]{3,2,1,0:T(8,128)(2,1)S(1)} %pad_maximum_fusion.9), channel_id=1, source_target_pairs={{0,16},{8,24},{16,0},{24,8},{1,17},{9,25},{17,1},{25,9},{2,18},{10... | collective-permute-start | bytes 294920 | tf_op jit(solution)/shard_map/ppermute | solution.py:254
  9.8 2.7 %collective-permute-done.1 = bf16[2,1,32,768]{3,2,1,0:T(8,128)(2,1)S(1)} collective-permute-done((bf16[2,1,32,768]{3,2,1,0:T(8,128)(2,1)S(1)}, bf16[2,1,32,768]{3,2,1,0:T(8,128)(2,1)S(1)}, u32[]{:S(2)}, u32[]{:S(2)}) %collective-permute-start.1) | collective-permute-done | bytes 98336 | tf_op jit(solution)/shard_map/ppermute | solution.py:254
  12.6 0.1 collective-permute-start.2
  12.7 1.4 collective-permute-done.2
  14.2 1.8 collective-permute-start.3
  16.0 9.4 %collective-permute-done.3 = bf16[4,2,32,768]{3,2,1,0:T(8,128)(2,1)S(1)} collective-permute-done((bf16[4,2,32,768]{3,2,1,0:T(8,128)(2,1)S(1)}, bf16[4,2,32,768]{3,2,1,0:T(8,128)(2,1)S(1)}, u32[]{:S(2)}, u32[]{:S(2)}) %collective-permute-start.3) | collective-permute-done | bytes 393248 | tf_op jit(solution)/shard_map/ppermute | solution.py:254
  25.4 0.1 broadcast_select_fusion.5
  25.5 0.1 pad_maximum_fusion.3
  25.5 1.8 collective-permute-start.4
  27.4 0.8 constant_dynamic-slice_fusion.5.own_ref
  28.2 16.2 %collective-permute-done.4 = bf16[4,4,32,768]{3,2,1,0:T(8,128)(2,1)S(1)} collective-permute-done((bf16[4,4,32,768]{3,2,1,0:T(8,128)(2,1)S(1)}, bf16[4,4,32,768]{3,2,1,0:T(8,128)(2,1)S(1)}, u32[]{:S(2)}, u32[]{:S(2)}) %collective-permute-start.4) | collective-permute-done | bytes 786464 | tf_op jit(solution)/shard_map/ppermute | solution.py:254
  44.4 0.1 broadcast_select_fusion.1
  44.5 0.0 copy-start
  44.5 0.1 pad_maximum_fusion.1
  44.6 1.3 copy-done
  45.9 32.5 %gram.1 = f32[4608,128]{1,0:T(8,128)S(1)} custom-call(s32[1]{0:T(128)} %bitcast.pos_ref, bf16[1024,768]{1,0:T(8,128)(2,1)S(1)} %copy-done, bf16[1024,768]{1,0:T(8,128)(2,1)S(1)} %bitcast.6, bf16[32,768]{1,0:T(8,128)(2,1)S(1)} %constant_dynamic-slice_fusion.5.own_ref), custom_call_target="tpu_custom_call" | custom-call | tf_op jit(solution)/shard_map/gram/pallas_call | solution.py:123
  78.4 0.1 constant_dynamic-slice_fusion.4
  78.5 0.1 collective-permute-start.5
  78.6 3.0 %collective-permute-done.5 = f32[2304,128]{1,0:T(8,128)} collective-permute-done((f32[2304,128]{1,0:T(8,128)S(1)}, f32[2304,128]{1,0:T(8,128)}, u32[]{:S(2)}, u32[]{:S(2)}) %collective-permute-start.5) | collective-permute-done | bytes 1179680 | tf_op jit(solution)/shard_map/ppermute | solution.py:254
  81.5 1.4 dynamic-slice_add_fusion
  83.0 1.8 collective-permute-start.6
  84.8 13.7 %collective-permute-done.6 = f32[1152,128]{1,0:T(8,128)S(1)} collective-permute-done((f32[1152,128]{1,0:T(8,128)S(1)}, f32[1152,128]{1,0:T(8,128)S(1)}, u32[]{:S(2)}, u32[]{:S(2)}) %collective-permute-start.6) | collective-permute-done | bytes 589856 | tf_op jit(solution)/shard_map/ppermute | solution.py:254
  98.4 0.1 dynamic-slice_add_fusion.1
  98.5 1.8 collective-permute-start.7
  100.3 6.5 %collective-permute-done.7 = f32[576,128]{1,0:T(8,128)S(1)} collective-permute-done((f32[576,128]{1,0:T(8,128)S(1)}, f32[576,128]{1,0:T(8,128)S(1)}, u32[]{:S(2)}, u32[]{:S(2)}) %collective-permute-start.7) | collective-permute-done | bytes 294944 | tf_op jit(solution)/shard_map/ppermute | solution.py:254
  106.9 2.0 %collective-permute-start.8 = (f32[288,128]{1,0:T(8,128)S(1)}, f32[288,128]{1,0:T(8,128)S(1)}, u32[]{:S(2)}, u32[]{:S(2)}) collective-permute-start(f32[288,128]{1,0:T(8,128)S(1)} %constant_dynamic-slice_fusion.1), channel_id=1, source_target_pairs={{0,8},{8,0},{16,24},{24,16},{1,9},{9,1},{17,25},{25,17},{2,10},{10... | collective-permute-start | bytes 442376 | tf_op jit(solution)/shard_map/ppermute | solution.py:254
  108.9 3.2 %collective-permute-done.8 = f32[288,128]{1,0:T(8,128)S(1)} collective-permute-done((f32[288,128]{1,0:T(8,128)S(1)}, f32[288,128]{1,0:T(8,128)S(1)}, u32[]{:S(2)}, u32[]{:S(2)}) %collective-permute-start.8) | collective-permute-done | bytes 147488 | tf_op jit(solution)/shard_map/ppermute | solution.py:254
  112.1 3.4 %collective-permute-start.9 = (f32[144,128]{1,0:T(8,128)S(1)}, f32[144,128]{1,0:T(8,128)S(1)}, u32[]{:S(2)}, u32[]{:S(2)}) collective-permute-start(f32[144,128]{1,0:T(8,128)S(1)} %constant_dynamic-slice_fusion), channel_id=1, source_target_pairs={{0,16},{8,24},{16,0},{24,8},{1,17},{9,25},{17,1},{25,9},{2,18},{10... | collective-permute-start | bytes 221192 | tf_op jit(solution)/shard_map/ppermute | solution.py:254
  115.5 2.3 %collective-permute-done.9 = f32[144,128]{1,0:T(8,128)S(1)} collective-permute-done((f32[144,128]{1,0:T(8,128)S(1)}, f32[144,128]{1,0:T(8,128)S(1)}, u32[]{:S(2)}, u32[]{:S(2)}) %collective-permute-start.9) | collective-permute-done | bytes 73760 | tf_op jit(solution)/shard_map/ppermute | solution.py:254
  117.8 3.0 %collective-permute-start.10 = (f32[144,128]{1,0:T(8,128)S(1)}, f32[144,128]{1,0:T(8,128)S(1)}, u32[]{:S(2)}, u32[]{:S(2)}) collective-permute-start(f32[144,128]{1,0:T(8,128)S(1)} %dynamic-slice_add_fusion.4), channel_id=1, source_target_pairs={{0,16},{8,24},{16,0},{24,8},{1,17},{9,25},{17,1},{25,9},{2,18},{10... | collective-permute-start | bytes 221192 | tf_op jit(solution)/shard_map/ppermute | solution.py:254
  120.8 2.7 %collective-permute-done.10 = f32[144,128]{1,0:T(8,128)S(1)} collective-permute-done((f32[144,128]{1,0:T(8,128)S(1)}, f32[144,128]{1,0:T(8,128)S(1)}, u32[]{:S(2)}, u32[]{:S(2)}) %collective-permute-start.10) | collective-permute-done | bytes 73760 | tf_op jit(solution)/shard_map/ppermute | solution.py:254
  123.5 4.2 %collective-permute-start.11 = (f32[288,128]{1,0:T(8,128)S(1)}, f32[288,128]{1,0:T(8,128)S(1)}, u32[]{:S(2)}, u32[]{:S(2)}) collective-permute-start(f32[288,128]{1,0:T(8,128)S(1)} %pad_maximum_fusion.8), channel_id=1, source_target_pairs={{0,8},{8,0},{16,24},{24,16},{1,9},{9,1},{17,25},{25,17},{2,10},{10... | collective-permute-start | bytes 442376 | tf_op jit(solution)/shard_map/ppermute | solution.py:254
  127.7 3.1 %collective-permute-done.11 = f32[288,128]{1,0:T(8,128)S(1)} collective-permute-done((f32[288,128]{1,0:T(8,128)S(1)}, f32[288,128]{1,0:T(8,128)S(1)}, u32[]{:S(2)}, u32[]{:S(2)}) %collective-permute-start.11) | collective-permute-done | bytes 147488 | tf_op jit(solution)/shard_map/ppermute | solution.py:254
  130.9 1.6 collective-permute-start.12
  132.5 5.2 %collective-permute-done.12 = f32[576,128]{1,0:T(8,128)S(1)} collective-permute-done((f32[576,128]{1,0:T(8,128)S(1)}, f32[576,128]{1,0:T(8,128)S(1)}, u32[]{:S(2)}, u32[]{:S(2)}) %collective-permute-start.12) | collective-permute-done | bytes 294944 | tf_op jit(solution)/shard_map/ppermute | solution.py:254
  137.8 1.6 collective-permute-start.13
  139.3 8.4 %collective-permute-done.13 = f32[1152,128]{1,0:T(8,128)S(1)} collective-permute-done((f32[1152,128]{1,0:T(8,128)S(1)}, f32[1152,128]{1,0:T(8,128)S(1)}, u32[]{:S(2)}, u32[]{:S(2)}) %collective-permute-start.13) | collective-permute-done | bytes 589856 | tf_op jit(solution)/shard_map/ppermute | solution.py:254
  147.7 0.1 broadcast_select_fusion.7
  147.8 0.1 pad_maximum_fusion.2
  147.9 0.1 collective-permute-start.14
  148.0 2.8 %collective-permute-done.14 = f32[2304,128]{1,0:T(8,128)S(1)} collective-permute-done((f32[2304,128]{1,0:T(8,128)S(1)}, f32[2304,128]{1,0:T(8,128)S(1)}, u32[]{:S(2)}, u32[]{:S(2)}) %collective-permute-start.14) | collective-permute-done | bytes 1179680 | tf_op jit(solution)/shard_map/ppermute | solution.py:254
  150.8 0.2 broadcast_select_fusion.3
  151.0 0.2 pad_maximum_fusion.a_ref
  151.1 35.7 %chol.1 = f32[1024,1024]{1,0:T(8,128)} custom-call(f32[4608,128]{1,0:T(8,128)S(1)} %pad_maximum_fusion.a_ref), custom_call_target="tpu_custom_call" | custom-call | tf_op jit(solution)/shard_map/chol/pallas_call | solution.py:238
  (18 shorter events, 0.4 us)
Async XLA Ops:
  0.8 5.1 %collective-permute-start = (bf16[1,1,32,768]{3,2,1,0:T(8,128)(2,1)S(1)}, bf16[1,1,32,768]{3,2,1,0:T(8,128)(2,1)S(1)}, u32[]{:S(2)}, u32[]{:S(2)}) collective-permute-start(bf16[1,1,32,768]{3,2,1,0:T(8,128)(2,1)S(1)} %fusion), channel_id=1, source_target_pairs={{0,8},{8,0},{16,24},{24,16},{1,9},{9,1},{17,25},{25,17},{2,10},{10... | collective-permute-start | bytes 147464 | tf_op jit(solution)/shard_map/ppermute | solution.py:254
  6.7 5.8 %collective-permute-start.1 = (bf16[2,1,32,768]{3,2,1,0:T(8,128)(2,1)S(1)}, bf16[2,1,32,768]{3,2,1,0:T(8,128)(2,1)S(1)}, u32[]{:S(2)}, u32[]{:S(2)}) collective-permute-start(bf16[2,1,32,768]{3,2,1,0:T(8,128)(2,1)S(1)} %pad_maximum_fusion.9), channel_id=1, source_target_pairs={{0,16},{8,24},{16,0},{24,8},{1,17},{9,25},{17,1},{25,9},{2,18},{10... | collective-permute-start | bytes 294920 | tf_op jit(solution)/shard_map/ppermute | solution.py:254
  12.6 1.5 collective-permute-start.2
  14.2 11.2 %collective-permute-start.3 = (bf16[4,2,32,768]{3,2,1,0:T(8,128)(2,1)S(1)}, bf16[4,2,32,768]{3,2,1,0:T(8,128)(2,1)S(1)}, u32[]{:S(2)}, u32[]{:S(2)}) collective-permute-start(bf16[4,2,32,768]{3,2,1,0:T(8,128)(2,1)S(1)} %pad_maximum_fusion.5), channel_id=1, source_target_pairs={{0,2},{1,3},{2,0},{3,1},{4,6},{5,7},{6,4},{7,5},{8,10},{9,11},{10,... | collective-permute-start | bytes 1179656 | tf_op jit(solution)/shard_map/ppermute | solution.py:254
  25.5 18.8 %collective-permute-start.4 = (bf16[4,4,32,768]{3,2,1,0:T(8,128)(2,1)S(1)}, bf16[4,4,32,768]{3,2,1,0:T(8,128)(2,1)S(1)}, u32[]{:S(2)}, u32[]{:S(2)}) collective-permute-start(bf16[4,4,32,768]{3,2,1,0:T(8,128)(2,1)S(1)} %pad_maximum_fusion.3), channel_id=1, source_target_pairs={{0,4},{1,5},{2,6},{3,7},{4,0},{5,1},{6,2},{7,3},{8,12},{9,13},{10,... | collective-permute-start | bytes 2359304 | tf_op jit(solution)/shard_map/ppermute | solution.py:254
  44.5 1.4 copy-start
  78.5 3.0 %collective-permute-start.5 = (f32[2304,128]{1,0:T(8,128)S(1)}, f32[2304,128]{1,0:T(8,128)}, u32[]{:S(2)}, u32[]{:S(2)}) collective-permute-start(f32[2304,128]{1,0:T(8,128)S(1)} %constant_dynamic-slice_fusion.4), channel_id=1, source_target_pairs={{0,1},{1,0},{2,3},{3,2},{4,5},{5,4},{6,7},{7,6},{8,9},{9,8},{10,11... | collective-permute-start | bytes 3538952 | tf_op jit(solution)/shard_map/ppermute | solution.py:254
  83.0 15.4 %collective-permute-start.6 = (f32[1152,128]{1,0:T(8,128)S(1)}, f32[1152,128]{1,0:T(8,128)S(1)}, u32[]{:S(2)}, u32[]{:S(2)}) collective-permute-start(f32[1152,128]{1,0:T(8,128)S(1)} %constant_dynamic-slice_fusion.3), channel_id=1, source_target_pairs={{0,2},{1,3},{2,0},{3,1},{4,6},{5,7},{6,4},{7,5},{8,10},{9,11},{10,... | collective-permute-start | bytes 1769480 | tf_op jit(solution)/shard_map/ppermute | solution.py:254
  98.5 8.3 %collective-permute-start.7 = (f32[576,128]{1,0:T(8,128)S(1)}, f32[576,128]{1,0:T(8,128)S(1)}, u32[]{:S(2)}, u32[]{:S(2)}) collective-permute-start(f32[576,128]{1,0:T(8,128)S(1)} %constant_dynamic-slice_fusion.2), channel_id=1, source_target_pairs={{0,4},{1,5},{2,6},{3,7},{4,0},{5,1},{6,2},{7,3},{8,12},{9,13},{10,... | collective-permute-start | bytes 884744 | tf_op jit(solution)/shard_map/ppermute | solution.py:254
  106.9 5.2 %collective-permute-start.8 = (f32[288,128]{1,0:T(8,128)S(1)}, f32[288,128]{1,0:T(8,128)S(1)}, u32[]{:S(2)}, u32[]{:S(2)}) collective-permute-start(f32[288,128]{1,0:T(8,128)S(1)} %constant_dynamic-slice_fusion.1), channel_id=1, source_target_pairs={{0,8},{8,0},{16,24},{24,16},{1,9},{9,1},{17,25},{25,17},{2,10},{10... | collective-permute-start | bytes 442376 | tf_op jit(solution)/shard_map/ppermute | solution.py:254
  112.1 5.7 %collective-permute-start.9 = (f32[144,128]{1,0:T(8,128)S(1)}, f32[144,128]{1,0:T(8,128)S(1)}, u32[]{:S(2)}, u32[]{:S(2)}) collective-permute-start(f32[144,128]{1,0:T(8,128)S(1)} %constant_dynamic-slice_fusion), channel_id=1, source_target_pairs={{0,16},{8,24},{16,0},{24,8},{1,17},{9,25},{17,1},{25,9},{2,18},{10... | collective-permute-start | bytes 221192 | tf_op jit(solution)/shard_map/ppermute | solution.py:254
  117.8 5.7 %collective-permute-start.10 = (f32[144,128]{1,0:T(8,128)S(1)}, f32[144,128]{1,0:T(8,128)S(1)}, u32[]{:S(2)}, u32[]{:S(2)}) collective-permute-start(f32[144,128]{1,0:T(8,128)S(1)} %dynamic-slice_add_fusion.4), channel_id=1, source_target_pairs={{0,16},{8,24},{16,0},{24,8},{1,17},{9,25},{17,1},{25,9},{2,18},{10... | collective-permute-start | bytes 221192 | tf_op jit(solution)/shard_map/ppermute | solution.py:254
  123.5 7.3 %collective-permute-start.11 = (f32[288,128]{1,0:T(8,128)S(1)}, f32[288,128]{1,0:T(8,128)S(1)}, u32[]{:S(2)}, u32[]{:S(2)}) collective-permute-start(f32[288,128]{1,0:T(8,128)S(1)} %pad_maximum_fusion.8), channel_id=1, source_target_pairs={{0,8},{8,0},{16,24},{24,16},{1,9},{9,1},{17,25},{25,17},{2,10},{10... | collective-permute-start | bytes 442376 | tf_op jit(solution)/shard_map/ppermute | solution.py:254
  130.9 6.8 %collective-permute-start.12 = (f32[576,128]{1,0:T(8,128)S(1)}, f32[576,128]{1,0:T(8,128)S(1)}, u32[]{:S(2)}, u32[]{:S(2)}) collective-permute-start(f32[576,128]{1,0:T(8,128)S(1)} %pad_maximum_fusion.6), channel_id=1, source_target_pairs={{0,4},{1,5},{2,6},{3,7},{4,0},{5,1},{6,2},{7,3},{8,12},{9,13},{10,... | collective-permute-start | bytes 884744 | tf_op jit(solution)/shard_map/ppermute | solution.py:254
  137.8 9.9 %collective-permute-start.13 = (f32[1152,128]{1,0:T(8,128)S(1)}, f32[1152,128]{1,0:T(8,128)S(1)}, u32[]{:S(2)}, u32[]{:S(2)}) collective-permute-start(f32[1152,128]{1,0:T(8,128)S(1)} %pad_maximum_fusion.4), channel_id=1, source_target_pairs={{0,2},{1,3},{2,0},{3,1},{4,6},{5,7},{6,4},{7,5},{8,10},{9,11},{10,... | collective-permute-start | bytes 1769480 | tf_op jit(solution)/shard_map/ppermute | solution.py:254
  147.9 2.9 %collective-permute-start.14 = (f32[2304,128]{1,0:T(8,128)S(1)}, f32[2304,128]{1,0:T(8,128)S(1)}, u32[]{:S(2)}, u32[]{:S(2)}) collective-permute-start(f32[2304,128]{1,0:T(8,128)S(1)} %pad_maximum_fusion.2), channel_id=1, source_target_pairs={{0,1},{1,0},{2,3},{3,2},{4,5},{5,4},{6,7},{7,6},{8,9},{9,8},{10,11... | collective-permute-start | bytes 3538952 | tf_op jit(solution)/shard_map/ppermute | solution.py:254

commit v2 on v1

v2 whole, which is shorter than its diff:
```python
import functools
import math

import jax
import jax.numpy as jnp
from jax import lax
from jax.experimental import pallas as pl
from jax.experimental.pallas import tpu as pltpu
from jax.sharding import Mesh
from jax.sharding import PartitionSpec as P

LAYERS = 6
SCALE_SQ = 1.0 / 32.0
RIDGE = 0.1
EPS = 1e-06
HI = lax.Precision.HIGHEST
B = 128
W = 16
TINY = 1e-30

ARC = (0.9428362797873839, 0.04684592969277604, 0.008663018923508323, 1.324670644556325e-05, 0.0016412996811995852)
KEEP = 1.0 / (1.0 + SCALE_SQ)
ARC = tuple(c * SCALE_SQ * KEEP / math.pi for c in ARC)
GROWTH = (1.0 + SCALE_SQ) ** LAYERS


def recursion(c):
    for _ in range(LAYERS):
        w = jnp.maximum(1.0 - jnp.abs(c), TINY)
        t = (w * w) * lax.rsqrt(w)
        poly = ARC[4]
        for a in ARC[3::-1]:
            poly = poly * w + a
        c = jnp.maximum(c, KEEP * c) + t * poly
    return c


def squares(x):
    wide = x.astype(jnp.float32)
    wide = wide * wide
    hi = wide.astype(jnp.bfloat16)
    return hi, (wide - hi.astype(jnp.float32)).astype(jnp.bfloat16)


def nt(a, b):
    return lax.dot_general(a, b, (((1,), (1,)), ((), ())), preferred_element_type=jnp.float32)


def squares_mean_column(x):
    ones = jnp.ones((B, x.shape[1]), jnp.bfloat16)
    hi, lo = squares(x)
    return (nt(hi, ones) + nt(lo, ones)) / x.shape[1] + EPS


def squares_mean_row(x):
    ones = jnp.ones((8, x.shape[1]), jnp.bfloat16)
    hi, lo = squares(x)
    return (nt(ones, hi) + nt(ones, lo)) / x.shape[1] + EPS


def spread(column, lanes):
    return jnp.concatenate([column] * (lanes // B), axis=1)


def fill_cross(marks_ref, marks_row, rows, emb_ref, u_ref, k_ref, vq_ref, x_ref, x_row, chunk):
    e = emb_ref.shape[1]
    m = emb_ref.shape[0]

    def block(j, _):
        row = pl.multiple_of(marks_row + j * B, B)
        out = pl.multiple_of(x_row + j * B, B)
        tile = marks_ref[pl.ds(row, B), :]
        k_ref[...] = nt(tile, emb_ref[...])
        vq_ref[...] = squares_mean_column(tile)

        def part(i, _):
            r = pl.multiple_of(i * chunk, chunk)
            vq = vq_ref[pl.ds(r, chunk), :]
            v_inv = lax.rsqrt(vq)
            v_root = vq * v_inv
            up = jnp.concatenate([u_ref[:8, :]] * (chunk // 8), axis=0)
            ur = jnp.concatenate([u_ref[8:, :]] * (chunk // 8), axis=0)
            c = recursion(k_ref[pl.ds(r, chunk), :] * up * spread(v_inv * (1.0 / e), m))
            x_ref[pl.ds(out + r, chunk), :] = (c * ur * spread(v_root * GROWTH, m)).astype(jnp.bfloat16)
            return 0

        lax.fori_loop(0, B // chunk, part, 0)
        return 0

    lax.fori_loop(0, rows // B, block, 0)


def fill_u(emb_ref, u_ref):
    uq = squares_mean_row(emb_ref[...])
    inv = lax.rsqrt(uq)
    u_ref[:8, :] = inv
    u_ref[8:, :] = uq * inv


def own_kernel(marks_ref, emb_ref, x_ref, u_ref, k_ref, vq_ref):
    fill_u(emb_ref, u_ref)
    fill_cross(marks_ref, 0, marks_ref.shape[0], emb_ref, u_ref, k_ref, vq_ref, x_ref, 0, 16)


def own_cross(landmarks, embeddings):
    m = embeddings.shape[0]
    vmem = pl.BlockSpec(memory_space=pltpu.VMEM)
    return pl.pallas_call(
        own_kernel,
        out_shape=(
            jax.ShapeDtypeStruct((landmarks.shape[0], m), jnp.bfloat16),
            jax.ShapeDtypeStruct((16, m), jnp.float32),
        ),
        in_specs=[vmem, vmem],
        out_specs=(vmem, vmem),
        scratch_shapes=[pltpu.VMEM((B, m), jnp.float32), pltpu.VMEM((B, B), jnp.float32)],
        compiler_params=pltpu.CompilerParams(vmem_limit_bytes=24 << 20),
        cost_estimate=pl.CostEstimate(flops=10**10, transcendentals=10**7, bytes_accessed=10**7),
        name="own_cross",
    )(landmarks, embeddings)


def gram_kernel(plan, at_ref, emb_ref, mine_ref, own_ref, u_ref, x_mine_ref, *refs):
    lands, chips, cores, split, all_points, total_rows = plan
    count = (chips - 1 + 1) * (cores if split else 1)
    far = refs[:count]
    keep_ref, send_ref, marks_ref, x_ref, k_ref, vq_ref, ridge_ref, out_ref = refs[count:]
    shard, e = mine_ref.shape
    n = shard * lands
    m = emb_ref.shape[0]
    land, chip, core = at_ref[0], at_ref[1], at_ref[2]
    here = pl.multiple_of(land * shard, shard)
    marks_ref[pl.ds(here, shard), :] = mine_ref[...]
    x_ref[pl.ds(here, shard), :] = x_mine_ref[...]
    piece = far[0].shape[0] // (lands - 1)
    for a in range(cores if split else 1):
        for t in range(chips):
            slot = ((chip ^ t) * cores + (core ^ a)) if split else (chip ^ t)
            for s in range(1, lands):
                to = pl.multiple_of((land ^ s) * shard + slot * piece, piece)
                marks_ref[pl.ds(to, piece), :] = far[a * chips + t][(s - 1) * piece : s * piece, :]
    for s in range(1, lands):
        there = pl.multiple_of((land ^ s) * shard, shard)
        fill_cross(marks_ref, there, shard, emb_ref, u_ref, k_ref, vq_ref, x_ref, there, 16)

    share = own_ref.shape[0]
    oq = squares_mean_column(own_ref[...])
    vr = squares_mean_row(marks_ref[...])
    o_inv, v_inv = lax.rsqrt(oq), lax.rsqrt(vr)
    k_own = nt(own_ref[...], marks_ref[...])
    for i in range(share // 8):
        oi = o_inv[8 * i : 8 * i + 8]
        c = recursion(k_own[8 * i : 8 * i + 8] * v_inv * spread(oi * (1.0 / e), n))
        root = oq[8 * i : 8 * i + 8] * oi
        ridge_ref[8 * i : 8 * i + 8, :] = c * (vr * v_inv) * spread(root * (RIDGE * GROWTH), n)

    position = land * shard + (chip * cores + core) * share
    row_block = position // B
    offset = position % B
    for j in range(n // B):
        start = j * (j + 1) // 2 * B
        out_ref[start : start + (j + 1) * B, :] = nt(
            x_ref[: (j + 1) * B, :], x_ref[j * B : (j + 1) * B, :]
        ) * (1.0 / all_points)

        @pl.when(row_block <= j)
        def _():
            at = pl.ds(pl.multiple_of(start + row_block * B + offset, share), share)
            out_ref[at, :] = out_ref[at, :] + ridge_ref[:, j * B : (j + 1) * B]

    half = total_rows // cores
    keep_ref[...] = out_ref[pl.ds(pl.multiple_of(core * half, half), half), :]
    send_ref[...] = out_ref[pl.ds(pl.multiple_of((1 - core) * half, half), half), :]


def local_normal(at, plan, embeddings, landmarks, own, u, x_mine, far):
    lands, chips, cores, split, all_points, total_rows = plan
    n, m = landmarks.shape[0] * lands, embeddings.shape[0]
    half = jax.ShapeDtypeStruct((total_rows // cores, B), jnp.float32)
    vmem = pl.BlockSpec(memory_space=pltpu.VMEM)
    return pl.pallas_call(
        functools.partial(gram_kernel, plan),
        out_shape=(half, half),
        in_specs=[pl.BlockSpec(memory_space=pltpu.SMEM)] + [vmem] * (5 + len(far)),
        out_specs=(vmem, vmem),
        scratch_shapes=[
            pltpu.VMEM((n, landmarks.shape[1]), jnp.bfloat16),
            pltpu.VMEM((n, m), jnp.bfloat16),
            pltpu.VMEM((B, m), jnp.float32),
            pltpu.VMEM((B, B), jnp.float32),
            pltpu.VMEM((own.shape[0], n), jnp.float32),
            pltpu.VMEM((total_rows, B), jnp.float32),
        ],
        compiler_params=pltpu.CompilerParams(vmem_limit_bytes=40 << 20),
        name="gram",
    )(at, embeddings, landmarks, own, u, x_mine, *far)


def add_cut_kernel(ways, axis, at_ref, *refs):
    ins, outs = refs[: len(refs) - ways], refs[len(refs) - ways :]
    h = outs[0].shape[0]
    for s in range(ways):
        rows = pl.ds(pl.multiple_of((at_ref[axis] ^ s) * h, h), h) if ways > 1 else slice(None)
        total = ins[0][rows, :]
        for r in ins[1:]:
            total = total + r[rows, :]
        outs[s][...] = total


def add_cut(at, axis, ways, parts):
    h = parts[0].shape[0] // ways
    vmem = pl.BlockSpec(memory_space=pltpu.VMEM)
    return pl.pallas_call(
        functools.partial(add_cut_kernel, ways, axis),
        out_shape=tuple([jax.ShapeDtypeStruct((h, B), jnp.float32)] * ways),
        in_specs=[pl.BlockSpec(memory_space=pltpu.SMEM)] + [vmem] * len(parts),
        out_specs=tuple([vmem] * ways),
        name="add_cut",
    )(at, *parts)


def place_kernel(axis, at_ref, *refs):
    out = refs[-1]
    h = refs[0].shape[0]
    for s in range(len(refs) - 1):
        out[pl.ds(pl.multiple_of((at_ref[axis] ^ s) * h, h), h), :] = refs[s][...]


def place(at, axis, parts):
    vmem = pl.BlockSpec(memory_space=pltpu.VMEM)
    return pl.pallas_call(
        functools.partial(place_kernel, axis),
        out_shape=jax.ShapeDtypeStruct((parts[0].shape[0] * len(parts), B), jnp.float32),
        in_specs=[pl.BlockSpec(memory_space=pltpu.SMEM)] + [vmem] * len(parts),
        out_specs=vmem,
        name="place",
    )(at, *parts)


def factor_block(d):
    rows8 = lax.broadcasted_iota(jnp.int32, (8, 128), 0)
    eye = (lax.broadcasted_iota(jnp.int32, (B, B), 0) == lax.broadcasted_iota(jnp.int32, (B, B), 1)).astype(jnp.float32)
    n = B // W
    g = W // 8
    left = [d[8 * i:8 * i + 8] for i in range(B // 8)]
    right = [eye[8 * i:8 * i + 8] for i in range(B // 8)]
    for p in range(n):
        base = p * g
        last = p == n - 1
        groups = list(range(base, base + (g if last else 2 * g)))
        col = [[None] * len(groups) for _ in range(W)]
        for i in range(W):
            for t, r in enumerate(groups):
                if t < g and t < i // 8:
                    continue
                lane = p * W + i
                col[i][t] = jnp.broadcast_to(left[r][:, lane:lane + 1], (8, 128))
        diag = [jnp.ones((8, 128), jnp.float32) for _ in range(g)]
        for j in range(W):
            tj, sj = j // 8, j % 8
            pivot = jnp.broadcast_to(col[j][tj][sj:sj + 1], (8, 128))
            diag[tj] = jnp.where(rows8 == sj, pivot, diag[tj])
            inv = 1.0 / pivot
            coefs = {}
            for i in range(j + 1, W):
                coefs[i] = jnp.broadcast_to(col[j][i // 8][i % 8:i % 8 + 1], (8, 128))
            scaled = [None] * len(groups)
            for t in range(len(groups)):
                if col[j][t] is None:
                    continue
                scaled[t] = col[j][t] * inv
            for i in range(j + 1, W):
                for t in range(len(groups)):
                    if col[i][t] is None:
                        continue
                    if i == j + 1:
                        col[i][t] = col[i][t] - (col[j][t] * coefs[i]) * inv
                    else:
                        col[i][t] = col[i][t] - scaled[t] * coefs[i]
            rl = jnp.broadcast_to(left[base + tj][sj:sj + 1], (8, 128))
            rr = jnp.broadcast_to(right[base + tj][sj:sj + 1], (8, 128))
            for t, r in enumerate(groups):
                if scaled[t] is None:
                    continue
                c = scaled[t]
                if t == tj:
                    if sj == 7:
                        continue
                    c = jnp.where(rows8 > sj, c, 0.0)
                left[r] = left[r] - c * rl
                right[r] = right[r] - c * rr
        for t in range(g):
            s = lax.rsqrt(diag[t])
            left[base + t] = left[base + t] * s
            right[base + t] = right[base + t] * s
        rest = (n - p - 2) * W
        if rest > 0:
            ul = jnp.concatenate(left[base:base + g], 0)
            ur = jnp.concatenate(right[base:base + g], 0)
            u = jnp.concatenate([ul, ur], 1)
            lo_row = (p + 2) * W
            upd = lax.dot_general(ul, u, (((0,), (0,)), ((), ())), preferred_element_type=jnp.float32, precision=HI)
            for r in range(lo_row // 8, B // 8):
                left[r] = left[r] - upd[8 * r:8 * r + 8, :128]
                right[r] = right[r] - upd[8 * r:8 * r + 8, 128:]
    u = jnp.concatenate(left, 0)
    w = jnp.concatenate(right, 0)
    tri = lax.broadcasted_iota(jnp.int32, (B, B), 0) <= lax.broadcasted_iota(jnp.int32, (B, B), 1)
    return jnp.where(tri, u, 0.0), w

def chol_kernel(chips, cores, at_ref, *refs):
    parts = refs[: chips * cores]
    o_ref, a_ref, s_ref, w_ref = refs[chips * cores :]
    n = o_ref.shape[0] // B
    h = parts[0].shape[0]
    for a in range(cores):
        for t in range(chips):
            slot = (at_ref[2] ^ a) * chips + (at_ref[1] ^ t)
            a_ref[pl.ds(pl.multiple_of(slot * h, h), h), :] = parts[a * chips + t][...]
    o_ref[...] = jnp.zeros_like(o_ref)

    def step(k, _):
        for i in range(n):

            @pl.when(k == i)
            def _():
                starts = [(j * (j + 1) // 2 + i) * B for j in range(i, n)]
                blk = jnp.concatenate([a_ref[r : r + B, :] for r in starts], 1)
                if i:
                    left = o_ref[: i * B, i * B : (i + 1) * B]
                    right = o_ref[: i * B, i * B :]
                    blk = blk - lax.dot_general(
                        left, right, (((0,), (0,)), ((), ())), preferred_element_type=jnp.float32, precision=HI
                    )
                s_ref[:, : (n - i) * B] = blk

        u, w = factor_block(s_ref[:, :B])
        s_ref[:, :B] = u
        w_ref[...] = w
        for i in range(n):

            @pl.when(k == i)
            def _():
                o_ref[i * B : (i + 1) * B, i * B : (i + 1) * B] = s_ref[:, :B]
                if i < n - 1:
                    o_ref[i * B : (i + 1) * B, (i + 1) * B :] = lax.dot_general(
                        w_ref[...],
                        s_ref[:, B : (n - i) * B],
                        (((1,), (0,)), ((), ())),
                        preferred_element_type=jnp.float32,
                        precision=HI,
                    )

        return 0

    lax.fori_loop(0, n, step, 0)


def cholesky_upper(at, chips, cores, parts, n):
    vmem = pl.BlockSpec(memory_space=pltpu.VMEM)
    return pl.pallas_call(
        functools.partial(chol_kernel, chips, cores),
        out_shape=jax.ShapeDtypeStruct((n, n), jnp.float32),
        in_specs=[pl.BlockSpec(memory_space=pltpu.SMEM)] + [vmem] * len(parts),
        out_specs=vmem,
        scratch_shapes=[
            pltpu.VMEM((parts[0].shape[0] * len(parts), B), jnp.float32),
            pltpu.VMEM((B, n), jnp.float32),
            pltpu.VMEM((B, B), jnp.float32),
        ],
        compiler_params=pltpu.CompilerParams(vmem_limit_bytes=40 << 20),
        name="chol",
    )(at, *parts)


def swap(x, axis, s):
    return lax.ppermute(x, axis, [(i, i ^ s) for i in range(lax.axis_size(axis))])


def scatter(pieces, axis):
    return [pieces[0]] + [swap(p, axis, s) for s, p in enumerate(pieces) if s]


def spread_out(x, axis):
    return [x] + [swap(x, axis, s) for s in range(1, lax.axis_size(axis))]


def shards(embeddings, landmarks):
    lands, chips, cores = (lax.axis_size(a) for a in ("land", "chip", "core"))
    land, chip, core = (lax.axis_index(a) for a in ("land", "chip", "core"))
    at = jnp.stack([land, chip, core]).astype(jnp.int32)
    shard = landmarks.shape[0]
    n = shard * lands
    devices = lands * chips * cores
    blocks = n // B * (n // B + 1) // 2
    unit = 8 * devices
    total_rows = -(-blocks * B // unit) * unit
    split = shard // (chips * cores) % 16 == 0

    share = shard // (chips * cores)
    own = lax.dynamic_slice_in_dim(landmarks, (chip * cores + core) * share, share, 0)
    if split:
        piece = own
    else:
        piece = lax.dynamic_slice_in_dim(landmarks, chip * (shard // chips), shard // chips, 0)
    z = jnp.concatenate(spread_out(piece, "land")[1:], 0)
    far = spread_out(z, "chip")
    if split:
        for a in range(1, cores):
            far = far + [swap(f, "core", a) for f in far[:chips]]
    x_mine, u = own_cross(landmarks, embeddings)
    plan = (lands, chips, cores, split, embeddings.shape[0] * devices, total_rows)
    keep, send = local_normal(at, plan, embeddings, landmarks, own, u, x_mine, far)

    parts = scatter(add_cut(at, 1, chips, [keep, swap(send, "core", 1)]), "chip")
    parts = scatter(add_cut(at, 0, lands, parts), "land")
    (whole,) = add_cut(at, 0, 1, parts)
    whole = place(at, 0, spread_out(whole, "land"))
    parts = spread_out(whole, "chip")
    parts = parts + [swap(p, "core", 1) for p in parts]
    return cholesky_upper(at, chips, cores, parts, n)


def solution(mesh):
    land, rows = mesh.axis_names
    cores = 2
    fine = Mesh(mesh.devices.reshape(mesh.shape[land], mesh.shape[rows] // cores, cores), ("land", "chip", "core"))
    in_specs = (P(("land", "chip", "core"), None), P("land", None))
    return jax.shard_map(shards, mesh=fine, in_specs=in_specs, out_specs=P(), check_vma=False)
```

time: 187 us -> 159 us (0.85)
  waiting for transfers between devices: 82.7 us -> 45.4 us
  Pallas kernels: 68.2 us -> 78.2 us
  local copies, waits for them, and re-layouts: 3.06 us -> 8.97 us
  starting transfers between devices: 29.2 us -> 25.7 us
  other arithmetic: 3.44 us -> 0.08 us
    ppermute x15 -> x27, waiting for transfers between devices: 82.7 us -> 45.4 us  [swap(): lax.ppermute(x, axis, [(i, i ^ s) for i in range(lax.axis_size(axis))])]
    pallas_call x2 -> x7, Pallas kernels: 68.2 us -> 78.2 us  [the longest x1 36.4 us: cholesky_upper(): pl.pallas_call(functools.partial(chol_kernel, chips, cores), out_shape=ja...]
    unnamed x2 -> x38, local copies, waits for them, and re-layouts: 1.26 us -> 8.17 us
    ppermute x15 -> x27, starting transfers between devices: 29.2 us -> 25.7 us  [swap(): lax.ppermute(x, axis, [(i, i ^ s) for i in range(lax.axis_size(axis))])]
  transfers between devices with their start and end apart: 15 -> 27, of which waited for: 15 -> 17; matrix products, arithmetic and copies ran while one was open for 0% -> 0% of each run, Pallas kernels for 0% -> 4%
where the time goes in v2:
time: 159 us; the launch traced here: 158 us
  Pallas kernels  78.2 us (49%)
  waiting for transfers between devices  45.4 us (29%)
  starting transfers between devices  25.7 us (16%)
  local copies, waits for them, and re-layouts  8.97 us (6%)
    ppermute x27, waiting for transfers between devices, swap(): lax.ppermute(x, axis, [(i, i ^ s) for i in range(lax.axis_size(axis))])  45.4 us
    pallas_call x1, Pallas kernels, cholesky_upper(): pl.pallas_call(functools.partial(chol_kernel, chips, cores), out_shape=ja...  36.4 us
    pallas_call x1, Pallas kernels, local_normal(): pl.pallas_call(functools.partial(gram_kernel, plan), out_shape=(half, hal...  26.6 us
    ppermute x27, starting transfers between devices, swap(): lax.ppermute(x, axis, [(i, i ^ s) for i in range(lax.axis_size(axis))])  25.7 us
    unnamed x38, local copies, waits for them, and re-layouts  8.17 us
    pallas_call x1, Pallas kernels, own_cross(): pl.pallas_call(own_kernel, out_shape=(jax.ShapeDtypeStruct((landmarks.sha...  6.95 us
    pallas_call x3, Pallas kernels, add_cut(): pl.pallas_call(functools.partial(add_cut_kernel, ways, axis), out_shape=t...  6.47 us
  transfers between devices with their start and end apart: 27, of which 17 were waited for; matrix products, arithmetic and copies ran while one was open for 0% of the time, Pallas kernels for 4%

profile of v2, /device:TPU:0, one launch (start us, length us, event | category | flops | bytes accessed | tf_op | source)
XLA Modules:
  0.0 158.5 jit_solution(9986135627773530559)
XLA Ops:
  0.0 0.8 constant_dynamic-slice_fusion.own_ref
  0.8 3.0 %collective-permute-start = (bf16[32,768]{1,0:T(8,128)(2,1)S(1)}, bf16[32,768]{1,0:T(8,128)(2,1)S(1)}, u32[]{:S(2)}, u32[]{:S(2)}) collective-permute-start(bf16[32,768]{1,0:T(8,128)(2,1)S(1)} %constant_dynamic-slice_fusion.own_ref), channel_id=1, source_target_pairs={{0,8},{8,0},{16,24},{24,16},{1,9},{9,1},{17,25},{25,17},{2,10},{10... | collective-permute-start | bytes 147464 | tf_op jit(solution)/shard_map/ppermute | solution.py:377
  3.8 2.5 %collective-permute-start.2 = (bf16[32,768]{1,0:T(8,128)(2,1)S(1)}, bf16[32,768]{1,0:T(8,128)(2,1)S(1)}, u32[]{:S(2)}, u32[]{:S(2)}) collective-permute-start(bf16[32,768]{1,0:T(8,128)(2,1)S(1)} %constant_dynamic-slice_fusion.own_ref), channel_id=1, source_target_pairs={{0,24},{8,16},{16,8},{24,0},{1,25},{9,17},{17,9},{25,1},{2,26},{10... | collective-permute-start | bytes 147464 | tf_op jit(solution)/shard_map/ppermute | solution.py:377
  6.4 5.4 %collective-permute-done.1 = bf16[32,768]{1,0:T(8,128)(2,1)S(1)} collective-permute-done((bf16[32,768]{1,0:T(8,128)(2,1)S(1)}, bf16[32,768]{1,0:T(8,128)(2,1)S(1)}, u32[]{:S(2)}, u32[]{:S(2)}) %collective-permute-start.1) | collective-permute-done | bytes 49184 | tf_op jit(solution)/shard_map/ppermute | solution.py:377
  11.8 2.5 %collective-permute-start.5 = (bf16[96,768]{1,0:T(8,128)(2,1)S(1)}, bf16[96,768]{1,0:T(8,128)(2,1)S(1)}, u32[]{:S(2)}, u32[]{:S(2)}) collective-permute-start(bf16[96,768]{1,0:T(8,128)(2,1)S(1)} %constant_dynamic-update-slice_fusion.refs_0_), channel_id=1, source_target_pairs={{0,6},{2,4},{4,2},{6,0},{1,7},{3,5},{5,3},{7,1},{8,14},{10,12},{12... | collective-permute-start | bytes 442376 | tf_op jit(solution)/shard_map/ppermute | solution.py:377
  14.4 0.5 collective-permute-start.4
  14.9 0.5 collective-permute-start.3
  15.4 4.0 %collective-permute-done.5.refs_3_ = bf16[96,768]{1,0:T(8,128)(2,1)S(1)} collective-permute-done((bf16[96,768]{1,0:T(8,128)(2,1)S(1)}, bf16[96,768]{1,0:T(8,128)(2,1)S(1)}, u32[]{:S(2)}, u32[]{:S(2)}) %collective-permute-start.5) | collective-permute-done | bytes 147488 | tf_op jit(solution)/shard_map/ppermute | solution.py:377
  19.4 1.0 collective-permute-done.4.refs_2_
  20.4 0.5 collective-permute-start.7
  20.9 1.4 copy-done
  22.3 1.0 copy-done.4
  23.3 6.9 %own_cross.1 = (bf16[256,1024]{1,0:T(8,128)(2,1)S(1)}, f32[16,1024]{1,0:T(8,128)S(1)}) custom-call(bf16[256,768]{1,0:T(8,128)(2,1)S(1)} %copy-done.4, bf16[1024,768]{1,0:T(8,128)(2,1)S(1)} %copy-done), custom_call_target="tpu_custom_call" | custom-call | flops 10000000000 | bytes 10000000 | tf_op jit(solution)/shard_map/own_cross/pallas_call | solution.py:108
  30.4 26.6 %gram.1 = (f32[2304,128]{1,0:T(8,128)S(1)}, f32[2304,128]{1,0:T(8,128)S(1)}) custom-call(s32[3]{0:T(128)S(1)} %pad_add_fusion.at_ref, bf16[1024,768]{1,0:T(8,128)(2,1)S(1)} %copy-done.1, bf16[256,768]{1,0:T(8,128)(2,1)S(1)} %copy-done.5, bf16[32,768]{1,0:T(8,128)(2,1)S(1)} %constant_dynamic-slice_fusion.own_ref, f32[16,1024]{1,0:T(8,128)S(1)} %get-tuple-element.17.u_ref, ...), custom_call_target="tpu_custom_call" | custom-call | tf_op jit(solution)/shard_map/gram/pallas_call | solution.py:181
  57.1 1.0 copy-done.2
  58.1 2.8 %collective-permute-done.10.refs_1_ = f32[2304,128]{1,0:T(8,128)S(1)} collective-permute-done((f32[2304,128]{1,0:T(8,128)S(1)}, f32[2304,128]{1,0:T(8,128)S(1)}, u32[]{:S(2)}, u32[]{:S(2)}) %collective-permute-start.10) | collective-permute-done | bytes 1179680 | tf_op jit(solution)/shard_map/ppermute | solution.py:377
  60.9 1.0 copy-done.8
  61.9 2.8 %add_cut.3 = (f32[576,128]{1,0:T(8,128)}, f32[576,128]{1,0:T(8,128)}, f32[576,128]{1,0:T(8,128)}, f32[576,128]{1,0:T(8,128)}) custom-call(s32[3]{0:T(128)} %copy-done.6, f32[2304,128]{1,0:T(8,128)} %copy-done.2, f32[2304,128]{1,0:T(8,128)} %copy-done.8), custom_call_target="tpu_custom_call" | custom-call | tf_op jit(solution)/shard_map/add_cut/pallas_call | solution.py:213
  64.8 1.5 collective-permute-start.11
  66.2 0.8 collective-permute-start.12
  67.1 1.2 collective-permute-start.13
  68.2 6.6 %collective-permute-done.11.refs_1_ = f32[576,128]{1,0:T(8,128)S(1)} collective-permute-done((f32[576,128]{1,0:T(8,128)}, f32[576,128]{1,0:T(8,128)S(1)}, u32[]{:S(2)}, u32[]{:S(2)}) %collective-permute-start.11) | collective-permute-done | bytes 294944 | tf_op jit(solution)/shard_map/ppermute | solution.py:377
  74.8 6.7 %collective-permute-done.12.refs_2_ = f32[576,128]{1,0:T(8,128)S(1)} collective-permute-done((f32[576,128]{1,0:T(8,128)}, f32[576,128]{1,0:T(8,128)S(1)}, u32[]{:S(2)}, u32[]{:S(2)}) %collective-permute-start.12) | collective-permute-done | bytes 294944 | tf_op jit(solution)/shard_map/ppermute | solution.py:377
  81.6 0.7 copy-done.10
  82.4 2.0 %add_cut.4 = (f32[144,128]{1,0:T(8,128)}, f32[144,128]{1,0:T(8,128)}, f32[144,128]{1,0:T(8,128)}, f32[144,128]{1,0:T(8,128)}) custom-call(s32[3]{0:T(128)} %copy-done.6, f32[576,128]{1,0:T(8,128)} %get-tuple-element.21.refs_0_, f32[576,128]{1,0:T(8,128)} %copy-done.9, f32[576,128]{1,0:T(8,128)} %copy-done.10, f32[576,128]{1,0:T(8,128)} %copy-done.11), custom_call_target="tpu_custom_call" | custom-call | tf_op jit(solution)/shard_map/add_cut/pallas_call | solution.py:213
  84.6 3.0 %collective-permute-start.15 = (f32[144,128]{1,0:T(8,128)}, f32[144,128]{1,0:T(8,128)S(1)}, u32[]{:S(2)}, u32[]{:S(2)}) collective-permute-start(f32[144,128]{1,0:T(8,128)} %get-tuple-element.27), channel_id=1, source_target_pairs={{0,16},{8,24},{16,0},{24,8},{1,17},{9,25},{17,1},{25,9},{2,18},{10... | collective-permute-start | bytes 221192 | tf_op jit(solution)/shard_map/ppermute | solution.py:377
  87.7 1.1 collective-permute-start.16
  89.0 3.2 %collective-permute-done.15.refs_2_ = f32[144,128]{1,0:T(8,128)S(1)} collective-permute-done((f32[144,128]{1,0:T(8,128)}, f32[144,128]{1,0:T(8,128)S(1)}, u32[]{:S(2)}, u32[]{:S(2)}) %collective-permute-start.15) | collective-permute-done | bytes 73760 | tf_op jit(solution)/shard_map/ppermute | solution.py:377
  92.2 1.8 %collective-permute-done.16.refs_3_ = f32[144,128]{1,0:T(8,128)S(1)} collective-permute-done((f32[144,128]{1,0:T(8,128)}, f32[144,128]{1,0:T(8,128)S(1)}, u32[]{:S(2)}, u32[]{:S(2)}) %collective-permute-start.16) | collective-permute-done | bytes 73760 | tf_op jit(solution)/shard_map/ppermute | solution.py:377
  94.0 0.6 copy-done.15
  94.7 1.6 %add_cut.5.refs_0_ = f32[144,128]{1,0:T(8,128)} custom-call(s32[3]{0:T(128)} %copy-done.6, f32[144,128]{1,0:T(8,128)} %get-tuple-element.25.refs_0_, f32[144,128]{1,0:T(8,128)} %copy-done.12, f32[144,128]{1,0:T(8,128)} %copy-done.13, f32[144,128]{1,0:T(8,128)} %copy-done.15), custom_call_target="tpu_custom_call" | custom-call | tf_op jit(solution)/shard_map/add_cut/pallas_call | solution.py:213
  96.3 1.4 collective-permute-start.19
  97.7 3.0 %collective-permute-start.17 = (f32[144,128]{1,0:T(8,128)}, f32[144,128]{1,0:T(8,128)S(1)}, u32[]{:S(2)}, u32[]{:S(2)}) collective-permute-start(f32[144,128]{1,0:T(8,128)} %add_cut.5.refs_0_), channel_id=1, source_target_pairs={{0,8},{8,0},{16,24},{24,16},{1,9},{9,1},{17,25},{25,17},{2,10},{10... | collective-permute-start | bytes 221192 | tf_op jit(solution)/shard_map/ppermute | solution.py:377
  100.7 2.0 %collective-permute-done.19.refs_3_ = f32[144,128]{1,0:T(8,128)S(1)} collective-permute-done((f32[144,128]{1,0:T(8,128)}, f32[144,128]{1,0:T(8,128)S(1)}, u32[]{:S(2)}, u32[]{:S(2)}) %collective-permute-start.19) | collective-permute-done | bytes 73760 | tf_op jit(solution)/shard_map/ppermute | solution.py:377
  102.7 1.5 collective-permute-done.18.refs_2_
  104.3 0.6 copy-done.16
  104.9 0.6 copy-done.17
  105.5 1.7 %place.1.refs_0_ = f32[576,128]{1,0:T(8,128)} custom-call(s32[3]{0:T(128)} %copy-done.6, f32[144,128]{1,0:T(8,128)} %add_cut.5.refs_0_, f32[144,128]{1,0:T(8,128)} %copy-done.17, f32[144,128]{1,0:T(8,128)} %copy-done.16, f32[144,128]{1,0:T(8,128)} %copy-done.14), custom_call_target="tpu_custom_call" | custom-call | tf_op jit(solution)/shard_map/place/pallas_call | solution.py:231
  107.3 1.5 collective-permute-start.22
  108.8 0.5 collective-permute-start.21
  109.3 1.5 collective-permute-start.20
  110.8 5.3 %collective-permute-done.22.refs_3_ = f32[576,128]{1,0:T(8,128)S(1)} collective-permute-done((f32[576,128]{1,0:T(8,128)}, f32[576,128]{1,0:T(8,128)S(1)}, u32[]{:S(2)}, u32[]{:S(2)}) %collective-permute-start.22) | collective-permute-done | bytes 294944 | tf_op jit(solution)/shard_map/ppermute | solution.py:377
  116.1 3.0 %collective-permute-done.21.refs_2_ = f32[576,128]{1,0:T(8,128)S(1)} collective-permute-done((f32[576,128]{1,0:T(8,128)}, f32[576,128]{1,0:T(8,128)S(1)}, u32[]{:S(2)}, u32[]{:S(2)}) %collective-permute-start.21) | collective-permute-done | bytes 294944 | tf_op jit(solution)/shard_map/ppermute | solution.py:377
  119.4 0.3 collective-permute-start.24
  119.6 1.1 collective-permute-done.25.refs_6_
  120.7 0.4 collective-permute-done.24.refs_5_
  121.1 1.0 copy-done.3
  122.1 36.4 %chol.1 = f32[1024,1024]{1,0:T(8,128)} custom-call(s32[3]{0:T(128)S(1)} %copy-done.7, f32[576,128]{1,0:T(8,128)S(1)} %copy-done.3, f32[576,128]{1,0:T(8,128)S(1)} %collective-permute-done.20.refs_1_, f32[576,128]{1,0:T(8,128)S(1)} %collective-permute-done.21.refs_2_, f32[576,128]{1,0:T(8,128)S(1)} %collective-permute-done.22.refs_3_, ...), custom_call_target="tpu_custom_call" | custom-call | tf_op jit(solution)/shard_map/chol/pallas_call | solution.py:361
  (54 shorter events, 1.3 us)
Async XLA Ops:
  0.8 5.6 %collective-permute-start = (bf16[32,768]{1,0:T(8,128)(2,1)S(1)}, bf16[32,768]{1,0:T(8,128)(2,1)S(1)}, u32[]{:S(2)}, u32[]{:S(2)}) collective-permute-start(bf16[32,768]{1,0:T(8,128)(2,1)S(1)} %constant_dynamic-slice_fusion.own_ref), channel_id=1, source_target_pairs={{0,8},{8,0},{16,24},{24,16},{1,9},{9,1},{17,25},{25,17},{2,10},{10... | collective-permute-start | bytes 147464 | tf_op jit(solution)/shard_map/ppermute | solution.py:377
  3.8 8.0 %collective-permute-start.2 = (bf16[32,768]{1,0:T(8,128)(2,1)S(1)}, bf16[32,768]{1,0:T(8,128)(2,1)S(1)}, u32[]{:S(2)}, u32[]{:S(2)}) collective-permute-start(bf16[32,768]{1,0:T(8,128)(2,1)S(1)} %constant_dynamic-slice_fusion.own_ref), channel_id=1, source_target_pairs={{0,24},{8,16},{16,8},{24,0},{1,25},{9,17},{17,9},{25,1},{2,26},{10... | collective-permute-start | bytes 147464 | tf_op jit(solution)/shard_map/ppermute | solution.py:377
  6.3 5.5 %collective-permute-start.1 = (bf16[32,768]{1,0:T(8,128)(2,1)S(1)}, bf16[32,768]{1,0:T(8,128)(2,1)S(1)}, u32[]{:S(2)}, u32[]{:S(2)}) collective-permute-start(bf16[32,768]{1,0:T(8,128)(2,1)S(1)} %constant_dynamic-slice_fusion.own_ref), channel_id=1, source_target_pairs={{0,16},{8,24},{16,0},{24,8},{1,17},{9,25},{17,1},{25,9},{2,18},{10... | collective-permute-start | bytes 147464 | tf_op jit(solution)/shard_map/ppermute | solution.py:377
  11.8 7.6 %collective-permute-start.5 = (bf16[96,768]{1,0:T(8,128)(2,1)S(1)}, bf16[96,768]{1,0:T(8,128)(2,1)S(1)}, u32[]{:S(2)}, u32[]{:S(2)}) collective-permute-start(bf16[96,768]{1,0:T(8,128)(2,1)S(1)} %constant_dynamic-update-slice_fusion.refs_0_), channel_id=1, source_target_pairs={{0,6},{2,4},{4,2},{6,0},{1,7},{3,5},{5,3},{7,1},{8,14},{10,12},{12... | collective-permute-start | bytes 442376 | tf_op jit(solution)/shard_map/ppermute | solution.py:377
  14.4 6.0 %collective-permute-start.4 = (bf16[96,768]{1,0:T(8,128)(2,1)S(1)}, bf16[96,768]{1,0:T(8,128)(2,1)S(1)}, u32[]{:S(2)}, u32[]{:S(2)}) collective-permute-start(bf16[96,768]{1,0:T(8,128)(2,1)S(1)} %constant_dynamic-update-slice_fusion.refs_0_), channel_id=1, source_target_pairs={{0,4},{2,6},{4,0},{6,2},{1,5},{3,7},{5,1},{7,3},{8,12},{10,14},{12... | collective-permute-start | bytes 442376 | tf_op jit(solution)/shard_map/ppermute | solution.py:377
  14.9 5.6 %collective-permute-start.3 = (bf16[96,768]{1,0:T(8,128)(2,1)S(1)}, bf16[96,768]{1,0:T(8,128)(2,1)S(1)}, u32[]{:S(2)}, u32[]{:S(2)}) collective-permute-start(bf16[96,768]{1,0:T(8,128)(2,1)S(1)} %constant_dynamic-update-slice_fusion.refs_0_), channel_id=1, source_target_pairs={{0,2},{2,0},{4,6},{6,4},{1,3},{3,1},{5,7},{7,5},{8,10},{10,8},{12,... | collective-permute-start | bytes 442376 | tf_op jit(solution)/shard_map/ppermute | solution.py:377
  15.4 14.9 %collective-permute-start.6 = (bf16[96,768]{1,0:T(8,128)(2,1)S(1)}, bf16[96,768]{1,0:T(8,128)(2,1)S(1)}, u32[]{:S(2)}, u32[]{:S(2)}) collective-permute-start(bf16[96,768]{1,0:T(8,128)(2,1)S(1)} %constant_dynamic-update-slice_fusion.refs_0_), channel_id=1, source_target_pairs={{0,1},{1,0},{2,3},{3,2},{4,5},{5,4},{6,7},{7,6},{8,9},{9,8},{10,11... | collective-permute-start | bytes 442376 | tf_op jit(solution)/shard_map/ppermute | solution.py:377
  19.4 10.9 %collective-permute-start.9 = (bf16[96,768]{1,0:T(8,128)(2,1)S(1)}, bf16[96,768]{1,0:T(8,128)(2,1)S(1)}, u32[]{:S(2)}, u32[]{:S(2)}) collective-permute-start(bf16[96,768]{1,0:T(8,128)(2,1)S(1)} %collective-permute-done.5.refs_3_), channel_id=1, source_target_pairs={{0,1},{1,0},{2,3},{3,2},{4,5},{5,4},{6,7},{7,6},{8,9},{9,8},{10,11... | collective-permute-start | bytes 442376 | tf_op jit(solution)/shard_map/ppermute | solution.py:377
  20.4 10.0 %collective-permute-start.8 = (bf16[96,768]{1,0:T(8,128)(2,1)S(1)}, bf16[96,768]{1,0:T(8,128)(2,1)}, u32[]{:S(2)}, u32[]{:S(2)}) collective-permute-start(bf16[96,768]{1,0:T(8,128)(2,1)S(1)} %collective-permute-done.4.refs_2_), channel_id=1, source_target_pairs={{0,1},{1,0},{2,3},{3,2},{4,5},{5,4},{6,7},{7,6},{8,9},{9,8},{10,11... | collective-permute-start | bytes 442376 | tf_op jit(solution)/shard_map/ppermute | solution.py:377
  20.4 9.9 %collective-permute-start.7 = (bf16[96,768]{1,0:T(8,128)(2,1)S(1)}, bf16[96,768]{1,0:T(8,128)(2,1)}, u32[]{:S(2)}, u32[]{:S(2)}) collective-permute-start(bf16[96,768]{1,0:T(8,128)(2,1)S(1)} %collective-permute-done.3.refs_1_), channel_id=1, source_target_pairs={{0,1},{1,0},{2,3},{3,2},{4,5},{5,4},{6,7},{7,6},{8,9},{9,8},{10,11... | collective-permute-start | bytes 442376 | tf_op jit(solution)/shard_map/ppermute | solution.py:377
  20.9 1.4 copy-start
  22.3 1.0 copy-start.4
  23.3 7.1 %copy-start.1 = (bf16[1024,768]{1,0:T(8,128)(2,1)S(1)}, bf16[1024,768]{1,0:T(8,128)(2,1)}, u32[]{:S(2)}) copy-start(bf16[1024,768]{1,0:T(8,128)(2,1)} %emb_ref.3) | copy-start | bytes 4718596
  23.3 7.1 %copy-start.5 = (bf16[256,768]{1,0:T(8,128)(2,1)S(1)}, bf16[256,768]{1,0:T(8,128)(2,1)}, u32[]{:S(2)}) copy-start(bf16[256,768]{1,0:T(8,128)(2,1)} %mine_ref.1) | copy-start | bytes 1179652
  30.3 26.7 %copy-start.6 = (s32[3]{0:T(128)}, s32[3]{0:T(128)S(1)}, u32[]{:S(2)}) copy-start(s32[3]{0:T(128)S(1)} %pad_add_fusion.at_ref) | copy-start | bytes 40
  57.0 1.0 copy-start.2
  58.1 2.8 %collective-permute-start.10 = (f32[2304,128]{1,0:T(8,128)S(1)}, f32[2304,128]{1,0:T(8,128)S(1)}, u32[]{:S(2)}, u32[]{:S(2)}) collective-permute-start(f32[2304,128]{1,0:T(8,128)S(1)} %get-tuple-element.20), channel_id=1, source_target_pairs={{0,1},{1,0},{2,3},{3,2},{4,5},{5,4},{6,7},{7,6},{8,9},{9,8},{10,11... | collective-permute-start | bytes 3538952 | tf_op jit(solution)/shard_map/ppermute | solution.py:377
  60.9 1.0 copy-start.8
  64.7 56.4 %copy-start.7 = (s32[3]{0:T(128)S(1)}, s32[3]{0:T(128)}, u32[]{:S(2)}) copy-start(s32[3]{0:T(128)} %copy-done.6) | copy-start | bytes 40
  64.8 10.1 %collective-permute-start.11 = (f32[576,128]{1,0:T(8,128)}, f32[576,128]{1,0:T(8,128)S(1)}, u32[]{:S(2)}, u32[]{:S(2)}) collective-permute-start(f32[576,128]{1,0:T(8,128)} %get-tuple-element.22), channel_id=1, source_target_pairs={{0,2},{2,0},{4,6},{6,4},{1,3},{3,1},{5,7},{7,5},{8,10},{10,8},{12,... | collective-permute-start | bytes 884744 | tf_op jit(solution)/shard_map/ppermute | solution.py:377
  66.2 15.3 %collective-permute-start.12 = (f32[576,128]{1,0:T(8,128)}, f32[576,128]{1,0:T(8,128)S(1)}, u32[]{:S(2)}, u32[]{:S(2)}) collective-permute-start(f32[576,128]{1,0:T(8,128)} %get-tuple-element.23), channel_id=1, source_target_pairs={{0,4},{2,6},{4,0},{6,2},{1,5},{3,7},{5,1},{7,3},{8,12},{10,14},{12... | collective-permute-start | bytes 884744 | tf_op jit(solution)/shard_map/ppermute | solution.py:377
  67.1 14.5 %collective-permute-start.13 = (f32[576,128]{1,0:T(8,128)}, f32[576,128]{1,0:T(8,128)S(1)}, u32[]{:S(2)}, u32[]{:S(2)}) collective-permute-start(f32[576,128]{1,0:T(8,128)} %get-tuple-element.24), channel_id=1, source_target_pairs={{0,6},{2,4},{4,2},{6,0},{1,7},{3,5},{5,3},{7,1},{8,14},{10,12},{12... | collective-permute-start | bytes 884744 | tf_op jit(solution)/shard_map/ppermute | solution.py:377
  74.8 6.7 %copy-start.9 = (f32[576,128]{1,0:T(8,128)}, f32[576,128]{1,0:T(8,128)S(1)}, u32[]{:S(2)}) copy-start(f32[576,128]{1,0:T(8,128)S(1)} %collective-permute-done.11.refs_1_) | copy-start | bytes 884740
  81.5 0.7 copy-start.10
  81.5 0.8 copy-start.11
  84.4 4.6 %collective-permute-start.14 = (f32[144,128]{1,0:T(8,128)}, f32[144,128]{1,0:T(8,128)S(1)}, u32[]{:S(2)}, u32[]{:S(2)}) collective-permute-start(f32[144,128]{1,0:T(8,128)} %get-tuple-element.26), channel_id=1, source_target_pairs={{0,8},{8,0},{16,24},{24,16},{1,9},{9,1},{17,25},{25,17},{2,10},{10... | collective-permute-start | bytes 221192 | tf_op jit(solution)/shard_map/ppermute | solution.py:377
  84.6 7.6 %collective-permute-start.15 = (f32[144,128]{1,0:T(8,128)}, f32[144,128]{1,0:T(8,128)S(1)}, u32[]{:S(2)}, u32[]{:S(2)}) collective-permute-start(f32[144,128]{1,0:T(8,128)} %get-tuple-element.27), channel_id=1, source_target_pairs={{0,16},{8,24},{16,0},{24,8},{1,17},{9,25},{17,1},{25,9},{2,18},{10... | collective-permute-start | bytes 221192 | tf_op jit(solution)/shard_map/ppermute | solution.py:377
  87.7 6.4 %collective-permute-start.16 = (f32[144,128]{1,0:T(8,128)}, f32[144,128]{1,0:T(8,128)S(1)}, u32[]{:S(2)}, u32[]{:S(2)}) collective-permute-start(f32[144,128]{1,0:T(8,128)} %get-tuple-element.28), channel_id=1, source_target_pairs={{0,24},{8,16},{16,8},{24,0},{1,25},{9,17},{17,9},{25,1},{2,26},{10... | collective-permute-start | bytes 221192 | tf_op jit(solution)/shard_map/ppermute | solution.py:377
  89.0 5.0 %copy-start.12 = (f32[144,128]{1,0:T(8,128)}, f32[144,128]{1,0:T(8,128)S(1)}, u32[]{:S(2)}) copy-start(f32[144,128]{1,0:T(8,128)S(1)} %collective-permute-done.14.refs_1_) | copy-start | bytes 221188
  92.2 1.8 %copy-start.13 = (f32[144,128]{1,0:T(8,128)}, f32[144,128]{1,0:T(8,128)S(1)}, u32[]{:S(2)}) copy-start(f32[144,128]{1,0:T(8,128)S(1)} %collective-permute-done.15.refs_2_) | copy-start | bytes 221188
  94.0 0.7 copy-start.15
  96.3 6.4 %collective-permute-start.19 = (f32[144,128]{1,0:T(8,128)}, f32[144,128]{1,0:T(8,128)S(1)}, u32[]{:S(2)}, u32[]{:S(2)}) collective-permute-start(f32[144,128]{1,0:T(8,128)} %add_cut.5.refs_0_), channel_id=1, source_target_pairs={{0,24},{8,16},{16,8},{24,0},{1,25},{9,17},{17,9},{25,1},{2,26},{10... | collective-permute-start | bytes 221192 | tf_op jit(solution)/shard_map/ppermute | solution.py:377
  97.7 6.6 %collective-permute-start.18 = (f32[144,128]{1,0:T(8,128)}, f32[144,128]{1,0:T(8,128)S(1)}, u32[]{:S(2)}, u32[]{:S(2)}) collective-permute-start(f32[144,128]{1,0:T(8,128)} %add_cut.5.refs_0_), channel_id=1, source_target_pairs={{0,16},{8,24},{16,0},{24,8},{1,17},{9,25},{17,1},{25,9},{2,18},{10... | collective-permute-start | bytes 221192 | tf_op jit(solution)/shard_map/ppermute | solution.py:377
  97.7 6.6 %collective-permute-start.17 = (f32[144,128]{1,0:T(8,128)}, f32[144,128]{1,0:T(8,128)S(1)}, u32[]{:S(2)}, u32[]{:S(2)}) collective-permute-start(f32[144,128]{1,0:T(8,128)} %add_cut.5.refs_0_), channel_id=1, source_target_pairs={{0,8},{8,0},{16,24},{24,16},{1,9},{9,1},{17,25},{25,17},{2,10},{10... | collective-permute-start | bytes 221192 | tf_op jit(solution)/shard_map/ppermute | solution.py:377
  102.7 1.5 copy-start.14
  104.3 0.7 copy-start.16
  104.9 0.6 copy-start.17
  107.3 8.8 %collective-permute-start.22 = (f32[576,128]{1,0:T(8,128)}, f32[576,128]{1,0:T(8,128)S(1)}, u32[]{:S(2)}, u32[]{:S(2)}) collective-permute-start(f32[576,128]{1,0:T(8,128)} %place.1.refs_0_), channel_id=1, source_target_pairs={{0,6},{2,4},{4,2},{6,0},{1,7},{3,5},{5,3},{7,1},{8,14},{10,12},{12... | collective-permute-start | bytes 884744 | tf_op jit(solution)/shard_map/ppermute | solution.py:377
  108.8 10.3 %collective-permute-start.21 = (f32[576,128]{1,0:T(8,128)}, f32[576,128]{1,0:T(8,128)S(1)}, u32[]{:S(2)}, u32[]{:S(2)}) collective-permute-start(f32[576,128]{1,0:T(8,128)} %place.1.refs_0_), channel_id=1, source_target_pairs={{0,4},{2,6},{4,0},{6,2},{1,5},{3,7},{5,1},{7,3},{8,12},{10,14},{12... | collective-permute-start | bytes 884744 | tf_op jit(solution)/shard_map/ppermute | solution.py:377
  109.3 10.1 %collective-permute-start.20 = (f32[576,128]{1,0:T(8,128)}, f32[576,128]{1,0:T(8,128)S(1)}, u32[]{:S(2)}, u32[]{:S(2)}) collective-permute-start(f32[576,128]{1,0:T(8,128)} %place.1.refs_0_), channel_id=1, source_target_pairs={{0,2},{2,0},{4,6},{6,4},{1,3},{3,1},{5,7},{7,5},{8,10},{10,8},{12,... | collective-permute-start | bytes 884744 | tf_op jit(solution)/shard_map/ppermute | solution.py:377
  110.8 8.9 %collective-permute-start.23 = (f32[576,128]{1,0:T(8,128)}, f32[576,128]{1,0:T(8,128)S(1)}, u32[]{:S(2)}, u32[]{:S(2)}) collective-permute-start(f32[576,128]{1,0:T(8,128)} %place.1.refs_0_), channel_id=1, source_target_pairs={{0,1},{1,0},{2,3},{3,2},{4,5},{5,4},{6,7},{7,6},{8,9},{9,8},{10,11... | collective-permute-start | bytes 884744 | tf_op jit(solution)/shard_map/ppermute | solution.py:377
  116.1 3.5 %collective-permute-start.26 = (f32[576,128]{1,0:T(8,128)S(1)}, f32[576,128]{1,0:T(8,128)S(1)}, u32[]{:S(2)}, u32[]{:S(2)}) collective-permute-start(f32[576,128]{1,0:T(8,128)S(1)} %collective-permute-done.22.refs_3_), channel_id=1, source_target_pairs={{0,1},{1,0},{2,3},{3,2},{4,5},{5,4},{6,7},{7,6},{8,9},{9,8},{10,11... | collective-permute-start | bytes 884744 | tf_op jit(solution)/shard_map/ppermute | solution.py:377
  119.1 1.6 collective-permute-start.25
  119.4 1.8 %collective-permute-start.24 = (f32[576,128]{1,0:T(8,128)S(1)}, f32[576,128]{1,0:T(8,128)S(1)}, u32[]{:S(2)}, u32[]{:S(2)}) collective-permute-start(f32[576,128]{1,0:T(8,128)S(1)} %collective-permute-done.20.refs_1_), channel_id=1, source_target_pairs={{0,1},{1,0},{2,3},{3,2},{4,5},{5,4},{6,7},{7,6},{8,9},{9,8},{10,11... | collective-permute-start | bytes 884744 | tf_op jit(solution)/shard_map/ppermute | solution.py:377
  121.1 1.0 copy-start.3

commit v3 on v2

--- a/solution.py
+++ b/solution.py
@@ -35,133 +35,137 @@
     return c
 
 
-def squares(x):
-    wide = x.astype(jnp.float32)
-    wide = wide * wide
-    hi = wide.astype(jnp.bfloat16)
-    return hi, (wide - hi.astype(jnp.float32)).astype(jnp.bfloat16)
-
-
 def nt(a, b):
     return lax.dot_general(a, b, (((1,), (1,)), ((), ())), preferred_element_type=jnp.float32)
 
 
+def lane_tiles_of_squares(x):
+    total = None
+    for l in range(0, x.shape[1], B):
+        wide = x[:, l : l + B].astype(jnp.float32)
+        total = wide * wide if total is None else total + wide * wide
+    return total
+
+
 def squares_mean_column(x):
-    ones = jnp.ones((B, x.shape[1]), jnp.bfloat16)
-    hi, lo = squares(x)
-    return (nt(hi, ones) + nt(lo, ones)) / x.shape[1] + EPS
+    total = jnp.sum(lane_tiles_of_squares(x), axis=1, keepdims=True)
+    return jnp.broadcast_to(total * (1.0 / x.shape[1]) + EPS, (x.shape[0], B))
 
 
 def squares_mean_row(x):
-    ones = jnp.ones((8, x.shape[1]), jnp.bfloat16)
-    hi, lo = squares(x)
-    return (nt(ones, hi) + nt(ones, lo)) / x.shape[1] + EPS
+    total = lane_tiles_of_squares(x)
+    rows = [jnp.sum(total[i : i + B].T, axis=0, keepdims=True) for i in range(0, x.shape[0], B)]
+    row = jnp.concatenate(rows, axis=1) * (1.0 / x.shape[1]) + EPS
+    return jnp.broadcast_to(row, (8, x.shape[0]))
 
 
 def spread(column, lanes):
     return jnp.concatenate([column] * (lanes // B), axis=1)
 
 
-def fill_cross(marks_ref, marks_row, rows, emb_ref, u_ref, k_ref, vq_ref, x_ref, x_row, chunk):
-    e = emb_ref.shape[1]
-    m = emb_ref.shape[0]
-
-    def block(j, _):
-        row = pl.multiple_of(marks_row + j * B, B)
-        out = pl.multiple_of(x_row + j * B, B)
-        tile = marks_ref[pl.ds(row, B), :]
-        k_ref[...] = nt(tile, emb_ref[...])
-        vq_ref[...] = squares_mean_column(tile)
-
-        def part(i, _):
-            r = pl.multiple_of(i * chunk, chunk)
-            vq = vq_ref[pl.ds(r, chunk), :]
-            v_inv = lax.rsqrt(vq)
-            v_root = vq * v_inv
-            up = jnp.concatenate([u_ref[:8, :]] * (chunk // 8), axis=0)
-            ur = jnp.concatenate([u_ref[8:, :]] * (chunk // 8), axis=0)
-            c = recursion(k_ref[pl.ds(r, chunk), :] * up * spread(v_inv * (1.0 / e), m))
-            x_ref[pl.ds(out + r, chunk), :] = (c * ur * spread(v_root * GROWTH, m)).astype(jnp.bfloat16)
-            return 0
-
-        lax.fori_loop(0, B // chunk, part, 0)
+CHUNK = 16
+
+
+def fill_cross(marks_ref, emb_ref, u_ref, k_ref, vq_ref, x_ref, x_row):
+    m, e = emb_ref.shape
+    k_ref[...] = nt(marks_ref[...], emb_ref[...])
+    vq_ref[...] = squares_mean_column(marks_ref[...])
+
+    def part(i, _):
+        r = pl.multiple_of(i * CHUNK, CHUNK)
+        vq = vq_ref[pl.ds(r, CHUNK), :]
+        v_inv = lax.rsqrt(vq)
+        v_root = vq * v_inv
+        up = jnp.concatenate([u_ref[:8, :]] * (CHUNK // 8), axis=0)
+        ur = jnp.concatenate([u_ref[8:, :]] * (CHUNK // 8), axis=0)
+        c = recursion(k_ref[pl.ds(r, CHUNK), :] * up * spread(v_inv * (1.0 / e), m))
+        x_ref[pl.ds(x_row(r), CHUNK), :] = (c * ur * spread(v_root * GROWTH, m)).astype(jnp.bfloat16)
         return 0
 
-    lax.fori_loop(0, rows // B, block, 0)
-
-
-def fill_u(emb_ref, u_ref):
+    lax.fori_loop(0, marks_ref.shape[0] // CHUNK, part, 0)
+
+
+def own_kernel(marks_ref, emb_ref, x_ref, u_ref, k_ref, vq_ref):
     uq = squares_mean_row(emb_ref[...])
     inv = lax.rsqrt(uq)
     u_ref[:8, :] = inv
     u_ref[8:, :] = uq * inv
-
-
-def own_kernel(marks_ref, emb_ref, x_ref, u_ref, k_ref, vq_ref):
-    fill_u(emb_ref, u_ref)
-    fill_cross(marks_ref, 0, marks_ref.shape[0], emb_ref, u_ref, k_ref, vq_ref, x_ref, 0, 16)
+    fill_cross(marks_ref, emb_ref, u_ref, k_ref, vq_ref, x_ref, lambda r: r)
 
 
 def own_cross(landmarks, embeddings):
     m = embeddings.shape[0]
+    shard = landmarks.shape[0]
     vmem = pl.BlockSpec(memory_space=pltpu.VMEM)
     return pl.pallas_call(
         own_kernel,
         out_shape=(
-            jax.ShapeDtypeStruct((landmarks.shape[0], m), jnp.bfloat16),
+            jax.ShapeDtypeStruct((shard, m), jnp.bfloat16),
             jax.ShapeDtypeStruct((16, m), jnp.float32),
         ),
         in_specs=[vmem, vmem],
         out_specs=(vmem, vmem),
-        scratch_shapes=[pltpu.VMEM((B, m), jnp.float32), pltpu.VMEM((B, B), jnp.float32)],
-        compiler_params=pltpu.CompilerParams(vmem_limit_bytes=24 << 20),
-        cost_estimate=pl.CostEstimate(flops=10**10, transcendentals=10**7, bytes_accessed=10**7),
+        scratch_shapes=[pltpu.VMEM((shard, m), jnp.float32), pltpu.VMEM((shard, B), jnp.float32)],
+        compiler_params=pltpu.CompilerParams(vmem_limit_bytes=12 << 20),
         name="own_cross",
     )(landmarks, embeddings)
 
 
 def gram_kernel(plan, at_ref, emb_ref, mine_ref, own_ref, u_ref, x_mine_ref, *refs):
     lands, chips, cores, split, all_points, total_rows = plan
-    count = (chips - 1 + 1) * (cores if split else 1)
+    count = chips * (cores if split else 1)
     far = refs[:count]
     keep_ref, send_ref, marks_ref, x_ref, k_ref, vq_ref, ridge_ref, out_ref = refs[count:]
     shard, e = mine_ref.shape
     n = shard * lands
-    m = emb_ref.shape[0]
     land, chip, core = at_ref[0], at_ref[1], at_ref[2]
     here = pl.multiple_of(land * shard, shard)
-    marks_ref[pl.ds(here, shard), :] = mine_ref[...]
     x_ref[pl.ds(here, shard), :] = x_mine_ref[...]
     piece = far[0].shape[0] // (lands - 1)
     for a in range(cores if split else 1):
         for t in range(chips):
             slot = ((chip ^ t) * cores + (core ^ a)) if split else (chip ^ t)
             for s in range(1, lands):
-                to = pl.multiple_of((land ^ s) * shard + slot * piece, piece)
+                to = pl.multiple_of((s - 1) * shard + slot * piece, piece)
                 marks_ref[pl.ds(to, piece), :] = far[a * chips + t][(s - 1) * piece : s * piece, :]
-    for s in range(1, lands):
-        there = pl.multiple_of((land ^ s) * shard, shard)
-        fill_cross(marks_ref, there, shard, emb_ref, u_ref, k_ref, vq_ref, x_ref, there, 16)
+
+    def x_row(r):
+        s = r // shard + 1
+        return pl.multiple_of((land ^ s) * shard + r % shard, CHUNK)
+
+    fill_cross(marks_ref, emb_ref, u_ref, k_ref, vq_ref, x_ref, x_row)
 
     share = own_ref.shape[0]
     oq = squares_mean_column(own_ref[...])
-    vr = squares_mean_row(marks_ref[...])
-    o_inv, v_inv = lax.rsqrt(oq), lax.rsqrt(vr)
-    k_own = nt(own_ref[...], marks_ref[...])
-    for i in range(share // 8):
-        oi = o_inv[8 * i : 8 * i + 8]
-        c = recursion(k_own[8 * i : 8 * i + 8] * v_inv * spread(oi * (1.0 / e), n))
-        root = oq[8 * i : 8 * i + 8] * oi
-        ridge_ref[8 * i : 8 * i + 8, :] = c * (vr * v_inv) * spread(root * (RIDGE * GROWTH), n)
+    o_inv = lax.rsqrt(oq)
+
+    def ridge(marks, marks_q, to):
+        k_own = nt(own_ref[...], marks)
+        for l in range(0, shard, B):
+            vq = marks_q[l : l + B].T[:8]
+            v_inv = lax.rsqrt(vq)
+            for i in range(share // 8):
+                oi = o_inv[8 * i : 8 * i + 8]
+                c = recursion(k_own[8 * i : 8 * i + 8, l : l + B] * v_inv * (oi * (1.0 / e)))
+                root = oq[8 * i : 8 * i + 8] * oi
+                ridge_ref[8 * i : 8 * i + 8, pl.ds(to + l, B)] = c * (vq * v_inv) * (root * (RIDGE * GROWTH))
+
+    ridge(mine_ref[...], squares_mean_column(mine_ref[...]), here)
+    for s in range(1, lands):
+        rows = slice((s - 1) * shard, s * shard)
+        ridge(marks_ref[rows, :], vq_ref[rows, :], pl.multiple_of((land ^ s) * shard, shard))
 
     position = land * shard + (chip * cores + core) * share
     row_block = position // B
     offset = position % B
+    wide = 2 * B
+    for w in range(n // wide):
+        both = nt(x_ref[: (w + 1) * wide, :], x_ref[w * wide : (w + 1) * wide, :]) * (1.0 / all_points)
+        for j in (2 * w, 2 * w + 1):
+            start = j * (j + 1) // 2 * B
+            out_ref[start : start + (j + 1) * B, :] = both[: (j + 1) * B, (j % 2) * B : (j % 2 + 1) * B]
     for j in range(n // B):
         start = j * (j + 1) // 2 * B
-        out_ref[start : start + (j + 1) * B, :] = nt(
-            x_ref[: (j + 1) * B, :], x_ref[j * B : (j + 1) * B, :]
-        ) * (1.0 / all_points)
 
         @pl.when(row_block <= j)
         def _():
@@ -176,6 +180,7 @@
 def local_normal(at, plan, embeddings, landmarks, own, u, x_mine, far):
     lands, chips, cores, split, all_points, total_rows = plan
     n, m = landmarks.shape[0] * lands, embeddings.shape[0]
+    away = n - landmarks.shape[0]
     half = jax.ShapeDtypeStruct((total_rows // cores, B), jnp.float32)
     vmem = pl.BlockSpec(memory_space=pltpu.VMEM)
     return pl.pallas_call(
@@ -184,14 +189,14 @@
         in_specs=[pl.BlockSpec(memory_space=pltpu.SMEM)] + [vmem] * (5 + len(far)),
         out_specs=(vmem, vmem),
         scratch_shapes=[
-            pltpu.VMEM((n, landmarks.shape[1]), jnp.bfloat16),
+            pltpu.VMEM((away, landmarks.shape[1]), jnp.bfloat16),
             pltpu.VMEM((n, m), jnp.bfloat16),
-            pltpu.VMEM((B, m), jnp.float32),
-            pltpu.VMEM((B, B), jnp.float32),
+            pltpu.VMEM((away, m), jnp.float32),
+            pltpu.VMEM((away, B), jnp.float32),
             pltpu.VMEM((own.shape[0], n), jnp.float32),
             pltpu.VMEM((total_rows, B), jnp.float32),
         ],
-        compiler_params=pltpu.CompilerParams(vmem_limit_bytes=40 << 20),
+        compiler_params=pltpu.CompilerParams(vmem_limit_bytes=24 << 20),
         name="gram",
     )(at, embeddings, landmarks, own, u, x_mine, *far)
 
@@ -215,6 +220,7 @@
         out_shape=tuple([jax.ShapeDtypeStruct((h, B), jnp.float32)] * ways),
         in_specs=[pl.BlockSpec(memory_space=pltpu.SMEM)] + [vmem] * len(parts),
         out_specs=tuple([vmem] * ways),
+        compiler_params=pltpu.CompilerParams(vmem_limit_bytes=8 << 20),
         name="add_cut",
     )(at, *parts)
 
@@ -233,6 +239,7 @@
         out_shape=jax.ShapeDtypeStruct((parts[0].shape[0] * len(parts), B), jnp.float32),
         in_specs=[pl.BlockSpec(memory_space=pltpu.SMEM)] + [vmem] * len(parts),
         out_specs=vmem,
+        compiler_params=pltpu.CompilerParams(vmem_limit_bytes=8 << 20),
         name="place",
     )(at, *parts)
 
@@ -368,7 +375,7 @@
             pltpu.VMEM((B, n), jnp.float32),
             pltpu.VMEM((B, B), jnp.float32),
         ],
-        compiler_params=pltpu.CompilerParams(vmem_limit_bytes=40 << 20),
+        compiler_params=pltpu.CompilerParams(vmem_limit_bytes=24 << 20),
         name="chol",
     )(at, *parts)
 
@@ -405,10 +412,11 @@
         piece = lax.dynamic_slice_in_dim(landmarks, chip * (shard // chips), shard // chips, 0)
     z = jnp.concatenate(spread_out(piece, "land")[1:], 0)
     far = spread_out(z, "chip")
+    x_mine, u = own_cross(landmarks, embeddings)
     if split:
+        far, x_mine, u = lax.optimization_barrier((far, x_mine, u))
         for a in range(1, cores):
             far = far + [swap(f, "core", a) for f in far[:chips]]
-    x_mine, u = own_cross(landmarks, embeddings)
     plan = (lands, chips, cores, split, embeddings.shape[0] * devices, total_rows)
     keep, send = local_normal(at, plan, embeddings, landmarks, own, u, x_mine, far)
 

time: 159 us -> 136 us (0.86)
  Pallas kernels: 78.2 us -> 62.5 us
  local copies, waits for them, and re-layouts: 8.97 us -> 3.3 us
  waiting for transfers between devices: 45.4 us -> 42.9 us
    pallas_call x1, Pallas kernels: 26.6 us -> 18.6 us  [local_normal(): pl.pallas_call(functools.partial(gram_kernel, plan), out_shape=(half, hal...]
    unnamed x38 -> x10, local copies, waits for them, and re-layouts: 8.17 us -> 2.42 us
    pallas_call x3, Pallas kernels: 6.47 us -> 1.83 us  [add_cut(): pl.pallas_call(functools.partial(add_cut_kernel, ways, axis), out_shape=t...]
    ppermute x27, waiting for transfers between devices: 45.4 us -> 42.9 us  [swap(): lax.ppermute(x, axis, [(i, i ^ s) for i in range(lax.axis_size(axis))])]
    pallas_call x1, Pallas kernels: 6.95 us -> 5.12 us  [own_cross(): pl.pallas_call(own_kernel, out_shape=(jax.ShapeDtypeStruct((shard, m), jn...]
  transfers between devices with their start and end apart: 27 -> 27, of which waited for: 17 -> 16; matrix products, arithmetic and copies ran while one was open for 0% -> 0% of each run, Pallas kernels for 4% -> 4%
where the time goes in v3:
time: 136 us
  Pallas kernels  62.5 us (46%)
  waiting for transfers between devices  42.9 us (32%)
  starting transfers between devices  27.1 us (20%)
  local copies, waits for them, and re-layouts  3.3 us (2%)
    ppermute x27, waiting for transfers between devices, swap(): lax.ppermute(x, axis, [(i, i ^ s) for i in range(lax.axis_size(axis))])  42.9 us
    pallas_call x1, Pallas kernels, cholesky_upper(): pl.pallas_call(functools.partial(chol_kernel, chips, cores), out_shape=ja...  36.4 us
    ppermute x27, starting transfers between devices, swap(): lax.ppermute(x, axis, [(i, i ^ s) for i in range(lax.axis_size(axis))])  27.1 us
    pallas_call x1, Pallas kernels, local_normal(): pl.pallas_call(functools.partial(gram_kernel, plan), out_shape=(half, hal...  18.6 us
    pallas_call x1, Pallas kernels, own_cross(): pl.pallas_call(own_kernel, out_shape=(jax.ShapeDtypeStruct((shard, m), jn...  5.12 us
  transfers between devices with their start and end apart: 27, of which 16 were waited for; matrix products, arithmetic and copies ran while one was open for 0% of the time, Pallas kernels for 4%

profile of v3, /device:TPU:0, one launch (start us, length us, event | category | flops | bytes accessed | tf_op | source)
XLA Modules:
  0.0 136.0 jit_solution(7264934721511927199)
XLA Ops:
  0.0 0.9 constant_dynamic-slice_fusion.own_ref
  0.9 3.0 %collective-permute-start = (bf16[32,768]{1,0:T(8,128)(2,1)S(1)}, bf16[32,768]{1,0:T(8,128)(2,1)S(1)}, u32[]{:S(2)}, u32[]{:S(2)}) collective-permute-start(bf16[32,768]{1,0:T(8,128)(2,1)S(1)} %constant_dynamic-slice_fusion.own_ref), channel_id=1, source_target_pairs={{0,8},{8,0},{16,24},{24,16},{1,9},{9,1},{17,25},{25,17},{2,10},{10... | collective-permute-start | bytes 147464 | tf_op jit(solution)/shard_map/ppermute | solution.py:384
  3.9 2.5 %collective-permute-start.2 = (bf16[32,768]{1,0:T(8,128)(2,1)S(1)}, bf16[32,768]{1,0:T(8,128)(2,1)S(1)}, u32[]{:S(2)}, u32[]{:S(2)}) collective-permute-start(bf16[32,768]{1,0:T(8,128)(2,1)S(1)} %constant_dynamic-slice_fusion.own_ref), channel_id=1, source_target_pairs={{0,24},{8,16},{16,8},{24,0},{1,25},{9,17},{17,9},{25,1},{2,26},{10... | collective-permute-start | bytes 147464 | tf_op jit(solution)/shard_map/ppermute | solution.py:384
  6.4 0.1 collective-permute-start.1
  6.5 5.4 %collective-permute-done.1 = bf16[32,768]{1,0:T(8,128)(2,1)S(1)} collective-permute-done((bf16[32,768]{1,0:T(8,128)(2,1)S(1)}, bf16[32,768]{1,0:T(8,128)(2,1)S(1)}, u32[]{:S(2)}, u32[]{:S(2)}) %collective-permute-start.1) | collective-permute-done | bytes 49184 | tf_op jit(solution)/shard_map/ppermute | solution.py:384
  11.9 2.5 %collective-permute-start.5 = (bf16[96,768]{1,0:T(8,128)(2,1)S(1)}, bf16[96,768]{1,0:T(8,128)(2,1)S(1)}, u32[]{:S(2)}, u32[]{:S(2)}) collective-permute-start(bf16[96,768]{1,0:T(8,128)(2,1)S(1)} %constant_dynamic-update-slice_fusion.refs_0_), channel_id=1, source_target_pairs={{0,6},{2,4},{4,2},{6,0},{1,7},{3,5},{5,3},{7,1},{8,14},{10,12},{12... | collective-permute-start | bytes 442376 | tf_op jit(solution)/shard_map/ppermute | solution.py:384
  14.4 0.5 collective-permute-start.4
  14.9 0.5 collective-permute-start.3
  15.5 1.4 %copy-done = bf16[1024,768]{1,0:T(8,128)(2,1)S(1)} copy-done((bf16[1024,768]{1,0:T(8,128)(2,1)S(1)}, bf16[1024,768]{1,0:T(8,128)(2,1)}, u32[]{:S(2)}) %copy-start) | copy-done | bytes 1572888
  16.9 1.0 copy-done.2
  17.9 5.1 %own_cross.1 = (bf16[256,1024]{1,0:T(8,128)(2,1)S(1)}, f32[16,1024]{1,0:T(8,128)S(1)}) custom-call(bf16[256,768]{1,0:T(8,128)(2,1)S(1)} %copy-done.2, bf16[1024,768]{1,0:T(8,128)(2,1)S(1)} %copy-done), custom_call_target="tpu_custom_call" | custom-call | tf_op jit(solution)/shard_map/own_cross/pallas_call | solution.py:100
  23.1 0.5 collective-permute-start.7
  23.7 0.4 collective-permute-start.9
  24.2 0.3 collective-permute-done.6.refs_4_
  24.5 0.2 collective-permute-done.7.refs_5_
  24.7 0.4 collective-permute-done.8.refs_6_
  25.1 0.2 collective-permute-done.9.refs_7_
  25.3 18.6 %gram.1 = (f32[2304,128]{1,0:T(8,128)S(1)}, f32[2304,128]{1,0:T(8,128)S(1)}) custom-call(s32[3]{0:T(128)S(1)} %pad_add_fusion.at_ref, bf16[1024,768]{1,0:T(8,128)(2,1)S(1)} %copy-done.1, bf16[256,768]{1,0:T(8,128)(2,1)S(1)} %copy-done.3, bf16[32,768]{1,0:T(8,128)(2,1)S(1)} %constant_dynamic-slice_fusion.own_ref, f32[16,1024]{1,0:T(8,128)S(1)} %get-tuple-element.25.u_ref, ...), custom_call_target="tpu_custom_call" | custom-call | tf_op jit(solution)/shard_map/gram/pallas_call | solution.py:186
  43.9 0.4 collective-permute-start.10
  44.3 2.5 %collective-permute-done.10.refs_1_ = f32[2304,128]{1,0:T(8,128)S(1)} collective-permute-done((f32[2304,128]{1,0:T(8,128)S(1)}, f32[2304,128]{1,0:T(8,128)S(1)}, u32[]{:S(2)}, u32[]{:S(2)}) %collective-permute-start.10) | collective-permute-done | bytes 1179680 | tf_op jit(solution)/shard_map/ppermute | solution.py:384
  46.9 0.7 add_cut.3
  47.5 1.6 %collective-permute-start.11 = (f32[576,128]{1,0:T(8,128)S(1)}, f32[576,128]{1,0:T(8,128)S(1)}, u32[]{:S(2)}, u32[]{:S(2)}) collective-permute-start(f32[576,128]{1,0:T(8,128)S(1)} %get-tuple-element.34), channel_id=1, source_target_pairs={{0,2},{2,0},{4,6},{6,4},{1,3},{3,1},{5,7},{7,5},{8,10},{10,8},{12,... | collective-permute-start | bytes 884744 | tf_op jit(solution)/shard_map/ppermute | solution.py:384
  49.1 1.5 %collective-permute-start.12 = (f32[576,128]{1,0:T(8,128)S(1)}, f32[576,128]{1,0:T(8,128)S(1)}, u32[]{:S(2)}, u32[]{:S(2)}) collective-permute-start(f32[576,128]{1,0:T(8,128)S(1)} %get-tuple-element.35), channel_id=1, source_target_pairs={{0,4},{2,6},{4,0},{6,2},{1,5},{3,7},{5,1},{7,3},{8,12},{10,14},{12... | collective-permute-start | bytes 884744 | tf_op jit(solution)/shard_map/ppermute | solution.py:384
  50.6 0.5 collective-permute-start.13
  51.1 6.3 %collective-permute-done.11.refs_1_ = f32[576,128]{1,0:T(8,128)S(1)} collective-permute-done((f32[576,128]{1,0:T(8,128)S(1)}, f32[576,128]{1,0:T(8,128)S(1)}, u32[]{:S(2)}, u32[]{:S(2)}) %collective-permute-start.11) | collective-permute-done | bytes 294944 | tf_op jit(solution)/shard_map/ppermute | solution.py:384
  57.4 6.9 %collective-permute-done.12.refs_2_ = f32[576,128]{1,0:T(8,128)S(1)} collective-permute-done((f32[576,128]{1,0:T(8,128)S(1)}, f32[576,128]{1,0:T(8,128)S(1)}, u32[]{:S(2)}, u32[]{:S(2)}) %collective-permute-start.12) | collective-permute-done | bytes 294944 | tf_op jit(solution)/shard_map/ppermute | solution.py:384
  64.3 0.6 add_cut.4
  64.9 0.3 collective-permute-start.14
  65.3 2.4 %collective-permute-start.15 = (f32[144,128]{1,0:T(8,128)S(1)}, f32[144,128]{1,0:T(8,128)S(1)}, u32[]{:S(2)}, u32[]{:S(2)}) collective-permute-start(f32[144,128]{1,0:T(8,128)S(1)} %get-tuple-element.39), channel_id=1, source_target_pairs={{0,16},{8,24},{16,0},{24,8},{1,17},{9,25},{17,1},{25,9},{2,18},{10... | collective-permute-start | bytes 221192 | tf_op jit(solution)/shard_map/ppermute | solution.py:384
  67.7 1.7 %collective-permute-start.16 = (f32[144,128]{1,0:T(8,128)S(1)}, f32[144,128]{1,0:T(8,128)S(1)}, u32[]{:S(2)}, u32[]{:S(2)}) collective-permute-start(f32[144,128]{1,0:T(8,128)S(1)} %get-tuple-element.40), channel_id=1, source_target_pairs={{0,24},{8,16},{16,8},{24,0},{1,25},{9,17},{17,9},{25,1},{2,26},{10... | collective-permute-start | bytes 221192 | tf_op jit(solution)/shard_map/ppermute | solution.py:384
  69.4 3.3 %collective-permute-done.15.refs_2_ = f32[144,128]{1,0:T(8,128)S(1)} collective-permute-done((f32[144,128]{1,0:T(8,128)S(1)}, f32[144,128]{1,0:T(8,128)S(1)}, u32[]{:S(2)}, u32[]{:S(2)}) %collective-permute-start.15) | collective-permute-done | bytes 73760 | tf_op jit(solution)/shard_map/ppermute | solution.py:384
  72.8 1.2 collective-permute-done.16.refs_3_
  73.9 0.6 add_cut.5.refs_0_
  74.5 1.8 %collective-permute-start.19 = (f32[144,128]{1,0:T(8,128)S(1)}, f32[144,128]{1,0:T(8,128)S(1)}, u32[]{:S(2)}, u32[]{:S(2)}) collective-permute-start(f32[144,128]{1,0:T(8,128)S(1)} %add_cut.5.refs_0_), channel_id=1, source_target_pairs={{0,24},{8,16},{16,8},{24,0},{1,25},{9,17},{17,9},{25,1},{2,26},{10... | collective-permute-start | bytes 221192 | tf_op jit(solution)/shard_map/ppermute | solution.py:384
  76.3 1.0 collective-permute-start.18
  77.3 1.6 %collective-permute-start.17 = (f32[144,128]{1,0:T(8,128)S(1)}, f32[144,128]{1,0:T(8,128)S(1)}, u32[]{:S(2)}, u32[]{:S(2)}) collective-permute-start(f32[144,128]{1,0:T(8,128)S(1)} %add_cut.5.refs_0_), channel_id=1, source_target_pairs={{0,8},{8,0},{16,24},{24,16},{1,9},{9,1},{17,25},{25,17},{2,10},{10... | collective-permute-start | bytes 221192 | tf_op jit(solution)/shard_map/ppermute | solution.py:384
  79.0 1.9 %collective-permute-done.19.refs_3_ = f32[144,128]{1,0:T(8,128)S(1)} collective-permute-done((f32[144,128]{1,0:T(8,128)S(1)}, f32[144,128]{1,0:T(8,128)S(1)}, u32[]{:S(2)}, u32[]{:S(2)}) %collective-permute-start.19) | collective-permute-done | bytes 73760 | tf_op jit(solution)/shard_map/ppermute | solution.py:384
  80.8 1.9 %collective-permute-done.18.refs_2_ = f32[144,128]{1,0:T(8,128)S(1)} collective-permute-done((f32[144,128]{1,0:T(8,128)S(1)}, f32[144,128]{1,0:T(8,128)S(1)}, u32[]{:S(2)}, u32[]{:S(2)}) %collective-permute-start.18) | collective-permute-done | bytes 73760 | tf_op jit(solution)/shard_map/ppermute | solution.py:384
  82.7 0.6 place.1.refs_0_
  83.3 1.3 collective-permute-start.22
  84.6 1.7 %collective-permute-start.21 = (f32[576,128]{1,0:T(8,128)S(1)}, f32[576,128]{1,0:T(8,128)S(1)}, u32[]{:S(2)}, u32[]{:S(2)}) collective-permute-start(f32[576,128]{1,0:T(8,128)S(1)} %place.1.refs_0_), channel_id=1, source_target_pairs={{0,4},{2,6},{4,0},{6,2},{1,5},{3,7},{5,1},{7,3},{8,12},{10,14},{12... | collective-permute-start | bytes 884744 | tf_op jit(solution)/shard_map/ppermute | solution.py:384
  86.3 0.5 collective-permute-start.20
  86.9 7.4 %collective-permute-done.22.refs_3_ = f32[576,128]{1,0:T(8,128)S(1)} collective-permute-done((f32[576,128]{1,0:T(8,128)S(1)}, f32[576,128]{1,0:T(8,128)S(1)}, u32[]{:S(2)}, u32[]{:S(2)}) %collective-permute-start.22) | collective-permute-done | bytes 294944 | tf_op jit(solution)/shard_map/ppermute | solution.py:384
  94.2 3.4 %collective-permute-done.21.refs_2_ = f32[576,128]{1,0:T(8,128)S(1)} collective-permute-done((f32[576,128]{1,0:T(8,128)S(1)}, f32[576,128]{1,0:T(8,128)S(1)}, u32[]{:S(2)}, u32[]{:S(2)}) %collective-permute-start.21) | collective-permute-done | bytes 294944 | tf_op jit(solution)/shard_map/ppermute | solution.py:384
  97.7 0.5 collective-permute-start.24
  98.2 1.1 collective-permute-done.25.refs_6_
  99.2 0.4 collective-permute-done.24.refs_5_
  99.6 36.4 %chol.1 = f32[1024,1024]{1,0:T(8,128)} custom-call(s32[3]{0:T(128)S(1)} %pad_add_fusion.at_ref, f32[576,128]{1,0:T(8,128)S(1)} %place.1.refs_0_, f32[576,128]{1,0:T(8,128)S(1)} %collective-permute-done.20.refs_1_, f32[576,128]{1,0:T(8,128)S(1)} %collective-permute-done.21.refs_2_, f32[576,128]{1,0:T(8,128)S(1)} %collective-permute-done.22.refs_3_, ...), custom_call_target="tpu_custom_call" | custom-call | tf_op jit(solution)/shard_map/chol/pallas_call | solution.py:368
  (26 shorter events, 0.3 us)
Async XLA Ops:
  0.0 25.3 %copy-start.3 = (bf16[256,768]{1,0:T(8,128)(2,1)S(1)}, bf16[256,768]{1,0:T(8,128)(2,1)}, u32[]{:S(2)}) copy-start(bf16[256,768]{1,0:T(8,128)(2,1)} %mine_ref.1) | copy-start | bytes 1179652
  0.9 5.6 %collective-permute-start = (bf16[32,768]{1,0:T(8,128)(2,1)S(1)}, bf16[32,768]{1,0:T(8,128)(2,1)S(1)}, u32[]{:S(2)}, u32[]{:S(2)}) collective-permute-start(bf16[32,768]{1,0:T(8,128)(2,1)S(1)} %constant_dynamic-slice_fusion.own_ref), channel_id=1, source_target_pairs={{0,8},{8,0},{16,24},{24,16},{1,9},{9,1},{17,25},{25,17},{2,10},{10... | collective-permute-start | bytes 147464 | tf_op jit(solution)/shard_map/ppermute | solution.py:384
  3.9 8.0 %collective-permute-start.2 = (bf16[32,768]{1,0:T(8,128)(2,1)S(1)}, bf16[32,768]{1,0:T(8,128)(2,1)S(1)}, u32[]{:S(2)}, u32[]{:S(2)}) collective-permute-start(bf16[32,768]{1,0:T(8,128)(2,1)S(1)} %constant_dynamic-slice_fusion.own_ref), channel_id=1, source_target_pairs={{0,24},{8,16},{16,8},{24,0},{1,25},{9,17},{17,9},{25,1},{2,26},{10... | collective-permute-start | bytes 147464 | tf_op jit(solution)/shard_map/ppermute | solution.py:384
  6.4 5.5 %collective-permute-start.1 = (bf16[32,768]{1,0:T(8,128)(2,1)S(1)}, bf16[32,768]{1,0:T(8,128)(2,1)S(1)}, u32[]{:S(2)}, u32[]{:S(2)}) collective-permute-start(bf16[32,768]{1,0:T(8,128)(2,1)S(1)} %constant_dynamic-slice_fusion.own_ref), channel_id=1, source_target_pairs={{0,16},{8,24},{16,0},{24,8},{1,17},{9,25},{17,1},{25,9},{2,18},{10... | collective-permute-start | bytes 147464 | tf_op jit(solution)/shard_map/ppermute | solution.py:384
  11.9 11.1 %collective-permute-start.5 = (bf16[96,768]{1,0:T(8,128)(2,1)S(1)}, bf16[96,768]{1,0:T(8,128)(2,1)S(1)}, u32[]{:S(2)}, u32[]{:S(2)}) collective-permute-start(bf16[96,768]{1,0:T(8,128)(2,1)S(1)} %constant_dynamic-update-slice_fusion.refs_0_), channel_id=1, source_target_pairs={{0,6},{2,4},{4,2},{6,0},{1,7},{3,5},{5,3},{7,1},{8,14},{10,12},{12... | collective-permute-start | bytes 442376 | tf_op jit(solution)/shard_map/ppermute | solution.py:384
  14.4 8.6 %collective-permute-start.4 = (bf16[96,768]{1,0:T(8,128)(2,1)S(1)}, bf16[96,768]{1,0:T(8,128)(2,1)S(1)}, u32[]{:S(2)}, u32[]{:S(2)}) collective-permute-start(bf16[96,768]{1,0:T(8,128)(2,1)S(1)} %constant_dynamic-update-slice_fusion.refs_0_), channel_id=1, source_target_pairs={{0,4},{2,6},{4,0},{6,2},{1,5},{3,7},{5,1},{7,3},{8,12},{10,14},{12... | collective-permute-start | bytes 442376 | tf_op jit(solution)/shard_map/ppermute | solution.py:384
  14.9 8.1 %collective-permute-start.3 = (bf16[96,768]{1,0:T(8,128)(2,1)S(1)}, bf16[96,768]{1,0:T(8,128)(2,1)S(1)}, u32[]{:S(2)}, u32[]{:S(2)}) collective-permute-start(bf16[96,768]{1,0:T(8,128)(2,1)S(1)} %constant_dynamic-update-slice_fusion.refs_0_), channel_id=1, source_target_pairs={{0,2},{2,0},{4,6},{6,4},{1,3},{3,1},{5,7},{7,5},{8,10},{10,8},{12,... | collective-permute-start | bytes 442376 | tf_op jit(solution)/shard_map/ppermute | solution.py:384
  15.5 1.4 %copy-start = (bf16[1024,768]{1,0:T(8,128)(2,1)S(1)}, bf16[1024,768]{1,0:T(8,128)(2,1)}, u32[]{:S(2)}) copy-start(bf16[1024,768]{1,0:T(8,128)(2,1)} %emb_ref.3) | copy-start | bytes 4718596
  16.9 1.0 copy-start.2
  17.9 7.5 %copy-start.1 = (bf16[1024,768]{1,0:T(8,128)(2,1)S(1)}, bf16[1024,768]{1,0:T(8,128)(2,1)}, u32[]{:S(2)}) copy-start(bf16[1024,768]{1,0:T(8,128)(2,1)} %emb_ref.3) | copy-start | bytes 4718596
  23.0 1.4 %collective-permute-start.6 = (bf16[96,768]{1,0:T(8,128)(2,1)S(1)}, bf16[96,768]{1,0:T(8,128)(2,1)S(1)}, u32[]{:S(2)}, u32[]{:S(2)}) collective-permute-start(bf16[96,768]{1,0:T(8,128)(2,1)S(1)} %constant_dynamic-update-slice_fusion.refs_0_), channel_id=1, source_target_pairs={{0,1},{1,0},{2,3},{3,2},{4,5},{5,4},{6,7},{7,6},{8,9},{9,8},{10,11... | collective-permute-start | bytes 442376 | tf_op jit(solution)/shard_map/ppermute | solution.py:384
  23.1 1.6 %collective-permute-start.7 = (bf16[96,768]{1,0:T(8,128)(2,1)S(1)}, bf16[96,768]{1,0:T(8,128)(2,1)S(1)}, u32[]{:S(2)}, u32[]{:S(2)}) collective-permute-start(bf16[96,768]{1,0:T(8,128)(2,1)S(1)} %collective-permute-done.3.refs_1_), channel_id=1, source_target_pairs={{0,1},{1,0},{2,3},{3,2},{4,5},{5,4},{6,7},{7,6},{8,9},{9,8},{10,11... | collective-permute-start | bytes 442376 | tf_op jit(solution)/shard_map/ppermute | solution.py:384
  23.6 1.5 %collective-permute-start.8 = (bf16[96,768]{1,0:T(8,128)(2,1)S(1)}, bf16[96,768]{1,0:T(8,128)(2,1)}, u32[]{:S(2)}, u32[]{:S(2)}) collective-permute-start(bf16[96,768]{1,0:T(8,128)(2,1)S(1)} %collective-permute-done.4.refs_2_), channel_id=1, source_target_pairs={{0,1},{1,0},{2,3},{3,2},{4,5},{5,4},{6,7},{7,6},{8,9},{9,8},{10,11... | collective-permute-start | bytes 442376 | tf_op jit(solution)/shard_map/ppermute | solution.py:384
  23.7 1.6 %collective-permute-start.9 = (bf16[96,768]{1,0:T(8,128)(2,1)S(1)}, bf16[96,768]{1,0:T(8,128)(2,1)}, u32[]{:S(2)}, u32[]{:S(2)}) collective-permute-start(bf16[96,768]{1,0:T(8,128)(2,1)S(1)} %collective-permute-done.5.refs_3_), channel_id=1, source_target_pairs={{0,1},{1,0},{2,3},{3,2},{4,5},{5,4},{6,7},{7,6},{8,9},{9,8},{10,11... | collective-permute-start | bytes 442376 | tf_op jit(solution)/shard_map/ppermute | solution.py:384
  43.9 2.9 %collective-permute-start.10 = (f32[2304,128]{1,0:T(8,128)S(1)}, f32[2304,128]{1,0:T(8,128)S(1)}, u32[]{:S(2)}, u32[]{:S(2)}) collective-permute-start(f32[2304,128]{1,0:T(8,128)S(1)} %get-tuple-element.32), channel_id=1, source_target_pairs={{0,1},{1,0},{2,3},{3,2},{4,5},{5,4},{6,7},{7,6},{8,9},{9,8},{10,11... | collective-permute-start | bytes 3538952 | tf_op jit(solution)/shard_map/ppermute | solution.py:384
  47.5 9.9 %collective-permute-start.11 = (f32[576,128]{1,0:T(8,128)S(1)}, f32[576,128]{1,0:T(8,128)S(1)}, u32[]{:S(2)}, u32[]{:S(2)}) collective-permute-start(f32[576,128]{1,0:T(8,128)S(1)} %get-tuple-element.34), channel_id=1, source_target_pairs={{0,2},{2,0},{4,6},{6,4},{1,3},{3,1},{5,7},{7,5},{8,10},{10,8},{12,... | collective-permute-start | bytes 884744 | tf_op jit(solution)/shard_map/ppermute | solution.py:384
  49.1 15.3 %collective-permute-start.12 = (f32[576,128]{1,0:T(8,128)S(1)}, f32[576,128]{1,0:T(8,128)S(1)}, u32[]{:S(2)}, u32[]{:S(2)}) collective-permute-start(f32[576,128]{1,0:T(8,128)S(1)} %get-tuple-element.35), channel_id=1, source_target_pairs={{0,4},{2,6},{4,0},{6,2},{1,5},{3,7},{5,1},{7,3},{8,12},{10,14},{12... | collective-permute-start | bytes 884744 | tf_op jit(solution)/shard_map/ppermute | solution.py:384
  50.6 13.7 %collective-permute-start.13 = (f32[576,128]{1,0:T(8,128)S(1)}, f32[576,128]{1,0:T(8,128)S(1)}, u32[]{:S(2)}, u32[]{:S(2)}) collective-permute-start(f32[576,128]{1,0:T(8,128)S(1)} %get-tuple-element.36), channel_id=1, source_target_pairs={{0,6},{2,4},{4,2},{6,0},{1,7},{3,5},{5,3},{7,1},{8,14},{10,12},{12... | collective-permute-start | bytes 884744 | tf_op jit(solution)/shard_map/ppermute | solution.py:384
  64.9 4.5 %collective-permute-start.14 = (f32[144,128]{1,0:T(8,128)S(1)}, f32[144,128]{1,0:T(8,128)S(1)}, u32[]{:S(2)}, u32[]{:S(2)}) collective-permute-start(f32[144,128]{1,0:T(8,128)S(1)} %get-tuple-element.38), channel_id=1, source_target_pairs={{0,8},{8,0},{16,24},{24,16},{1,9},{9,1},{17,25},{25,17},{2,10},{10... | collective-permute-start | bytes 221192 | tf_op jit(solution)/shard_map/ppermute | solution.py:384
  65.3 7.5 %collective-permute-start.15 = (f32[144,128]{1,0:T(8,128)S(1)}, f32[144,128]{1,0:T(8,128)S(1)}, u32[]{:S(2)}, u32[]{:S(2)}) collective-permute-start(f32[144,128]{1,0:T(8,128)S(1)} %get-tuple-element.39), channel_id=1, source_target_pairs={{0,16},{8,24},{16,0},{24,8},{1,17},{9,25},{17,1},{25,9},{2,18},{10... | collective-permute-start | bytes 221192 | tf_op jit(solution)/shard_map/ppermute | solution.py:384
  67.7 6.3 %collective-permute-start.16 = (f32[144,128]{1,0:T(8,128)S(1)}, f32[144,128]{1,0:T(8,128)S(1)}, u32[]{:S(2)}, u32[]{:S(2)}) collective-permute-start(f32[144,128]{1,0:T(8,128)S(1)} %get-tuple-element.40), channel_id=1, source_target_pairs={{0,24},{8,16},{16,8},{24,0},{1,25},{9,17},{17,9},{25,1},{2,26},{10... | collective-permute-start | bytes 221192 | tf_op jit(solution)/shard_map/ppermute | solution.py:384
  74.5 6.3 %collective-permute-start.19 = (f32[144,128]{1,0:T(8,128)S(1)}, f32[144,128]{1,0:T(8,128)S(1)}, u32[]{:S(2)}, u32[]{:S(2)}) collective-permute-start(f32[144,128]{1,0:T(8,128)S(1)} %add_cut.5.refs_0_), channel_id=1, source_target_pairs={{0,24},{8,16},{16,8},{24,0},{1,25},{9,17},{17,9},{25,1},{2,26},{10... | collective-permute-start | bytes 221192 | tf_op jit(solution)/shard_map/ppermute | solution.py:384
  76.3 6.4 %collective-permute-start.18 = (f32[144,128]{1,0:T(8,128)S(1)}, f32[144,128]{1,0:T(8,128)S(1)}, u32[]{:S(2)}, u32[]{:S(2)}) collective-permute-start(f32[144,128]{1,0:T(8,128)S(1)} %add_cut.5.refs_0_), channel_id=1, source_target_pairs={{0,16},{8,24},{16,0},{24,8},{1,17},{9,25},{17,1},{25,9},{2,18},{10... | collective-permute-start | bytes 221192 | tf_op jit(solution)/shard_map/ppermute | solution.py:384
  77.3 5.4 %collective-permute-start.17 = (f32[144,128]{1,0:T(8,128)S(1)}, f32[144,128]{1,0:T(8,128)S(1)}, u32[]{:S(2)}, u32[]{:S(2)}) collective-permute-start(f32[144,128]{1,0:T(8,128)S(1)} %add_cut.5.refs_0_), channel_id=1, source_target_pairs={{0,8},{8,0},{16,24},{24,16},{1,9},{9,1},{17,25},{25,17},{2,10},{10... | collective-permute-start | bytes 221192 | tf_op jit(solution)/shard_map/ppermute | solution.py:384
  83.3 10.9 %collective-permute-start.22 = (f32[576,128]{1,0:T(8,128)S(1)}, f32[576,128]{1,0:T(8,128)S(1)}, u32[]{:S(2)}, u32[]{:S(2)}) collective-permute-start(f32[576,128]{1,0:T(8,128)S(1)} %place.1.refs_0_), channel_id=1, source_target_pairs={{0,6},{2,4},{4,2},{6,0},{1,7},{3,5},{5,3},{7,1},{8,14},{10,12},{12... | collective-permute-start | bytes 884744 | tf_op jit(solution)/shard_map/ppermute | solution.py:384
  84.6 13.0 %collective-permute-start.21 = (f32[576,128]{1,0:T(8,128)S(1)}, f32[576,128]{1,0:T(8,128)S(1)}, u32[]{:S(2)}, u32[]{:S(2)}) collective-permute-start(f32[576,128]{1,0:T(8,128)S(1)} %place.1.refs_0_), channel_id=1, source_target_pairs={{0,4},{2,6},{4,0},{6,2},{1,5},{3,7},{5,1},{7,3},{8,12},{10,14},{12... | collective-permute-start | bytes 884744 | tf_op jit(solution)/shard_map/ppermute | solution.py:384
  86.3 11.3 %collective-permute-start.20 = (f32[576,128]{1,0:T(8,128)S(1)}, f32[576,128]{1,0:T(8,128)S(1)}, u32[]{:S(2)}, u32[]{:S(2)}) collective-permute-start(f32[576,128]{1,0:T(8,128)S(1)} %place.1.refs_0_), channel_id=1, source_target_pairs={{0,2},{2,0},{4,6},{6,4},{1,3},{3,1},{5,7},{7,5},{8,10},{10,8},{12,... | collective-permute-start | bytes 884744 | tf_op jit(solution)/shard_map/ppermute | solution.py:384
  86.9 11.3 %collective-permute-start.23 = (f32[576,128]{1,0:T(8,128)S(1)}, f32[576,128]{1,0:T(8,128)S(1)}, u32[]{:S(2)}, u32[]{:S(2)}) collective-permute-start(f32[576,128]{1,0:T(8,128)S(1)} %place.1.refs_0_), channel_id=1, source_target_pairs={{0,1},{1,0},{2,3},{3,2},{4,5},{5,4},{6,7},{7,6},{8,9},{9,8},{10,11... | collective-permute-start | bytes 884744 | tf_op jit(solution)/shard_map/ppermute | solution.py:384
  94.2 3.9 %collective-permute-start.26 = (f32[576,128]{1,0:T(8,128)S(1)}, f32[576,128]{1,0:T(8,128)S(1)}, u32[]{:S(2)}, u32[]{:S(2)}) collective-permute-start(f32[576,128]{1,0:T(8,128)S(1)} %collective-permute-done.22.refs_3_), channel_id=1, source_target_pairs={{0,1},{1,0},{2,3},{3,2},{4,5},{5,4},{6,7},{7,6},{8,9},{9,8},{10,11... | collective-permute-start | bytes 884744 | tf_op jit(solution)/shard_map/ppermute | solution.py:384
  97.6 1.6 %collective-permute-start.25 = (f32[576,128]{1,0:T(8,128)S(1)}, f32[576,128]{1,0:T(8,128)S(1)}, u32[]{:S(2)}, u32[]{:S(2)}) collective-permute-start(f32[576,128]{1,0:T(8,128)S(1)} %collective-permute-done.21.refs_2_), channel_id=1, source_target_pairs={{0,1},{1,0},{2,3},{3,2},{4,5},{5,4},{6,7},{7,6},{8,9},{9,8},{10,11... | collective-permute-start | bytes 884744 | tf_op jit(solution)/shard_map/ppermute | solution.py:384
  97.7 2.0 %collective-permute-start.24 = (f32[576,128]{1,0:T(8,128)S(1)}, f32[576,128]{1,0:T(8,128)S(1)}, u32[]{:S(2)}, u32[]{:S(2)}) collective-permute-start(f32[576,128]{1,0:T(8,128)S(1)} %collective-permute-done.20.refs_1_), channel_id=1, source_target_pairs={{0,1},{1,0},{2,3},{3,2},{4,5},{5,4},{6,7},{7,6},{8,9},{9,8},{10,11... | collective-permute-start | bytes 884744 | tf_op jit(solution)/shard_map/ppermute | solution.py:384

commit v4 on v3

--- a/solution.py
+++ b/solution.py
@@ -1,5 +1,6 @@
 import functools
 import math
+import typing
 
 import jax
 import jax.numpy as jnp
@@ -13,7 +14,6 @@
 SCALE_SQ = 1.0 / 32.0
 RIDGE = 0.1
 EPS = 1e-06
-HI = lax.Precision.HIGHEST
 B = 128
 W = 16
 TINY = 1e-30
@@ -111,11 +111,19 @@
     )(landmarks, embeddings)
 
 
-def gram_kernel(plan, at_ref, emb_ref, mine_ref, own_ref, u_ref, x_mine_ref, *refs):
-    lands, chips, cores, split, all_points, total_rows = plan
+class Plan(typing.NamedTuple):
+    lands: int
+    chips: int
+    cores: int
+    split: bool
+    all_points: int
+
+
+def gram_kernel(plan, first, at_ref, emb_ref, mine_ref, own_ref, u_ref, x_mine_ref, *refs):
+    lands, chips, cores, split, _ = plan
     count = chips * (cores if split else 1)
     far = refs[:count]
-    keep_ref, send_ref, marks_ref, x_ref, k_ref, vq_ref, ridge_ref, out_ref = refs[count:]
+    keep_ref, send_ref, x_ref, ridge_ref, marks_ref, k_ref, vq_ref, out_ref = refs[count:]
     shard, e = mine_ref.shape
     n = shard * lands
     land, chip, core = at_ref[0], at_ref[1], at_ref[2]
@@ -155,50 +163,87 @@
         rows = slice((s - 1) * shard, s * shard)
         ridge(marks_ref[rows, :], vq_ref[rows, :], pl.multiple_of((land ^ s) * shard, shard))
 
-    position = land * shard + (chip * cores + core) * share
+    gram_columns(plan, first, position_of(at_ref, plan, share, shard), x_ref, ridge_ref, out_ref, at_ref[2], keep_ref, send_ref)
+
+
+def position_of(at_ref, plan, share, shard):
+    return at_ref[0] * shard + (at_ref[1] * plan.cores + at_ref[2]) * share
+
+
+def gram_columns(plan, span, position, x_ref, ridge_ref, out_ref, core, keep_ref, send_ref):
+    share = ridge_ref.shape[0]
     row_block = position // B
     offset = position % B
+    base = packed_start(span[0])
     wide = 2 * B
-    for w in range(n // wide):
-        both = nt(x_ref[: (w + 1) * wide, :], x_ref[w * wide : (w + 1) * wide, :]) * (1.0 / all_points)
+    for w in range(span[0] // 2, span[1] // 2):
+        both = nt(x_ref[: (w + 1) * wide, :], x_ref[w * wide : (w + 1) * wide, :]) * (1.0 / plan.all_points)
         for j in (2 * w, 2 * w + 1):
-            start = j * (j + 1) // 2 * B
+            start = packed_start(j) - base
             out_ref[start : start + (j + 1) * B, :] = both[: (j + 1) * B, (j % 2) * B : (j % 2 + 1) * B]
-    for j in range(n // B):
-        start = j * (j + 1) // 2 * B
+    for j in range(*span):
+        start = packed_start(j) - base
 
         @pl.when(row_block <= j)
         def _():
             at = pl.ds(pl.multiple_of(start + row_block * B + offset, share), share)
             out_ref[at, :] = out_ref[at, :] + ridge_ref[:, j * B : (j + 1) * B]
 
-    half = total_rows // cores
+    half = keep_ref.shape[0]
     keep_ref[...] = out_ref[pl.ds(pl.multiple_of(core * half, half), half), :]
     send_ref[...] = out_ref[pl.ds(pl.multiple_of((1 - core) * half, half), half), :]
 
 
-def local_normal(at, plan, embeddings, landmarks, own, u, x_mine, far):
-    lands, chips, cores, split, all_points, total_rows = plan
-    n, m = landmarks.shape[0] * lands, embeddings.shape[0]
+def last_kernel(plan, span, shard, at_ref, x_ref, ridge_ref, order_ref, keep_ref, send_ref, out_ref):
+    position = position_of(at_ref, plan, ridge_ref.shape[0], shard)
+    gram_columns(plan, span, position, x_ref, ridge_ref, out_ref, at_ref[2], keep_ref, send_ref)
+
+
+def halves(plan, span):
+    return (jax.ShapeDtypeStruct((packed_rows(plan, span) // plan.cores, B), jnp.float32),) * 2
+
+
+def packed_start(j):
+    return j * (j + 1) // 2 * B
+
+
+def packed_rows(plan, span):
+    unit = 8 * plan.lands * plan.chips * plan.cores
+    return -(-(packed_start(span[1]) - packed_start(span[0])) // unit) * unit
+
+
+def first_columns(at, plan, span, embeddings, landmarks, own, u, x_mine, far):
+    n, m = landmarks.shape[0] * plan.lands, embeddings.shape[0]
     away = n - landmarks.shape[0]
-    half = jax.ShapeDtypeStruct((total_rows // cores, B), jnp.float32)
-    vmem = pl.BlockSpec(memory_space=pltpu.VMEM)
-    return pl.pallas_call(
-        functools.partial(gram_kernel, plan),
-        out_shape=(half, half),
+    vmem = pl.BlockSpec(memory_space=pltpu.VMEM)
+    return pl.pallas_call(
+        functools.partial(gram_kernel, plan, span),
+        out_shape=halves(plan, span)
+        + (jax.ShapeDtypeStruct((n, m), jnp.bfloat16), jax.ShapeDtypeStruct((own.shape[0], n), jnp.float32)),
         in_specs=[pl.BlockSpec(memory_space=pltpu.SMEM)] + [vmem] * (5 + len(far)),
-        out_specs=(vmem, vmem),
+        out_specs=(vmem,) * 4,
         scratch_shapes=[
             pltpu.VMEM((away, landmarks.shape[1]), jnp.bfloat16),
-            pltpu.VMEM((n, m), jnp.bfloat16),
             pltpu.VMEM((away, m), jnp.float32),
             pltpu.VMEM((away, B), jnp.float32),
-            pltpu.VMEM((own.shape[0], n), jnp.float32),
-            pltpu.VMEM((total_rows, B), jnp.float32),
+            pltpu.VMEM((packed_rows(plan, span), B), jnp.float32),
         ],
         compiler_params=pltpu.CompilerParams(vmem_limit_bytes=24 << 20),
-        name="gram",
+        name="gram_first",
     )(at, embeddings, landmarks, own, u, x_mine, *far)
+
+
+def last_columns(at, plan, span, shard, x, ridge, order):
+    vmem = pl.BlockSpec(memory_space=pltpu.VMEM)
+    return pl.pallas_call(
+        functools.partial(last_kernel, plan, span, shard),
+        out_shape=halves(plan, span),
+        in_specs=[pl.BlockSpec(memory_space=pltpu.SMEM), vmem, vmem, pl.BlockSpec(memory_space=pl.ANY)],
+        out_specs=(vmem,) * 2,
+        scratch_shapes=[pltpu.VMEM((packed_rows(plan, span), B), jnp.float32)],
+        compiler_params=pltpu.CompilerParams(vmem_limit_bytes=16 << 20),
+        name="gram_last",
+    )(at, x, ridge, order)
 
 
 def add_cut_kernel(ways, axis, at_ref, *refs):
@@ -243,6 +288,26 @@
         name="place",
     )(at, *parts)
 
+
+def thirds(x):
+    h = x.astype(jnp.bfloat16)
+    r = x - h.astype(jnp.float32)
+    m = r.astype(jnp.bfloat16)
+    return h, m, (r - m.astype(jnp.float32)).astype(jnp.bfloat16)
+
+def left_terms(x, axis):
+    h, m, l = thirds(x)
+    return jnp.concatenate([h, h, h, m, m, l], axis)
+
+def right_terms(x, axis):
+    h, m, l = thirds(x)
+    return jnp.concatenate([h, m, l, h, m, h], axis)
+
+def dot32(a, b):
+    return lax.dot_general(left_terms(a, 1), right_terms(b, 0), (((1,), (0,)), ((), ())), preferred_element_type=jnp.float32)
+
+def dot32_t(a, b):
+    return dot32(a.T, b)
 
 def factor_block(d):
     rows8 = lax.broadcasted_iota(jnp.int32, (8, 128), 0)
@@ -306,7 +371,7 @@
             ur = jnp.concatenate(right[base:base + g], 0)
             u = jnp.concatenate([ul, ur], 1)
             lo_row = (p + 2) * W
-            upd = lax.dot_general(ul, u, (((0,), (0,)), ((), ())), preferred_element_type=jnp.float32, precision=HI)
+            upd = lax.dot_general(left_terms(ul, 0), right_terms(u, 0), (((0,), (0,)), ((), ())), preferred_element_type=jnp.float32)
             for r in range(lo_row // 8, B // 8):
                 left[r] = left[r] - upd[8 * r:8 * r + 8, :128]
                 right[r] = right[r] - upd[8 * r:8 * r + 8, 128:]
@@ -315,69 +380,120 @@
     tri = lax.broadcasted_iota(jnp.int32, (B, B), 0) <= lax.broadcasted_iota(jnp.int32, (B, B), 1)
     return jnp.where(tri, u, 0.0), w
 
-def chol_kernel(chips, cores, at_ref, *refs):
-    parts = refs[: chips * cores]
-    o_ref, a_ref, s_ref, w_ref = refs[chips * cores :]
-    n = o_ref.shape[0] // B
+
+def eliminate(nb, m_ref, d_ref, r_ref, store):
+    lane_block = lax.broadcasted_iota(jnp.int32, (B, nb * B), 1) // B
+    d_ref[...] = m_ref[:B, :B]
+    r_ref[...] = jnp.zeros_like(r_ref)
+
+    def step(k, _):
+        u, w = factor_block(d_ref[...])
+        prev = r_ref[...]
+        m_ref[...] = m_ref[...] - dot32_t(prev, prev)
+        row = dot32(w, m_ref[pl.ds(pl.multiple_of(k * B, B), B), :])
+        row = jnp.where(lane_block > k, row, 0.0)
+        r_ref[...] = row
+        nxt = pl.multiple_of(jnp.minimum(k + 1, nb - 1) * B, B)
+        rn = r_ref[:, pl.ds(nxt, B)]
+        d_ref[...] = m_ref[pl.ds(nxt, B), pl.ds(nxt, B)] - dot32_t(rn, rn)
+        store(pl.multiple_of(k * B, B), row, u, w)
+        return 0
+
+    lax.fori_loop(0, nb, step, 0)
+
+
+def place_parts(plan, at_ref, parts, a_ref):
     h = parts[0].shape[0]
-    for a in range(cores):
-        for t in range(chips):
-            slot = (at_ref[2] ^ a) * chips + (at_ref[1] ^ t)
-            a_ref[pl.ds(pl.multiple_of(slot * h, h), h), :] = parts[a * chips + t][...]
-    o_ref[...] = jnp.zeros_like(o_ref)
-
-    def step(k, _):
-        for i in range(n):
-
-            @pl.when(k == i)
-            def _():
-                starts = [(j * (j + 1) // 2 + i) * B for j in range(i, n)]
-                blk = jnp.concatenate([a_ref[r : r + B, :] for r in starts], 1)
-                if i:
-                    left = o_ref[: i * B, i * B : (i + 1) * B]
-                    right = o_ref[: i * B, i * B :]
-                    blk = blk - lax.dot_general(
-                        left, right, (((0,), (0,)), ((), ())), preferred_element_type=jnp.float32, precision=HI
-                    )
-                s_ref[:, : (n - i) * B] = blk
-
-        u, w = factor_block(s_ref[:, :B])
-        s_ref[:, :B] = u
-        w_ref[...] = w
-        for i in range(n):
-
-            @pl.when(k == i)
-            def _():
-                o_ref[i * B : (i + 1) * B, i * B : (i + 1) * B] = s_ref[:, :B]
-                if i < n - 1:
-                    o_ref[i * B : (i + 1) * B, (i + 1) * B :] = lax.dot_general(
-                        w_ref[...],
-                        s_ref[:, B : (n - i) * B],
-                        (((1,), (0,)), ((), ())),
-                        preferred_element_type=jnp.float32,
-                        precision=HI,
-                    )
-
-        return 0
-
-    lax.fori_loop(0, n, step, 0)
-
-
-def cholesky_upper(at, chips, cores, parts, n):
-    vmem = pl.BlockSpec(memory_space=pltpu.VMEM)
-    return pl.pallas_call(
-        functools.partial(chol_kernel, chips, cores),
+    for a in range(plan.cores):
+        for t in range(plan.chips):
+            slot = (at_ref[2] ^ a) * plan.chips + (at_ref[1] ^ t)
+            a_ref[pl.ds(pl.multiple_of(slot * h, h), h), :] = parts[a * plan.chips + t][...]
+
+
+def first_factor_kernel(plan, at_ref, *refs):
+    count = plan.chips * plan.cores
+    f_ref, w_ref, a_ref, m_ref, d_ref, r_ref = refs[count + 1 :]
+    na = f_ref.shape[0] // B
+    place_parts(plan, at_ref, refs[:count], a_ref)
+    for j in range(na):
+        m_ref[: (j + 1) * B, j * B : (j + 1) * B] = a_ref[packed_start(j) : packed_start(j) + (j + 1) * B, :]
+
+    def store(at, row, u, w):
+        f_ref[pl.ds(at, B), :] = row
+        f_ref[pl.ds(at, B), pl.ds(at, B)] = u
+        w_ref[pl.ds(at, B), :] = w
+
+    eliminate(na, m_ref, d_ref, r_ref, store)
+
+
+def first_factor(at, plan, na, parts, order):
+    vmem = pl.BlockSpec(memory_space=pltpu.VMEM)
+    return pl.pallas_call(
+        functools.partial(first_factor_kernel, plan),
+        out_shape=(
+            jax.ShapeDtypeStruct((na * B, na * B), jnp.float32),
+            jax.ShapeDtypeStruct((na * B, B), jnp.float32),
+        ),
+        in_specs=[pl.BlockSpec(memory_space=pltpu.SMEM)] + [vmem] * len(parts) + [pl.BlockSpec(memory_space=pl.ANY)],
+        out_specs=(vmem,) * 2,
+        scratch_shapes=[
+            pltpu.VMEM((parts[0].shape[0] * len(parts), B), jnp.float32),
+            pltpu.VMEM((na * B, na * B), jnp.float32),
+            pltpu.VMEM((B, B), jnp.float32),
+            pltpu.VMEM((B, na * B), jnp.float32),
+        ],
+        compiler_params=pltpu.CompilerParams(vmem_limit_bytes=16 << 20),
+        name="chol_first",
+    )(at, *parts, order)
+
+
+def last_factor_kernel(plan, at_ref, f_ref, w_ref, *refs):
+    count = plan.chips * plan.cores
+    o_ref, a_ref, t_ref, m_ref, d_ref, r_ref = refs[count:]
+    n, top = o_ref.shape[0] // B, f_ref.shape[0]
+    na = top // B
+    place_parts(plan, at_ref, refs[:count], a_ref)
+    for j in range(na, n):
+        start = packed_start(j) - packed_start(na)
+        lanes = slice((j - na) * B, (j - na + 1) * B)
+        t_ref[:, lanes] = a_ref[start : start + top, :]
+        m_ref[: (j - na + 1) * B, lanes] = a_ref[start + top : start + (j + 1) * B, :]
+    o_ref[:top, :top] = f_ref[...]
+    o_ref[top:, :top] = jnp.zeros((n * B - top, top), jnp.float32)
+    for k in range(na):
+        rows = slice(k * B, (k + 1) * B)
+        row = dot32(w_ref[rows, :], t_ref[rows, :])
+        o_ref[rows, top:] = row
+        if k < na - 1:
+            t_ref[(k + 1) * B :, :] = t_ref[(k + 1) * B :, :] - dot32_t(f_ref[rows, (k + 1) * B :], row)
+        m_ref[...] = m_ref[...] - dot32_t(row, row)
+
+    def store(at, row, u, w):
+        down = pl.multiple_of(top + at, B)
+        o_ref[pl.ds(down, B), top:] = row
+        o_ref[pl.ds(down, B), pl.ds(down, B)] = u
+
+    eliminate(n - na, m_ref, d_ref, r_ref, store)
+
+
+def last_factor(at, plan, n, f, w, parts):
+    vmem = pl.BlockSpec(memory_space=pltpu.VMEM)
+    top = f.shape[0]
+    return pl.pallas_call(
+        functools.partial(last_factor_kernel, plan),
         out_shape=jax.ShapeDtypeStruct((n, n), jnp.float32),
-        in_specs=[pl.BlockSpec(memory_space=pltpu.SMEM)] + [vmem] * len(parts),
+        in_specs=[pl.BlockSpec(memory_space=pltpu.SMEM)] + [vmem] * (2 + len(parts)),
         out_specs=vmem,
         scratch_shapes=[
             pltpu.VMEM((parts[0].shape[0] * len(parts), B), jnp.float32),
-            pltpu.VMEM((B, n), jnp.float32),
+            pltpu.VMEM((top, n - top), jnp.float32),
+            pltpu.VMEM((n - top, n - top), jnp.float32),
             pltpu.VMEM((B, B), jnp.float32),
+            pltpu.VMEM((B, n - top), jnp.float32),
         ],
         compiler_params=pltpu.CompilerParams(vmem_limit_bytes=24 << 20),
-        name="chol",
-    )(at, *parts)
+        name="chol_last",
+    )(at, f, w, *parts)
 
 
 def swap(x, axis, s):
@@ -398,35 +514,42 @@
     at = jnp.stack([land, chip, core]).astype(jnp.int32)
     shard = landmarks.shape[0]
     n = shard * lands
-    devices = lands * chips * cores
-    blocks = n // B * (n // B + 1) // 2
-    unit = 8 * devices
-    total_rows = -(-blocks * B // unit) * unit
-    split = shard // (chips * cores) % 16 == 0
+    plan = Plan(lands, chips, cores, shard // (chips * cores) % 16 == 0, embeddings.shape[0] * lands * chips * cores)
 
     share = shard // (chips * cores)
     own = lax.dynamic_slice_in_dim(landmarks, (chip * cores + core) * share, share, 0)
-    if split:
+    if plan.split:
         piece = own
     else:
         piece = lax.dynamic_slice_in_dim(landmarks, chip * (shard // chips), shard // chips, 0)
     z = jnp.concatenate(spread_out(piece, "land")[1:], 0)
     far = spread_out(z, "chip")
     x_mine, u = own_cross(landmarks, embeddings)
-    if split:
+    if plan.split:
         far, x_mine, u = lax.optimization_barrier((far, x_mine, u))
         for a in range(1, cores):
             far = far + [swap(f, "core", a) for f in far[:chips]]
-    plan = (lands, chips, cores, split, embeddings.shape[0] * devices, total_rows)
-    keep, send = local_normal(at, plan, embeddings, landmarks, own, u, x_mine, far)
-
-    parts = scatter(add_cut(at, 1, chips, [keep, swap(send, "core", 1)]), "chip")
+
+    na = n // B // 2
+    first, last = (0, na), (na, n // B)
+    keep, send, x, ridge = first_columns(at, plan, first, embeddings, landmarks, own, u, x_mine, far)
+    cut_a = add_cut(at, 1, chips, [keep, swap(send, "core", 1)])
+    keep, send = last_columns(at, plan, last, shard, x, ridge, cut_a[0])
+    cut_b = add_cut(at, 1, chips, [keep, swap(send, "core", 1)])
+    whole_a = land_reduce(at, lands, scatter(cut_a, "chip"))
+    whole_b = land_reduce(at, lands, scatter(cut_b, "chip"))
+    parts_a = spread_out(whole_a, "chip")
+    parts_a = parts_a + [swap(p, "core", 1) for p in parts_a]
+    f, w = first_factor(at, plan, na, parts_a, whole_b)
+    parts_b, f, w = lax.optimization_barrier((spread_out(whole_b, "chip"), f, w))
+    parts_b = parts_b + [swap(p, "core", 1) for p in parts_b]
+    return last_factor(at, plan, n, f, w, parts_b)
+
+
+def land_reduce(at, lands, parts):
     parts = scatter(add_cut(at, 0, lands, parts), "land")
     (whole,) = add_cut(at, 0, 1, parts)
-    whole = place(at, 0, spread_out(whole, "land"))
-    parts = spread_out(whole, "chip")
-    parts = parts + [swap(p, "core", 1) for p in parts]
-    return cholesky_upper(at, chips, cores, parts, n)
+    return place(at, 0, spread_out(whole, "land"))
 
 
 def solution(mesh):

time: 136 us -> 146 us (1.074)
  starting transfers between devices: 27.1 us -> 46.2 us
  waiting for transfers between devices: 42.9 us -> 33.2 us
    ppermute x27 -> x44, starting transfers between devices: 27.1 us -> 46.2 us  [swap(): lax.ppermute(x, axis, [(i, i ^ s) for i in range(lax.axis_size(axis))])]
    ppermute x27 -> x44, waiting for transfers between devices: 42.9 us -> 33.2 us  [swap(): lax.ppermute(x, axis, [(i, i ^ s) for i in range(lax.axis_size(axis))])]
    pallas_call x2 -> x4, Pallas kernels: 55 us -> 53.2 us  [the longest x1 19.5 us: last_factor(): pl.pallas_call(functools.partial(last_factor_kernel, plan), out_shape=jax...]
    pallas_call x3 -> x6, Pallas kernels: 1.83 us -> 3.47 us  [add_cut(): pl.pallas_call(functools.partial(add_cut_kernel, ways, axis), out_shape=t...]
  transfers between devices with their start and end apart: 27 -> 44, of which waited for: 16 -> 21; matrix products, arithmetic and copies ran while one was open for 0% -> 0% of each run, Pallas kernels for 4% -> 15%
where the time goes in v4:
time: 146 us
  Pallas kernels  62.9 us (43%)
  starting transfers between devices  46.2 us (32%)
  waiting for transfers between devices  33.2 us (23%)
  local copies, waits for them, and re-layouts  3.3 us (2%)
    ppermute x44, starting transfers between devices, swap(): lax.ppermute(x, axis, [(i, i ^ s) for i in range(lax.axis_size(axis))])  46.2 us
    ppermute x44, waiting for transfers between devices, swap(): lax.ppermute(x, axis, [(i, i ^ s) for i in range(lax.axis_size(axis))])  33.2 us
    pallas_call x1, Pallas kernels, last_factor(): pl.pallas_call(functools.partial(last_factor_kernel, plan), out_shape=jax...  19.5 us
    pallas_call x1, Pallas kernels, first_columns(): pl.pallas_call(functools.partial(gram_kernel, plan, span), out_shape=halv...  17.6 us
    pallas_call x1, Pallas kernels, first_factor(): pl.pallas_call(functools.partial(first_factor_kernel, plan), out_shape=(j...  14.1 us
    pallas_call x1, Pallas kernels, own_cross(): pl.pallas_call(own_kernel, out_shape=(jax.ShapeDtypeStruct((shard, m), jn...  5.12 us
    pallas_call x6, Pallas kernels, add_cut(): pl.pallas_call(functools.partial(add_cut_kernel, ways, axis), out_shape=t...  3.47 us
  transfers between devices with their start and end apart: 44, of which 21 were waited for; matrix products, arithmetic and copies ran while one was open for 0% of the time, Pallas kernels for 15%

profile of v4, /device:TPU:0, one launch (start us, length us, event | category | flops | bytes accessed | tf_op | source)
XLA Modules:
  0.0 146.0 jit_solution(14406180335728904012)
XLA Ops:
  0.0 0.9 constant_dynamic-slice_fusion.own_ref
  0.9 3.0 %collective-permute-start = (bf16[32,768]{1,0:T(8,128)(2,1)S(1)}, bf16[32,768]{1,0:T(8,128)(2,1)S(1)}, u32[]{:S(2)}, u32[]{:S(2)}) collective-permute-start(bf16[32,768]{1,0:T(8,128)(2,1)S(1)} %constant_dynamic-slice_fusion.own_ref), channel_id=1, source_target_pairs={{0,8},{8,0},{16,24},{24,16},{1,9},{9,1},{17,25},{25,17},{2,10},{10... | collective-permute-start | bytes 147464 | tf_op jit(solution)/shard_map/ppermute | solution.py:500
  3.9 2.5 %collective-permute-start.2 = (bf16[32,768]{1,0:T(8,128)(2,1)S(1)}, bf16[32,768]{1,0:T(8,128)(2,1)S(1)}, u32[]{:S(2)}, u32[]{:S(2)}) collective-permute-start(bf16[32,768]{1,0:T(8,128)(2,1)S(1)} %constant_dynamic-slice_fusion.own_ref), channel_id=1, source_target_pairs={{0,24},{8,16},{16,8},{24,0},{1,25},{9,17},{17,9},{25,1},{2,26},{10... | collective-permute-start | bytes 147464 | tf_op jit(solution)/shard_map/ppermute | solution.py:500
  6.5 5.4 %collective-permute-done.1 = bf16[32,768]{1,0:T(8,128)(2,1)S(1)} collective-permute-done((bf16[32,768]{1,0:T(8,128)(2,1)S(1)}, bf16[32,768]{1,0:T(8,128)(2,1)S(1)}, u32[]{:S(2)}, u32[]{:S(2)}) %collective-permute-start.1) | collective-permute-done | bytes 49184 | tf_op jit(solution)/shard_map/ppermute | solution.py:500
  11.9 2.5 %collective-permute-start.5 = (bf16[96,768]{1,0:T(8,128)(2,1)S(1)}, bf16[96,768]{1,0:T(8,128)(2,1)S(1)}, u32[]{:S(2)}, u32[]{:S(2)}) collective-permute-start(bf16[96,768]{1,0:T(8,128)(2,1)S(1)} %constant_dynamic-update-slice_fusion.refs_0_), channel_id=1, source_target_pairs={{0,6},{2,4},{4,2},{6,0},{1,7},{3,5},{5,3},{7,1},{8,14},{10,12},{12... | collective-permute-start | bytes 442376 | tf_op jit(solution)/shard_map/ppermute | solution.py:500
  15.5 1.4 copy-done
  16.9 1.0 copy-done.2
  17.9 5.1 %own_cross.1 = (bf16[256,1024]{1,0:T(8,128)(2,1)S(1)}, f32[16,1024]{1,0:T(8,128)S(1)}) custom-call(bf16[256,768]{1,0:T(8,128)(2,1)S(1)} %copy-done.2, bf16[1024,768]{1,0:T(8,128)(2,1)S(1)} %copy-done), custom_call_target="tpu_custom_call" | custom-call | tf_op jit(solution)/shard_map/own_cross/pallas_call | solution.py:100
  25.3 17.6 %gram_first.1 = (f32[640,128]{1,0:T(8,128)S(1)}, f32[640,128]{1,0:T(8,128)S(1)}, bf16[1024,1024]{1,0:T(8,128)(2,1)S(1)}, f32[32,1024]{1,0:T(8,128)S(1)}) custom-call(s32[3]{0:T(128)S(1)} %pad_add_fusion.at_ref, bf16[1024,768]{1,0:T(8,128)(2,1)S(1)} %copy-done.1, bf16[256,768]{1,0:T(8,128)(2,1)S(1)} %copy-done.3, ...), custom_call_target="tpu_custom_call" | custom-call | tf_op jit(solution)/shard_map/gram_first/pallas_call | solution.py:219
  43.3 1.3 collective-permute-done.10.refs_1_
  44.6 0.6 add_cut.6
  45.2 2.0 %gram_last.1 = (f32[1664,128]{1,0:T(8,128)S(1)}, f32[1664,128]{1,0:T(8,128)S(1)}) custom-call(s32[3]{0:T(128)S(1)} %pad_add_fusion.at_ref, bf16[1024,1024]{1,0:T(8,128)(2,1)S(1)} %get-tuple-element.51.x_ref, f32[32,1024]{1,0:T(8,128)S(1)} %get-tuple-element.52.ridge_ref, f32[160,128]{1,0:T(8,128)S(1)} %get-tuple-element.55.order_ref.refs_0_), custom_call_target="tpu_custom_call" | custom-call | tf_op jit(solution)/shard_map/gram_last/pallas_call | solution.py:238
  47.6 2.1 %collective-permute-done.11.refs_1_ = f32[1664,128]{1,0:T(8,128)S(1)} collective-permute-done((f32[1664,128]{1,0:T(8,128)S(1)}, f32[1664,128]{1,0:T(8,128)S(1)}, u32[]{:S(2)}, u32[]{:S(2)}) %collective-permute-start.11) | collective-permute-done | bytes 852000 | tf_op jit(solution)/shard_map/ppermute | solution.py:500
  49.7 0.6 add_cut.7
  50.3 1.6 %collective-permute-start.12 = (f32[416,128]{1,0:T(8,128)S(1)}, f32[416,128]{1,0:T(8,128)S(1)}, u32[]{:S(2)}, u32[]{:S(2)}) collective-permute-start(f32[416,128]{1,0:T(8,128)S(1)} %get-tuple-element.59), channel_id=1, source_target_pairs={{0,2},{2,0},{4,6},{6,4},{1,3},{3,1},{5,7},{7,5},{8,10},{10,8},{12,... | collective-permute-start | bytes 638984 | tf_op jit(solution)/shard_map/ppermute | solution.py:500
  51.9 1.5 %collective-permute-start.13 = (f32[416,128]{1,0:T(8,128)S(1)}, f32[416,128]{1,0:T(8,128)S(1)}, u32[]{:S(2)}, u32[]{:S(2)}) collective-permute-start(f32[416,128]{1,0:T(8,128)S(1)} %get-tuple-element.60), channel_id=1, source_target_pairs={{0,4},{2,6},{4,0},{6,2},{1,5},{3,7},{5,1},{7,3},{8,12},{10,14},{12... | collective-permute-start | bytes 638984 | tf_op jit(solution)/shard_map/ppermute | solution.py:500
  53.9 1.5 %collective-permute-start.24 = (f32[160,128]{1,0:T(8,128)S(1)}, f32[160,128]{1,0:T(8,128)S(1)}, u32[]{:S(2)}, u32[]{:S(2)}) collective-permute-start(f32[160,128]{1,0:T(8,128)S(1)} %get-tuple-element.66), channel_id=1, source_target_pairs={{0,2},{2,0},{4,6},{6,4},{1,3},{3,1},{5,7},{7,5},{8,10},{10,8},{12,... | collective-permute-start | bytes 245768 | tf_op jit(solution)/shard_map/ppermute | solution.py:500
  55.4 1.5 %collective-permute-start.25 = (f32[160,128]{1,0:T(8,128)S(1)}, f32[160,128]{1,0:T(8,128)S(1)}, u32[]{:S(2)}, u32[]{:S(2)}) collective-permute-start(f32[160,128]{1,0:T(8,128)S(1)} %get-tuple-element.67), channel_id=1, source_target_pairs={{0,4},{2,6},{4,0},{6,2},{1,5},{3,7},{5,1},{7,3},{8,12},{10,14},{12... | collective-permute-start | bytes 245768 | tf_op jit(solution)/shard_map/ppermute | solution.py:500
  56.9 1.6 %collective-permute-done.12.refs_1_ = f32[416,128]{1,0:T(8,128)S(1)} collective-permute-done((f32[416,128]{1,0:T(8,128)S(1)}, f32[416,128]{1,0:T(8,128)S(1)}, u32[]{:S(2)}, u32[]{:S(2)}) %collective-permute-start.12) | collective-permute-done | bytes 213024 | tf_op jit(solution)/shard_map/ppermute | solution.py:500
  58.5 2.4 %collective-permute-start.26 = (f32[160,128]{1,0:T(8,128)S(1)}, f32[160,128]{1,0:T(8,128)S(1)}, u32[]{:S(2)}, u32[]{:S(2)}) collective-permute-start(f32[160,128]{1,0:T(8,128)S(1)} %get-tuple-element.68), channel_id=1, source_target_pairs={{0,6},{2,4},{4,2},{6,0},{1,7},{3,5},{5,3},{7,1},{8,14},{10,12},{12... | collective-permute-start | bytes 245768 | tf_op jit(solution)/shard_map/ppermute | solution.py:500
  60.9 3.6 %collective-permute-done.13.refs_2_ = f32[416,128]{1,0:T(8,128)S(1)} collective-permute-done((f32[416,128]{1,0:T(8,128)S(1)}, f32[416,128]{1,0:T(8,128)S(1)}, u32[]{:S(2)}, u32[]{:S(2)}) %collective-permute-start.13) | collective-permute-done | bytes 213024 | tf_op jit(solution)/shard_map/ppermute | solution.py:500
  64.5 0.6 add_cut.8
  65.4 1.7 %collective-permute-done.25.refs_2_ = f32[160,128]{1,0:T(8,128)S(1)} collective-permute-done((f32[160,128]{1,0:T(8,128)S(1)}, f32[160,128]{1,0:T(8,128)S(1)}, u32[]{:S(2)}, u32[]{:S(2)}) %collective-permute-start.25) | collective-permute-done | bytes 81952 | tf_op jit(solution)/shard_map/ppermute | solution.py:500
  67.1 0.6 add_cut.10
  68.0 2.4 %collective-permute-start.16 = (f32[104,128]{1,0:T(8,128)S(1)}, f32[104,128]{1,0:T(8,128)S(1)}, u32[]{:S(2)}, u32[]{:S(2)}) collective-permute-start(f32[104,128]{1,0:T(8,128)S(1)} %get-tuple-element.64), channel_id=1, source_target_pairs={{0,16},{8,24},{16,0},{24,8},{1,17},{9,25},{17,1},{25,9},{2,18},{10... | collective-permute-start | bytes 159752 | tf_op jit(solution)/shard_map/ppermute | solution.py:500
  70.4 1.7 %collective-permute-start.17 = (f32[104,128]{1,0:T(8,128)S(1)}, f32[104,128]{1,0:T(8,128)S(1)}, u32[]{:S(2)}, u32[]{:S(2)}) collective-permute-start(f32[104,128]{1,0:T(8,128)S(1)} %get-tuple-element.65), channel_id=1, source_target_pairs={{0,24},{8,16},{16,8},{24,0},{1,25},{9,17},{17,9},{25,1},{2,26},{10... | collective-permute-start | bytes 159752 | tf_op jit(solution)/shard_map/ppermute | solution.py:500
  72.2 2.1 %collective-permute-start.29 = (f32[40,128]{1,0:T(8,128)S(1)}, f32[40,128]{1,0:T(8,128)S(1)}, u32[]{:S(2)}, u32[]{:S(2)}) collective-permute-start(f32[40,128]{1,0:T(8,128)S(1)} %get-tuple-element.72), channel_id=1, source_target_pairs={{0,24},{8,16},{16,8},{24,0},{1,25},{9,17},{17,9},{25,1},{2,26},{10... | collective-permute-start | bytes 61448 | tf_op jit(solution)/shard_map/ppermute | solution.py:500
  74.3 2.8 %collective-permute-done.28.refs_2_ = f32[40,128]{1,0:T(8,128)S(1)} collective-permute-done((f32[40,128]{1,0:T(8,128)S(1)}, f32[40,128]{1,0:T(8,128)S(1)}, u32[]{:S(2)}, u32[]{:S(2)}) %collective-permute-start.28) | collective-permute-done | bytes 20512 | tf_op jit(solution)/shard_map/ppermute | solution.py:500
  77.1 0.6 collective-permute-done.29.refs_3_
  77.8 0.5 add_cut.11.refs_0_
  78.3 2.3 %collective-permute-start.32 = (f32[40,128]{1,0:T(8,128)S(1)}, f32[40,128]{1,0:T(8,128)S(1)}, u32[]{:S(2)}, u32[]{:S(2)}) collective-permute-start(f32[40,128]{1,0:T(8,128)S(1)} %add_cut.11.refs_0_), channel_id=1, source_target_pairs={{0,24},{8,16},{16,8},{24,0},{1,25},{9,17},{17,9},{25,1},{2,26},{10... | collective-permute-start | bytes 61448 | tf_op jit(solution)/shard_map/ppermute | solution.py:500
  80.7 2.1 %collective-permute-start.30 = (f32[40,128]{1,0:T(8,128)S(1)}, f32[40,128]{1,0:T(8,128)S(1)}, u32[]{:S(2)}, u32[]{:S(2)}) collective-permute-start(f32[40,128]{1,0:T(8,128)S(1)} %add_cut.11.refs_0_), channel_id=1, source_target_pairs={{0,8},{8,0},{16,24},{24,16},{1,9},{9,1},{17,25},{25,17},{2,10},{10... | collective-permute-start | bytes 61448 | tf_op jit(solution)/shard_map/ppermute | solution.py:500
  82.8 0.6 add_cut.9.refs_0_
  83.3 2.3 %collective-permute-start.20 = (f32[104,128]{1,0:T(8,128)S(1)}, f32[104,128]{1,0:T(8,128)S(1)}, u32[]{:S(2)}, u32[]{:S(2)}) collective-permute-start(f32[104,128]{1,0:T(8,128)S(1)} %add_cut.9.refs_0_), channel_id=1, source_target_pairs={{0,24},{8,16},{16,8},{24,0},{1,25},{9,17},{17,9},{25,1},{2,26},{10... | collective-permute-start | bytes 159752 | tf_op jit(solution)/shard_map/ppermute | solution.py:500
  85.6 0.6 place.3.refs_0_
  86.3 1.7 %collective-permute-start.19 = (f32[104,128]{1,0:T(8,128)S(1)}, f32[104,128]{1,0:T(8,128)S(1)}, u32[]{:S(2)}, u32[]{:S(2)}) collective-permute-start(f32[104,128]{1,0:T(8,128)S(1)} %add_cut.9.refs_0_), channel_id=1, source_target_pairs={{0,16},{8,24},{16,0},{24,8},{1,17},{9,25},{17,1},{25,9},{2,18},{10... | collective-permute-start | bytes 159752 | tf_op jit(solution)/shard_map/ppermute | solution.py:500
  88.0 0.7 collective-permute-start.18
  88.7 1.5 %collective-permute-start.35 = (f32[160,128]{1,0:T(8,128)S(1)}, f32[160,128]{1,0:T(8,128)S(1)}, u32[]{:S(2)}, u32[]{:S(2)}) collective-permute-start(f32[160,128]{1,0:T(8,128)S(1)} %place.3.refs_0_), channel_id=1, source_target_pairs={{0,6},{2,4},{4,2},{6,0},{1,7},{3,5},{5,3},{7,1},{8,14},{10,12},{12... | collective-permute-start | bytes 245768 | tf_op jit(solution)/shard_map/ppermute | solution.py:500
  90.1 2.3 %collective-permute-start.34 = (f32[160,128]{1,0:T(8,128)S(1)}, f32[160,128]{1,0:T(8,128)S(1)}, u32[]{:S(2)}, u32[]{:S(2)}) collective-permute-start(f32[160,128]{1,0:T(8,128)S(1)} %place.3.refs_0_), channel_id=1, source_target_pairs={{0,4},{2,6},{4,0},{6,2},{1,5},{3,7},{5,1},{7,3},{8,12},{10,14},{12... | collective-permute-start | bytes 245768 | tf_op jit(solution)/shard_map/ppermute | solution.py:500
  92.8 0.6 place.2.refs_8_.refs_0_
  93.4 1.8 %collective-permute-start.23 = (f32[416,128]{1,0:T(8,128)S(1)}, f32[416,128]{1,0:T(8,128)S(1)}, u32[]{:S(2)}, u32[]{:S(2)}) collective-permute-start(f32[416,128]{1,0:T(8,128)S(1)} %place.2.refs_8_.refs_0_), channel_id=1, source_target_pairs={{0,6},{2,4},{4,2},{6,0},{1,7},{3,5},{5,3},{7,1},{8,14},{10,12},{12... | collective-permute-start | bytes 638984 | tf_op jit(solution)/shard_map/ppermute | solution.py:500
  95.1 1.1 collective-permute-start.22
  96.2 1.0 collective-permute-start.21
  97.2 1.0 collective-permute-start.33
  98.3 10.1 %collective-permute-done.33.refs_1_ = f32[160,128]{1,0:T(8,128)S(1)} collective-permute-done((f32[160,128]{1,0:T(8,128)S(1)}, f32[160,128]{1,0:T(8,128)S(1)}, u32[]{:S(2)}, u32[]{:S(2)}) %collective-permute-start.33) | collective-permute-done | bytes 81952 | tf_op jit(solution)/shard_map/ppermute | solution.py:500
  108.9 0.8 collective-permute-done.38.refs_6_
  109.8 14.1 %chol_first.1 = (f32[512,512]{1,0:T(8,128)S(1)}, f32[512,128]{1,0:T(8,128)S(1)}) custom-call(s32[3]{0:T(128)S(1)} %pad_add_fusion.at_ref, f32[160,128]{1,0:T(8,128)S(1)} %place.3.refs_0_, f32[160,128]{1,0:T(8,128)S(1)} %collective-permute-done.33.refs_1_, f32[160,128]{1,0:T(8,128)S(1)} %collective-permute-done.34.refs_2_, ...), custom_call_target="tpu_custom_call" | custom-call | tf_op jit(solution)/shard_map/chol_first/pallas_call | solution.py:431
  126.4 19.5 %chol_last.1 = f32[1024,1024]{1,0:T(8,128)} custom-call(s32[3]{0:T(128)S(1)} %pad_add_fusion.at_ref, f32[512,512]{1,0:T(8,128)S(1)} %get-tuple-element.75.f_ref, f32[512,128]{1,0:T(8,128)S(1)} %get-tuple-element.76.w_ref, f32[416,128]{1,0:T(8,128)S(1)} %place.2.refs_8_.refs_0_, f32[416,128]{1,0:T(8,128)S(1)} %collective-permute-done.21.refs_1_, ...), custom_call_target="tpu_custom_call" | custom-call | tf_op jit(solution)/shard_map/chol_last/pallas_call | solution.py:482
  (66 shorter events, 9.1 us)
Async XLA Ops:
  0.0 25.3 %copy-start.3 = (bf16[256,768]{1,0:T(8,128)(2,1)S(1)}, bf16[256,768]{1,0:T(8,128)(2,1)}, u32[]{:S(2)}) copy-start(bf16[256,768]{1,0:T(8,128)(2,1)} %mine_ref.1) | copy-start | bytes 1179652
  0.9 5.6 %collective-permute-start = (bf16[32,768]{1,0:T(8,128)(2,1)S(1)}, bf16[32,768]{1,0:T(8,128)(2,1)S(1)}, u32[]{:S(2)}, u32[]{:S(2)}) collective-permute-start(bf16[32,768]{1,0:T(8,128)(2,1)S(1)} %constant_dynamic-slice_fusion.own_ref), channel_id=1, source_target_pairs={{0,8},{8,0},{16,24},{24,16},{1,9},{9,1},{17,25},{25,17},{2,10},{10... | collective-permute-start | bytes 147464 | tf_op jit(solution)/shard_map/ppermute | solution.py:500
  3.9 8.0 %collective-permute-start.2 = (bf16[32,768]{1,0:T(8,128)(2,1)S(1)}, bf16[32,768]{1,0:T(8,128)(2,1)S(1)}, u32[]{:S(2)}, u32[]{:S(2)}) collective-permute-start(bf16[32,768]{1,0:T(8,128)(2,1)S(1)} %constant_dynamic-slice_fusion.own_ref), channel_id=1, source_target_pairs={{0,24},{8,16},{16,8},{24,0},{1,25},{9,17},{17,9},{25,1},{2,26},{10... | collective-permute-start | bytes 147464 | tf_op jit(solution)/shard_map/ppermute | solution.py:500
  6.4 5.5 %collective-permute-start.1 = (bf16[32,768]{1,0:T(8,128)(2,1)S(1)}, bf16[32,768]{1,0:T(8,128)(2,1)S(1)}, u32[]{:S(2)}, u32[]{:S(2)}) collective-permute-start(bf16[32,768]{1,0:T(8,128)(2,1)S(1)} %constant_dynamic-slice_fusion.own_ref), channel_id=1, source_target_pairs={{0,16},{8,24},{16,0},{24,8},{1,17},{9,25},{17,1},{25,9},{2,18},{10... | collective-permute-start | bytes 147464 | tf_op jit(solution)/shard_map/ppermute | solution.py:500
  11.9 11.1 %collective-permute-start.5 = (bf16[96,768]{1,0:T(8,128)(2,1)S(1)}, bf16[96,768]{1,0:T(8,128)(2,1)S(1)}, u32[]{:S(2)}, u32[]{:S(2)}) collective-permute-start(bf16[96,768]{1,0:T(8,128)(2,1)S(1)} %constant_dynamic-update-slice_fusion.refs_0_), channel_id=1, source_target_pairs={{0,6},{2,4},{4,2},{6,0},{1,7},{3,5},{5,3},{7,1},{8,14},{10,12},{12... | collective-permute-start | bytes 442376 | tf_op jit(solution)/shard_map/ppermute | solution.py:500
  14.4 8.6 %collective-permute-start.4 = (bf16[96,768]{1,0:T(8,128)(2,1)S(1)}, bf16[96,768]{1,0:T(8,128)(2,1)S(1)}, u32[]{:S(2)}, u32[]{:S(2)}) collective-permute-start(bf16[96,768]{1,0:T(8,128)(2,1)S(1)} %constant_dynamic-update-slice_fusion.refs_0_), channel_id=1, source_target_pairs={{0,4},{2,6},{4,0},{6,2},{1,5},{3,7},{5,1},{7,3},{8,12},{10,14},{12... | collective-permute-start | bytes 442376 | tf_op jit(solution)/shard_map/ppermute | solution.py:500
  14.9 8.1 %collective-permute-start.3 = (bf16[96,768]{1,0:T(8,128)(2,1)S(1)}, bf16[96,768]{1,0:T(8,128)(2,1)S(1)}, u32[]{:S(2)}, u32[]{:S(2)}) collective-permute-start(bf16[96,768]{1,0:T(8,128)(2,1)S(1)} %constant_dynamic-update-slice_fusion.refs_0_), channel_id=1, source_target_pairs={{0,2},{2,0},{4,6},{6,4},{1,3},{3,1},{5,7},{7,5},{8,10},{10,8},{12,... | collective-permute-start | bytes 442376 | tf_op jit(solution)/shard_map/ppermute | solution.py:500
  15.5 1.4 copy-start
  16.9 1.0 copy-start.2
  17.9 7.5 %copy-start.1 = (bf16[1024,768]{1,0:T(8,128)(2,1)S(1)}, bf16[1024,768]{1,0:T(8,128)(2,1)}, u32[]{:S(2)}) copy-start(bf16[1024,768]{1,0:T(8,128)(2,1)} %emb_ref.3) | copy-start | bytes 4718596
  23.0 1.4 collective-permute-start.6
  23.1 1.6 %collective-permute-start.7 = (bf16[96,768]{1,0:T(8,128)(2,1)S(1)}, bf16[96,768]{1,0:T(8,128)(2,1)S(1)}, u32[]{:S(2)}, u32[]{:S(2)}) collective-permute-start(bf16[96,768]{1,0:T(8,128)(2,1)S(1)} %collective-permute-done.3.refs_1_), channel_id=1, source_target_pairs={{0,1},{1,0},{2,3},{3,2},{4,5},{5,4},{6,7},{7,6},{8,9},{9,8},{10,11... | collective-permute-start | bytes 442376 | tf_op jit(solution)/shard_map/ppermute | solution.py:500
  23.6 1.5 %collective-permute-start.8 = (bf16[96,768]{1,0:T(8,128)(2,1)S(1)}, bf16[96,768]{1,0:T(8,128)(2,1)}, u32[]{:S(2)}, u32[]{:S(2)}) collective-permute-start(bf16[96,768]{1,0:T(8,128)(2,1)S(1)} %collective-permute-done.4.refs_2_), channel_id=1, source_target_pairs={{0,1},{1,0},{2,3},{3,2},{4,5},{5,4},{6,7},{7,6},{8,9},{9,8},{10,11... | collective-permute-start | bytes 442376 | tf_op jit(solution)/shard_map/ppermute | solution.py:500
  23.7 1.6 %collective-permute-start.9 = (bf16[96,768]{1,0:T(8,128)(2,1)S(1)}, bf16[96,768]{1,0:T(8,128)(2,1)}, u32[]{:S(2)}, u32[]{:S(2)}) collective-permute-start(bf16[96,768]{1,0:T(8,128)(2,1)S(1)} %collective-permute-done.5.refs_3_), channel_id=1, source_target_pairs={{0,1},{1,0},{2,3},{3,2},{4,5},{5,4},{6,7},{7,6},{8,9},{9,8},{10,11... | collective-permute-start | bytes 442376 | tf_op jit(solution)/shard_map/ppermute | solution.py:500
  42.9 1.7 %collective-permute-start.10 = (f32[640,128]{1,0:T(8,128)S(1)}, f32[640,128]{1,0:T(8,128)S(1)}, u32[]{:S(2)}, u32[]{:S(2)}) collective-permute-start(f32[640,128]{1,0:T(8,128)S(1)} %get-tuple-element.54), channel_id=1, source_target_pairs={{0,1},{1,0},{2,3},{3,2},{4,5},{5,4},{6,7},{7,6},{8,9},{9,8},{10,11... | collective-permute-start | bytes 983048 | tf_op jit(solution)/shard_map/ppermute | solution.py:500
  47.2 2.4 %collective-permute-start.11 = (f32[1664,128]{1,0:T(8,128)S(1)}, f32[1664,128]{1,0:T(8,128)S(1)}, u32[]{:S(2)}, u32[]{:S(2)}) collective-permute-start(f32[1664,128]{1,0:T(8,128)S(1)} %get-tuple-element.57), channel_id=1, source_target_pairs={{0,1},{1,0},{2,3},{3,2},{4,5},{5,4},{6,7},{7,6},{8,9},{9,8},{10,11... | collective-permute-start | bytes 2555912 | tf_op jit(solution)/shard_map/ppermute | solution.py:500
  50.3 8.1 %collective-permute-start.12 = (f32[416,128]{1,0:T(8,128)S(1)}, f32[416,128]{1,0:T(8,128)S(1)}, u32[]{:S(2)}, u32[]{:S(2)}) collective-permute-start(f32[416,128]{1,0:T(8,128)S(1)} %get-tuple-element.59), channel_id=1, source_target_pairs={{0,2},{2,0},{4,6},{6,4},{1,3},{3,1},{5,7},{7,5},{8,10},{10,8},{12,... | collective-permute-start | bytes 638984 | tf_op jit(solution)/shard_map/ppermute | solution.py:500
  51.9 12.6 %collective-permute-start.13 = (f32[416,128]{1,0:T(8,128)S(1)}, f32[416,128]{1,0:T(8,128)S(1)}, u32[]{:S(2)}, u32[]{:S(2)}) collective-permute-start(f32[416,128]{1,0:T(8,128)S(1)} %get-tuple-element.60), channel_id=1, source_target_pairs={{0,4},{2,6},{4,0},{6,2},{1,5},{3,7},{5,1},{7,3},{8,12},{10,14},{12... | collective-permute-start | bytes 638984 | tf_op jit(solution)/shard_map/ppermute | solution.py:500
  53.4 11.1 %collective-permute-start.14 = (f32[416,128]{1,0:T(8,128)S(1)}, f32[416,128]{1,0:T(8,128)S(1)}, u32[]{:S(2)}, u32[]{:S(2)}) collective-permute-start(f32[416,128]{1,0:T(8,128)S(1)} %get-tuple-element.61), channel_id=1, source_target_pairs={{0,6},{2,4},{4,2},{6,0},{1,7},{3,5},{5,3},{7,1},{8,14},{10,12},{12... | collective-permute-start | bytes 638984 | tf_op jit(solution)/shard_map/ppermute | solution.py:500
  53.9 11.5 %collective-permute-start.24 = (f32[160,128]{1,0:T(8,128)S(1)}, f32[160,128]{1,0:T(8,128)S(1)}, u32[]{:S(2)}, u32[]{:S(2)}) collective-permute-start(f32[160,128]{1,0:T(8,128)S(1)} %get-tuple-element.66), channel_id=1, source_target_pairs={{0,2},{2,0},{4,6},{6,4},{1,3},{3,1},{5,7},{7,5},{8,10},{10,8},{12,... | collective-permute-start | bytes 245768 | tf_op jit(solution)/shard_map/ppermute | solution.py:500
  55.4 11.8 %collective-permute-start.25 = (f32[160,128]{1,0:T(8,128)S(1)}, f32[160,128]{1,0:T(8,128)S(1)}, u32[]{:S(2)}, u32[]{:S(2)}) collective-permute-start(f32[160,128]{1,0:T(8,128)S(1)} %get-tuple-element.67), channel_id=1, source_target_pairs={{0,4},{2,6},{4,0},{6,2},{1,5},{3,7},{5,1},{7,3},{8,12},{10,14},{12... | collective-permute-start | bytes 245768 | tf_op jit(solution)/shard_map/ppermute | solution.py:500
  58.5 8.7 %collective-permute-start.26 = (f32[160,128]{1,0:T(8,128)S(1)}, f32[160,128]{1,0:T(8,128)S(1)}, u32[]{:S(2)}, u32[]{:S(2)}) collective-permute-start(f32[160,128]{1,0:T(8,128)S(1)} %get-tuple-element.68), channel_id=1, source_target_pairs={{0,6},{2,4},{4,2},{6,0},{1,7},{3,5},{5,3},{7,1},{8,14},{10,12},{12... | collective-permute-start | bytes 245768 | tf_op jit(solution)/shard_map/ppermute | solution.py:500
  65.1 15.6 %collective-permute-start.15 = (f32[104,128]{1,0:T(8,128)S(1)}, f32[104,128]{1,0:T(8,128)S(1)}, u32[]{:S(2)}, u32[]{:S(2)}) collective-permute-start(f32[104,128]{1,0:T(8,128)S(1)} %get-tuple-element.63), channel_id=1, source_target_pairs={{0,8},{8,0},{16,24},{24,16},{1,9},{9,1},{17,25},{25,17},{2,10},{10... | collective-permute-start | bytes 159752 | tf_op jit(solution)/shard_map/ppermute | solution.py:500
  67.7 4.5 %collective-permute-start.27 = (f32[40,128]{1,0:T(8,128)S(1)}, f32[40,128]{1,0:T(8,128)S(1)}, u32[]{:S(2)}, u32[]{:S(2)}) collective-permute-start(f32[40,128]{1,0:T(8,128)S(1)} %get-tuple-element.70), channel_id=1, source_target_pairs={{0,8},{8,0},{16,24},{24,16},{1,9},{9,1},{17,25},{25,17},{2,10},{10... | collective-permute-start | bytes 61448 | tf_op jit(solution)/shard_map/ppermute | solution.py:500
  68.0 14.8 %collective-permute-start.16 = (f32[104,128]{1,0:T(8,128)S(1)}, f32[104,128]{1,0:T(8,128)S(1)}, u32[]{:S(2)}, u32[]{:S(2)}) collective-permute-start(f32[104,128]{1,0:T(8,128)S(1)} %get-tuple-element.64), channel_id=1, source_target_pairs={{0,16},{8,24},{16,0},{24,8},{1,17},{9,25},{17,1},{25,9},{2,18},{10... | collective-permute-start | bytes 159752 | tf_op jit(solution)/shard_map/ppermute | solution.py:500
  70.4 12.3 %collective-permute-start.17 = (f32[104,128]{1,0:T(8,128)S(1)}, f32[104,128]{1,0:T(8,128)S(1)}, u32[]{:S(2)}, u32[]{:S(2)}) collective-permute-start(f32[104,128]{1,0:T(8,128)S(1)} %get-tuple-element.65), channel_id=1, source_target_pairs={{0,24},{8,16},{16,8},{24,0},{1,25},{9,17},{17,9},{25,1},{2,26},{10... | collective-permute-start | bytes 159752 | tf_op jit(solution)/shard_map/ppermute | solution.py:500
  72.2 4.9 %collective-permute-start.28 = (f32[40,128]{1,0:T(8,128)S(1)}, f32[40,128]{1,0:T(8,128)S(1)}, u32[]{:S(2)}, u32[]{:S(2)}) collective-permute-start(f32[40,128]{1,0:T(8,128)S(1)} %get-tuple-element.71), channel_id=1, source_target_pairs={{0,16},{8,24},{16,0},{24,8},{1,17},{9,25},{17,1},{25,9},{2,18},{10... | collective-permute-start | bytes 61448 | tf_op jit(solution)/shard_map/ppermute | solution.py:500
  72.2 5.6 %collective-permute-start.29 = (f32[40,128]{1,0:T(8,128)S(1)}, f32[40,128]{1,0:T(8,128)S(1)}, u32[]{:S(2)}, u32[]{:S(2)}) collective-permute-start(f32[40,128]{1,0:T(8,128)S(1)} %get-tuple-element.72), channel_id=1, source_target_pairs={{0,24},{8,16},{16,8},{24,0},{1,25},{9,17},{17,9},{25,1},{2,26},{10... | collective-permute-start | bytes 61448 | tf_op jit(solution)/shard_map/ppermute | solution.py:500
  78.3 7.3 %collective-permute-start.32 = (f32[40,128]{1,0:T(8,128)S(1)}, f32[40,128]{1,0:T(8,128)S(1)}, u32[]{:S(2)}, u32[]{:S(2)}) collective-permute-start(f32[40,128]{1,0:T(8,128)S(1)} %add_cut.11.refs_0_), channel_id=1, source_target_pairs={{0,24},{8,16},{16,8},{24,0},{1,25},{9,17},{17,9},{25,1},{2,26},{10... | collective-permute-start | bytes 61448 | tf_op jit(solution)/shard_map/ppermute | solution.py:500
  80.6 5.0 %collective-permute-start.31 = (f32[40,128]{1,0:T(8,128)S(1)}, f32[40,128]{1,0:T(8,128)S(1)}, u32[]{:S(2)}, u32[]{:S(2)}) collective-permute-start(f32[40,128]{1,0:T(8,128)S(1)} %add_cut.11.refs_0_), channel_id=1, source_target_pairs={{0,16},{8,24},{16,0},{24,8},{1,17},{9,25},{17,1},{25,9},{2,18},{10... | collective-permute-start | bytes 61448 | tf_op jit(solution)/shard_map/ppermute | solution.py:500
  80.7 4.9 %collective-permute-start.30 = (f32[40,128]{1,0:T(8,128)S(1)}, f32[40,128]{1,0:T(8,128)S(1)}, u32[]{:S(2)}, u32[]{:S(2)}) collective-permute-start(f32[40,128]{1,0:T(8,128)S(1)} %add_cut.11.refs_0_), channel_id=1, source_target_pairs={{0,8},{8,0},{16,24},{24,16},{1,9},{9,1},{17,25},{25,17},{2,10},{10... | collective-permute-start | bytes 61448 | tf_op jit(solution)/shard_map/ppermute | solution.py:500
  83.3 6.8 %collective-permute-start.20 = (f32[104,128]{1,0:T(8,128)S(1)}, f32[104,128]{1,0:T(8,128)S(1)}, u32[]{:S(2)}, u32[]{:S(2)}) collective-permute-start(f32[104,128]{1,0:T(8,128)S(1)} %add_cut.9.refs_0_), channel_id=1, source_target_pairs={{0,24},{8,16},{16,8},{24,0},{1,25},{9,17},{17,9},{25,1},{2,26},{10... | collective-permute-start | bytes 159752 | tf_op jit(solution)/shard_map/ppermute | solution.py:500
  86.2 10.0 %collective-permute-start.36 = (f32[160,128]{1,0:T(8,128)S(1)}, f32[160,128]{1,0:T(8,128)S(1)}, u32[]{:S(2)}, u32[]{:S(2)}) collective-permute-start(f32[160,128]{1,0:T(8,128)S(1)} %place.3.refs_0_), channel_id=1, source_target_pairs={{0,1},{1,0},{2,3},{3,2},{4,5},{5,4},{6,7},{7,6},{8,9},{9,8},{10,11... | collective-permute-start | bytes 245768 | tf_op jit(solution)/shard_map/ppermute | solution.py:500
  86.3 6.4 %collective-permute-start.19 = (f32[104,128]{1,0:T(8,128)S(1)}, f32[104,128]{1,0:T(8,128)S(1)}, u32[]{:S(2)}, u32[]{:S(2)}) collective-permute-start(f32[104,128]{1,0:T(8,128)S(1)} %add_cut.9.refs_0_), channel_id=1, source_target_pairs={{0,16},{8,24},{16,0},{24,8},{1,17},{9,25},{17,1},{25,9},{2,18},{10... | collective-permute-start | bytes 159752 | tf_op jit(solution)/shard_map/ppermute | solution.py:500
  88.0 4.8 %collective-permute-start.18 = (f32[104,128]{1,0:T(8,128)S(1)}, f32[104,128]{1,0:T(8,128)S(1)}, u32[]{:S(2)}, u32[]{:S(2)}) collective-permute-start(f32[104,128]{1,0:T(8,128)S(1)} %add_cut.9.refs_0_), channel_id=1, source_target_pairs={{0,8},{8,0},{16,24},{24,16},{1,9},{9,1},{17,25},{25,17},{2,10},{10... | collective-permute-start | bytes 159752 | tf_op jit(solution)/shard_map/ppermute | solution.py:500
  88.7 8.6 %collective-permute-start.35 = (f32[160,128]{1,0:T(8,128)S(1)}, f32[160,128]{1,0:T(8,128)S(1)}, u32[]{:S(2)}, u32[]{:S(2)}) collective-permute-start(f32[160,128]{1,0:T(8,128)S(1)} %place.3.refs_0_), channel_id=1, source_target_pairs={{0,6},{2,4},{4,2},{6,0},{1,7},{3,5},{5,3},{7,1},{8,14},{10,12},{12... | collective-permute-start | bytes 245768 | tf_op jit(solution)/shard_map/ppermute | solution.py:500
  90.1 8.1 %collective-permute-start.34 = (f32[160,128]{1,0:T(8,128)S(1)}, f32[160,128]{1,0:T(8,128)S(1)}, u32[]{:S(2)}, u32[]{:S(2)}) collective-permute-start(f32[160,128]{1,0:T(8,128)S(1)} %place.3.refs_0_), channel_id=1, source_target_pairs={{0,4},{2,6},{4,0},{6,2},{1,5},{3,7},{5,1},{7,3},{8,12},{10,14},{12... | collective-permute-start | bytes 245768 | tf_op jit(solution)/shard_map/ppermute | solution.py:500
  93.4 30.5 %collective-permute-start.23 = (f32[416,128]{1,0:T(8,128)S(1)}, f32[416,128]{1,0:T(8,128)S(1)}, u32[]{:S(2)}, u32[]{:S(2)}) collective-permute-start(f32[416,128]{1,0:T(8,128)S(1)} %place.2.refs_8_.refs_0_), channel_id=1, source_target_pairs={{0,6},{2,4},{4,2},{6,0},{1,7},{3,5},{5,3},{7,1},{8,14},{10,12},{12... | collective-permute-start | bytes 638984 | tf_op jit(solution)/shard_map/ppermute | solution.py:500
  95.1 28.8 %collective-permute-start.22 = (f32[416,128]{1,0:T(8,128)S(1)}, f32[416,128]{1,0:T(8,128)S(1)}, u32[]{:S(2)}, u32[]{:S(2)}) collective-permute-start(f32[416,128]{1,0:T(8,128)S(1)} %place.2.refs_8_.refs_0_), channel_id=1, source_target_pairs={{0,4},{2,6},{4,0},{6,2},{1,5},{3,7},{5,1},{7,3},{8,12},{10,14},{12... | collective-permute-start | bytes 638984 | tf_op jit(solution)/shard_map/ppermute | solution.py:500
  96.2 27.7 %collective-permute-start.21 = (f32[416,128]{1,0:T(8,128)S(1)}, f32[416,128]{1,0:T(8,128)S(1)}, u32[]{:S(2)}, u32[]{:S(2)}) collective-permute-start(f32[416,128]{1,0:T(8,128)S(1)} %place.2.refs_8_.refs_0_), channel_id=1, source_target_pairs={{0,2},{2,0},{4,6},{6,4},{1,3},{3,1},{5,7},{7,5},{8,10},{10,8},{12,... | collective-permute-start | bytes 638984 | tf_op jit(solution)/shard_map/ppermute | solution.py:500
  97.2 11.1 %collective-permute-start.33 = (f32[160,128]{1,0:T(8,128)S(1)}, f32[160,128]{1,0:T(8,128)S(1)}, u32[]{:S(2)}, u32[]{:S(2)}) collective-permute-start(f32[160,128]{1,0:T(8,128)S(1)} %place.3.refs_0_), channel_id=1, source_target_pairs={{0,2},{2,0},{4,6},{6,4},{1,3},{3,1},{5,7},{7,5},{8,10},{10,8},{12,... | collective-permute-start | bytes 245768 | tf_op jit(solution)/shard_map/ppermute | solution.py:500
  98.3 10.1 %collective-permute-start.39 = (f32[160,128]{1,0:T(8,128)S(1)}, f32[160,128]{1,0:T(8,128)S(1)}, u32[]{:S(2)}, u32[]{:S(2)}) collective-permute-start(f32[160,128]{1,0:T(8,128)S(1)} %collective-permute-done.35.refs_3_), channel_id=1, source_target_pairs={{0,1},{1,0},{2,3},{3,2},{4,5},{5,4},{6,7},{7,6},{8,9},{9,8},{10,11... | collective-permute-start | bytes 245768 | tf_op jit(solution)/shard_map/ppermute | solution.py:500
  108.4 1.3 collective-permute-start.38
  108.4 1.4 collective-permute-start.37
  123.9 1.5 %collective-permute-start.40 = (f32[416,128]{1,0:T(8,128)S(1)}, f32[416,128]{1,0:T(8,128)S(1)}, u32[]{:S(2)}, u32[]{:S(2)}) collective-permute-start(f32[416,128]{1,0:T(8,128)S(1)} %place.2.refs_8_.refs_0_), channel_id=1, source_target_pairs={{0,1},{1,0},{2,3},{3,2},{4,5},{5,4},{6,7},{7,6},{8,9},{9,8},{10,11... | collective-permute-start | bytes 638984 | tf_op jit(solution)/shard_map/ppermute | solution.py:500
  124.3 1.5 %collective-permute-start.41 = (f32[416,128]{1,0:T(8,128)S(1)}, f32[416,128]{1,0:T(8,128)S(1)}, u32[]{:S(2)}, u32[]{:S(2)}) collective-permute-start(f32[416,128]{1,0:T(8,128)S(1)} %collective-permute-done.21.refs_1_), channel_id=1, source_target_pairs={{0,1},{1,0},{2,3},{3,2},{4,5},{5,4},{6,7},{7,6},{8,9},{9,8},{10,11... | collective-permute-start | bytes 638984 | tf_op jit(solution)/shard_map/ppermute | solution.py:500
  124.5 1.6 %collective-permute-start.42 = (f32[416,128]{1,0:T(8,128)S(1)}, f32[416,128]{1,0:T(8,128)S(1)}, u32[]{:S(2)}, u32[]{:S(2)}) collective-permute-start(f32[416,128]{1,0:T(8,128)S(1)} %collective-permute-done.22.refs_2_), channel_id=1, source_target_pairs={{0,1},{1,0},{2,3},{3,2},{4,5},{5,4},{6,7},{7,6},{8,9},{9,8},{10,11... | collective-permute-start | bytes 638984 | tf_op jit(solution)/shard_map/ppermute | solution.py:500
  124.9 1.6 %collective-permute-start.43 = (f32[416,128]{1,0:T(8,128)S(1)}, f32[416,128]{1,0:T(8,128)S(1)}, u32[]{:S(2)}, u32[]{:S(2)}) collective-permute-start(f32[416,128]{1,0:T(8,128)S(1)} %collective-permute-done.23.refs_3_), channel_id=1, source_target_pairs={{0,1},{1,0},{2,3},{3,2},{4,5},{5,4},{6,7},{7,6},{8,9},{9,8},{10,11... | collective-permute-start | bytes 638984 | tf_op jit(solution)/shard_map/ppermute | solution.py:500

commit v5 on v4

--- a/solution.py
+++ b/solution.py
@@ -18,7 +18,7 @@
 W = 16
 TINY = 1e-30
 
-ARC = (0.9428362797873839, 0.04684592969277604, 0.008663018923508323, 1.324670644556325e-05, 0.0016412996811995852)
+ARC = (0.9426497266634519, 0.04833294295062493, 0.004716300148249888, 0.004298816276929029)
 KEEP = 1.0 / (1.0 + SCALE_SQ)
 ARC = tuple(c * SCALE_SQ * KEEP / math.pi for c in ARC)
 GROWTH = (1.0 + SCALE_SQ) ** LAYERS
@@ -28,8 +28,8 @@
     for _ in range(LAYERS):
         w = jnp.maximum(1.0 - jnp.abs(c), TINY)
         t = (w * w) * lax.rsqrt(w)
-        poly = ARC[4]
-        for a in ARC[3::-1]:
+        poly = ARC[3]
+        for a in ARC[2::-1]:
             poly = poly * w + a
         c = jnp.maximum(c, KEEP * c) + t * poly
     return c
@@ -119,8 +119,8 @@
     all_points: int
 
 
-def gram_kernel(plan, first, at_ref, emb_ref, mine_ref, own_ref, u_ref, x_mine_ref, *refs):
-    lands, chips, cores, split, _ = plan
+def gram_kernel(plan, na, at_ref, emb_ref, mine_ref, own_ref, u_ref, x_mine_ref, *refs):
+    lands, chips, cores, split, all_points = plan
     count = chips * (cores if split else 1)
     far = refs[:count]
     keep_ref, send_ref, x_ref, ridge_ref, marks_ref, k_ref, vq_ref, out_ref = refs[count:]
@@ -163,130 +163,115 @@
         rows = slice((s - 1) * shard, s * shard)
         ridge(marks_ref[rows, :], vq_ref[rows, :], pl.multiple_of((land ^ s) * shard, shard))
 
-    gram_columns(plan, first, position_of(at_ref, plan, share, shard), x_ref, ridge_ref, out_ref, at_ref[2], keep_ref, send_ref)
-
-
-def position_of(at_ref, plan, share, shard):
-    return at_ref[0] * shard + (at_ref[1] * plan.cores + at_ref[2]) * share
-
-
-def gram_columns(plan, span, position, x_ref, ridge_ref, out_ref, core, keep_ref, send_ref):
-    share = ridge_ref.shape[0]
+    position = land * shard + (chip * cores + core) * share
     row_block = position // B
     offset = position % B
-    base = packed_start(span[0])
     wide = 2 * B
-    for w in range(span[0] // 2, span[1] // 2):
-        both = nt(x_ref[: (w + 1) * wide, :], x_ref[w * wide : (w + 1) * wide, :]) * (1.0 / plan.all_points)
+    for w in range(n // wide):
+        both = nt(x_ref[: (w + 1) * wide, :], x_ref[w * wide : (w + 1) * wide, :]) * (1.0 / all_points)
         for j in (2 * w, 2 * w + 1):
-            start = packed_start(j) - base
+            start = column_start(plan, na, j)
             out_ref[start : start + (j + 1) * B, :] = both[: (j + 1) * B, (j % 2) * B : (j % 2 + 1) * B]
-    for j in range(*span):
-        start = packed_start(j) - base
+    for j in range(n // B):
+        start = column_start(plan, na, j)
 
         @pl.when(row_block <= j)
         def _():
             at = pl.ds(pl.multiple_of(start + row_block * B + offset, share), share)
             out_ref[at, :] = out_ref[at, :] + ridge_ref[:, j * B : (j + 1) * B]
 
-    half = keep_ref.shape[0]
-    keep_ref[...] = out_ref[pl.ds(pl.multiple_of(core * half, half), half), :]
-    send_ref[...] = out_ref[pl.ds(pl.multiple_of((1 - core) * half, half), half), :]
-
-
-def last_kernel(plan, span, shard, at_ref, x_ref, ridge_ref, order_ref, keep_ref, send_ref, out_ref):
-    position = position_of(at_ref, plan, ridge_ref.shape[0], shard)
-    gram_columns(plan, span, position, x_ref, ridge_ref, out_ref, at_ref[2], keep_ref, send_ref)
-
-
-def halves(plan, span):
-    return (jax.ShapeDtypeStruct((packed_rows(plan, span) // plan.cores, B), jnp.float32),) * 2
+    done = base = 0
+    for rows in segments(plan, na, n // B):
+        half = rows // cores
+        to = slice(done, done + half)
+        keep_ref[to, :] = out_ref[pl.ds(pl.multiple_of(base + core * half, 8), half), :]
+        send_ref[to, :] = out_ref[pl.ds(pl.multiple_of(base + (1 - core) * half, 8), half), :]
+        done, base = done + half, base + rows
 
 
 def packed_start(j):
     return j * (j + 1) // 2 * B
 
 
-def packed_rows(plan, span):
+def segments(plan, na, nb):
     unit = 8 * plan.lands * plan.chips * plan.cores
-    return -(-(packed_start(span[1]) - packed_start(span[0])) // unit) * unit
-
-
-def first_columns(at, plan, span, embeddings, landmarks, own, u, x_mine, far):
+    return [-(-rows // unit) * unit for rows in (packed_start(na), packed_start(nb) - packed_start(na))]
+
+
+def column_start(plan, na, j):
+    return packed_start(j) if j < na else packed_start(j) - packed_start(na) + segments(plan, na, j)[0]
+
+
+def local_normal(at, plan, na, embeddings, landmarks, own, u, x_mine, far):
     n, m = landmarks.shape[0] * plan.lands, embeddings.shape[0]
     away = n - landmarks.shape[0]
+    rows = sum(segments(plan, na, n // B))
+    half = jax.ShapeDtypeStruct((rows // plan.cores, B), jnp.float32)
     vmem = pl.BlockSpec(memory_space=pltpu.VMEM)
     return pl.pallas_call(
-        functools.partial(gram_kernel, plan, span),
-        out_shape=halves(plan, span)
-        + (jax.ShapeDtypeStruct((n, m), jnp.bfloat16), jax.ShapeDtypeStruct((own.shape[0], n), jnp.float32)),
+        functools.partial(gram_kernel, plan, na),
+        out_shape=(half, half),
         in_specs=[pl.BlockSpec(memory_space=pltpu.SMEM)] + [vmem] * (5 + len(far)),
-        out_specs=(vmem,) * 4,
+        out_specs=(vmem,) * 2,
         scratch_shapes=[
+            pltpu.VMEM((n, m), jnp.bfloat16),
+            pltpu.VMEM((own.shape[0], n), jnp.float32),
             pltpu.VMEM((away, landmarks.shape[1]), jnp.bfloat16),
             pltpu.VMEM((away, m), jnp.float32),
             pltpu.VMEM((away, B), jnp.float32),
-            pltpu.VMEM((packed_rows(plan, span), B), jnp.float32),
+            pltpu.VMEM((rows, B), jnp.float32),
         ],
         compiler_params=pltpu.CompilerParams(vmem_limit_bytes=24 << 20),
-        name="gram_first",
+        name="gram",
     )(at, embeddings, landmarks, own, u, x_mine, *far)
 
 
-def last_columns(at, plan, span, shard, x, ridge, order):
+def add_cut_kernel(ways, axis, parts, at_ref, *refs):
+    ins, outs = refs[: len(refs) - ways], refs[len(refs) - ways :]
+    base = 0
+    for rows in parts:
+        h = rows // ways
+        for s in range(ways):
+            at = pl.ds(pl.multiple_of(base + (at_ref[axis] ^ s) * h, 8), h) if ways > 1 else slice(base, base + h)
+            total = ins[0][at, :]
+            for r in ins[1:]:
+                total = total + r[at, :]
+            outs[s][base // ways : base // ways + h, :] = total
+        base += rows
+
+
+def add_cut(at, axis, ways, parts, ins):
+    h = sum(parts) // ways
     vmem = pl.BlockSpec(memory_space=pltpu.VMEM)
     return pl.pallas_call(
-        functools.partial(last_kernel, plan, span, shard),
-        out_shape=halves(plan, span),
-        in_specs=[pl.BlockSpec(memory_space=pltpu.SMEM), vmem, vmem, pl.BlockSpec(memory_space=pl.ANY)],
-        out_specs=(vmem,) * 2,
-        scratch_shapes=[pltpu.VMEM((packed_rows(plan, span), B), jnp.float32)],
-        compiler_params=pltpu.CompilerParams(vmem_limit_bytes=16 << 20),
-        name="gram_last",
-    )(at, x, ridge, order)
-
-
-def add_cut_kernel(ways, axis, at_ref, *refs):
-    ins, outs = refs[: len(refs) - ways], refs[len(refs) - ways :]
-    h = outs[0].shape[0]
-    for s in range(ways):
-        rows = pl.ds(pl.multiple_of((at_ref[axis] ^ s) * h, h), h) if ways > 1 else slice(None)
-        total = ins[0][rows, :]
-        for r in ins[1:]:
-            total = total + r[rows, :]
-        outs[s][...] = total
-
-
-def add_cut(at, axis, ways, parts):
-    h = parts[0].shape[0] // ways
-    vmem = pl.BlockSpec(memory_space=pltpu.VMEM)
-    return pl.pallas_call(
-        functools.partial(add_cut_kernel, ways, axis),
+        functools.partial(add_cut_kernel, ways, axis, parts),
         out_shape=tuple([jax.ShapeDtypeStruct((h, B), jnp.float32)] * ways),
-        in_specs=[pl.BlockSpec(memory_space=pltpu.SMEM)] + [vmem] * len(parts),
+        in_specs=[pl.BlockSpec(memory_space=pltpu.SMEM)] + [vmem] * len(ins),
         out_specs=tuple([vmem] * ways),
         compiler_params=pltpu.CompilerParams(vmem_limit_bytes=8 << 20),
         name="add_cut",
-    )(at, *parts)
-
-
-def place_kernel(axis, at_ref, *refs):
-    out = refs[-1]
-    h = refs[0].shape[0]
-    for s in range(len(refs) - 1):
-        out[pl.ds(pl.multiple_of((at_ref[axis] ^ s) * h, h), h), :] = refs[s][...]
-
-
-def place(at, axis, parts):
+    )(at, *ins)
+
+
+def place_kernel(axis, ways, parts, at_ref, *refs):
+    ins, outs = refs[:ways], refs[ways:]
+    base = 0
+    for out, h in zip(outs, parts):
+        for s in range(ways):
+            out[pl.ds(pl.multiple_of((at_ref[axis] ^ s) * h, 8), h), :] = ins[s][base : base + h, :]
+        base += h
+
+
+def place(at, axis, parts, ins):
     vmem = pl.BlockSpec(memory_space=pltpu.VMEM)
     return pl.pallas_call(
-        functools.partial(place_kernel, axis),
-        out_shape=jax.ShapeDtypeStruct((parts[0].shape[0] * len(parts), B), jnp.float32),
-        in_specs=[pl.BlockSpec(memory_space=pltpu.SMEM)] + [vmem] * len(parts),
-        out_specs=vmem,
+        functools.partial(place_kernel, axis, len(ins), parts),
+        out_shape=tuple(jax.ShapeDtypeStruct((h * len(ins), B), jnp.float32) for h in parts),
+        in_specs=[pl.BlockSpec(memory_space=pltpu.SMEM)] + [vmem] * len(ins),
+        out_specs=(vmem,) * len(parts),
         compiler_params=pltpu.CompilerParams(vmem_limit_bytes=8 << 20),
         name="place",
-    )(at, *parts)
+    )(at, *ins)
 
 
 def thirds(x):
@@ -412,7 +397,7 @@
 
 def first_factor_kernel(plan, at_ref, *refs):
     count = plan.chips * plan.cores
-    f_ref, w_ref, a_ref, m_ref, d_ref, r_ref = refs[count + 1 :]
+    f_ref, w_ref, a_ref, m_ref, d_ref, r_ref = refs[count:]
     na = f_ref.shape[0] // B
     place_parts(plan, at_ref, refs[:count], a_ref)
     for j in range(na):
@@ -426,7 +411,7 @@
     eliminate(na, m_ref, d_ref, r_ref, store)
 
 
-def first_factor(at, plan, na, parts, order):
+def first_factor(at, plan, na, parts):
     vmem = pl.BlockSpec(memory_space=pltpu.VMEM)
     return pl.pallas_call(
         functools.partial(first_factor_kernel, plan),
@@ -434,7 +419,7 @@
             jax.ShapeDtypeStruct((na * B, na * B), jnp.float32),
             jax.ShapeDtypeStruct((na * B, B), jnp.float32),
         ),
-        in_specs=[pl.BlockSpec(memory_space=pltpu.SMEM)] + [vmem] * len(parts) + [pl.BlockSpec(memory_space=pl.ANY)],
+        in_specs=[pl.BlockSpec(memory_space=pltpu.SMEM)] + [vmem] * len(parts),
         out_specs=(vmem,) * 2,
         scratch_shapes=[
             pltpu.VMEM((parts[0].shape[0] * len(parts), B), jnp.float32),
@@ -444,7 +429,7 @@
         ],
         compiler_params=pltpu.CompilerParams(vmem_limit_bytes=16 << 20),
         name="chol_first",
-    )(at, *parts, order)
+    )(at, *parts)
 
 
 def last_factor_kernel(plan, at_ref, f_ref, w_ref, *refs):
@@ -501,7 +486,8 @@
 
 
 def scatter(pieces, axis):
-    return [pieces[0]] + [swap(p, axis, s) for s, p in enumerate(pieces) if s]
+    arrived = [swap(p, axis, s) for s, p in reversed(list(enumerate(pieces))) if s]
+    return [pieces[0]] + arrived[::-1]
 
 
 def spread_out(x, axis):
@@ -531,25 +517,20 @@
             far = far + [swap(f, "core", a) for f in far[:chips]]
 
     na = n // B // 2
-    first, last = (0, na), (na, n // B)
-    keep, send, x, ridge = first_columns(at, plan, first, embeddings, landmarks, own, u, x_mine, far)
-    cut_a = add_cut(at, 1, chips, [keep, swap(send, "core", 1)])
-    keep, send = last_columns(at, plan, last, shard, x, ridge, cut_a[0])
-    cut_b = add_cut(at, 1, chips, [keep, swap(send, "core", 1)])
-    whole_a = land_reduce(at, lands, scatter(cut_a, "chip"))
-    whole_b = land_reduce(at, lands, scatter(cut_b, "chip"))
-    parts_a = spread_out(whole_a, "chip")
-    parts_a = parts_a + [swap(p, "core", 1) for p in parts_a]
-    f, w = first_factor(at, plan, na, parts_a, whole_b)
-    parts_b, f, w = lax.optimization_barrier((spread_out(whole_b, "chip"), f, w))
-    parts_b = parts_b + [swap(p, "core", 1) for p in parts_b]
-    return last_factor(at, plan, n, f, w, parts_b)
-
-
-def land_reduce(at, lands, parts):
-    parts = scatter(add_cut(at, 0, lands, parts), "land")
-    (whole,) = add_cut(at, 0, 1, parts)
-    return place(at, 0, spread_out(whole, "land"))
+    keep, send = local_normal(at, plan, na, embeddings, landmarks, own, u, x_mine, far)
+    rows = [r // cores for r in segments(plan, na, n // B)]
+    parts = scatter(add_cut(at, 1, chips, rows, [keep, swap(send, "core", 1)]), "chip")
+    rows = [r // chips for r in rows]
+    parts = scatter(add_cut(at, 0, lands, rows, parts), "land")
+    rows = [r // lands for r in rows]
+    (whole,) = add_cut(at, 0, 1, rows, parts)
+    first, last = place(at, 0, rows, spread_out(whole, "land"))
+    first = spread_out(first, "chip")
+    first = first + [swap(p, "core", 1) for p in first]
+    f, w = first_factor(at, plan, na, first)
+    last, f, w = lax.optimization_barrier((spread_out(last, "chip"), f, w))
+    last = last + [swap(p, "core", 1) for p in last]
+    return last_factor(at, plan, n, f, w, last)
 
 
 def solution(mesh):

time: 146 us -> 136 us (0.932)
  starting transfers between devices: 46.2 us -> 32.4 us
  waiting for transfers between devices: 33.2 us -> 41.8 us
  Pallas kernels: 62.9 us -> 57.8 us
    ppermute x44 -> x34, starting transfers between devices: 46.2 us -> 32.4 us  [swap(): lax.ppermute(x, axis, [(i, i ^ s) for i in range(lax.axis_size(axis))])]
    ppermute x44 -> x34, waiting for transfers between devices: 33.2 us -> 41.8 us  [swap(): lax.ppermute(x, axis, [(i, i ^ s) for i in range(lax.axis_size(axis))])]
    pallas_call x10 -> x5, Pallas kernels: 24.2 us -> 19.5 us  [the longest x1 17.1 us: local_normal(): pl.pallas_call(functools.partial(gram_kernel, plan, na), out_shape=(half,...]
  transfers between devices with their start and end apart: 44 -> 34, of which waited for: 21 -> 20; matrix products, arithmetic and copies ran while one was open for 0% -> 0% of each run, Pallas kernels for 15% -> 14%
where the time goes in v5:
time: 136 us; the launch traced here: 135 us
  Pallas kernels  57.8 us (42%)
  waiting for transfers between devices  41.8 us (31%)
  starting transfers between devices  32.4 us (24%)
  local copies, waits for them, and re-layouts  3.3 us (2%)
    ppermute x34, waiting for transfers between devices, swap(): lax.ppermute(x, axis, [(i, i ^ s) for i in range(lax.axis_size(axis))])  41.8 us
    ppermute x34, starting transfers between devices, swap(): lax.ppermute(x, axis, [(i, i ^ s) for i in range(lax.axis_size(axis))])  32.4 us
    pallas_call x1, Pallas kernels, last_factor(): pl.pallas_call(functools.partial(last_factor_kernel, plan), out_shape=jax...  19.5 us
    pallas_call x1, Pallas kernels, local_normal(): pl.pallas_call(functools.partial(gram_kernel, plan, na), out_shape=(half,...  17.1 us
    pallas_call x1, Pallas kernels, first_factor(): pl.pallas_call(functools.partial(first_factor_kernel, plan), out_shape=(j...  14.1 us
    pallas_call x1, Pallas kernels, own_cross(): pl.pallas_call(own_kernel, out_shape=(jax.ShapeDtypeStruct((shard, m), jn...  4.65 us
  transfers between devices with their start and end apart: 34, of which 20 were waited for; matrix products, arithmetic and copies ran while one was open for 0% of the time, Pallas kernels for 14%

profile of v5, /device:TPU:0, one launch (start us, length us, event | category | flops | bytes accessed | tf_op | source)
XLA Modules:
  0.0 135.5 jit_solution(1721378690213709647)
XLA Ops:
  0.0 0.9 constant_dynamic-slice_fusion.own_ref
  0.9 3.0 %collective-permute-start = (bf16[32,768]{1,0:T(8,128)(2,1)S(1)}, bf16[32,768]{1,0:T(8,128)(2,1)S(1)}, u32[]{:S(2)}, u32[]{:S(2)}) collective-permute-start(bf16[32,768]{1,0:T(8,128)(2,1)S(1)} %constant_dynamic-slice_fusion.own_ref), channel_id=1, source_target_pairs={{0,8},{8,0},{16,24},{24,16},{1,9},{9,1},{17,25},{25,17},{2,10},{10... | collective-permute-start | bytes 147464 | tf_op jit(solution)/shard_map/ppermute | solution.py:485
  3.9 2.5 %collective-permute-start.2 = (bf16[32,768]{1,0:T(8,128)(2,1)S(1)}, bf16[32,768]{1,0:T(8,128)(2,1)S(1)}, u32[]{:S(2)}, u32[]{:S(2)}) collective-permute-start(bf16[32,768]{1,0:T(8,128)(2,1)S(1)} %constant_dynamic-slice_fusion.own_ref), channel_id=1, source_target_pairs={{0,24},{8,16},{16,8},{24,0},{1,25},{9,17},{17,9},{25,1},{2,26},{10... | collective-permute-start | bytes 147464 | tf_op jit(solution)/shard_map/ppermute | solution.py:485
  6.5 5.4 %collective-permute-done.1 = bf16[32,768]{1,0:T(8,128)(2,1)S(1)} collective-permute-done((bf16[32,768]{1,0:T(8,128)(2,1)S(1)}, bf16[32,768]{1,0:T(8,128)(2,1)S(1)}, u32[]{:S(2)}, u32[]{:S(2)}) %collective-permute-start.1) | collective-permute-done | bytes 49184 | tf_op jit(solution)/shard_map/ppermute | solution.py:485
  11.9 2.5 %collective-permute-start.5 = (bf16[96,768]{1,0:T(8,128)(2,1)S(1)}, bf16[96,768]{1,0:T(8,128)(2,1)S(1)}, u32[]{:S(2)}, u32[]{:S(2)}) collective-permute-start(bf16[96,768]{1,0:T(8,128)(2,1)S(1)} %constant_dynamic-update-slice_fusion.refs_0_), channel_id=1, source_target_pairs={{0,6},{2,4},{4,2},{6,0},{1,7},{3,5},{5,3},{7,1},{8,14},{10,12},{12... | collective-permute-start | bytes 442376 | tf_op jit(solution)/shard_map/ppermute | solution.py:485
  14.4 0.5 collective-permute-start.4
  14.9 0.5 collective-permute-start.3
  15.5 1.4 %copy-done = bf16[1024,768]{1,0:T(8,128)(2,1)S(1)} copy-done((bf16[1024,768]{1,0:T(8,128)(2,1)S(1)}, bf16[1024,768]{1,0:T(8,128)(2,1)}, u32[]{:S(2)}) %copy-start) | copy-done | bytes 1572888
  16.9 1.0 copy-done.2
  17.9 4.6 %own_cross.1 = (bf16[256,1024]{1,0:T(8,128)(2,1)S(1)}, f32[16,1024]{1,0:T(8,128)S(1)}) custom-call(bf16[256,768]{1,0:T(8,128)(2,1)S(1)} %copy-done.2, bf16[1024,768]{1,0:T(8,128)(2,1)S(1)} %copy-done), custom_call_target="tpu_custom_call" | custom-call | tf_op jit(solution)/shard_map/own_cross/pallas_call | solution.py:100
  22.6 0.5 collective-permute-start.7
  23.2 0.4 collective-permute-start.9
  24.2 0.4 collective-permute-done.8.refs_6_
  24.9 17.1 %gram.1 = (f32[2304,128]{1,0:T(8,128)S(1)}, f32[2304,128]{1,0:T(8,128)S(1)}) custom-call(s32[3]{0:T(128)S(1)} %pad_add_fusion.at_ref, bf16[1024,768]{1,0:T(8,128)(2,1)S(1)} %copy-done.1, bf16[256,768]{1,0:T(8,128)(2,1)S(1)} %copy-done.3, bf16[32,768]{1,0:T(8,128)(2,1)S(1)} %constant_dynamic-slice_fusion.own_ref, f32[16,1024]{1,0:T(8,128)S(1)} %get-tuple-element.35.u_ref, ...), custom_call_target="tpu_custom_call" | custom-call | tf_op jit(solution)/shard_map/gram/pallas_call | solution.py:211
  42.0 0.4 collective-permute-start.10
  42.4 2.5 %collective-permute-done.10.refs_1_ = f32[2304,128]{1,0:T(8,128)S(1)} collective-permute-done((f32[2304,128]{1,0:T(8,128)S(1)}, f32[2304,128]{1,0:T(8,128)S(1)}, u32[]{:S(2)}, u32[]{:S(2)}) %collective-permute-start.10) | collective-permute-done | bytes 1179680 | tf_op jit(solution)/shard_map/ppermute | solution.py:485
  44.9 0.7 add_cut.3
  45.6 1.6 %collective-permute-start.11 = (f32[576,128]{1,0:T(8,128)S(1)}, f32[576,128]{1,0:T(8,128)S(1)}, u32[]{:S(2)}, u32[]{:S(2)}) collective-permute-start(f32[576,128]{1,0:T(8,128)S(1)} %get-tuple-element.44), channel_id=1, source_target_pairs={{0,2},{2,0},{4,6},{6,4},{1,3},{3,1},{5,7},{7,5},{8,10},{10,8},{12,... | collective-permute-start | bytes 884744 | tf_op jit(solution)/shard_map/ppermute | solution.py:485
  47.1 1.5 %collective-permute-start.12 = (f32[576,128]{1,0:T(8,128)S(1)}, f32[576,128]{1,0:T(8,128)S(1)}, u32[]{:S(2)}, u32[]{:S(2)}) collective-permute-start(f32[576,128]{1,0:T(8,128)S(1)} %get-tuple-element.45), channel_id=1, source_target_pairs={{0,4},{2,6},{4,0},{6,2},{1,5},{3,7},{5,1},{7,3},{8,12},{10,14},{12... | collective-permute-start | bytes 884744 | tf_op jit(solution)/shard_map/ppermute | solution.py:485
  48.7 0.5 collective-permute-start.13
  49.1 6.3 %collective-permute-done.11.refs_1_ = f32[576,128]{1,0:T(8,128)S(1)} collective-permute-done((f32[576,128]{1,0:T(8,128)S(1)}, f32[576,128]{1,0:T(8,128)S(1)}, u32[]{:S(2)}, u32[]{:S(2)}) %collective-permute-start.11) | collective-permute-done | bytes 294944 | tf_op jit(solution)/shard_map/ppermute | solution.py:485
  55.5 6.9 %collective-permute-done.12.refs_2_ = f32[576,128]{1,0:T(8,128)S(1)} collective-permute-done((f32[576,128]{1,0:T(8,128)S(1)}, f32[576,128]{1,0:T(8,128)S(1)}, u32[]{:S(2)}, u32[]{:S(2)}) %collective-permute-start.12) | collective-permute-done | bytes 294944 | tf_op jit(solution)/shard_map/ppermute | solution.py:485
  62.4 0.6 add_cut.4
  63.3 2.4 %collective-permute-start.15 = (f32[144,128]{1,0:T(8,128)S(1)}, f32[144,128]{1,0:T(8,128)S(1)}, u32[]{:S(2)}, u32[]{:S(2)}) collective-permute-start(f32[144,128]{1,0:T(8,128)S(1)} %get-tuple-element.49), channel_id=1, source_target_pairs={{0,16},{8,24},{16,0},{24,8},{1,17},{9,25},{17,1},{25,9},{2,18},{10... | collective-permute-start | bytes 221192 | tf_op jit(solution)/shard_map/ppermute | solution.py:485
  65.7 1.7 %collective-permute-start.16 = (f32[144,128]{1,0:T(8,128)S(1)}, f32[144,128]{1,0:T(8,128)S(1)}, u32[]{:S(2)}, u32[]{:S(2)}) collective-permute-start(f32[144,128]{1,0:T(8,128)S(1)} %get-tuple-element.50), channel_id=1, source_target_pairs={{0,24},{8,16},{16,8},{24,0},{1,25},{9,17},{17,9},{25,1},{2,26},{10... | collective-permute-start | bytes 221192 | tf_op jit(solution)/shard_map/ppermute | solution.py:485
  67.5 3.3 %collective-permute-done.15.refs_2_ = f32[144,128]{1,0:T(8,128)S(1)} collective-permute-done((f32[144,128]{1,0:T(8,128)S(1)}, f32[144,128]{1,0:T(8,128)S(1)}, u32[]{:S(2)}, u32[]{:S(2)}) %collective-permute-start.15) | collective-permute-done | bytes 73760 | tf_op jit(solution)/shard_map/ppermute | solution.py:485
  70.8 1.2 collective-permute-done.16.refs_3_
  72.0 0.6 add_cut.5.refs_0_
  72.6 1.8 %collective-permute-start.19 = (f32[144,128]{1,0:T(8,128)S(1)}, f32[144,128]{1,0:T(8,128)S(1)}, u32[]{:S(2)}, u32[]{:S(2)}) collective-permute-start(f32[144,128]{1,0:T(8,128)S(1)} %add_cut.5.refs_0_), channel_id=1, source_target_pairs={{0,24},{8,16},{16,8},{24,0},{1,25},{9,17},{17,9},{25,1},{2,26},{10... | collective-permute-start | bytes 221192 | tf_op jit(solution)/shard_map/ppermute | solution.py:485
  74.3 1.0 collective-permute-start.18
  75.4 1.7 %collective-permute-start.17 = (f32[144,128]{1,0:T(8,128)S(1)}, f32[144,128]{1,0:T(8,128)S(1)}, u32[]{:S(2)}, u32[]{:S(2)}) collective-permute-start(f32[144,128]{1,0:T(8,128)S(1)} %add_cut.5.refs_0_), channel_id=1, source_target_pairs={{0,8},{8,0},{16,24},{24,16},{1,9},{9,1},{17,25},{25,17},{2,10},{10... | collective-permute-start | bytes 221192 | tf_op jit(solution)/shard_map/ppermute | solution.py:485
  77.0 1.9 %collective-permute-done.19.refs_3_ = f32[144,128]{1,0:T(8,128)S(1)} collective-permute-done((f32[144,128]{1,0:T(8,128)S(1)}, f32[144,128]{1,0:T(8,128)S(1)}, u32[]{:S(2)}, u32[]{:S(2)}) %collective-permute-start.19) | collective-permute-done | bytes 73760 | tf_op jit(solution)/shard_map/ppermute | solution.py:485
  78.9 1.9 %collective-permute-done.18.refs_2_ = f32[144,128]{1,0:T(8,128)S(1)} collective-permute-done((f32[144,128]{1,0:T(8,128)S(1)}, f32[144,128]{1,0:T(8,128)S(1)}, u32[]{:S(2)}, u32[]{:S(2)}) %collective-permute-start.18) | collective-permute-done | bytes 73760 | tf_op jit(solution)/shard_map/ppermute | solution.py:485
  80.8 0.6 place.1
  81.4 1.3 collective-permute-start.25
  82.8 1.7 %collective-permute-start.24 = (f32[160,128]{1,0:T(8,128)S(1)}, f32[160,128]{1,0:T(8,128)S(1)}, u32[]{:S(2)}, u32[]{:S(2)}) collective-permute-start(f32[160,128]{1,0:T(8,128)S(1)} %get-tuple-element.52.refs_0_), channel_id=1, source_target_pairs={{0,4},{2,6},{4,0},{6,2},{1,5},{3,7},{5,1},{7,3},{8,12},{10,14},{12... | collective-permute-start | bytes 245768 | tf_op jit(solution)/shard_map/ppermute | solution.py:485
  84.5 1.2 collective-permute-start.22
  85.6 0.8 collective-permute-start.21
  86.5 1.5 %collective-permute-start.20 = (f32[416,128]{1,0:T(8,128)S(1)}, f32[416,128]{1,0:T(8,128)S(1)}, u32[]{:S(2)}, u32[]{:S(2)}) collective-permute-start(f32[416,128]{1,0:T(8,128)S(1)} %get-tuple-element.57.refs_0_), channel_id=1, source_target_pairs={{0,2},{2,0},{4,6},{6,4},{1,3},{3,1},{5,7},{7,5},{8,10},{10,8},{12,... | collective-permute-start | bytes 638984 | tf_op jit(solution)/shard_map/ppermute | solution.py:485
  88.0 1.2 collective-permute-start.23
  89.1 4.5 %collective-permute-done.24.refs_2_ = f32[160,128]{1,0:T(8,128)S(1)} collective-permute-done((f32[160,128]{1,0:T(8,128)S(1)}, f32[160,128]{1,0:T(8,128)S(1)}, u32[]{:S(2)}, u32[]{:S(2)}) %collective-permute-start.24) | collective-permute-done | bytes 81952 | tf_op jit(solution)/shard_map/ppermute | solution.py:485
  93.6 4.3 %collective-permute-done.23.refs_1_ = f32[160,128]{1,0:T(8,128)S(1)} collective-permute-done((f32[160,128]{1,0:T(8,128)S(1)}, f32[160,128]{1,0:T(8,128)S(1)}, u32[]{:S(2)}, u32[]{:S(2)}) %collective-permute-start.23) | collective-permute-done | bytes 81952 | tf_op jit(solution)/shard_map/ppermute | solution.py:485
  97.9 0.5 collective-permute-start.27
  98.4 0.8 collective-permute-done.28.refs_6_
  99.3 14.1 %chol_first.1 = (f32[512,512]{1,0:T(8,128)S(1)}, f32[512,128]{1,0:T(8,128)S(1)}) custom-call(s32[3]{0:T(128)S(1)} %pad_add_fusion.at_ref, f32[160,128]{1,0:T(8,128)S(1)} %get-tuple-element.52.refs_0_, f32[160,128]{1,0:T(8,128)S(1)} %collective-permute-done.23.refs_1_, f32[160,128]{1,0:T(8,128)S(1)} %collective-permute-done.24.refs_2_, ...), custom_call_target="tpu_custom_call" | custom-call | tf_op jit(solution)/shard_map/chol_first/pallas_call | solution.py:416
  113.4 0.4 collective-permute-start.30
  114.5 0.4 collective-permute-done.30.refs_4_
  115.9 19.5 %chol_last.1 = f32[1024,1024]{1,0:T(8,128)} custom-call(s32[3]{0:T(128)S(1)} %pad_add_fusion.at_ref, f32[512,512]{1,0:T(8,128)S(1)} %get-tuple-element.55.f_ref, f32[512,128]{1,0:T(8,128)S(1)} %get-tuple-element.56.w_ref, f32[416,128]{1,0:T(8,128)S(1)} %get-tuple-element.57.refs_0_, f32[416,128]{1,0:T(8,128)S(1)} %collective-permute-done.20.refs_1_, ...), custom_call_target="tpu_custom_call" | custom-call | tf_op jit(solution)/shard_map/chol_last/pallas_call | solution.py:467
  (41 shorter events, 3.3 us)
Async XLA Ops:
  0.0 24.9 %copy-start.3 = (bf16[256,768]{1,0:T(8,128)(2,1)S(1)}, bf16[256,768]{1,0:T(8,128)(2,1)}, u32[]{:S(2)}) copy-start(bf16[256,768]{1,0:T(8,128)(2,1)} %mine_ref.1) | copy-start | bytes 1179652
  0.9 5.6 %collective-permute-start = (bf16[32,768]{1,0:T(8,128)(2,1)S(1)}, bf16[32,768]{1,0:T(8,128)(2,1)S(1)}, u32[]{:S(2)}, u32[]{:S(2)}) collective-permute-start(bf16[32,768]{1,0:T(8,128)(2,1)S(1)} %constant_dynamic-slice_fusion.own_ref), channel_id=1, source_target_pairs={{0,8},{8,0},{16,24},{24,16},{1,9},{9,1},{17,25},{25,17},{2,10},{10... | collective-permute-start | bytes 147464 | tf_op jit(solution)/shard_map/ppermute | solution.py:485
  3.9 8.0 %collective-permute-start.2 = (bf16[32,768]{1,0:T(8,128)(2,1)S(1)}, bf16[32,768]{1,0:T(8,128)(2,1)S(1)}, u32[]{:S(2)}, u32[]{:S(2)}) collective-permute-start(bf16[32,768]{1,0:T(8,128)(2,1)S(1)} %constant_dynamic-slice_fusion.own_ref), channel_id=1, source_target_pairs={{0,24},{8,16},{16,8},{24,0},{1,25},{9,17},{17,9},{25,1},{2,26},{10... | collective-permute-start | bytes 147464 | tf_op jit(solution)/shard_map/ppermute | solution.py:485
  6.4 5.5 %collective-permute-start.1 = (bf16[32,768]{1,0:T(8,128)(2,1)S(1)}, bf16[32,768]{1,0:T(8,128)(2,1)S(1)}, u32[]{:S(2)}, u32[]{:S(2)}) collective-permute-start(bf16[32,768]{1,0:T(8,128)(2,1)S(1)} %constant_dynamic-slice_fusion.own_ref), channel_id=1, source_target_pairs={{0,16},{8,24},{16,0},{24,8},{1,17},{9,25},{17,1},{25,9},{2,18},{10... | collective-permute-start | bytes 147464 | tf_op jit(solution)/shard_map/ppermute | solution.py:485
  11.9 10.6 %collective-permute-start.5 = (bf16[96,768]{1,0:T(8,128)(2,1)S(1)}, bf16[96,768]{1,0:T(8,128)(2,1)S(1)}, u32[]{:S(2)}, u32[]{:S(2)}) collective-permute-start(bf16[96,768]{1,0:T(8,128)(2,1)S(1)} %constant_dynamic-update-slice_fusion.refs_0_), channel_id=1, source_target_pairs={{0,6},{2,4},{4,2},{6,0},{1,7},{3,5},{5,3},{7,1},{8,14},{10,12},{12... | collective-permute-start | bytes 442376 | tf_op jit(solution)/shard_map/ppermute | solution.py:485
  14.4 8.1 %collective-permute-start.4 = (bf16[96,768]{1,0:T(8,128)(2,1)S(1)}, bf16[96,768]{1,0:T(8,128)(2,1)S(1)}, u32[]{:S(2)}, u32[]{:S(2)}) collective-permute-start(bf16[96,768]{1,0:T(8,128)(2,1)S(1)} %constant_dynamic-update-slice_fusion.refs_0_), channel_id=1, source_target_pairs={{0,4},{2,6},{4,0},{6,2},{1,5},{3,7},{5,1},{7,3},{8,12},{10,14},{12... | collective-permute-start | bytes 442376 | tf_op jit(solution)/shard_map/ppermute | solution.py:485
  14.9 7.6 %collective-permute-start.3 = (bf16[96,768]{1,0:T(8,128)(2,1)S(1)}, bf16[96,768]{1,0:T(8,128)(2,1)S(1)}, u32[]{:S(2)}, u32[]{:S(2)}) collective-permute-start(bf16[96,768]{1,0:T(8,128)(2,1)S(1)} %constant_dynamic-update-slice_fusion.refs_0_), channel_id=1, source_target_pairs={{0,2},{2,0},{4,6},{6,4},{1,3},{3,1},{5,7},{7,5},{8,10},{10,8},{12,... | collective-permute-start | bytes 442376 | tf_op jit(solution)/shard_map/ppermute | solution.py:485
  15.5 1.4 %copy-start = (bf16[1024,768]{1,0:T(8,128)(2,1)S(1)}, bf16[1024,768]{1,0:T(8,128)(2,1)}, u32[]{:S(2)}) copy-start(bf16[1024,768]{1,0:T(8,128)(2,1)} %emb_ref.3) | copy-start | bytes 4718596
  16.9 1.0 copy-start.2
  17.9 7.0 %copy-start.1 = (bf16[1024,768]{1,0:T(8,128)(2,1)S(1)}, bf16[1024,768]{1,0:T(8,128)(2,1)}, u32[]{:S(2)}) copy-start(bf16[1024,768]{1,0:T(8,128)(2,1)} %emb_ref.3) | copy-start | bytes 4718596
  22.6 1.4 %collective-permute-start.6 = (bf16[96,768]{1,0:T(8,128)(2,1)S(1)}, bf16[96,768]{1,0:T(8,128)(2,1)S(1)}, u32[]{:S(2)}, u32[]{:S(2)}) collective-permute-start(bf16[96,768]{1,0:T(8,128)(2,1)S(1)} %constant_dynamic-update-slice_fusion.refs_0_), channel_id=1, source_target_pairs={{0,1},{1,0},{2,3},{3,2},{4,5},{5,4},{6,7},{7,6},{8,9},{9,8},{10,11... | collective-permute-start | bytes 442376 | tf_op jit(solution)/shard_map/ppermute | solution.py:485
  22.6 1.6 %collective-permute-start.7 = (bf16[96,768]{1,0:T(8,128)(2,1)S(1)}, bf16[96,768]{1,0:T(8,128)(2,1)S(1)}, u32[]{:S(2)}, u32[]{:S(2)}) collective-permute-start(bf16[96,768]{1,0:T(8,128)(2,1)S(1)} %collective-permute-done.3.refs_1_), channel_id=1, source_target_pairs={{0,1},{1,0},{2,3},{3,2},{4,5},{5,4},{6,7},{7,6},{8,9},{9,8},{10,11... | collective-permute-start | bytes 442376 | tf_op jit(solution)/shard_map/ppermute | solution.py:485
  23.1 1.5 %collective-permute-start.8 = (bf16[96,768]{1,0:T(8,128)(2,1)S(1)}, bf16[96,768]{1,0:T(8,128)(2,1)}, u32[]{:S(2)}, u32[]{:S(2)}) collective-permute-start(bf16[96,768]{1,0:T(8,128)(2,1)S(1)} %collective-permute-done.4.refs_2_), channel_id=1, source_target_pairs={{0,1},{1,0},{2,3},{3,2},{4,5},{5,4},{6,7},{7,6},{8,9},{9,8},{10,11... | collective-permute-start | bytes 442376 | tf_op jit(solution)/shard_map/ppermute | solution.py:485
  23.2 1.6 %collective-permute-start.9 = (bf16[96,768]{1,0:T(8,128)(2,1)S(1)}, bf16[96,768]{1,0:T(8,128)(2,1)}, u32[]{:S(2)}, u32[]{:S(2)}) collective-permute-start(bf16[96,768]{1,0:T(8,128)(2,1)S(1)} %collective-permute-done.5.refs_3_), channel_id=1, source_target_pairs={{0,1},{1,0},{2,3},{3,2},{4,5},{5,4},{6,7},{7,6},{8,9},{9,8},{10,11... | collective-permute-start | bytes 442376 | tf_op jit(solution)/shard_map/ppermute | solution.py:485
  42.0 2.9 %collective-permute-start.10 = (f32[2304,128]{1,0:T(8,128)S(1)}, f32[2304,128]{1,0:T(8,128)S(1)}, u32[]{:S(2)}, u32[]{:S(2)}) collective-permute-start(f32[2304,128]{1,0:T(8,128)S(1)} %get-tuple-element.42), channel_id=1, source_target_pairs={{0,1},{1,0},{2,3},{3,2},{4,5},{5,4},{6,7},{7,6},{8,9},{9,8},{10,11... | collective-permute-start | bytes 3538952 | tf_op jit(solution)/shard_map/ppermute | solution.py:485
  45.6 9.9 %collective-permute-start.11 = (f32[576,128]{1,0:T(8,128)S(1)}, f32[576,128]{1,0:T(8,128)S(1)}, u32[]{:S(2)}, u32[]{:S(2)}) collective-permute-start(f32[576,128]{1,0:T(8,128)S(1)} %get-tuple-element.44), channel_id=1, source_target_pairs={{0,2},{2,0},{4,6},{6,4},{1,3},{3,1},{5,7},{7,5},{8,10},{10,8},{12,... | collective-permute-start | bytes 884744 | tf_op jit(solution)/shard_map/ppermute | solution.py:485
  47.1 15.3 %collective-permute-start.12 = (f32[576,128]{1,0:T(8,128)S(1)}, f32[576,128]{1,0:T(8,128)S(1)}, u32[]{:S(2)}, u32[]{:S(2)}) collective-permute-start(f32[576,128]{1,0:T(8,128)S(1)} %get-tuple-element.45), channel_id=1, source_target_pairs={{0,4},{2,6},{4,0},{6,2},{1,5},{3,7},{5,1},{7,3},{8,12},{10,14},{12... | collective-permute-start | bytes 884744 | tf_op jit(solution)/shard_map/ppermute | solution.py:485
  48.7 13.7 %collective-permute-start.13 = (f32[576,128]{1,0:T(8,128)S(1)}, f32[576,128]{1,0:T(8,128)S(1)}, u32[]{:S(2)}, u32[]{:S(2)}) collective-permute-start(f32[576,128]{1,0:T(8,128)S(1)} %get-tuple-element.46), channel_id=1, source_target_pairs={{0,6},{2,4},{4,2},{6,0},{1,7},{3,5},{5,3},{7,1},{8,14},{10,12},{12... | collective-permute-start | bytes 884744 | tf_op jit(solution)/shard_map/ppermute | solution.py:485
  63.0 4.5 %collective-permute-start.14 = (f32[144,128]{1,0:T(8,128)S(1)}, f32[144,128]{1,0:T(8,128)S(1)}, u32[]{:S(2)}, u32[]{:S(2)}) collective-permute-start(f32[144,128]{1,0:T(8,128)S(1)} %get-tuple-element.48), channel_id=1, source_target_pairs={{0,8},{8,0},{16,24},{24,16},{1,9},{9,1},{17,25},{25,17},{2,10},{10... | collective-permute-start | bytes 221192 | tf_op jit(solution)/shard_map/ppermute | solution.py:485
  63.3 7.5 %collective-permute-start.15 = (f32[144,128]{1,0:T(8,128)S(1)}, f32[144,128]{1,0:T(8,128)S(1)}, u32[]{:S(2)}, u32[]{:S(2)}) collective-permute-start(f32[144,128]{1,0:T(8,128)S(1)} %get-tuple-element.49), channel_id=1, source_target_pairs={{0,16},{8,24},{16,0},{24,8},{1,17},{9,25},{17,1},{25,9},{2,18},{10... | collective-permute-start | bytes 221192 | tf_op jit(solution)/shard_map/ppermute | solution.py:485
  65.7 6.3 %collective-permute-start.16 = (f32[144,128]{1,0:T(8,128)S(1)}, f32[144,128]{1,0:T(8,128)S(1)}, u32[]{:S(2)}, u32[]{:S(2)}) collective-permute-start(f32[144,128]{1,0:T(8,128)S(1)} %get-tuple-element.50), channel_id=1, source_target_pairs={{0,24},{8,16},{16,8},{24,0},{1,25},{9,17},{17,9},{25,1},{2,26},{10... | collective-permute-start | bytes 221192 | tf_op jit(solution)/shard_map/ppermute | solution.py:485
  72.6 6.3 %collective-permute-start.19 = (f32[144,128]{1,0:T(8,128)S(1)}, f32[144,128]{1,0:T(8,128)S(1)}, u32[]{:S(2)}, u32[]{:S(2)}) collective-permute-start(f32[144,128]{1,0:T(8,128)S(1)} %add_cut.5.refs_0_), channel_id=1, source_target_pairs={{0,24},{8,16},{16,8},{24,0},{1,25},{9,17},{17,9},{25,1},{2,26},{10... | collective-permute-start | bytes 221192 | tf_op jit(solution)/shard_map/ppermute | solution.py:485
  74.3 6.4 %collective-permute-start.18 = (f32[144,128]{1,0:T(8,128)S(1)}, f32[144,128]{1,0:T(8,128)S(1)}, u32[]{:S(2)}, u32[]{:S(2)}) collective-permute-start(f32[144,128]{1,0:T(8,128)S(1)} %add_cut.5.refs_0_), channel_id=1, source_target_pairs={{0,16},{8,24},{16,0},{24,8},{1,17},{9,25},{17,1},{25,9},{2,18},{10... | collective-permute-start | bytes 221192 | tf_op jit(solution)/shard_map/ppermute | solution.py:485
  75.4 5.4 %collective-permute-start.17 = (f32[144,128]{1,0:T(8,128)S(1)}, f32[144,128]{1,0:T(8,128)S(1)}, u32[]{:S(2)}, u32[]{:S(2)}) collective-permute-start(f32[144,128]{1,0:T(8,128)S(1)} %add_cut.5.refs_0_), channel_id=1, source_target_pairs={{0,8},{8,0},{16,24},{24,16},{1,9},{9,1},{17,25},{25,17},{2,10},{10... | collective-permute-start | bytes 221192 | tf_op jit(solution)/shard_map/ppermute | solution.py:485
  81.4 5.1 %collective-permute-start.26 = (f32[160,128]{1,0:T(8,128)S(1)}, f32[160,128]{1,0:T(8,128)S(1)}, u32[]{:S(2)}, u32[]{:S(2)}) collective-permute-start(f32[160,128]{1,0:T(8,128)S(1)} %get-tuple-element.52.refs_0_), channel_id=1, source_target_pairs={{0,1},{1,0},{2,3},{3,2},{4,5},{5,4},{6,7},{7,6},{8,9},{9,8},{10,11... | collective-permute-start | bytes 245768 | tf_op jit(solution)/shard_map/ppermute | solution.py:485
  81.4 6.5 %collective-permute-start.25 = (f32[160,128]{1,0:T(8,128)S(1)}, f32[160,128]{1,0:T(8,128)S(1)}, u32[]{:S(2)}, u32[]{:S(2)}) collective-permute-start(f32[160,128]{1,0:T(8,128)S(1)} %get-tuple-element.52.refs_0_), channel_id=1, source_target_pairs={{0,6},{2,4},{4,2},{6,0},{1,7},{3,5},{5,3},{7,1},{8,14},{10,12},{12... | collective-permute-start | bytes 245768 | tf_op jit(solution)/shard_map/ppermute | solution.py:485
  82.8 10.8 %collective-permute-start.24 = (f32[160,128]{1,0:T(8,128)S(1)}, f32[160,128]{1,0:T(8,128)S(1)}, u32[]{:S(2)}, u32[]{:S(2)}) collective-permute-start(f32[160,128]{1,0:T(8,128)S(1)} %get-tuple-element.52.refs_0_), channel_id=1, source_target_pairs={{0,4},{2,6},{4,0},{6,2},{1,5},{3,7},{5,1},{7,3},{8,12},{10,14},{12... | collective-permute-start | bytes 245768 | tf_op jit(solution)/shard_map/ppermute | solution.py:485
  84.5 29.0 %collective-permute-start.22 = (f32[416,128]{1,0:T(8,128)S(1)}, f32[416,128]{1,0:T(8,128)S(1)}, u32[]{:S(2)}, u32[]{:S(2)}) collective-permute-start(f32[416,128]{1,0:T(8,128)S(1)} %get-tuple-element.57.refs_0_), channel_id=1, source_target_pairs={{0,6},{2,4},{4,2},{6,0},{1,7},{3,5},{5,3},{7,1},{8,14},{10,12},{12... | collective-permute-start | bytes 638984 | tf_op jit(solution)/shard_map/ppermute | solution.py:485
  85.6 27.8 %collective-permute-start.21 = (f32[416,128]{1,0:T(8,128)S(1)}, f32[416,128]{1,0:T(8,128)S(1)}, u32[]{:S(2)}, u32[]{:S(2)}) collective-permute-start(f32[416,128]{1,0:T(8,128)S(1)} %get-tuple-element.57.refs_0_), channel_id=1, source_target_pairs={{0,4},{2,6},{4,0},{6,2},{1,5},{3,7},{5,1},{7,3},{8,12},{10,14},{12... | collective-permute-start | bytes 638984 | tf_op jit(solution)/shard_map/ppermute | solution.py:485
  86.5 27.0 %collective-permute-start.20 = (f32[416,128]{1,0:T(8,128)S(1)}, f32[416,128]{1,0:T(8,128)S(1)}, u32[]{:S(2)}, u32[]{:S(2)}) collective-permute-start(f32[416,128]{1,0:T(8,128)S(1)} %get-tuple-element.57.refs_0_), channel_id=1, source_target_pairs={{0,2},{2,0},{4,6},{6,4},{1,3},{3,1},{5,7},{7,5},{8,10},{10,8},{12,... | collective-permute-start | bytes 638984 | tf_op jit(solution)/shard_map/ppermute | solution.py:485
  88.0 9.9 %collective-permute-start.23 = (f32[160,128]{1,0:T(8,128)S(1)}, f32[160,128]{1,0:T(8,128)S(1)}, u32[]{:S(2)}, u32[]{:S(2)}) collective-permute-start(f32[160,128]{1,0:T(8,128)S(1)} %get-tuple-element.52.refs_0_), channel_id=1, source_target_pairs={{0,2},{2,0},{4,6},{6,4},{1,3},{3,1},{5,7},{7,5},{8,10},{10,8},{12,... | collective-permute-start | bytes 245768 | tf_op jit(solution)/shard_map/ppermute | solution.py:485
  93.6 4.3 %collective-permute-start.29 = (f32[160,128]{1,0:T(8,128)S(1)}, f32[160,128]{1,0:T(8,128)S(1)}, u32[]{:S(2)}, u32[]{:S(2)}) collective-permute-start(f32[160,128]{1,0:T(8,128)S(1)} %collective-permute-done.25.refs_3_), channel_id=1, source_target_pairs={{0,1},{1,0},{2,3},{3,2},{4,5},{5,4},{6,7},{7,6},{8,9},{9,8},{10,11... | collective-permute-start | bytes 245768 | tf_op jit(solution)/shard_map/ppermute | solution.py:485
  97.9 1.3 collective-permute-start.28
  97.9 1.4 %collective-permute-start.27 = (f32[160,128]{1,0:T(8,128)S(1)}, f32[160,128]{1,0:T(8,128)S(1)}, u32[]{:S(2)}, u32[]{:S(2)}) collective-permute-start(f32[160,128]{1,0:T(8,128)S(1)} %collective-permute-done.23.refs_1_), channel_id=1, source_target_pairs={{0,1},{1,0},{2,3},{3,2},{4,5},{5,4},{6,7},{7,6},{8,9},{9,8},{10,11... | collective-permute-start | bytes 245768 | tf_op jit(solution)/shard_map/ppermute | solution.py:485
  113.4 1.5 %collective-permute-start.30 = (f32[416,128]{1,0:T(8,128)S(1)}, f32[416,128]{1,0:T(8,128)S(1)}, u32[]{:S(2)}, u32[]{:S(2)}) collective-permute-start(f32[416,128]{1,0:T(8,128)S(1)} %get-tuple-element.57.refs_0_), channel_id=1, source_target_pairs={{0,1},{1,0},{2,3},{3,2},{4,5},{5,4},{6,7},{7,6},{8,9},{9,8},{10,11... | collective-permute-start | bytes 638984 | tf_op jit(solution)/shard_map/ppermute | solution.py:485
  113.9 1.5 %collective-permute-start.31 = (f32[416,128]{1,0:T(8,128)S(1)}, f32[416,128]{1,0:T(8,128)S(1)}, u32[]{:S(2)}, u32[]{:S(2)}) collective-permute-start(f32[416,128]{1,0:T(8,128)S(1)} %collective-permute-done.20.refs_1_), channel_id=1, source_target_pairs={{0,1},{1,0},{2,3},{3,2},{4,5},{5,4},{6,7},{7,6},{8,9},{9,8},{10,11... | collective-permute-start | bytes 638984 | tf_op jit(solution)/shard_map/ppermute | solution.py:485
  114.0 1.6 %collective-permute-start.32 = (f32[416,128]{1,0:T(8,128)S(1)}, f32[416,128]{1,0:T(8,128)S(1)}, u32[]{:S(2)}, u32[]{:S(2)}) collective-permute-start(f32[416,128]{1,0:T(8,128)S(1)} %collective-permute-done.21.refs_2_), channel_id=1, source_target_pairs={{0,1},{1,0},{2,3},{3,2},{4,5},{5,4},{6,7},{7,6},{8,9},{9,8},{10,11... | collective-permute-start | bytes 638984 | tf_op jit(solution)/shard_map/ppermute | solution.py:485
  114.4 1.6 %collective-permute-start.33 = (f32[416,128]{1,0:T(8,128)S(1)}, f32[416,128]{1,0:T(8,128)S(1)}, u32[]{:S(2)}, u32[]{:S(2)}) collective-permute-start(f32[416,128]{1,0:T(8,128)S(1)} %collective-permute-done.22.refs_3_), channel_id=1, source_target_pairs={{0,1},{1,0},{2,3},{3,2},{4,5},{5,4},{6,7},{7,6},{8,9},{9,8},{10,11... | collective-permute-start | bytes 638984 | tf_op jit(solution)/shard_map/ppermute | solution.py:485

commit v6 on v5

--- a/solution.py
+++ b/solution.py
@@ -231,12 +231,13 @@
     base = 0
     for rows in parts:
         h = rows // ways
-        for s in range(ways):
+        for q in range(ways):
+            s = -q % ways
             at = pl.ds(pl.multiple_of(base + (at_ref[axis] ^ s) * h, 8), h) if ways > 1 else slice(base, base + h)
             total = ins[0][at, :]
             for r in ins[1:]:
                 total = total + r[at, :]
-            outs[s][base // ways : base // ways + h, :] = total
+            outs[q][base // ways : base // ways + h, :] = total
         base += rows
 
 
@@ -486,8 +487,7 @@
 
 
 def scatter(pieces, axis):
-    arrived = [swap(p, axis, s) for s, p in reversed(list(enumerate(pieces))) if s]
-    return [pieces[0]] + arrived[::-1]
+    return [pieces[0]] + [swap(p, axis, -q % len(pieces)) for q, p in enumerate(pieces) if q]
 
 
 def spread_out(x, axis):
@@ -526,7 +526,7 @@
     (whole,) = add_cut(at, 0, 1, rows, parts)
     first, last = place(at, 0, rows, spread_out(whole, "land"))
     first = spread_out(first, "chip")
-    first = first + [swap(p, "core", 1) for p in first]
+    first, last = lax.optimization_barrier((first + [swap(p, "core", 1) for p in first], last))
     f, w = first_factor(at, plan, na, first)
     last, f, w = lax.optimization_barrier((spread_out(last, "chip"), f, w))
     last = last + [swap(p, "core", 1) for p in last]

time: 136 us -> 131 us (0.963)
  waiting for transfers between devices: 41.8 us -> 37.9 us
    ppermute x34, waiting for transfers between devices: 41.8 us -> 37.9 us  [swap(): lax.ppermute(x, axis, [(i, i ^ s) for i in range(lax.axis_size(axis))])]
  transfers between devices with their start and end apart: 34 -> 34, of which waited for: 20 -> 22; matrix products, arithmetic and copies ran while one was open for 0% -> 0% of each run, Pallas kernels for 14% -> 14%
where the time goes in v6:
time: 131 us
  Pallas kernels  57.8 us (44%)
  waiting for transfers between devices  37.9 us (29%)
  starting transfers between devices  31.3 us (24%)
  local copies, waits for them, and re-layouts  3.3 us (3%)
    ppermute x34, waiting for transfers between devices, swap(): lax.ppermute(x, axis, [(i, i ^ s) for i in range(lax.axis_size(axis))])  37.9 us
    ppermute x34, starting transfers between devices, swap(): lax.ppermute(x, axis, [(i, i ^ s) for i in range(lax.axis_size(axis))])  31.3 us
    pallas_call x1, Pallas kernels, last_factor(): pl.pallas_call(functools.partial(last_factor_kernel, plan), out_shape=jax...  19.5 us
    pallas_call x1, Pallas kernels, local_normal(): pl.pallas_call(functools.partial(gram_kernel, plan, na), out_shape=(half,...  17.1 us
    pallas_call x1, Pallas kernels, first_factor(): pl.pallas_call(functools.partial(first_factor_kernel, plan), out_shape=(j...  14.1 us
    pallas_call x1, Pallas kernels, own_cross(): pl.pallas_call(own_kernel, out_shape=(jax.ShapeDtypeStruct((shard, m), jn...  4.65 us
  transfers between devices with their start and end apart: 34, of which 22 were waited for; matrix products, arithmetic and copies ran while one was open for 0% of the time, Pallas kernels for 14%

profile of v6, /device:TPU:0, one launch (start us, length us, event | category | flops | bytes accessed | tf_op | source)
XLA Modules:
  0.0 130.6 jit_solution(3514484125744393948)
XLA Ops:
  0.0 0.9 constant_dynamic-slice_fusion.own_ref
  0.9 3.0 %collective-permute-start = (bf16[32,768]{1,0:T(8,128)(2,1)S(1)}, bf16[32,768]{1,0:T(8,128)(2,1)S(1)}, u32[]{:S(2)}, u32[]{:S(2)}) collective-permute-start(bf16[32,768]{1,0:T(8,128)(2,1)S(1)} %constant_dynamic-slice_fusion.own_ref), channel_id=1, source_target_pairs={{0,8},{8,0},{16,24},{24,16},{1,9},{9,1},{17,25},{25,17},{2,10},{10... | collective-permute-start | bytes 147464 | tf_op jit(solution)/shard_map/ppermute | solution.py:486
  3.9 2.5 %collective-permute-start.2 = (bf16[32,768]{1,0:T(8,128)(2,1)S(1)}, bf16[32,768]{1,0:T(8,128)(2,1)S(1)}, u32[]{:S(2)}, u32[]{:S(2)}) collective-permute-start(bf16[32,768]{1,0:T(8,128)(2,1)S(1)} %constant_dynamic-slice_fusion.own_ref), channel_id=1, source_target_pairs={{0,24},{8,16},{16,8},{24,0},{1,25},{9,17},{17,9},{25,1},{2,26},{10... | collective-permute-start | bytes 147464 | tf_op jit(solution)/shard_map/ppermute | solution.py:486
  6.5 5.4 %collective-permute-done.1 = bf16[32,768]{1,0:T(8,128)(2,1)S(1)} collective-permute-done((bf16[32,768]{1,0:T(8,128)(2,1)S(1)}, bf16[32,768]{1,0:T(8,128)(2,1)S(1)}, u32[]{:S(2)}, u32[]{:S(2)}) %collective-permute-start.1) | collective-permute-done | bytes 49184 | tf_op jit(solution)/shard_map/ppermute | solution.py:486
  11.9 2.5 %collective-permute-start.5 = (bf16[96,768]{1,0:T(8,128)(2,1)S(1)}, bf16[96,768]{1,0:T(8,128)(2,1)S(1)}, u32[]{:S(2)}, u32[]{:S(2)}) collective-permute-start(bf16[96,768]{1,0:T(8,128)(2,1)S(1)} %constant_dynamic-update-slice_fusion.refs_0_), channel_id=1, source_target_pairs={{0,6},{2,4},{4,2},{6,0},{1,7},{3,5},{5,3},{7,1},{8,14},{10,12},{12... | collective-permute-start | bytes 442376 | tf_op jit(solution)/shard_map/ppermute | solution.py:486
  14.4 0.5 collective-permute-start.4
  14.9 0.5 collective-permute-start.3
  15.5 1.4 %copy-done = bf16[1024,768]{1,0:T(8,128)(2,1)S(1)} copy-done((bf16[1024,768]{1,0:T(8,128)(2,1)S(1)}, bf16[1024,768]{1,0:T(8,128)(2,1)}, u32[]{:S(2)}) %copy-start) | copy-done | bytes 1572888
  16.9 1.0 copy-done.2
  17.9 4.6 %own_cross.1 = (bf16[256,1024]{1,0:T(8,128)(2,1)S(1)}, f32[16,1024]{1,0:T(8,128)S(1)}) custom-call(bf16[256,768]{1,0:T(8,128)(2,1)S(1)} %copy-done.2, bf16[1024,768]{1,0:T(8,128)(2,1)S(1)} %copy-done), custom_call_target="tpu_custom_call" | custom-call | tf_op jit(solution)/shard_map/own_cross/pallas_call | solution.py:100
  22.6 0.5 collective-permute-start.7
  23.2 0.4 collective-permute-start.9
  24.2 0.4 collective-permute-done.8.refs_6_
  24.9 17.1 %gram.1 = (f32[2304,128]{1,0:T(8,128)S(1)}, f32[2304,128]{1,0:T(8,128)S(1)}) custom-call(s32[3]{0:T(128)S(1)} %pad_add_fusion.at_ref, bf16[1024,768]{1,0:T(8,128)(2,1)S(1)} %copy-done.1, bf16[256,768]{1,0:T(8,128)(2,1)S(1)} %copy-done.3, bf16[32,768]{1,0:T(8,128)(2,1)S(1)} %constant_dynamic-slice_fusion.own_ref, f32[16,1024]{1,0:T(8,128)S(1)} %get-tuple-element.44.u_ref, ...), custom_call_target="tpu_custom_call" | custom-call | tf_op jit(solution)/shard_map/gram/pallas_call | solution.py:211
  42.4 2.5 %collective-permute-done.10.refs_1_ = f32[2304,128]{1,0:T(8,128)S(1)} collective-permute-done((f32[2304,128]{1,0:T(8,128)S(1)}, f32[2304,128]{1,0:T(8,128)S(1)}, u32[]{:S(2)}, u32[]{:S(2)}) %collective-permute-start.10) | collective-permute-done | bytes 1179680 | tf_op jit(solution)/shard_map/ppermute | solution.py:486
  44.9 0.7 add_cut.3
  45.6 2.5 %collective-permute-start.11 = (f32[576,128]{1,0:T(8,128)S(1)}, f32[576,128]{1,0:T(8,128)S(1)}, u32[]{:S(2)}, u32[]{:S(2)}) collective-permute-start(f32[576,128]{1,0:T(8,128)S(1)} %get-tuple-element.53), channel_id=1, source_target_pairs={{0,6},{2,4},{4,2},{6,0},{1,7},{3,5},{5,3},{7,1},{8,14},{10,12},{12... | collective-permute-start | bytes 884744 | tf_op jit(solution)/shard_map/ppermute | solution.py:486
  48.1 0.5 collective-permute-start.12
  48.6 0.5 collective-permute-start.13
  49.1 7.3 %collective-permute-done.11.refs_1_ = f32[576,128]{1,0:T(8,128)S(1)} collective-permute-done((f32[576,128]{1,0:T(8,128)S(1)}, f32[576,128]{1,0:T(8,128)S(1)}, u32[]{:S(2)}, u32[]{:S(2)}) %collective-permute-start.11) | collective-permute-done | bytes 294944 | tf_op jit(solution)/shard_map/ppermute | solution.py:486
  56.4 5.7 %collective-permute-done.12.refs_2_ = f32[576,128]{1,0:T(8,128)S(1)} collective-permute-done((f32[576,128]{1,0:T(8,128)S(1)}, f32[576,128]{1,0:T(8,128)S(1)}, u32[]{:S(2)}, u32[]{:S(2)}) %collective-permute-start.12) | collective-permute-done | bytes 294944 | tf_op jit(solution)/shard_map/ppermute | solution.py:486
  62.2 0.6 add_cut.4
  62.8 2.2 %collective-permute-start.14 = (f32[144,128]{1,0:T(8,128)S(1)}, f32[144,128]{1,0:T(8,128)S(1)}, u32[]{:S(2)}, u32[]{:S(2)}) collective-permute-start(f32[144,128]{1,0:T(8,128)S(1)} %get-tuple-element.57), channel_id=1, source_target_pairs={{0,24},{8,16},{16,8},{24,0},{1,25},{9,17},{17,9},{25,1},{2,26},{10... | collective-permute-start | bytes 221192 | tf_op jit(solution)/shard_map/ppermute | solution.py:486
  65.0 2.3 %collective-permute-start.16 = (f32[144,128]{1,0:T(8,128)S(1)}, f32[144,128]{1,0:T(8,128)S(1)}, u32[]{:S(2)}, u32[]{:S(2)}) collective-permute-start(f32[144,128]{1,0:T(8,128)S(1)} %get-tuple-element.59), channel_id=1, source_target_pairs={{0,8},{8,0},{16,24},{24,16},{1,9},{9,1},{17,25},{25,17},{2,10},{10... | collective-permute-start | bytes 221192 | tf_op jit(solution)/shard_map/ppermute | solution.py:486
  67.2 2.6 %collective-permute-done.14.refs_1_ = f32[144,128]{1,0:T(8,128)S(1)} collective-permute-done((f32[144,128]{1,0:T(8,128)S(1)}, f32[144,128]{1,0:T(8,128)S(1)}, u32[]{:S(2)}, u32[]{:S(2)}) %collective-permute-start.14) | collective-permute-done | bytes 73760 | tf_op jit(solution)/shard_map/ppermute | solution.py:486
  69.8 2.1 %collective-permute-done.15.refs_2_ = f32[144,128]{1,0:T(8,128)S(1)} collective-permute-done((f32[144,128]{1,0:T(8,128)S(1)}, f32[144,128]{1,0:T(8,128)S(1)}, u32[]{:S(2)}, u32[]{:S(2)}) %collective-permute-start.15) | collective-permute-done | bytes 73760 | tf_op jit(solution)/shard_map/ppermute | solution.py:486
  71.9 0.6 add_cut.5.refs_0_
  72.5 2.2 %collective-permute-start.19 = (f32[144,128]{1,0:T(8,128)S(1)}, f32[144,128]{1,0:T(8,128)S(1)}, u32[]{:S(2)}, u32[]{:S(2)}) collective-permute-start(f32[144,128]{1,0:T(8,128)S(1)} %add_cut.5.refs_0_), channel_id=1, source_target_pairs={{0,24},{8,16},{16,8},{24,0},{1,25},{9,17},{17,9},{25,1},{2,26},{10... | collective-permute-start | bytes 221192 | tf_op jit(solution)/shard_map/ppermute | solution.py:486
  74.7 2.3 %collective-permute-start.17 = (f32[144,128]{1,0:T(8,128)S(1)}, f32[144,128]{1,0:T(8,128)S(1)}, u32[]{:S(2)}, u32[]{:S(2)}) collective-permute-start(f32[144,128]{1,0:T(8,128)S(1)} %add_cut.5.refs_0_), channel_id=1, source_target_pairs={{0,8},{8,0},{16,24},{24,16},{1,9},{9,1},{17,25},{25,17},{2,10},{10... | collective-permute-start | bytes 221192 | tf_op jit(solution)/shard_map/ppermute | solution.py:486
  76.9 2.6 %collective-permute-done.19.refs_3_ = f32[144,128]{1,0:T(8,128)S(1)} collective-permute-done((f32[144,128]{1,0:T(8,128)S(1)}, f32[144,128]{1,0:T(8,128)S(1)}, u32[]{:S(2)}, u32[]{:S(2)}) %collective-permute-start.19) | collective-permute-done | bytes 73760 | tf_op jit(solution)/shard_map/ppermute | solution.py:486
  79.5 2.2 %collective-permute-done.18.refs_2_ = f32[144,128]{1,0:T(8,128)S(1)} collective-permute-done((f32[144,128]{1,0:T(8,128)S(1)}, f32[144,128]{1,0:T(8,128)S(1)}, u32[]{:S(2)}, u32[]{:S(2)}) %collective-permute-start.18) | collective-permute-done | bytes 73760 | tf_op jit(solution)/shard_map/ppermute | solution.py:486
  81.7 0.6 place.1
  82.3 1.4 %collective-permute-start.22 = (f32[160,128]{1,0:T(8,128)S(1)}, f32[160,128]{1,0:T(8,128)S(1)}, u32[]{:S(2)}, u32[]{:S(2)}) collective-permute-start(f32[160,128]{1,0:T(8,128)S(1)} %get-tuple-element.63.refs_0_), channel_id=1, source_target_pairs={{0,6},{2,4},{4,2},{6,0},{1,7},{3,5},{5,3},{7,1},{8,14},{10,12},{12... | collective-permute-start | bytes 245768 | tf_op jit(solution)/shard_map/ppermute | solution.py:486
  83.6 1.7 %collective-permute-start.21 = (f32[160,128]{1,0:T(8,128)S(1)}, f32[160,128]{1,0:T(8,128)S(1)}, u32[]{:S(2)}, u32[]{:S(2)}) collective-permute-start(f32[160,128]{1,0:T(8,128)S(1)} %get-tuple-element.63.refs_0_), channel_id=1, source_target_pairs={{0,4},{2,6},{4,0},{6,2},{1,5},{3,7},{5,1},{7,3},{8,12},{10,14},{12... | collective-permute-start | bytes 245768 | tf_op jit(solution)/shard_map/ppermute | solution.py:486
  85.3 0.5 collective-permute-start.20
  85.8 2.5 %collective-permute-done.22.refs_3_ = f32[160,128]{1,0:T(8,128)S(1)} collective-permute-done((f32[160,128]{1,0:T(8,128)S(1)}, f32[160,128]{1,0:T(8,128)S(1)}, u32[]{:S(2)}, u32[]{:S(2)}) %collective-permute-start.22) | collective-permute-done | bytes 81952 | tf_op jit(solution)/shard_map/ppermute | solution.py:486
  88.3 1.1 collective-permute-done.21.refs_2_
  89.4 0.4 collective-permute-done.20.refs_1_
  89.9 0.8 collective-permute-done.25.refs_6_
  90.6 0.4 collective-permute-done.24.refs_5_
  91.0 1.5 %collective-permute-start.29 = (f32[416,128]{1,0:T(8,128)S(1)}, f32[416,128]{1,0:T(8,128)S(1)}, u32[]{:S(2)}, u32[]{:S(2)}) collective-permute-start(f32[416,128]{1,0:T(8,128)S(1)} %get-tuple-element.75.refs_0_), channel_id=1, source_target_pairs={{0,6},{2,4},{4,2},{6,0},{1,7},{3,5},{5,3},{7,1},{8,14},{10,12},{12... | collective-permute-start | bytes 638984 | tf_op jit(solution)/shard_map/ppermute | solution.py:486
  92.5 1.2 collective-permute-start.28
  93.8 0.8 collective-permute-start.27
  94.5 14.1 %chol_first.1 = (f32[512,512]{1,0:T(8,128)S(1)}, f32[512,128]{1,0:T(8,128)S(1)}) custom-call(s32[3]{0:T(128)S(1)} %pad_add_fusion.at_ref, f32[160,128]{1,0:T(8,128)S(1)} %get-tuple-element.63.refs_0_, f32[160,128]{1,0:T(8,128)S(1)} %collective-permute-done.20.refs_1_, f32[160,128]{1,0:T(8,128)S(1)} %collective-permute-done.21.refs_2_, ...), custom_call_target="tpu_custom_call" | custom-call | tf_op jit(solution)/shard_map/chol_first/pallas_call | solution.py:417
  108.7 0.5 collective-permute-start.31
  109.3 0.4 collective-permute-start.33
  109.7 0.4 collective-permute-done.30.refs_4_
  111.1 19.5 %chol_last.1 = f32[1024,1024]{1,0:T(8,128)} custom-call(s32[3]{0:T(128)S(1)} %pad_add_fusion.at_ref, f32[512,512]{1,0:T(8,128)S(1)} %get-tuple-element.73.f_ref, f32[512,128]{1,0:T(8,128)S(1)} %get-tuple-element.74.w_ref, f32[416,128]{1,0:T(8,128)S(1)} %get-tuple-element.75.refs_0_, f32[416,128]{1,0:T(8,128)S(1)} %collective-permute-done.27.refs_1_, ...), custom_call_target="tpu_custom_call" | custom-call | tf_op jit(solution)/shard_map/chol_last/pallas_call | solution.py:468
  (41 shorter events, 2.8 us)
Async XLA Ops:
  0.0 24.9 %copy-start.3 = (bf16[256,768]{1,0:T(8,128)(2,1)S(1)}, bf16[256,768]{1,0:T(8,128)(2,1)}, u32[]{:S(2)}) copy-start(bf16[256,768]{1,0:T(8,128)(2,1)} %mine_ref.1) | copy-start | bytes 1179652
  0.9 5.6 %collective-permute-start = (bf16[32,768]{1,0:T(8,128)(2,1)S(1)}, bf16[32,768]{1,0:T(8,128)(2,1)S(1)}, u32[]{:S(2)}, u32[]{:S(2)}) collective-permute-start(bf16[32,768]{1,0:T(8,128)(2,1)S(1)} %constant_dynamic-slice_fusion.own_ref), channel_id=1, source_target_pairs={{0,8},{8,0},{16,24},{24,16},{1,9},{9,1},{17,25},{25,17},{2,10},{10... | collective-permute-start | bytes 147464 | tf_op jit(solution)/shard_map/ppermute | solution.py:486
  3.9 8.0 %collective-permute-start.2 = (bf16[32,768]{1,0:T(8,128)(2,1)S(1)}, bf16[32,768]{1,0:T(8,128)(2,1)S(1)}, u32[]{:S(2)}, u32[]{:S(2)}) collective-permute-start(bf16[32,768]{1,0:T(8,128)(2,1)S(1)} %constant_dynamic-slice_fusion.own_ref), channel_id=1, source_target_pairs={{0,24},{8,16},{16,8},{24,0},{1,25},{9,17},{17,9},{25,1},{2,26},{10... | collective-permute-start | bytes 147464 | tf_op jit(solution)/shard_map/ppermute | solution.py:486
  6.4 5.5 %collective-permute-start.1 = (bf16[32,768]{1,0:T(8,128)(2,1)S(1)}, bf16[32,768]{1,0:T(8,128)(2,1)S(1)}, u32[]{:S(2)}, u32[]{:S(2)}) collective-permute-start(bf16[32,768]{1,0:T(8,128)(2,1)S(1)} %constant_dynamic-slice_fusion.own_ref), channel_id=1, source_target_pairs={{0,16},{8,24},{16,0},{24,8},{1,17},{9,25},{17,1},{25,9},{2,18},{10... | collective-permute-start | bytes 147464 | tf_op jit(solution)/shard_map/ppermute | solution.py:486
  11.9 10.6 %collective-permute-start.5 = (bf16[96,768]{1,0:T(8,128)(2,1)S(1)}, bf16[96,768]{1,0:T(8,128)(2,1)S(1)}, u32[]{:S(2)}, u32[]{:S(2)}) collective-permute-start(bf16[96,768]{1,0:T(8,128)(2,1)S(1)} %constant_dynamic-update-slice_fusion.refs_0_), channel_id=1, source_target_pairs={{0,6},{2,4},{4,2},{6,0},{1,7},{3,5},{5,3},{7,1},{8,14},{10,12},{12... | collective-permute-start | bytes 442376 | tf_op jit(solution)/shard_map/ppermute | solution.py:486
  14.4 8.1 %collective-permute-start.4 = (bf16[96,768]{1,0:T(8,128)(2,1)S(1)}, bf16[96,768]{1,0:T(8,128)(2,1)S(1)}, u32[]{:S(2)}, u32[]{:S(2)}) collective-permute-start(bf16[96,768]{1,0:T(8,128)(2,1)S(1)} %constant_dynamic-update-slice_fusion.refs_0_), channel_id=1, source_target_pairs={{0,4},{2,6},{4,0},{6,2},{1,5},{3,7},{5,1},{7,3},{8,12},{10,14},{12... | collective-permute-start | bytes 442376 | tf_op jit(solution)/shard_map/ppermute | solution.py:486
  14.9 7.6 %collective-permute-start.3 = (bf16[96,768]{1,0:T(8,128)(2,1)S(1)}, bf16[96,768]{1,0:T(8,128)(2,1)S(1)}, u32[]{:S(2)}, u32[]{:S(2)}) collective-permute-start(bf16[96,768]{1,0:T(8,128)(2,1)S(1)} %constant_dynamic-update-slice_fusion.refs_0_), channel_id=1, source_target_pairs={{0,2},{2,0},{4,6},{6,4},{1,3},{3,1},{5,7},{7,5},{8,10},{10,8},{12,... | collective-permute-start | bytes 442376 | tf_op jit(solution)/shard_map/ppermute | solution.py:486
  15.5 1.4 %copy-start = (bf16[1024,768]{1,0:T(8,128)(2,1)S(1)}, bf16[1024,768]{1,0:T(8,128)(2,1)}, u32[]{:S(2)}) copy-start(bf16[1024,768]{1,0:T(8,128)(2,1)} %emb_ref.3) | copy-start | bytes 4718596
  16.9 1.0 copy-start.2
  17.9 7.0 %copy-start.1 = (bf16[1024,768]{1,0:T(8,128)(2,1)S(1)}, bf16[1024,768]{1,0:T(8,128)(2,1)}, u32[]{:S(2)}) copy-start(bf16[1024,768]{1,0:T(8,128)(2,1)} %emb_ref.3) | copy-start | bytes 4718596
  22.6 1.4 %collective-permute-start.6 = (bf16[96,768]{1,0:T(8,128)(2,1)S(1)}, bf16[96,768]{1,0:T(8,128)(2,1)S(1)}, u32[]{:S(2)}, u32[]{:S(2)}) collective-permute-start(bf16[96,768]{1,0:T(8,128)(2,1)S(1)} %constant_dynamic-update-slice_fusion.refs_0_), channel_id=1, source_target_pairs={{0,1},{1,0},{2,3},{3,2},{4,5},{5,4},{6,7},{7,6},{8,9},{9,8},{10,11... | collective-permute-start | bytes 442376 | tf_op jit(solution)/shard_map/ppermute | solution.py:486
  22.6 1.6 %collective-permute-start.7 = (bf16[96,768]{1,0:T(8,128)(2,1)S(1)}, bf16[96,768]{1,0:T(8,128)(2,1)S(1)}, u32[]{:S(2)}, u32[]{:S(2)}) collective-permute-start(bf16[96,768]{1,0:T(8,128)(2,1)S(1)} %collective-permute-done.3.refs_1_), channel_id=1, source_target_pairs={{0,1},{1,0},{2,3},{3,2},{4,5},{5,4},{6,7},{7,6},{8,9},{9,8},{10,11... | collective-permute-start | bytes 442376 | tf_op jit(solution)/shard_map/ppermute | solution.py:486
  23.1 1.5 %collective-permute-start.8 = (bf16[96,768]{1,0:T(8,128)(2,1)S(1)}, bf16[96,768]{1,0:T(8,128)(2,1)}, u32[]{:S(2)}, u32[]{:S(2)}) collective-permute-start(bf16[96,768]{1,0:T(8,128)(2,1)S(1)} %collective-permute-done.4.refs_2_), channel_id=1, source_target_pairs={{0,1},{1,0},{2,3},{3,2},{4,5},{5,4},{6,7},{7,6},{8,9},{9,8},{10,11... | collective-permute-start | bytes 442376 | tf_op jit(solution)/shard_map/ppermute | solution.py:486
  23.2 1.6 %collective-permute-start.9 = (bf16[96,768]{1,0:T(8,128)(2,1)S(1)}, bf16[96,768]{1,0:T(8,128)(2,1)}, u32[]{:S(2)}, u32[]{:S(2)}) collective-permute-start(bf16[96,768]{1,0:T(8,128)(2,1)S(1)} %collective-permute-done.5.refs_3_), channel_id=1, source_target_pairs={{0,1},{1,0},{2,3},{3,2},{4,5},{5,4},{6,7},{7,6},{8,9},{9,8},{10,11... | collective-permute-start | bytes 442376 | tf_op jit(solution)/shard_map/ppermute | solution.py:486
  42.0 2.9 %collective-permute-start.10 = (f32[2304,128]{1,0:T(8,128)S(1)}, f32[2304,128]{1,0:T(8,128)S(1)}, u32[]{:S(2)}, u32[]{:S(2)}) collective-permute-start(f32[2304,128]{1,0:T(8,128)S(1)} %get-tuple-element.51), channel_id=1, source_target_pairs={{0,1},{1,0},{2,3},{3,2},{4,5},{5,4},{6,7},{7,6},{8,9},{9,8},{10,11... | collective-permute-start | bytes 3538952 | tf_op jit(solution)/shard_map/ppermute | solution.py:486
  45.6 10.8 %collective-permute-start.11 = (f32[576,128]{1,0:T(8,128)S(1)}, f32[576,128]{1,0:T(8,128)S(1)}, u32[]{:S(2)}, u32[]{:S(2)}) collective-permute-start(f32[576,128]{1,0:T(8,128)S(1)} %get-tuple-element.53), channel_id=1, source_target_pairs={{0,6},{2,4},{4,2},{6,0},{1,7},{3,5},{5,3},{7,1},{8,14},{10,12},{12... | collective-permute-start | bytes 884744 | tf_op jit(solution)/shard_map/ppermute | solution.py:486
  48.1 14.0 %collective-permute-start.12 = (f32[576,128]{1,0:T(8,128)S(1)}, f32[576,128]{1,0:T(8,128)S(1)}, u32[]{:S(2)}, u32[]{:S(2)}) collective-permute-start(f32[576,128]{1,0:T(8,128)S(1)} %get-tuple-element.54), channel_id=1, source_target_pairs={{0,4},{2,6},{4,0},{6,2},{1,5},{3,7},{5,1},{7,3},{8,12},{10,14},{12... | collective-permute-start | bytes 884744 | tf_op jit(solution)/shard_map/ppermute | solution.py:486
  48.6 13.6 %collective-permute-start.13 = (f32[576,128]{1,0:T(8,128)S(1)}, f32[576,128]{1,0:T(8,128)S(1)}, u32[]{:S(2)}, u32[]{:S(2)}) collective-permute-start(f32[576,128]{1,0:T(8,128)S(1)} %get-tuple-element.55), channel_id=1, source_target_pairs={{0,2},{2,0},{4,6},{6,4},{1,3},{3,1},{5,7},{7,5},{8,10},{10,8},{12,... | collective-permute-start | bytes 884744 | tf_op jit(solution)/shard_map/ppermute | solution.py:486
  62.8 7.0 %collective-permute-start.14 = (f32[144,128]{1,0:T(8,128)S(1)}, f32[144,128]{1,0:T(8,128)S(1)}, u32[]{:S(2)}, u32[]{:S(2)}) collective-permute-start(f32[144,128]{1,0:T(8,128)S(1)} %get-tuple-element.57), channel_id=1, source_target_pairs={{0,24},{8,16},{16,8},{24,0},{1,25},{9,17},{17,9},{25,1},{2,26},{10... | collective-permute-start | bytes 221192 | tf_op jit(solution)/shard_map/ppermute | solution.py:486
  65.0 6.9 %collective-permute-start.15 = (f32[144,128]{1,0:T(8,128)S(1)}, f32[144,128]{1,0:T(8,128)S(1)}, u32[]{:S(2)}, u32[]{:S(2)}) collective-permute-start(f32[144,128]{1,0:T(8,128)S(1)} %get-tuple-element.58), channel_id=1, source_target_pairs={{0,16},{8,24},{16,0},{24,8},{1,17},{9,25},{17,1},{25,9},{2,18},{10... | collective-permute-start | bytes 221192 | tf_op jit(solution)/shard_map/ppermute | solution.py:486
  65.0 6.9 %collective-permute-start.16 = (f32[144,128]{1,0:T(8,128)S(1)}, f32[144,128]{1,0:T(8,128)S(1)}, u32[]{:S(2)}, u32[]{:S(2)}) collective-permute-start(f32[144,128]{1,0:T(8,128)S(1)} %get-tuple-element.59), channel_id=1, source_target_pairs={{0,8},{8,0},{16,24},{24,16},{1,9},{9,1},{17,25},{25,17},{2,10},{10... | collective-permute-start | bytes 221192 | tf_op jit(solution)/shard_map/ppermute | solution.py:486
  72.5 7.0 %collective-permute-start.19 = (f32[144,128]{1,0:T(8,128)S(1)}, f32[144,128]{1,0:T(8,128)S(1)}, u32[]{:S(2)}, u32[]{:S(2)}) collective-permute-start(f32[144,128]{1,0:T(8,128)S(1)} %add_cut.5.refs_0_), channel_id=1, source_target_pairs={{0,24},{8,16},{16,8},{24,0},{1,25},{9,17},{17,9},{25,1},{2,26},{10... | collective-permute-start | bytes 221192 | tf_op jit(solution)/shard_map/ppermute | solution.py:486
  74.7 7.0 %collective-permute-start.18 = (f32[144,128]{1,0:T(8,128)S(1)}, f32[144,128]{1,0:T(8,128)S(1)}, u32[]{:S(2)}, u32[]{:S(2)}) collective-permute-start(f32[144,128]{1,0:T(8,128)S(1)} %add_cut.5.refs_0_), channel_id=1, source_target_pairs={{0,16},{8,24},{16,0},{24,8},{1,17},{9,25},{17,1},{25,9},{2,18},{10... | collective-permute-start | bytes 221192 | tf_op jit(solution)/shard_map/ppermute | solution.py:486
  74.7 7.0 %collective-permute-start.17 = (f32[144,128]{1,0:T(8,128)S(1)}, f32[144,128]{1,0:T(8,128)S(1)}, u32[]{:S(2)}, u32[]{:S(2)}) collective-permute-start(f32[144,128]{1,0:T(8,128)S(1)} %add_cut.5.refs_0_), channel_id=1, source_target_pairs={{0,8},{8,0},{16,24},{24,16},{1,9},{9,1},{17,25},{25,17},{2,10},{10... | collective-permute-start | bytes 221192 | tf_op jit(solution)/shard_map/ppermute | solution.py:486
  82.3 6.0 %collective-permute-start.22 = (f32[160,128]{1,0:T(8,128)S(1)}, f32[160,128]{1,0:T(8,128)S(1)}, u32[]{:S(2)}, u32[]{:S(2)}) collective-permute-start(f32[160,128]{1,0:T(8,128)S(1)} %get-tuple-element.63.refs_0_), channel_id=1, source_target_pairs={{0,6},{2,4},{4,2},{6,0},{1,7},{3,5},{5,3},{7,1},{8,14},{10,12},{12... | collective-permute-start | bytes 245768 | tf_op jit(solution)/shard_map/ppermute | solution.py:486
  83.6 5.7 %collective-permute-start.21 = (f32[160,128]{1,0:T(8,128)S(1)}, f32[160,128]{1,0:T(8,128)S(1)}, u32[]{:S(2)}, u32[]{:S(2)}) collective-permute-start(f32[160,128]{1,0:T(8,128)S(1)} %get-tuple-element.63.refs_0_), channel_id=1, source_target_pairs={{0,4},{2,6},{4,0},{6,2},{1,5},{3,7},{5,1},{7,3},{8,12},{10,14},{12... | collective-permute-start | bytes 245768 | tf_op jit(solution)/shard_map/ppermute | solution.py:486
  85.3 4.4 %collective-permute-start.20 = (f32[160,128]{1,0:T(8,128)S(1)}, f32[160,128]{1,0:T(8,128)S(1)}, u32[]{:S(2)}, u32[]{:S(2)}) collective-permute-start(f32[160,128]{1,0:T(8,128)S(1)} %get-tuple-element.63.refs_0_), channel_id=1, source_target_pairs={{0,2},{2,0},{4,6},{6,4},{1,3},{3,1},{5,7},{7,5},{8,10},{10,8},{12,... | collective-permute-start | bytes 245768 | tf_op jit(solution)/shard_map/ppermute | solution.py:486
  85.8 4.0 %collective-permute-start.23 = (f32[160,128]{1,0:T(8,128)S(1)}, f32[160,128]{1,0:T(8,128)S(1)}, u32[]{:S(2)}, u32[]{:S(2)}) collective-permute-start(f32[160,128]{1,0:T(8,128)S(1)} %get-tuple-element.63.refs_0_), channel_id=1, source_target_pairs={{0,1},{1,0},{2,3},{3,2},{4,5},{5,4},{6,7},{7,6},{8,9},{9,8},{10,11... | collective-permute-start | bytes 245768 | tf_op jit(solution)/shard_map/ppermute | solution.py:486
  88.3 1.6 %collective-permute-start.26 = (f32[160,128]{1,0:T(8,128)S(1)}, f32[160,128]{1,0:T(8,128)S(1)}, u32[]{:S(2)}, u32[]{:S(2)}) collective-permute-start(f32[160,128]{1,0:T(8,128)S(1)} %collective-permute-done.22.refs_3_), channel_id=1, source_target_pairs={{0,1},{1,0},{2,3},{3,2},{4,5},{5,4},{6,7},{7,6},{8,9},{9,8},{10,11... | collective-permute-start | bytes 245768 | tf_op jit(solution)/shard_map/ppermute | solution.py:486
  89.4 1.3 collective-permute-start.25
  89.7 1.3 collective-permute-start.24
  91.0 17.6 %collective-permute-start.29 = (f32[416,128]{1,0:T(8,128)S(1)}, f32[416,128]{1,0:T(8,128)S(1)}, u32[]{:S(2)}, u32[]{:S(2)}) collective-permute-start(f32[416,128]{1,0:T(8,128)S(1)} %get-tuple-element.75.refs_0_), channel_id=1, source_target_pairs={{0,6},{2,4},{4,2},{6,0},{1,7},{3,5},{5,3},{7,1},{8,14},{10,12},{12... | collective-permute-start | bytes 638984 | tf_op jit(solution)/shard_map/ppermute | solution.py:486
  92.5 16.1 %collective-permute-start.28 = (f32[416,128]{1,0:T(8,128)S(1)}, f32[416,128]{1,0:T(8,128)S(1)}, u32[]{:S(2)}, u32[]{:S(2)}) collective-permute-start(f32[416,128]{1,0:T(8,128)S(1)} %get-tuple-element.75.refs_0_), channel_id=1, source_target_pairs={{0,4},{2,6},{4,0},{6,2},{1,5},{3,7},{5,1},{7,3},{8,12},{10,14},{12... | collective-permute-start | bytes 638984 | tf_op jit(solution)/shard_map/ppermute | solution.py:486
  93.8 14.9 %collective-permute-start.27 = (f32[416,128]{1,0:T(8,128)S(1)}, f32[416,128]{1,0:T(8,128)S(1)}, u32[]{:S(2)}, u32[]{:S(2)}) collective-permute-start(f32[416,128]{1,0:T(8,128)S(1)} %get-tuple-element.75.refs_0_), channel_id=1, source_target_pairs={{0,2},{2,0},{4,6},{6,4},{1,3},{3,1},{5,7},{7,5},{8,10},{10,8},{12,... | collective-permute-start | bytes 638984 | tf_op jit(solution)/shard_map/ppermute | solution.py:486
  108.6 1.5 %collective-permute-start.30 = (f32[416,128]{1,0:T(8,128)S(1)}, f32[416,128]{1,0:T(8,128)S(1)}, u32[]{:S(2)}, u32[]{:S(2)}) collective-permute-start(f32[416,128]{1,0:T(8,128)S(1)} %get-tuple-element.75.refs_0_), channel_id=1, source_target_pairs={{0,1},{1,0},{2,3},{3,2},{4,5},{5,4},{6,7},{7,6},{8,9},{9,8},{10,11... | collective-permute-start | bytes 638984 | tf_op jit(solution)/shard_map/ppermute | solution.py:486
  108.7 1.8 %collective-permute-start.31 = (f32[416,128]{1,0:T(8,128)S(1)}, f32[416,128]{1,0:T(8,128)S(1)}, u32[]{:S(2)}, u32[]{:S(2)}) collective-permute-start(f32[416,128]{1,0:T(8,128)S(1)} %collective-permute-done.27.refs_1_), channel_id=1, source_target_pairs={{0,1},{1,0},{2,3},{3,2},{4,5},{5,4},{6,7},{7,6},{8,9},{9,8},{10,11... | collective-permute-start | bytes 638984 | tf_op jit(solution)/shard_map/ppermute | solution.py:486
  109.2 1.6 %collective-permute-start.32 = (f32[416,128]{1,0:T(8,128)S(1)}, f32[416,128]{1,0:T(8,128)S(1)}, u32[]{:S(2)}, u32[]{:S(2)}) collective-permute-start(f32[416,128]{1,0:T(8,128)S(1)} %collective-permute-done.28.refs_2_), channel_id=1, source_target_pairs={{0,1},{1,0},{2,3},{3,2},{4,5},{5,4},{6,7},{7,6},{8,9},{9,8},{10,11... | collective-permute-start | bytes 638984 | tf_op jit(solution)/shard_map/ppermute | solution.py:486
  109.3 1.8 %collective-permute-start.33 = (f32[416,128]{1,0:T(8,128)S(1)}, f32[416,128]{1,0:T(8,128)S(1)}, u32[]{:S(2)}, u32[]{:S(2)}) collective-permute-start(f32[416,128]{1,0:T(8,128)S(1)} %collective-permute-done.29.refs_3_), channel_id=1, source_target_pairs={{0,1},{1,0},{2,3},{3,2},{4,5},{5,4},{6,7},{7,6},{8,9},{9,8},{10,11... | collective-permute-start | bytes 638984 | tf_op jit(solution)/shard_map/ppermute | solution.py:486

commit v7 on v6

--- a/solution.py
+++ b/solution.py
@@ -15,8 +15,8 @@
 RIDGE = 0.1
 EPS = 1e-06
 B = 128
-W = 16
-TINY = 1e-30
+HALF = 64
+CLIP = 1.0 - 2.0**-24
 
 ARC = (0.9426497266634519, 0.04833294295062493, 0.004716300148249888, 0.004298816276929029)
 KEEP = 1.0 / (1.0 + SCALE_SQ)
@@ -25,8 +25,9 @@
 
 
 def recursion(c):
+    c = jnp.clip(c, -CLIP, CLIP)
     for _ in range(LAYERS):
-        w = jnp.maximum(1.0 - jnp.abs(c), TINY)
+        w = 1.0 - jnp.abs(c)
         t = (w * w) * lax.rsqrt(w)
         poly = ARC[3]
         for a in ARC[2::-1]:
@@ -93,22 +94,26 @@
     fill_cross(marks_ref, emb_ref, u_ref, k_ref, vq_ref, x_ref, lambda r: r)
 
 
-def own_cross(landmarks, embeddings):
+def own_rest_kernel(marks_ref, emb_ref, u_ref, x_ref, k_ref, vq_ref):
+    fill_cross(marks_ref, emb_ref, u_ref, k_ref, vq_ref, x_ref, lambda r: r)
+
+
+def own_cross(landmarks, embeddings, u=None):
     m = embeddings.shape[0]
-    shard = landmarks.shape[0]
+    rows = landmarks.shape[0]
     vmem = pl.BlockSpec(memory_space=pltpu.VMEM)
+    x_shape = jax.ShapeDtypeStruct((rows, m), jnp.bfloat16)
+    u_shape = jax.ShapeDtypeStruct((16, m), jnp.float32)
+    given = () if u is None else (u,)
     return pl.pallas_call(
-        own_kernel,
-        out_shape=(
-            jax.ShapeDtypeStruct((shard, m), jnp.bfloat16),
-            jax.ShapeDtypeStruct((16, m), jnp.float32),
-        ),
-        in_specs=[vmem, vmem],
-        out_specs=(vmem, vmem),
-        scratch_shapes=[pltpu.VMEM((shard, m), jnp.float32), pltpu.VMEM((shard, B), jnp.float32)],
+        own_rest_kernel if given else own_kernel,
+        out_shape=x_shape if given else (x_shape, u_shape),
+        in_specs=[vmem] * (2 + len(given)),
+        out_specs=vmem if given else (vmem, vmem),
+        scratch_shapes=[pltpu.VMEM((rows, m), jnp.float32), pltpu.VMEM((rows, B), jnp.float32)],
         compiler_params=pltpu.CompilerParams(vmem_limit_bytes=12 << 20),
         name="own_cross",
-    )(landmarks, embeddings)
+    )(landmarks, embeddings, *given)
 
 
 class Plan(typing.NamedTuple):
@@ -119,7 +124,7 @@
     all_points: int
 
 
-def gram_kernel(plan, na, at_ref, emb_ref, mine_ref, own_ref, u_ref, x_mine_ref, *refs):
+def gram_kernel(plan, na, at_ref, emb_ref, mine_ref, own_ref, u_ref, x_upper_ref, x_lower_ref, *refs):
     lands, chips, cores, split, all_points = plan
     count = chips * (cores if split else 1)
     far = refs[:count]
@@ -128,7 +133,8 @@
     n = shard * lands
     land, chip, core = at_ref[0], at_ref[1], at_ref[2]
     here = pl.multiple_of(land * shard, shard)
-    x_ref[pl.ds(here, shard), :] = x_mine_ref[...]
+    x_ref[pl.ds(here, shard // 2), :] = x_upper_ref[...]
+    x_ref[pl.ds(pl.multiple_of(here + shard // 2, CHUNK), shard // 2), :] = x_lower_ref[...]
     piece = far[0].shape[0] // (lands - 1)
     for a in range(cores if split else 1):
         for t in range(chips):
@@ -202,7 +208,7 @@
     return packed_start(j) if j < na else packed_start(j) - packed_start(na) + segments(plan, na, j)[0]
 
 
-def local_normal(at, plan, na, embeddings, landmarks, own, u, x_mine, far):
+def local_normal(at, plan, na, embeddings, landmarks, own, u, x_upper, x_lower, far):
     n, m = landmarks.shape[0] * plan.lands, embeddings.shape[0]
     away = n - landmarks.shape[0]
     rows = sum(segments(plan, na, n // B))
@@ -211,7 +217,7 @@
     return pl.pallas_call(
         functools.partial(gram_kernel, plan, na),
         out_shape=(half, half),
-        in_specs=[pl.BlockSpec(memory_space=pltpu.SMEM)] + [vmem] * (5 + len(far)),
+        in_specs=[pl.BlockSpec(memory_space=pltpu.SMEM)] + [vmem] * (6 + len(far)),
         out_specs=(vmem,) * 2,
         scratch_shapes=[
             pltpu.VMEM((n, m), jnp.bfloat16),
@@ -223,7 +229,7 @@
         ],
         compiler_params=pltpu.CompilerParams(vmem_limit_bytes=24 << 20),
         name="gram",
-    )(at, embeddings, landmarks, own, u, x_mine, *far)
+    )(at, embeddings, landmarks, own, u, x_upper, x_lower, *far)
 
 
 def add_cut_kernel(ways, axis, parts, at_ref, *refs):
@@ -296,75 +302,61 @@
     return dot32(a.T, b)
 
 def factor_block(d):
-    rows8 = lax.broadcasted_iota(jnp.int32, (8, 128), 0)
+    row8 = lax.broadcasted_iota(jnp.int32, (8, B), 0)
     eye = (lax.broadcasted_iota(jnp.int32, (B, B), 0) == lax.broadcasted_iota(jnp.int32, (B, B), 1)).astype(jnp.float32)
-    n = B // W
-    g = W // 8
-    left = [d[8 * i:8 * i + 8] for i in range(B // 8)]
-    right = [eye[8 * i:8 * i + 8] for i in range(B // 8)]
-    for p in range(n):
-        base = p * g
-        last = p == n - 1
-        groups = list(range(base, base + (g if last else 2 * g)))
-        col = [[None] * len(groups) for _ in range(W)]
-        for i in range(W):
-            for t, r in enumerate(groups):
-                if t < g and t < i // 8:
-                    continue
-                lane = p * W + i
-                col[i][t] = jnp.broadcast_to(left[r][:, lane:lane + 1], (8, 128))
-        diag = [jnp.ones((8, 128), jnp.float32) for _ in range(g)]
-        for j in range(W):
-            tj, sj = j // 8, j % 8
-            pivot = jnp.broadcast_to(col[j][tj][sj:sj + 1], (8, 128))
-            diag[tj] = jnp.where(rows8 == sj, pivot, diag[tj])
-            inv = 1.0 / pivot
-            coefs = {}
-            for i in range(j + 1, W):
-                coefs[i] = jnp.broadcast_to(col[j][i // 8][i % 8:i % 8 + 1], (8, 128))
-            scaled = [None] * len(groups)
-            for t in range(len(groups)):
-                if col[j][t] is None:
-                    continue
-                scaled[t] = col[j][t] * inv
-            for i in range(j + 1, W):
-                for t in range(len(groups)):
-                    if col[i][t] is None:
-                        continue
-                    if i == j + 1:
-                        col[i][t] = col[i][t] - (col[j][t] * coefs[i]) * inv
-                    else:
-                        col[i][t] = col[i][t] - scaled[t] * coefs[i]
-            rl = jnp.broadcast_to(left[base + tj][sj:sj + 1], (8, 128))
-            rr = jnp.broadcast_to(right[base + tj][sj:sj + 1], (8, 128))
-            for t, r in enumerate(groups):
-                if scaled[t] is None:
-                    continue
-                c = scaled[t]
-                if t == tj:
-                    if sj == 7:
-                        continue
-                    c = jnp.where(rows8 > sj, c, 0.0)
-                left[r] = left[r] - c * rl
-                right[r] = right[r] - c * rr
-        for t in range(g):
-            s = lax.rsqrt(diag[t])
-            left[base + t] = left[base + t] * s
-            right[base + t] = right[base + t] * s
-        rest = (n - p - 2) * W
-        if rest > 0:
-            ul = jnp.concatenate(left[base:base + g], 0)
-            ur = jnp.concatenate(right[base:base + g], 0)
-            u = jnp.concatenate([ul, ur], 1)
-            lo_row = (p + 2) * W
-            upd = lax.dot_general(left_terms(ul, 0), right_terms(u, 0), (((0,), (0,)), ((), ())), preferred_element_type=jnp.float32)
-            for r in range(lo_row // 8, B // 8):
-                left[r] = left[r] - upd[8 * r:8 * r + 8, :128]
-                right[r] = right[r] - upd[8 * r:8 * r + 8, 128:]
-    u = jnp.concatenate(left, 0)
-    w = jnp.concatenate(right, 0)
+    left = [d[i : i + 8] for i in range(0, B, 8)]
+    right = [eye[i : i + 8] for i in range(0, B, 8)]
+    zero = left[0] * 0.0
+    half = HALF // 8
+
+    def spread_columns(x, lane):
+        columns = [jnp.broadcast_to(x[:, lane + i : lane + i + 1], (8, B)) for i in range(8)]
+        return [columns[0] + zero] + columns[1:]
+
+    def splat(x, r):
+        return jnp.broadcast_to(x[r : r + 1], (8, B))
+
+    for start in range(0, B // 8, half):
+        end = start + half
+        diag = spread_columns(left[start], 8 * start)
+        for p in range(start, end):
+            col = {r: spread_columns(left[r], 8 * p) for r in range(p + 1, end)}
+            after = spread_columns(left[p + 1], 8 * p + 8) if p + 1 < end else None
+            pivots = jnp.ones((8, B), jnp.float32)
+            for j in range(8):
+                pivot = splat(diag[j], j)
+                pivots = jnp.where(row8 == j, pivot, pivots)
+                inv = 1.0 / pivot
+                coef = {i: splat(diag[j], i) for i in range(j + 1, 8)}
+                for i in coef:
+                    diag[i] = diag[i] - (diag[j] * coef[i]) * inv
+                rl, rr = splat(left[p], j), splat(right[p], j)
+                if j < 7:
+                    c = jnp.where(row8 > j, diag[j] * inv, 0.0)
+                    left[p] = left[p] - c * rl
+                    right[p] = right[p] - c * rr
+                for r in col:
+                    c = col[r][j] * inv
+                    if r == p + 1:
+                        for i in range(8):
+                            after[i] = after[i] - c * splat(col[r][j], i)
+                    for i in coef:
+                        col[r][i] = col[r][i] - c * coef[i]
+                    left[r] = left[r] - c * rl
+                    right[r] = right[r] - c * rr
+            s = lax.rsqrt(pivots)
+            left[p] = left[p] * s
+            right[p] = right[p] * s
+            diag = after
+        if end < B // 8:
+            ul = jnp.concatenate(left[start:end], 0)
+            u = jnp.concatenate([ul, jnp.concatenate(right[start:end], 0)], 1)
+            upd = dot32_t(ul, u)
+            for r in range(end, B // 8):
+                left[r] = left[r] - upd[8 * r : 8 * r + 8, :B]
+                right[r] = right[r] - upd[8 * r : 8 * r + 8, B:]
     tri = lax.broadcasted_iota(jnp.int32, (B, B), 0) <= lax.broadcasted_iota(jnp.int32, (B, B), 1)
-    return jnp.where(tri, u, 0.0), w
+    return jnp.where(tri, jnp.concatenate(left, 0), 0.0), jnp.concatenate(right, 0)
 
 
 def eliminate(nb, m_ref, d_ref, r_ref, store):
@@ -508,16 +500,17 @@
         piece = own
     else:
         piece = lax.dynamic_slice_in_dim(landmarks, chip * (shard // chips), shard // chips, 0)
-    z = jnp.concatenate(spread_out(piece, "land")[1:], 0)
-    far = spread_out(z, "chip")
-    x_mine, u = own_cross(landmarks, embeddings)
+    x_upper, u = own_cross(landmarks[: shard // 2], embeddings)
+    z, x_upper, u = lax.optimization_barrier((spread_out(piece, "land")[1:], x_upper, u))
+    far = spread_out(jnp.concatenate(z, 0), "chip")
+    x_lower = own_cross(landmarks[shard // 2 :], embeddings, u)
+    far, x_lower = lax.optimization_barrier((far, x_lower))
     if plan.split:
-        far, x_mine, u = lax.optimization_barrier((far, x_mine, u))
         for a in range(1, cores):
             far = far + [swap(f, "core", a) for f in far[:chips]]
 
     na = n // B // 2
-    keep, send = local_normal(at, plan, na, embeddings, landmarks, own, u, x_mine, far)
+    keep, send = local_normal(at, plan, na, embeddings, landmarks, own, u, x_upper, x_lower, far)
     rows = [r // cores for r in segments(plan, na, n // B)]
     parts = scatter(add_cut(at, 1, chips, rows, [keep, swap(send, "core", 1)]), "chip")
     rows = [r // chips for r in rows]

time: 131 us -> 126 us (0.962)
  Pallas kernels: 57.8 us -> 54.1 us
    pallas_call x1, Pallas kernels: 14.1 us -> 12.3 us  [first_factor(): pl.pallas_call(functools.partial(first_factor_kernel, plan), out_shape=(j...]
    pallas_call x1, Pallas kernels: 19.5 us -> 17.8 us  [last_factor(): pl.pallas_call(functools.partial(last_factor_kernel, plan), out_shape=jax...]
    pallas_call x1 -> x2, Pallas kernels: 4.65 us -> 5.13 us  [own_cross(): pl.pallas_call(own_rest_kernel if given else own_kernel, out_shape=x_shap...]
  transfers between devices with their start and end apart: 34 -> 34, of which waited for: 22 -> 23; matrix products, arithmetic and copies ran while one was open for 0% -> 1% of each run, Pallas kernels for 14% -> 14%
where the time goes in v7:
time: 126 us
  Pallas kernels  54.1 us (43%)
  waiting for transfers between devices  36.9 us (29%)
  starting transfers between devices  31.2 us (25%)
  local copies, waits for them, and re-layouts  3.28 us (3%)
    ppermute x34, waiting for transfers between devices, swap(): lax.ppermute(x, axis, [(i, i ^ s) for i in range(lax.axis_size(axis))])  36.9 us
    ppermute x34, starting transfers between devices, swap(): lax.ppermute(x, axis, [(i, i ^ s) for i in range(lax.axis_size(axis))])  31.2 us
    pallas_call x1, Pallas kernels, last_factor(): pl.pallas_call(functools.partial(last_factor_kernel, plan), out_shape=jax...  17.8 us
    pallas_call x1, Pallas kernels, local_normal(): pl.pallas_call(functools.partial(gram_kernel, plan, na), out_shape=(half,...  16.5 us
    pallas_call x1, Pallas kernels, first_factor(): pl.pallas_call(functools.partial(first_factor_kernel, plan), out_shape=(j...  12.3 us
    pallas_call x2, Pallas kernels, own_cross(): pl.pallas_call(own_rest_kernel if given else own_kernel, out_shape=x_shap...  5.13 us
  transfers between devices with their start and end apart: 34, of which 23 were waited for; matrix products, arithmetic and copies ran while one was open for 1% of the time, Pallas kernels for 14%

profile of v7, /device:TPU:0, one launch (start us, length us, event | category | flops | bytes accessed | tf_op | source)
XLA Modules:
  0.0 125.8 jit_solution(14860285021197790489)
XLA Ops:
  0.0 0.8 constant_dynamic-slice_fusion.own_ref
  0.8 5.0 %collective-permute-start.2 = (bf16[32,768]{1,0:T(8,128)(2,1)S(1)}, bf16[32,768]{1,0:T(8,128)(2,1)S(1)}, u32[]{:S(2)}, u32[]{:S(2)}) collective-permute-start(bf16[32,768]{1,0:T(8,128)(2,1)S(1)} %constant_dynamic-slice_fusion.own_ref), channel_id=1, source_target_pairs={{0,24},{8,16},{16,8},{24,0},{1,25},{9,17},{17,9},{25,1},{2,26},{10... | collective-permute-start | bytes 147464 | tf_op jit(solution)/shard_map/ppermute | solution.py:478
  5.9 0.6 collective-permute-start
  6.4 1.0 fusion
  7.5 1.4 %copy-done = bf16[1024,768]{1,0:T(8,128)(2,1)S(1)} copy-done((bf16[1024,768]{1,0:T(8,128)(2,1)S(1)}, bf16[1024,768]{1,0:T(8,128)(2,1)}, u32[]{:S(2)}) %copy-start) | copy-done | bytes 1572888
  8.9 2.6 %own_cross.2 = (bf16[128,1024]{1,0:T(8,128)(2,1)S(1)}, f32[16,1024]{1,0:T(8,128)S(1)}) custom-call(bf16[128,768]{1,0:T(8,128)(2,1)S(1)} %get-tuple-element.88.marks_ref, bf16[1024,768]{1,0:T(8,128)(2,1)S(1)} %copy-done), custom_call_target="tpu_custom_call" | custom-call | tf_op jit(solution)/shard_map/own_cross/pallas_call | solution.py:108
  11.6 2.7 %collective-permute-start.5 = (bf16[96,768]{1,0:T(8,128)(2,1)S(1)}, bf16[96,768]{1,0:T(8,128)(2,1)S(1)}, u32[]{:S(2)}, u32[]{:S(2)}) collective-permute-start(bf16[96,768]{1,0:T(8,128)(2,1)S(1)} %constant_dynamic-update-slice_fusion.refs_0_), channel_id=1, source_target_pairs={{0,6},{2,4},{4,2},{6,0},{1,7},{3,5},{5,3},{7,1},{8,14},{10,12},{12... | collective-permute-start | bytes 442376 | tf_op jit(solution)/shard_map/ppermute | solution.py:478
  14.3 0.5 collective-permute-start.4
  15.1 2.5 %own_cross.3.x_lower_ref = bf16[128,1024]{1,0:T(8,128)(2,1)S(1)} custom-call(bf16[128,768]{1,0:T(8,128)(2,1)S(1)} %get-tuple-element.87.marks_ref, bf16[1024,768]{1,0:T(8,128)(2,1)S(1)} %copy-done.1, f32[16,1024]{1,0:T(8,128)S(1)} %get-tuple-element.48.u_ref), custom_call_target="tpu_custom_call" | custom-call | tf_op jit(solution)/shard_map/own_cross/pallas_call | solution.py:108
  17.7 0.9 collective-permute-done.5.refs_3_
  18.6 2.2 %collective-permute-done.4.refs_2_ = bf16[96,768]{1,0:T(8,128)(2,1)S(1)} collective-permute-done((bf16[96,768]{1,0:T(8,128)(2,1)S(1)}, bf16[96,768]{1,0:T(8,128)(2,1)S(1)}, u32[]{:S(2)}, u32[]{:S(2)}) %collective-permute-start.4) | collective-permute-done | bytes 147488 | tf_op jit(solution)/shard_map/ppermute | solution.py:478
  20.8 0.5 collective-permute-start.7
  21.3 0.5 collective-permute-start.9
  23.0 16.5 %gram.1 = (f32[2304,128]{1,0:T(8,128)S(1)}, f32[2304,128]{1,0:T(8,128)S(1)}) custom-call(s32[3]{0:T(128)S(1)} %pad_add_fusion.at_ref, bf16[1024,768]{1,0:T(8,128)(2,1)S(1)} %copy-done.1, bf16[256,768]{1,0:T(8,128)(2,1)S(1)} %copy-done.2, bf16[32,768]{1,0:T(8,128)(2,1)S(1)} %constant_dynamic-slice_fusion.own_ref, f32[16,1024]{1,0:T(8,128)S(1)} %get-tuple-element.48.u_ref, ...), custom_call_target="tpu_custom_call" | custom-call | tf_op jit(solution)/shard_map/gram/pallas_call | solution.py:217
  39.8 2.5 %collective-permute-done.10.refs_1_ = f32[2304,128]{1,0:T(8,128)S(1)} collective-permute-done((f32[2304,128]{1,0:T(8,128)S(1)}, f32[2304,128]{1,0:T(8,128)S(1)}, u32[]{:S(2)}, u32[]{:S(2)}) %collective-permute-start.10) | collective-permute-done | bytes 1179680 | tf_op jit(solution)/shard_map/ppermute | solution.py:478
  42.4 0.7 add_cut.3
  43.1 1.8 %collective-permute-start.11 = (f32[576,128]{1,0:T(8,128)S(1)}, f32[576,128]{1,0:T(8,128)S(1)}, u32[]{:S(2)}, u32[]{:S(2)}) collective-permute-start(f32[576,128]{1,0:T(8,128)S(1)} %get-tuple-element.61), channel_id=1, source_target_pairs={{0,6},{2,4},{4,2},{6,0},{1,7},{3,5},{5,3},{7,1},{8,14},{10,12},{12... | collective-permute-start | bytes 884744 | tf_op jit(solution)/shard_map/ppermute | solution.py:478
  44.8 1.3 %collective-permute-start.12 = (f32[576,128]{1,0:T(8,128)S(1)}, f32[576,128]{1,0:T(8,128)S(1)}, u32[]{:S(2)}, u32[]{:S(2)}) collective-permute-start(f32[576,128]{1,0:T(8,128)S(1)} %get-tuple-element.62), channel_id=1, source_target_pairs={{0,4},{2,6},{4,0},{6,2},{1,5},{3,7},{5,1},{7,3},{8,12},{10,14},{12... | collective-permute-start | bytes 884744 | tf_op jit(solution)/shard_map/ppermute | solution.py:478
  46.1 0.5 collective-permute-start.13
  46.6 7.3 %collective-permute-done.11.refs_1_ = f32[576,128]{1,0:T(8,128)S(1)} collective-permute-done((f32[576,128]{1,0:T(8,128)S(1)}, f32[576,128]{1,0:T(8,128)S(1)}, u32[]{:S(2)}, u32[]{:S(2)}) %collective-permute-start.11) | collective-permute-done | bytes 294944 | tf_op jit(solution)/shard_map/ppermute | solution.py:478
  53.9 5.7 %collective-permute-done.12.refs_2_ = f32[576,128]{1,0:T(8,128)S(1)} collective-permute-done((f32[576,128]{1,0:T(8,128)S(1)}, f32[576,128]{1,0:T(8,128)S(1)}, u32[]{:S(2)}, u32[]{:S(2)}) %collective-permute-start.12) | collective-permute-done | bytes 294944 | tf_op jit(solution)/shard_map/ppermute | solution.py:478
  59.6 0.6 add_cut.4
  60.2 3.6 %collective-permute-start.14 = (f32[144,128]{1,0:T(8,128)S(1)}, f32[144,128]{1,0:T(8,128)S(1)}, u32[]{:S(2)}, u32[]{:S(2)}) collective-permute-start(f32[144,128]{1,0:T(8,128)S(1)} %get-tuple-element.65), channel_id=1, source_target_pairs={{0,24},{8,16},{16,8},{24,0},{1,25},{9,17},{17,9},{25,1},{2,26},{10... | collective-permute-start | bytes 221192 | tf_op jit(solution)/shard_map/ppermute | solution.py:478
  63.8 0.8 collective-permute-start.16
  64.7 2.4 %collective-permute-done.14.refs_1_ = f32[144,128]{1,0:T(8,128)S(1)} collective-permute-done((f32[144,128]{1,0:T(8,128)S(1)}, f32[144,128]{1,0:T(8,128)S(1)}, u32[]{:S(2)}, u32[]{:S(2)}) %collective-permute-start.14) | collective-permute-done | bytes 73760 | tf_op jit(solution)/shard_map/ppermute | solution.py:478
  67.1 3.1 %collective-permute-done.15.refs_2_ = f32[144,128]{1,0:T(8,128)S(1)} collective-permute-done((f32[144,128]{1,0:T(8,128)S(1)}, f32[144,128]{1,0:T(8,128)S(1)}, u32[]{:S(2)}, u32[]{:S(2)}) %collective-permute-start.15) | collective-permute-done | bytes 73760 | tf_op jit(solution)/shard_map/ppermute | solution.py:478
  70.2 0.6 add_cut.5.refs_0_
  70.8 2.5 %collective-permute-start.19 = (f32[144,128]{1,0:T(8,128)S(1)}, f32[144,128]{1,0:T(8,128)S(1)}, u32[]{:S(2)}, u32[]{:S(2)}) collective-permute-start(f32[144,128]{1,0:T(8,128)S(1)} %add_cut.5.refs_0_), channel_id=1, source_target_pairs={{0,24},{8,16},{16,8},{24,0},{1,25},{9,17},{17,9},{25,1},{2,26},{10... | collective-permute-start | bytes 221192 | tf_op jit(solution)/shard_map/ppermute | solution.py:478
  73.3 1.9 %collective-permute-start.17 = (f32[144,128]{1,0:T(8,128)S(1)}, f32[144,128]{1,0:T(8,128)S(1)}, u32[]{:S(2)}, u32[]{:S(2)}) collective-permute-start(f32[144,128]{1,0:T(8,128)S(1)} %add_cut.5.refs_0_), channel_id=1, source_target_pairs={{0,8},{8,0},{16,24},{24,16},{1,9},{9,1},{17,25},{25,17},{2,10},{10... | collective-permute-start | bytes 221192 | tf_op jit(solution)/shard_map/ppermute | solution.py:478
  75.2 2.2 %collective-permute-done.19.refs_3_ = f32[144,128]{1,0:T(8,128)S(1)} collective-permute-done((f32[144,128]{1,0:T(8,128)S(1)}, f32[144,128]{1,0:T(8,128)S(1)}, u32[]{:S(2)}, u32[]{:S(2)}) %collective-permute-start.19) | collective-permute-done | bytes 73760 | tf_op jit(solution)/shard_map/ppermute | solution.py:478
  77.4 2.9 %collective-permute-done.18.refs_2_ = f32[144,128]{1,0:T(8,128)S(1)} collective-permute-done((f32[144,128]{1,0:T(8,128)S(1)}, f32[144,128]{1,0:T(8,128)S(1)}, u32[]{:S(2)}, u32[]{:S(2)}) %collective-permute-start.18) | collective-permute-done | bytes 73760 | tf_op jit(solution)/shard_map/ppermute | solution.py:478
  80.3 0.6 place.1
  80.9 1.7 %collective-permute-start.22 = (f32[160,128]{1,0:T(8,128)S(1)}, f32[160,128]{1,0:T(8,128)S(1)}, u32[]{:S(2)}, u32[]{:S(2)}) collective-permute-start(f32[160,128]{1,0:T(8,128)S(1)} %get-tuple-element.71.refs_0_), channel_id=1, source_target_pairs={{0,6},{2,4},{4,2},{6,0},{1,7},{3,5},{5,3},{7,1},{8,14},{10,12},{12... | collective-permute-start | bytes 245768 | tf_op jit(solution)/shard_map/ppermute | solution.py:478
  82.6 1.3 %collective-permute-start.21 = (f32[160,128]{1,0:T(8,128)S(1)}, f32[160,128]{1,0:T(8,128)S(1)}, u32[]{:S(2)}, u32[]{:S(2)}) collective-permute-start(f32[160,128]{1,0:T(8,128)S(1)} %get-tuple-element.71.refs_0_), channel_id=1, source_target_pairs={{0,4},{2,6},{4,0},{6,2},{1,5},{3,7},{5,1},{7,3},{8,12},{10,14},{12... | collective-permute-start | bytes 245768 | tf_op jit(solution)/shard_map/ppermute | solution.py:478
  83.9 0.5 collective-permute-start.20
  84.5 2.6 %collective-permute-done.22.refs_3_ = f32[160,128]{1,0:T(8,128)S(1)} collective-permute-done((f32[160,128]{1,0:T(8,128)S(1)}, f32[160,128]{1,0:T(8,128)S(1)}, u32[]{:S(2)}, u32[]{:S(2)}) %collective-permute-start.22) | collective-permute-done | bytes 81952 | tf_op jit(solution)/shard_map/ppermute | solution.py:478
  87.1 0.4 collective-permute-done.21.refs_2_
  87.6 0.8 collective-permute-done.20.refs_1_
  88.4 0.4 collective-permute-done.25.refs_6_
  88.8 0.9 collective-permute-done.24.refs_5_
  89.6 1.4 %collective-permute-start.29 = (f32[416,128]{1,0:T(8,128)S(1)}, f32[416,128]{1,0:T(8,128)S(1)}, u32[]{:S(2)}, u32[]{:S(2)}) collective-permute-start(f32[416,128]{1,0:T(8,128)S(1)} %get-tuple-element.83.refs_0_), channel_id=1, source_target_pairs={{0,6},{2,4},{4,2},{6,0},{1,7},{3,5},{5,3},{7,1},{8,14},{10,12},{12... | collective-permute-start | bytes 638984 | tf_op jit(solution)/shard_map/ppermute | solution.py:478
  91.0 0.9 collective-permute-start.28
  91.9 1.2 collective-permute-start.27
  93.1 12.3 %chol_first.1 = (f32[512,512]{1,0:T(8,128)S(1)}, f32[512,128]{1,0:T(8,128)S(1)}) custom-call(s32[3]{0:T(128)S(1)} %pad_add_fusion.at_ref, f32[160,128]{1,0:T(8,128)S(1)} %get-tuple-element.71.refs_0_, f32[160,128]{1,0:T(8,128)S(1)} %collective-permute-done.20.refs_1_, f32[160,128]{1,0:T(8,128)S(1)} %collective-permute-done.21.refs_2_, ...), custom_call_target="tpu_custom_call" | custom-call | tf_op jit(solution)/shard_map/chol_first/pallas_call | solution.py:409
  105.6 0.5 collective-permute-start.31
  106.2 0.4 collective-permute-start.33
  106.6 0.4 collective-permute-done.30.refs_4_
  107.9 17.8 %chol_last.1 = f32[1024,1024]{1,0:T(8,128)} custom-call(s32[3]{0:T(128)S(1)} %pad_add_fusion.at_ref, f32[512,512]{1,0:T(8,128)S(1)} %get-tuple-element.81.f_ref, f32[512,128]{1,0:T(8,128)S(1)} %get-tuple-element.82.w_ref, f32[416,128]{1,0:T(8,128)S(1)} %get-tuple-element.83.refs_0_, f32[416,128]{1,0:T(8,128)S(1)} %collective-permute-done.27.refs_1_, ...), custom_call_target="tpu_custom_call" | custom-call | tf_op jit(solution)/shard_map/chol_last/pallas_call | solution.py:460
  (41 shorter events, 3.2 us)
Async XLA Ops:
  0.8 10.7 %collective-permute-start.2 = (bf16[32,768]{1,0:T(8,128)(2,1)S(1)}, bf16[32,768]{1,0:T(8,128)(2,1)S(1)}, u32[]{:S(2)}, u32[]{:S(2)}) collective-permute-start(bf16[32,768]{1,0:T(8,128)(2,1)S(1)} %constant_dynamic-slice_fusion.own_ref), channel_id=1, source_target_pairs={{0,24},{8,16},{16,8},{24,0},{1,25},{9,17},{17,9},{25,1},{2,26},{10... | collective-permute-start | bytes 147464 | tf_op jit(solution)/shard_map/ppermute | solution.py:478
  5.9 5.7 %collective-permute-start.1 = (bf16[32,768]{1,0:T(8,128)(2,1)S(1)}, bf16[32,768]{1,0:T(8,128)(2,1)S(1)}, u32[]{:S(2)}, u32[]{:S(2)}) collective-permute-start(bf16[32,768]{1,0:T(8,128)(2,1)S(1)} %constant_dynamic-slice_fusion.own_ref), channel_id=1, source_target_pairs={{0,16},{8,24},{16,0},{24,8},{1,17},{9,25},{17,1},{25,9},{2,18},{10... | collective-permute-start | bytes 147464 | tf_op jit(solution)/shard_map/ppermute | solution.py:478
  5.9 5.7 %collective-permute-start = (bf16[32,768]{1,0:T(8,128)(2,1)S(1)}, bf16[32,768]{1,0:T(8,128)(2,1)S(1)}, u32[]{:S(2)}, u32[]{:S(2)}) collective-permute-start(bf16[32,768]{1,0:T(8,128)(2,1)S(1)} %constant_dynamic-slice_fusion.own_ref), channel_id=1, source_target_pairs={{0,8},{8,0},{16,24},{24,16},{1,9},{9,1},{17,25},{25,17},{2,10},{10... | collective-permute-start | bytes 147464 | tf_op jit(solution)/shard_map/ppermute | solution.py:478
  7.5 1.4 %copy-start = (bf16[1024,768]{1,0:T(8,128)(2,1)S(1)}, bf16[1024,768]{1,0:T(8,128)(2,1)}, u32[]{:S(2)}) copy-start(bf16[1024,768]{1,0:T(8,128)(2,1)} %emb_ref.5) | copy-start | bytes 4718596
  8.9 6.3 %copy-start.1 = (bf16[1024,768]{1,0:T(8,128)(2,1)S(1)}, bf16[1024,768]{1,0:T(8,128)(2,1)}, u32[]{:S(2)}) copy-start(bf16[1024,768]{1,0:T(8,128)(2,1)} %emb_ref.5) | copy-start | bytes 4718596
  11.5 11.5 %copy-start.2 = (bf16[256,768]{1,0:T(8,128)(2,1)S(1)}, bf16[256,768]{1,0:T(8,128)(2,1)}, u32[]{:S(2)}) copy-start(bf16[256,768]{1,0:T(8,128)(2,1)} %mine_ref.1) | copy-start | bytes 1179652
  11.6 7.0 %collective-permute-start.5 = (bf16[96,768]{1,0:T(8,128)(2,1)S(1)}, bf16[96,768]{1,0:T(8,128)(2,1)S(1)}, u32[]{:S(2)}, u32[]{:S(2)}) collective-permute-start(bf16[96,768]{1,0:T(8,128)(2,1)S(1)} %constant_dynamic-update-slice_fusion.refs_0_), channel_id=1, source_target_pairs={{0,6},{2,4},{4,2},{6,0},{1,7},{3,5},{5,3},{7,1},{8,14},{10,12},{12... | collective-permute-start | bytes 442376 | tf_op jit(solution)/shard_map/ppermute | solution.py:478
  14.3 6.4 %collective-permute-start.4 = (bf16[96,768]{1,0:T(8,128)(2,1)S(1)}, bf16[96,768]{1,0:T(8,128)(2,1)S(1)}, u32[]{:S(2)}, u32[]{:S(2)}) collective-permute-start(bf16[96,768]{1,0:T(8,128)(2,1)S(1)} %constant_dynamic-update-slice_fusion.refs_0_), channel_id=1, source_target_pairs={{0,4},{2,6},{4,0},{6,2},{1,5},{3,7},{5,1},{7,3},{8,12},{10,14},{12... | collective-permute-start | bytes 442376 | tf_op jit(solution)/shard_map/ppermute | solution.py:478
  14.8 6.0 %collective-permute-start.3 = (bf16[96,768]{1,0:T(8,128)(2,1)S(1)}, bf16[96,768]{1,0:T(8,128)(2,1)S(1)}, u32[]{:S(2)}, u32[]{:S(2)}) collective-permute-start(bf16[96,768]{1,0:T(8,128)(2,1)S(1)} %constant_dynamic-update-slice_fusion.refs_0_), channel_id=1, source_target_pairs={{0,2},{2,0},{4,6},{6,4},{1,3},{3,1},{5,7},{7,5},{8,10},{10,8},{12,... | collective-permute-start | bytes 442376 | tf_op jit(solution)/shard_map/ppermute | solution.py:478
  20.8 1.4 %collective-permute-start.6 = (bf16[96,768]{1,0:T(8,128)(2,1)S(1)}, bf16[96,768]{1,0:T(8,128)(2,1)S(1)}, u32[]{:S(2)}, u32[]{:S(2)}) collective-permute-start(bf16[96,768]{1,0:T(8,128)(2,1)S(1)} %constant_dynamic-update-slice_fusion.refs_0_), channel_id=1, source_target_pairs={{0,1},{1,0},{2,3},{3,2},{4,5},{5,4},{6,7},{7,6},{8,9},{9,8},{10,11... | collective-permute-start | bytes 442376 | tf_op jit(solution)/shard_map/ppermute | solution.py:478
  20.8 1.7 %collective-permute-start.7 = (bf16[96,768]{1,0:T(8,128)(2,1)S(1)}, bf16[96,768]{1,0:T(8,128)(2,1)S(1)}, u32[]{:S(2)}, u32[]{:S(2)}) collective-permute-start(bf16[96,768]{1,0:T(8,128)(2,1)S(1)} %collective-permute-done.3.refs_1_), channel_id=1, source_target_pairs={{0,1},{1,0},{2,3},{3,2},{4,5},{5,4},{6,7},{7,6},{8,9},{9,8},{10,11... | collective-permute-start | bytes 442376 | tf_op jit(solution)/shard_map/ppermute | solution.py:478
  21.3 1.5 %collective-permute-start.8 = (bf16[96,768]{1,0:T(8,128)(2,1)S(1)}, bf16[96,768]{1,0:T(8,128)(2,1)}, u32[]{:S(2)}, u32[]{:S(2)}) collective-permute-start(bf16[96,768]{1,0:T(8,128)(2,1)S(1)} %collective-permute-done.4.refs_2_), channel_id=1, source_target_pairs={{0,1},{1,0},{2,3},{3,2},{4,5},{5,4},{6,7},{7,6},{8,9},{9,8},{10,11... | collective-permute-start | bytes 442376 | tf_op jit(solution)/shard_map/ppermute | solution.py:478
  21.3 1.7 %collective-permute-start.9 = (bf16[96,768]{1,0:T(8,128)(2,1)S(1)}, bf16[96,768]{1,0:T(8,128)(2,1)}, u32[]{:S(2)}, u32[]{:S(2)}) collective-permute-start(bf16[96,768]{1,0:T(8,128)(2,1)S(1)} %collective-permute-done.5.refs_3_), channel_id=1, source_target_pairs={{0,1},{1,0},{2,3},{3,2},{4,5},{5,4},{6,7},{7,6},{8,9},{9,8},{10,11... | collective-permute-start | bytes 442376 | tf_op jit(solution)/shard_map/ppermute | solution.py:478
  39.5 2.9 %collective-permute-start.10 = (f32[2304,128]{1,0:T(8,128)S(1)}, f32[2304,128]{1,0:T(8,128)S(1)}, u32[]{:S(2)}, u32[]{:S(2)}) collective-permute-start(f32[2304,128]{1,0:T(8,128)S(1)} %get-tuple-element.59), channel_id=1, source_target_pairs={{0,1},{1,0},{2,3},{3,2},{4,5},{5,4},{6,7},{7,6},{8,9},{9,8},{10,11... | collective-permute-start | bytes 3538952 | tf_op jit(solution)/shard_map/ppermute | solution.py:478
  43.1 10.8 %collective-permute-start.11 = (f32[576,128]{1,0:T(8,128)S(1)}, f32[576,128]{1,0:T(8,128)S(1)}, u32[]{:S(2)}, u32[]{:S(2)}) collective-permute-start(f32[576,128]{1,0:T(8,128)S(1)} %get-tuple-element.61), channel_id=1, source_target_pairs={{0,6},{2,4},{4,2},{6,0},{1,7},{3,5},{5,3},{7,1},{8,14},{10,12},{12... | collective-permute-start | bytes 884744 | tf_op jit(solution)/shard_map/ppermute | solution.py:478
  44.8 14.7 %collective-permute-start.12 = (f32[576,128]{1,0:T(8,128)S(1)}, f32[576,128]{1,0:T(8,128)S(1)}, u32[]{:S(2)}, u32[]{:S(2)}) collective-permute-start(f32[576,128]{1,0:T(8,128)S(1)} %get-tuple-element.62), channel_id=1, source_target_pairs={{0,4},{2,6},{4,0},{6,2},{1,5},{3,7},{5,1},{7,3},{8,12},{10,14},{12... | collective-permute-start | bytes 884744 | tf_op jit(solution)/shard_map/ppermute | solution.py:478
  46.1 13.5 %collective-permute-start.13 = (f32[576,128]{1,0:T(8,128)S(1)}, f32[576,128]{1,0:T(8,128)S(1)}, u32[]{:S(2)}, u32[]{:S(2)}) collective-permute-start(f32[576,128]{1,0:T(8,128)S(1)} %get-tuple-element.63), channel_id=1, source_target_pairs={{0,2},{2,0},{4,6},{6,4},{1,3},{3,1},{5,7},{7,5},{8,10},{10,8},{12,... | collective-permute-start | bytes 884744 | tf_op jit(solution)/shard_map/ppermute | solution.py:478
  60.2 6.9 %collective-permute-start.14 = (f32[144,128]{1,0:T(8,128)S(1)}, f32[144,128]{1,0:T(8,128)S(1)}, u32[]{:S(2)}, u32[]{:S(2)}) collective-permute-start(f32[144,128]{1,0:T(8,128)S(1)} %get-tuple-element.65), channel_id=1, source_target_pairs={{0,24},{8,16},{16,8},{24,0},{1,25},{9,17},{17,9},{25,1},{2,26},{10... | collective-permute-start | bytes 221192 | tf_op jit(solution)/shard_map/ppermute | solution.py:478
  63.8 6.4 %collective-permute-start.15 = (f32[144,128]{1,0:T(8,128)S(1)}, f32[144,128]{1,0:T(8,128)S(1)}, u32[]{:S(2)}, u32[]{:S(2)}) collective-permute-start(f32[144,128]{1,0:T(8,128)S(1)} %get-tuple-element.66), channel_id=1, source_target_pairs={{0,16},{8,24},{16,0},{24,8},{1,17},{9,25},{17,1},{25,9},{2,18},{10... | collective-permute-start | bytes 221192 | tf_op jit(solution)/shard_map/ppermute | solution.py:478
  63.8 6.4 %collective-permute-start.16 = (f32[144,128]{1,0:T(8,128)S(1)}, f32[144,128]{1,0:T(8,128)S(1)}, u32[]{:S(2)}, u32[]{:S(2)}) collective-permute-start(f32[144,128]{1,0:T(8,128)S(1)} %get-tuple-element.67), channel_id=1, source_target_pairs={{0,8},{8,0},{16,24},{24,16},{1,9},{9,1},{17,25},{25,17},{2,10},{10... | collective-permute-start | bytes 221192 | tf_op jit(solution)/shard_map/ppermute | solution.py:478
  70.8 6.7 %collective-permute-start.19 = (f32[144,128]{1,0:T(8,128)S(1)}, f32[144,128]{1,0:T(8,128)S(1)}, u32[]{:S(2)}, u32[]{:S(2)}) collective-permute-start(f32[144,128]{1,0:T(8,128)S(1)} %add_cut.5.refs_0_), channel_id=1, source_target_pairs={{0,24},{8,16},{16,8},{24,0},{1,25},{9,17},{17,9},{25,1},{2,26},{10... | collective-permute-start | bytes 221192 | tf_op jit(solution)/shard_map/ppermute | solution.py:478
  73.3 7.0 %collective-permute-start.18 = (f32[144,128]{1,0:T(8,128)S(1)}, f32[144,128]{1,0:T(8,128)S(1)}, u32[]{:S(2)}, u32[]{:S(2)}) collective-permute-start(f32[144,128]{1,0:T(8,128)S(1)} %add_cut.5.refs_0_), channel_id=1, source_target_pairs={{0,16},{8,24},{16,0},{24,8},{1,17},{9,25},{17,1},{25,9},{2,18},{10... | collective-permute-start | bytes 221192 | tf_op jit(solution)/shard_map/ppermute | solution.py:478
  73.3 7.0 %collective-permute-start.17 = (f32[144,128]{1,0:T(8,128)S(1)}, f32[144,128]{1,0:T(8,128)S(1)}, u32[]{:S(2)}, u32[]{:S(2)}) collective-permute-start(f32[144,128]{1,0:T(8,128)S(1)} %add_cut.5.refs_0_), channel_id=1, source_target_pairs={{0,8},{8,0},{16,24},{24,16},{1,9},{9,1},{17,25},{25,17},{2,10},{10... | collective-permute-start | bytes 221192 | tf_op jit(solution)/shard_map/ppermute | solution.py:478
  80.9 6.2 %collective-permute-start.22 = (f32[160,128]{1,0:T(8,128)S(1)}, f32[160,128]{1,0:T(8,128)S(1)}, u32[]{:S(2)}, u32[]{:S(2)}) collective-permute-start(f32[160,128]{1,0:T(8,128)S(1)} %get-tuple-element.71.refs_0_), channel_id=1, source_target_pairs={{0,6},{2,4},{4,2},{6,0},{1,7},{3,5},{5,3},{7,1},{8,14},{10,12},{12... | collective-permute-start | bytes 245768 | tf_op jit(solution)/shard_map/ppermute | solution.py:478
  82.6 4.9 %collective-permute-start.21 = (f32[160,128]{1,0:T(8,128)S(1)}, f32[160,128]{1,0:T(8,128)S(1)}, u32[]{:S(2)}, u32[]{:S(2)}) collective-permute-start(f32[160,128]{1,0:T(8,128)S(1)} %get-tuple-element.71.refs_0_), channel_id=1, source_target_pairs={{0,4},{2,6},{4,0},{6,2},{1,5},{3,7},{5,1},{7,3},{8,12},{10,14},{12... | collective-permute-start | bytes 245768 | tf_op jit(solution)/shard_map/ppermute | solution.py:478
  83.9 4.4 %collective-permute-start.20 = (f32[160,128]{1,0:T(8,128)S(1)}, f32[160,128]{1,0:T(8,128)S(1)}, u32[]{:S(2)}, u32[]{:S(2)}) collective-permute-start(f32[160,128]{1,0:T(8,128)S(1)} %get-tuple-element.71.refs_0_), channel_id=1, source_target_pairs={{0,2},{2,0},{4,6},{6,4},{1,3},{3,1},{5,7},{7,5},{8,10},{10,8},{12,... | collective-permute-start | bytes 245768 | tf_op jit(solution)/shard_map/ppermute | solution.py:478
  84.4 3.9 %collective-permute-start.23 = (f32[160,128]{1,0:T(8,128)S(1)}, f32[160,128]{1,0:T(8,128)S(1)}, u32[]{:S(2)}, u32[]{:S(2)}) collective-permute-start(f32[160,128]{1,0:T(8,128)S(1)} %get-tuple-element.71.refs_0_), channel_id=1, source_target_pairs={{0,1},{1,0},{2,3},{3,2},{4,5},{5,4},{6,7},{7,6},{8,9},{9,8},{10,11... | collective-permute-start | bytes 245768 | tf_op jit(solution)/shard_map/ppermute | solution.py:478
  87.1 1.3 %collective-permute-start.26 = (f32[160,128]{1,0:T(8,128)S(1)}, f32[160,128]{1,0:T(8,128)S(1)}, u32[]{:S(2)}, u32[]{:S(2)}) collective-permute-start(f32[160,128]{1,0:T(8,128)S(1)} %collective-permute-done.22.refs_3_), channel_id=1, source_target_pairs={{0,1},{1,0},{2,3},{3,2},{4,5},{5,4},{6,7},{7,6},{8,9},{9,8},{10,11... | collective-permute-start | bytes 245768 | tf_op jit(solution)/shard_map/ppermute | solution.py:478
  87.5 1.3 %collective-permute-start.25 = (f32[160,128]{1,0:T(8,128)S(1)}, f32[160,128]{1,0:T(8,128)S(1)}, u32[]{:S(2)}, u32[]{:S(2)}) collective-permute-start(f32[160,128]{1,0:T(8,128)S(1)} %collective-permute-done.21.refs_2_), channel_id=1, source_target_pairs={{0,1},{1,0},{2,3},{3,2},{4,5},{5,4},{6,7},{7,6},{8,9},{9,8},{10,11... | collective-permute-start | bytes 245768 | tf_op jit(solution)/shard_map/ppermute | solution.py:478
  88.4 1.3 %collective-permute-start.24 = (f32[160,128]{1,0:T(8,128)S(1)}, f32[160,128]{1,0:T(8,128)S(1)}, u32[]{:S(2)}, u32[]{:S(2)}) collective-permute-start(f32[160,128]{1,0:T(8,128)S(1)} %collective-permute-done.20.refs_1_), channel_id=1, source_target_pairs={{0,1},{1,0},{2,3},{3,2},{4,5},{5,4},{6,7},{7,6},{8,9},{9,8},{10,11... | collective-permute-start | bytes 245768 | tf_op jit(solution)/shard_map/ppermute | solution.py:478
  89.6 15.8 %collective-permute-start.29 = (f32[416,128]{1,0:T(8,128)S(1)}, f32[416,128]{1,0:T(8,128)S(1)}, u32[]{:S(2)}, u32[]{:S(2)}) collective-permute-start(f32[416,128]{1,0:T(8,128)S(1)} %get-tuple-element.83.refs_0_), channel_id=1, source_target_pairs={{0,6},{2,4},{4,2},{6,0},{1,7},{3,5},{5,3},{7,1},{8,14},{10,12},{12... | collective-permute-start | bytes 638984 | tf_op jit(solution)/shard_map/ppermute | solution.py:478
  91.0 14.5 %collective-permute-start.28 = (f32[416,128]{1,0:T(8,128)S(1)}, f32[416,128]{1,0:T(8,128)S(1)}, u32[]{:S(2)}, u32[]{:S(2)}) collective-permute-start(f32[416,128]{1,0:T(8,128)S(1)} %get-tuple-element.83.refs_0_), channel_id=1, source_target_pairs={{0,4},{2,6},{4,0},{6,2},{1,5},{3,7},{5,1},{7,3},{8,12},{10,14},{12... | collective-permute-start | bytes 638984 | tf_op jit(solution)/shard_map/ppermute | solution.py:478
  91.9 13.6 %collective-permute-start.27 = (f32[416,128]{1,0:T(8,128)S(1)}, f32[416,128]{1,0:T(8,128)S(1)}, u32[]{:S(2)}, u32[]{:S(2)}) collective-permute-start(f32[416,128]{1,0:T(8,128)S(1)} %get-tuple-element.83.refs_0_), channel_id=1, source_target_pairs={{0,2},{2,0},{4,6},{6,4},{1,3},{3,1},{5,7},{7,5},{8,10},{10,8},{12,... | collective-permute-start | bytes 638984 | tf_op jit(solution)/shard_map/ppermute | solution.py:478
  105.5 1.5 %collective-permute-start.30 = (f32[416,128]{1,0:T(8,128)S(1)}, f32[416,128]{1,0:T(8,128)S(1)}, u32[]{:S(2)}, u32[]{:S(2)}) collective-permute-start(f32[416,128]{1,0:T(8,128)S(1)} %get-tuple-element.83.refs_0_), channel_id=1, source_target_pairs={{0,1},{1,0},{2,3},{3,2},{4,5},{5,4},{6,7},{7,6},{8,9},{9,8},{10,11... | collective-permute-start | bytes 638984 | tf_op jit(solution)/shard_map/ppermute | solution.py:478
  105.6 1.8 %collective-permute-start.31 = (f32[416,128]{1,0:T(8,128)S(1)}, f32[416,128]{1,0:T(8,128)S(1)}, u32[]{:S(2)}, u32[]{:S(2)}) collective-permute-start(f32[416,128]{1,0:T(8,128)S(1)} %collective-permute-done.27.refs_1_), channel_id=1, source_target_pairs={{0,1},{1,0},{2,3},{3,2},{4,5},{5,4},{6,7},{7,6},{8,9},{9,8},{10,11... | collective-permute-start | bytes 638984 | tf_op jit(solution)/shard_map/ppermute | solution.py:478
  106.1 1.6 %collective-permute-start.32 = (f32[416,128]{1,0:T(8,128)S(1)}, f32[416,128]{1,0:T(8,128)S(1)}, u32[]{:S(2)}, u32[]{:S(2)}) collective-permute-start(f32[416,128]{1,0:T(8,128)S(1)} %collective-permute-done.28.refs_2_), channel_id=1, source_target_pairs={{0,1},{1,0},{2,3},{3,2},{4,5},{5,4},{6,7},{7,6},{8,9},{9,8},{10,11... | collective-permute-start | bytes 638984 | tf_op jit(solution)/shard_map/ppermute | solution.py:478
  106.2 1.8 %collective-permute-start.33 = (f32[416,128]{1,0:T(8,128)S(1)}, f32[416,128]{1,0:T(8,128)S(1)}, u32[]{:S(2)}, u32[]{:S(2)}) collective-permute-start(f32[416,128]{1,0:T(8,128)S(1)} %collective-permute-done.29.refs_3_), channel_id=1, source_target_pairs={{0,1},{1,0},{2,3},{3,2},{4,5},{5,4},{6,7},{7,6},{8,9},{9,8},{10,11... | collective-permute-start | bytes 638984 | tf_op jit(solution)/shard_map/ppermute | solution.py:478

commit v8 on v7

--- a/solution.py
+++ b/solution.py
@@ -67,23 +67,28 @@
 CHUNK = 16
 
 
-def fill_cross(marks_ref, emb_ref, u_ref, k_ref, vq_ref, x_ref, x_row):
+def fill_cross(marks_ref, emb_ref, u_ref, k_ref, vq_ref, x_ref, chunks, rows_of):
     m, e = emb_ref.shape
-    k_ref[...] = nt(marks_ref[...], emb_ref[...])
-    vq_ref[...] = squares_mean_column(marks_ref[...])
+    rows = marks_ref.shape[0]
+    k_ref[:rows, :] = nt(marks_ref[...], emb_ref[...])
+    vq_ref[:rows, :] = squares_mean_column(marks_ref[...])
 
     def part(i, _):
-        r = pl.multiple_of(i * CHUNK, CHUNK)
+        r, to = (pl.multiple_of(at, CHUNK) for at in rows_of(i))
         vq = vq_ref[pl.ds(r, CHUNK), :]
         v_inv = lax.rsqrt(vq)
         v_root = vq * v_inv
         up = jnp.concatenate([u_ref[:8, :]] * (CHUNK // 8), axis=0)
         ur = jnp.concatenate([u_ref[8:, :]] * (CHUNK // 8), axis=0)
         c = recursion(k_ref[pl.ds(r, CHUNK), :] * up * spread(v_inv * (1.0 / e), m))
-        x_ref[pl.ds(x_row(r), CHUNK), :] = (c * ur * spread(v_root * GROWTH, m)).astype(jnp.bfloat16)
+        x_ref[pl.ds(to, CHUNK), :] = (c * ur * spread(v_root * GROWTH, m)).astype(jnp.bfloat16)
         return 0
 
-    lax.fori_loop(0, marks_ref.shape[0] // CHUNK, part, 0)
+    lax.fori_loop(0, chunks, part, 0)
+
+
+def in_order(i):
+    return i * CHUNK, i * CHUNK
 
 
 def own_kernel(marks_ref, emb_ref, x_ref, u_ref, k_ref, vq_ref):
@@ -91,29 +96,42 @@
     inv = lax.rsqrt(uq)
     u_ref[:8, :] = inv
     u_ref[8:, :] = uq * inv
-    fill_cross(marks_ref, emb_ref, u_ref, k_ref, vq_ref, x_ref, lambda r: r)
-
-
-def own_rest_kernel(marks_ref, emb_ref, u_ref, x_ref, k_ref, vq_ref):
-    fill_cross(marks_ref, emb_ref, u_ref, k_ref, vq_ref, x_ref, lambda r: r)
-
-
-def own_cross(landmarks, embeddings, u=None):
+    fill_cross(marks_ref, emb_ref, u_ref, k_ref, vq_ref, x_ref, x_ref.shape[0] // CHUNK, in_order)
+
+
+def own_cross(landmarks, embeddings):
     m = embeddings.shape[0]
     rows = landmarks.shape[0]
     vmem = pl.BlockSpec(memory_space=pltpu.VMEM)
-    x_shape = jax.ShapeDtypeStruct((rows, m), jnp.bfloat16)
-    u_shape = jax.ShapeDtypeStruct((16, m), jnp.float32)
-    given = () if u is None else (u,)
-    return pl.pallas_call(
-        own_rest_kernel if given else own_kernel,
-        out_shape=x_shape if given else (x_shape, u_shape),
-        in_specs=[vmem] * (2 + len(given)),
-        out_specs=vmem if given else (vmem, vmem),
+    return pl.pallas_call(
+        own_kernel,
+        out_shape=(jax.ShapeDtypeStruct((rows, m), jnp.bfloat16), jax.ShapeDtypeStruct((16, m), jnp.float32)),
+        in_specs=[vmem] * 2,
+        out_specs=(vmem, vmem),
         scratch_shapes=[pltpu.VMEM((rows, m), jnp.float32), pltpu.VMEM((rows, B), jnp.float32)],
         compiler_params=pltpu.CompilerParams(vmem_limit_bytes=12 << 20),
         name="own_cross",
-    )(landmarks, embeddings, *given)
+    )(landmarks, embeddings)
+
+
+def next_kernel(marks_ref, slices_ref, emb_ref, u_ref, x_ref, x_slices_ref, k_ref, vq_ref):
+    for m_ref, to_ref in ((marks_ref, x_ref), (slices_ref, x_slices_ref)):
+        fill_cross(m_ref, emb_ref, u_ref, k_ref, vq_ref, to_ref, to_ref.shape[0] // CHUNK, in_order)
+
+
+def next_cross(landmarks, slices, embeddings, u):
+    m = embeddings.shape[0]
+    rows = max(landmarks.shape[0], slices.shape[0])
+    vmem = pl.BlockSpec(memory_space=pltpu.VMEM)
+    return pl.pallas_call(
+        next_kernel,
+        out_shape=tuple(jax.ShapeDtypeStruct((x.shape[0], m), jnp.bfloat16) for x in (landmarks, slices)),
+        in_specs=[vmem] * 4,
+        out_specs=(vmem, vmem),
+        scratch_shapes=[pltpu.VMEM((rows, m), jnp.float32), pltpu.VMEM((rows, B), jnp.float32)],
+        compiler_params=pltpu.CompilerParams(vmem_limit_bytes=12 << 20),
+        name="next_cross",
+    )(landmarks, slices, embeddings, u)
 
 
 class Plan(typing.NamedTuple):
@@ -124,7 +142,7 @@
     all_points: int
 
 
-def gram_kernel(plan, na, at_ref, emb_ref, mine_ref, own_ref, u_ref, x_upper_ref, x_lower_ref, *refs):
+def gram_kernel(plan, na, at_ref, emb_ref, mine_ref, own_ref, u_ref, x_upper_ref, x_lower_ref, x_slices_ref, *refs):
     lands, chips, cores, split, all_points = plan
     count = chips * (cores if split else 1)
     far = refs[:count]
@@ -143,11 +161,19 @@
                 to = pl.multiple_of((s - 1) * shard + slot * piece, piece)
                 marks_ref[pl.ds(to, piece), :] = far[a * chips + t][(s - 1) * piece : s * piece, :]
 
-    def x_row(r):
-        s = r // shard + 1
-        return pl.multiple_of((land ^ s) * shard + r % shard, CHUNK)
-
-    fill_cross(marks_ref, emb_ref, u_ref, k_ref, vq_ref, x_ref, x_row)
+    slots = shard // piece
+    mine = chip * cores + core if split else chip
+    for s in range(1, lands):
+        to = pl.multiple_of((land ^ s) * shard + mine * piece, piece)
+        x_ref[pl.ds(to, piece), :] = x_slices_ref[(s - 1) * piece : s * piece, :]
+    steps = piece // CHUNK
+
+    def rows_of(i):
+        s, rest = i // ((slots - 1) * steps), i % ((slots - 1) * steps)
+        at = (mine ^ (rest // steps + 1)) * piece + rest % steps * CHUNK
+        return s * shard + at, (land ^ (s + 1)) * shard + at
+
+    fill_cross(marks_ref, emb_ref, u_ref, k_ref, vq_ref, x_ref, (lands - 1) * (slots - 1) * steps, rows_of)
 
     share = own_ref.shape[0]
     oq = squares_mean_column(own_ref[...])
@@ -208,7 +234,7 @@
     return packed_start(j) if j < na else packed_start(j) - packed_start(na) + segments(plan, na, j)[0]
 
 
-def local_normal(at, plan, na, embeddings, landmarks, own, u, x_upper, x_lower, far):
+def local_normal(at, plan, na, embeddings, landmarks, own, u, x_upper, x_lower, x_slices, far):
     n, m = landmarks.shape[0] * plan.lands, embeddings.shape[0]
     away = n - landmarks.shape[0]
     rows = sum(segments(plan, na, n // B))
@@ -217,7 +243,7 @@
     return pl.pallas_call(
         functools.partial(gram_kernel, plan, na),
         out_shape=(half, half),
-        in_specs=[pl.BlockSpec(memory_space=pltpu.SMEM)] + [vmem] * (6 + len(far)),
+        in_specs=[pl.BlockSpec(memory_space=pltpu.SMEM)] + [vmem] * (7 + len(far)),
         out_specs=(vmem,) * 2,
         scratch_shapes=[
             pltpu.VMEM((n, m), jnp.bfloat16),
@@ -229,7 +255,7 @@
         ],
         compiler_params=pltpu.CompilerParams(vmem_limit_bytes=24 << 20),
         name="gram",
-    )(at, embeddings, landmarks, own, u, x_upper, x_lower, *far)
+    )(at, embeddings, landmarks, own, u, x_upper, x_lower, x_slices, *far)
 
 
 def add_cut_kernel(ways, axis, parts, at_ref, *refs):
@@ -374,7 +400,7 @@
         nxt = pl.multiple_of(jnp.minimum(k + 1, nb - 1) * B, B)
         rn = r_ref[:, pl.ds(nxt, B)]
         d_ref[...] = m_ref[pl.ds(nxt, B), pl.ds(nxt, B)] - dot32_t(rn, rn)
-        store(pl.multiple_of(k * B, B), row, u, w)
+        store(k, row, u, w)
         return 0
 
     lax.fori_loop(0, nb, step, 0)
@@ -396,7 +422,8 @@
     for j in range(na):
         m_ref[: (j + 1) * B, j * B : (j + 1) * B] = a_ref[packed_start(j) : packed_start(j) + (j + 1) * B, :]
 
-    def store(at, row, u, w):
+    def store(k, row, u, w):
+        at = pl.multiple_of(k * B, B)
         f_ref[pl.ds(at, B), :] = row
         f_ref[pl.ds(at, B), pl.ds(at, B)] = u
         w_ref[pl.ds(at, B), :] = w
@@ -427,7 +454,7 @@
 
 def last_factor_kernel(plan, at_ref, f_ref, w_ref, *refs):
     count = plan.chips * plan.cores
-    o_ref, a_ref, t_ref, m_ref, d_ref, r_ref = refs[count:]
+    out_ref, o_ref, a_ref, t_ref, m_ref, d_ref, r_ref, sem = refs[count:]
     n, top = o_ref.shape[0] // B, f_ref.shape[0]
     na = top // B
     place_parts(plan, at_ref, refs[:count], a_ref)
@@ -446,12 +473,23 @@
             t_ref[(k + 1) * B :, :] = t_ref[(k + 1) * B :, :] - dot32_t(f_ref[rows, (k + 1) * B :], row)
         m_ref[...] = m_ref[...] - dot32_t(row, row)
 
-    def store(at, row, u, w):
-        down = pl.multiple_of(top + at, B)
+    head = pltpu.make_async_copy(o_ref.at[pl.ds(0, top), :], out_ref.at[pl.ds(0, top), :], sem.at[n - na])
+    head.start()
+
+    def block_row(k):
+        rows = pl.ds(pl.multiple_of(top + k * B, B), B)
+        return pltpu.make_async_copy(o_ref.at[rows, :], out_ref.at[rows, :], sem.at[k])
+
+    def store(k, row, u, w):
+        down = pl.multiple_of(top + k * B, B)
         o_ref[pl.ds(down, B), top:] = row
         o_ref[pl.ds(down, B), pl.ds(down, B)] = u
+        block_row(k).start()
 
     eliminate(n - na, m_ref, d_ref, r_ref, store)
+    for k in range(n - na):
+        block_row(k).wait()
+    head.wait()
 
 
 def last_factor(at, plan, n, f, w, parts):
@@ -461,13 +499,15 @@
         functools.partial(last_factor_kernel, plan),
         out_shape=jax.ShapeDtypeStruct((n, n), jnp.float32),
         in_specs=[pl.BlockSpec(memory_space=pltpu.SMEM)] + [vmem] * (2 + len(parts)),
-        out_specs=vmem,
+        out_specs=pl.BlockSpec(memory_space=pl.ANY),
         scratch_shapes=[
+            pltpu.VMEM((n, n), jnp.float32),
             pltpu.VMEM((parts[0].shape[0] * len(parts), B), jnp.float32),
             pltpu.VMEM((top, n - top), jnp.float32),
             pltpu.VMEM((n - top, n - top), jnp.float32),
             pltpu.VMEM((B, B), jnp.float32),
             pltpu.VMEM((B, n - top), jnp.float32),
+            pltpu.SemaphoreType.DMA(((n - top) // B + 1,)),
         ],
         compiler_params=pltpu.CompilerParams(vmem_limit_bytes=24 << 20),
         name="chol_last",
@@ -502,15 +542,16 @@
         piece = lax.dynamic_slice_in_dim(landmarks, chip * (shard // chips), shard // chips, 0)
     x_upper, u = own_cross(landmarks[: shard // 2], embeddings)
     z, x_upper, u = lax.optimization_barrier((spread_out(piece, "land")[1:], x_upper, u))
-    far = spread_out(jnp.concatenate(z, 0), "chip")
-    x_lower = own_cross(landmarks[shard // 2 :], embeddings, u)
-    far, x_lower = lax.optimization_barrier((far, x_lower))
+    slices = jnp.concatenate(z, 0)
+    far = spread_out(slices, "chip")
+    x_lower, x_slices = next_cross(landmarks[shard // 2 :], slices, embeddings, u)
+    far, x_lower, x_slices = lax.optimization_barrier((far, x_lower, x_slices))
     if plan.split:
         for a in range(1, cores):
             far = far + [swap(f, "core", a) for f in far[:chips]]
 
     na = n // B // 2
-    keep, send = local_normal(at, plan, na, embeddings, landmarks, own, u, x_upper, x_lower, far)
+    keep, send = local_normal(at, plan, na, embeddings, landmarks, own, u, x_upper, x_lower, x_slices, far)
     rows = [r // cores for r in segments(plan, na, n // B)]
     parts = scatter(add_cut(at, 1, chips, rows, [keep, swap(send, "core", 1)]), "chip")
     rows = [r // chips for r in rows]

time: 126 us -> 124 us (0.984)
  waiting for transfers between devices: 36.9 us -> 34.9 us
    ppermute x34, waiting for transfers between devices: 36.9 us -> 34.9 us  [swap(): lax.ppermute(x, axis, [(i, i ^ s) for i in range(lax.axis_size(axis))])]
    pallas_call x2, Pallas kernels: 5.13 us -> 7.11 us  [the longest x1 4.49 us: next_cross(): pl.pallas_call(next_kernel, out_shape=tuple((jax.ShapeDtypeStruct((x.shap...]
  transfers between devices with their start and end apart: 34 -> 34, of which waited for: 23 -> 22; matrix products, arithmetic and copies ran while one was open for 1% -> 1% of each run, Pallas kernels for 14% -> 16%
where the time goes in v8:
time: 124 us
  Pallas kernels  54.2 us (44%)
  waiting for transfers between devices  34.9 us (28%)
  starting transfers between devices  31.2 us (25%)
  local copies, waits for them, and re-layouts  3.28 us (3%)
    ppermute x34, waiting for transfers between devices, swap(): lax.ppermute(x, axis, [(i, i ^ s) for i in range(lax.axis_size(axis))])  34.9 us
    ppermute x34, starting transfers between devices, swap(): lax.ppermute(x, axis, [(i, i ^ s) for i in range(lax.axis_size(axis))])  31.2 us
    pallas_call x1, Pallas kernels, last_factor(): pl.pallas_call(functools.partial(last_factor_kernel, plan), out_shape=jax...  16.6 us
    pallas_call x1, Pallas kernels, local_normal(): pl.pallas_call(functools.partial(gram_kernel, plan, na), out_shape=(half,...  15.8 us
    pallas_call x1, Pallas kernels, first_factor(): pl.pallas_call(functools.partial(first_factor_kernel, plan), out_shape=(j...  12.3 us
    pallas_call x1, Pallas kernels, next_cross(): pl.pallas_call(next_kernel, out_shape=tuple((jax.ShapeDtypeStruct((x.shap...  4.49 us
    pallas_call x1, Pallas kernels, own_cross(): pl.pallas_call(own_kernel, out_shape=(jax.ShapeDtypeStruct((rows, m), jnp...  2.61 us
  transfers between devices with their start and end apart: 34, of which 22 were waited for; matrix products, arithmetic and copies ran while one was open for 1% of the time, Pallas kernels for 16%

profile of v8, /device:TPU:0, one launch (start us, length us, event | category | flops | bytes accessed | tf_op | source)
XLA Modules:
  0.0 124.0 jit_solution(9560794905644663736)
XLA Ops:
  0.0 0.8 constant_dynamic-slice_fusion.own_ref
  0.8 5.0 %collective-permute-start.2 = (bf16[32,768]{1,0:T(8,128)(2,1)S(1)}, bf16[32,768]{1,0:T(8,128)(2,1)S(1)}, u32[]{:S(2)}, u32[]{:S(2)}) collective-permute-start(bf16[32,768]{1,0:T(8,128)(2,1)S(1)} %constant_dynamic-slice_fusion.own_ref), channel_id=1, source_target_pairs={{0,24},{8,16},{16,8},{24,0},{1,25},{9,17},{17,9},{25,1},{2,26},{10... | collective-permute-start | bytes 147464 | tf_op jit(solution)/shard_map/ppermute | solution.py:518
  5.9 0.6 collective-permute-start
  6.4 1.0 fusion
  7.5 1.4 %copy-done = bf16[1024,768]{1,0:T(8,128)(2,1)S(1)} copy-done((bf16[1024,768]{1,0:T(8,128)(2,1)S(1)}, bf16[1024,768]{1,0:T(8,128)(2,1)}, u32[]{:S(2)}) %copy-start) | copy-done | bytes 1572888
  8.9 2.6 %own_cross.1 = (bf16[128,1024]{1,0:T(8,128)(2,1)S(1)}, f32[16,1024]{1,0:T(8,128)S(1)}) custom-call(bf16[128,768]{1,0:T(8,128)(2,1)S(1)} %get-tuple-element.94.marks_ref, bf16[1024,768]{1,0:T(8,128)(2,1)S(1)} %copy-done), custom_call_target="tpu_custom_call" | custom-call | tf_op jit(solution)/shard_map/own_cross/pallas_call | solution.py:106
  11.6 2.7 %collective-permute-start.5 = (bf16[96,768]{1,0:T(8,128)(2,1)S(1)}, bf16[96,768]{1,0:T(8,128)(2,1)S(1)}, u32[]{:S(2)}, u32[]{:S(2)}) collective-permute-start(bf16[96,768]{1,0:T(8,128)(2,1)S(1)} %constant_dynamic-update-slice_fusion.slices_ref.refs_0_), channel_id=1, source_target_pairs={{0,6},{2,4},{4,2},{6,0},{1,7},{3,5},{5,3},{7,1},{8,14},{10,12},{12... | collective-permute-start | bytes 442376 | tf_op jit(solution)/shard_map/ppermute | solution.py:518
  14.3 0.5 collective-permute-start.4
  15.1 4.5 %next_cross.1 = (bf16[128,1024]{1,0:T(8,128)(2,1)S(1)}, bf16[96,1024]{1,0:T(8,128)(2,1)S(1)}) custom-call(bf16[128,768]{1,0:T(8,128)(2,1)S(1)} %get-tuple-element.93.marks_ref, bf16[96,768]{1,0:T(8,128)(2,1)S(1)} %constant_dynamic-update-slice_fusion.slices_ref.refs_0_, bf16[1024,768]{1,0:T(8,128)(2,1)S(1)} %copy-done.1, f32[16,1024]{1,0:T(8,128)S(1)} %get-tuple-element.51.u_ref), custom_call_target="tpu_custom_call" | custom-call | tf_op jit(solution)/shard_map/next_cross/pallas_call | solution.py:126
  19.7 1.1 collective-permute-done.4.refs_2_
  20.8 0.5 collective-permute-start.7
  21.3 0.5 collective-permute-start.9
  21.9 0.4 collective-permute-done.6.refs_4_
  23.0 15.8 %gram.1 = (f32[2304,128]{1,0:T(8,128)S(1)}, f32[2304,128]{1,0:T(8,128)S(1)}) custom-call(s32[3]{0:T(128)S(1)} %pad_add_fusion.at_ref, bf16[1024,768]{1,0:T(8,128)(2,1)S(1)} %copy-done.1, bf16[256,768]{1,0:T(8,128)(2,1)S(1)} %copy-done.2, bf16[32,768]{1,0:T(8,128)(2,1)S(1)} %constant_dynamic-slice_fusion.own_ref, f32[16,1024]{1,0:T(8,128)S(1)} %get-tuple-element.51.u_ref, ...), custom_call_target="tpu_custom_call" | custom-call | tf_op jit(solution)/shard_map/gram/pallas_call | solution.py:243
  39.2 2.5 %collective-permute-done.10.refs_1_ = f32[2304,128]{1,0:T(8,128)S(1)} collective-permute-done((f32[2304,128]{1,0:T(8,128)S(1)}, f32[2304,128]{1,0:T(8,128)S(1)}, u32[]{:S(2)}, u32[]{:S(2)}) %collective-permute-start.10) | collective-permute-done | bytes 1179680 | tf_op jit(solution)/shard_map/ppermute | solution.py:518
  41.7 0.7 add_cut.3
  42.4 1.8 %collective-permute-start.11 = (f32[576,128]{1,0:T(8,128)S(1)}, f32[576,128]{1,0:T(8,128)S(1)}, u32[]{:S(2)}, u32[]{:S(2)}) collective-permute-start(f32[576,128]{1,0:T(8,128)S(1)} %get-tuple-element.67), channel_id=1, source_target_pairs={{0,6},{2,4},{4,2},{6,0},{1,7},{3,5},{5,3},{7,1},{8,14},{10,12},{12... | collective-permute-start | bytes 884744 | tf_op jit(solution)/shard_map/ppermute | solution.py:518
  44.1 1.3 %collective-permute-start.12 = (f32[576,128]{1,0:T(8,128)S(1)}, f32[576,128]{1,0:T(8,128)S(1)}, u32[]{:S(2)}, u32[]{:S(2)}) collective-permute-start(f32[576,128]{1,0:T(8,128)S(1)} %get-tuple-element.68), channel_id=1, source_target_pairs={{0,4},{2,6},{4,0},{6,2},{1,5},{3,7},{5,1},{7,3},{8,12},{10,14},{12... | collective-permute-start | bytes 884744 | tf_op jit(solution)/shard_map/ppermute | solution.py:518
  45.4 0.5 collective-permute-start.13
  45.9 7.3 %collective-permute-done.11.refs_1_ = f32[576,128]{1,0:T(8,128)S(1)} collective-permute-done((f32[576,128]{1,0:T(8,128)S(1)}, f32[576,128]{1,0:T(8,128)S(1)}, u32[]{:S(2)}, u32[]{:S(2)}) %collective-permute-start.11) | collective-permute-done | bytes 294944 | tf_op jit(solution)/shard_map/ppermute | solution.py:518
  53.2 5.7 %collective-permute-done.12.refs_2_ = f32[576,128]{1,0:T(8,128)S(1)} collective-permute-done((f32[576,128]{1,0:T(8,128)S(1)}, f32[576,128]{1,0:T(8,128)S(1)}, u32[]{:S(2)}, u32[]{:S(2)}) %collective-permute-start.12) | collective-permute-done | bytes 294944 | tf_op jit(solution)/shard_map/ppermute | solution.py:518
  58.9 0.6 add_cut.4
  59.5 3.6 %collective-permute-start.14 = (f32[144,128]{1,0:T(8,128)S(1)}, f32[144,128]{1,0:T(8,128)S(1)}, u32[]{:S(2)}, u32[]{:S(2)}) collective-permute-start(f32[144,128]{1,0:T(8,128)S(1)} %get-tuple-element.71), channel_id=1, source_target_pairs={{0,24},{8,16},{16,8},{24,0},{1,25},{9,17},{17,9},{25,1},{2,26},{10... | collective-permute-start | bytes 221192 | tf_op jit(solution)/shard_map/ppermute | solution.py:518
  63.1 0.9 collective-permute-start.16
  64.0 2.4 %collective-permute-done.14.refs_1_ = f32[144,128]{1,0:T(8,128)S(1)} collective-permute-done((f32[144,128]{1,0:T(8,128)S(1)}, f32[144,128]{1,0:T(8,128)S(1)}, u32[]{:S(2)}, u32[]{:S(2)}) %collective-permute-start.14) | collective-permute-done | bytes 73760 | tf_op jit(solution)/shard_map/ppermute | solution.py:518
  66.4 3.1 %collective-permute-done.15.refs_2_ = f32[144,128]{1,0:T(8,128)S(1)} collective-permute-done((f32[144,128]{1,0:T(8,128)S(1)}, f32[144,128]{1,0:T(8,128)S(1)}, u32[]{:S(2)}, u32[]{:S(2)}) %collective-permute-start.15) | collective-permute-done | bytes 73760 | tf_op jit(solution)/shard_map/ppermute | solution.py:518
  69.5 0.6 add_cut.5.refs_0_
  70.1 2.5 %collective-permute-start.19 = (f32[144,128]{1,0:T(8,128)S(1)}, f32[144,128]{1,0:T(8,128)S(1)}, u32[]{:S(2)}, u32[]{:S(2)}) collective-permute-start(f32[144,128]{1,0:T(8,128)S(1)} %add_cut.5.refs_0_), channel_id=1, source_target_pairs={{0,24},{8,16},{16,8},{24,0},{1,25},{9,17},{17,9},{25,1},{2,26},{10... | collective-permute-start | bytes 221192 | tf_op jit(solution)/shard_map/ppermute | solution.py:518
  72.6 1.9 %collective-permute-start.17 = (f32[144,128]{1,0:T(8,128)S(1)}, f32[144,128]{1,0:T(8,128)S(1)}, u32[]{:S(2)}, u32[]{:S(2)}) collective-permute-start(f32[144,128]{1,0:T(8,128)S(1)} %add_cut.5.refs_0_), channel_id=1, source_target_pairs={{0,8},{8,0},{16,24},{24,16},{1,9},{9,1},{17,25},{25,17},{2,10},{10... | collective-permute-start | bytes 221192 | tf_op jit(solution)/shard_map/ppermute | solution.py:518
  74.5 2.2 %collective-permute-done.19.refs_3_ = f32[144,128]{1,0:T(8,128)S(1)} collective-permute-done((f32[144,128]{1,0:T(8,128)S(1)}, f32[144,128]{1,0:T(8,128)S(1)}, u32[]{:S(2)}, u32[]{:S(2)}) %collective-permute-start.19) | collective-permute-done | bytes 73760 | tf_op jit(solution)/shard_map/ppermute | solution.py:518
  76.8 2.9 %collective-permute-done.18.refs_2_ = f32[144,128]{1,0:T(8,128)S(1)} collective-permute-done((f32[144,128]{1,0:T(8,128)S(1)}, f32[144,128]{1,0:T(8,128)S(1)}, u32[]{:S(2)}, u32[]{:S(2)}) %collective-permute-start.18) | collective-permute-done | bytes 73760 | tf_op jit(solution)/shard_map/ppermute | solution.py:518
  79.6 0.6 place.1
  80.2 1.7 %collective-permute-start.22 = (f32[160,128]{1,0:T(8,128)S(1)}, f32[160,128]{1,0:T(8,128)S(1)}, u32[]{:S(2)}, u32[]{:S(2)}) collective-permute-start(f32[160,128]{1,0:T(8,128)S(1)} %get-tuple-element.77.refs_0_), channel_id=1, source_target_pairs={{0,6},{2,4},{4,2},{6,0},{1,7},{3,5},{5,3},{7,1},{8,14},{10,12},{12... | collective-permute-start | bytes 245768 | tf_op jit(solution)/shard_map/ppermute | solution.py:518
  81.9 1.3 %collective-permute-start.21 = (f32[160,128]{1,0:T(8,128)S(1)}, f32[160,128]{1,0:T(8,128)S(1)}, u32[]{:S(2)}, u32[]{:S(2)}) collective-permute-start(f32[160,128]{1,0:T(8,128)S(1)} %get-tuple-element.77.refs_0_), channel_id=1, source_target_pairs={{0,4},{2,6},{4,0},{6,2},{1,5},{3,7},{5,1},{7,3},{8,12},{10,14},{12... | collective-permute-start | bytes 245768 | tf_op jit(solution)/shard_map/ppermute | solution.py:518
  83.2 0.5 collective-permute-start.20
  83.8 2.6 %collective-permute-done.22.refs_3_ = f32[160,128]{1,0:T(8,128)S(1)} collective-permute-done((f32[160,128]{1,0:T(8,128)S(1)}, f32[160,128]{1,0:T(8,128)S(1)}, u32[]{:S(2)}, u32[]{:S(2)}) %collective-permute-start.22) | collective-permute-done | bytes 81952 | tf_op jit(solution)/shard_map/ppermute | solution.py:518
  86.4 0.4 collective-permute-done.21.refs_2_
  86.9 0.8 collective-permute-done.20.refs_1_
  87.7 0.4 collective-permute-done.25.refs_6_
  88.1 0.9 collective-permute-done.24.refs_5_
  88.9 1.4 %collective-permute-start.29 = (f32[416,128]{1,0:T(8,128)S(1)}, f32[416,128]{1,0:T(8,128)S(1)}, u32[]{:S(2)}, u32[]{:S(2)}) collective-permute-start(f32[416,128]{1,0:T(8,128)S(1)} %get-tuple-element.89.refs_0_), channel_id=1, source_target_pairs={{0,6},{2,4},{4,2},{6,0},{1,7},{3,5},{5,3},{7,1},{8,14},{10,12},{12... | collective-permute-start | bytes 638984 | tf_op jit(solution)/shard_map/ppermute | solution.py:518
  90.3 0.9 collective-permute-start.28
  91.2 1.2 %collective-permute-start.27 = (f32[416,128]{1,0:T(8,128)S(1)}, f32[416,128]{1,0:T(8,128)S(1)}, u32[]{:S(2)}, u32[]{:S(2)}) collective-permute-start(f32[416,128]{1,0:T(8,128)S(1)} %get-tuple-element.89.refs_0_), channel_id=1, source_target_pairs={{0,2},{2,0},{4,6},{6,4},{1,3},{3,1},{5,7},{7,5},{8,10},{10,8},{12,... | collective-permute-start | bytes 638984 | tf_op jit(solution)/shard_map/ppermute | solution.py:518
  92.4 12.3 %chol_first.1 = (f32[512,512]{1,0:T(8,128)S(1)}, f32[512,128]{1,0:T(8,128)S(1)}) custom-call(s32[3]{0:T(128)S(1)} %pad_add_fusion.at_ref, f32[160,128]{1,0:T(8,128)S(1)} %get-tuple-element.77.refs_0_, f32[160,128]{1,0:T(8,128)S(1)} %collective-permute-done.20.refs_1_, f32[160,128]{1,0:T(8,128)S(1)} %collective-permute-done.21.refs_2_, ...), custom_call_target="tpu_custom_call" | custom-call | tf_op jit(solution)/shard_map/chol_first/pallas_call | solution.py:436
  104.9 0.5 collective-permute-start.31
  105.5 0.4 collective-permute-start.33
  105.9 0.4 collective-permute-done.30.refs_4_
  107.2 16.6 %chol_last.1 = f32[1024,1024]{1,0:T(8,128)} custom-call(s32[3]{0:T(128)S(1)} %pad_add_fusion.at_ref, f32[512,512]{1,0:T(8,128)S(1)} %get-tuple-element.87.f_ref, f32[512,128]{1,0:T(8,128)S(1)} %get-tuple-element.88.w_ref, f32[416,128]{1,0:T(8,128)S(1)} %get-tuple-element.89.refs_0_, f32[416,128]{1,0:T(8,128)S(1)} %collective-permute-done.27.refs_1_, ...), custom_call_target="tpu_custom_call" | custom-call | tf_op jit(solution)/shard_map/chol_last/pallas_call | solution.py:498
  (41 shorter events, 2.8 us)
Async XLA Ops:
  0.8 10.7 %collective-permute-start.2 = (bf16[32,768]{1,0:T(8,128)(2,1)S(1)}, bf16[32,768]{1,0:T(8,128)(2,1)S(1)}, u32[]{:S(2)}, u32[]{:S(2)}) collective-permute-start(bf16[32,768]{1,0:T(8,128)(2,1)S(1)} %constant_dynamic-slice_fusion.own_ref), channel_id=1, source_target_pairs={{0,24},{8,16},{16,8},{24,0},{1,25},{9,17},{17,9},{25,1},{2,26},{10... | collective-permute-start | bytes 147464 | tf_op jit(solution)/shard_map/ppermute | solution.py:518
  5.9 5.7 %collective-permute-start.1 = (bf16[32,768]{1,0:T(8,128)(2,1)S(1)}, bf16[32,768]{1,0:T(8,128)(2,1)S(1)}, u32[]{:S(2)}, u32[]{:S(2)}) collective-permute-start(bf16[32,768]{1,0:T(8,128)(2,1)S(1)} %constant_dynamic-slice_fusion.own_ref), channel_id=1, source_target_pairs={{0,16},{8,24},{16,0},{24,8},{1,17},{9,25},{17,1},{25,9},{2,18},{10... | collective-permute-start | bytes 147464 | tf_op jit(solution)/shard_map/ppermute | solution.py:518
  5.9 5.7 %collective-permute-start = (bf16[32,768]{1,0:T(8,128)(2,1)S(1)}, bf16[32,768]{1,0:T(8,128)(2,1)S(1)}, u32[]{:S(2)}, u32[]{:S(2)}) collective-permute-start(bf16[32,768]{1,0:T(8,128)(2,1)S(1)} %constant_dynamic-slice_fusion.own_ref), channel_id=1, source_target_pairs={{0,8},{8,0},{16,24},{24,16},{1,9},{9,1},{17,25},{25,17},{2,10},{10... | collective-permute-start | bytes 147464 | tf_op jit(solution)/shard_map/ppermute | solution.py:518
  7.5 1.4 %copy-start = (bf16[1024,768]{1,0:T(8,128)(2,1)S(1)}, bf16[1024,768]{1,0:T(8,128)(2,1)}, u32[]{:S(2)}) copy-start(bf16[1024,768]{1,0:T(8,128)(2,1)} %emb_ref.5) | copy-start | bytes 4718596
  8.9 6.3 %copy-start.1 = (bf16[1024,768]{1,0:T(8,128)(2,1)S(1)}, bf16[1024,768]{1,0:T(8,128)(2,1)}, u32[]{:S(2)}) copy-start(bf16[1024,768]{1,0:T(8,128)(2,1)} %emb_ref.5) | copy-start | bytes 4718596
  11.5 11.5 %copy-start.2 = (bf16[256,768]{1,0:T(8,128)(2,1)S(1)}, bf16[256,768]{1,0:T(8,128)(2,1)}, u32[]{:S(2)}) copy-start(bf16[256,768]{1,0:T(8,128)(2,1)} %mine_ref.1) | copy-start | bytes 1179652
  11.6 8.1 %collective-permute-start.5 = (bf16[96,768]{1,0:T(8,128)(2,1)S(1)}, bf16[96,768]{1,0:T(8,128)(2,1)S(1)}, u32[]{:S(2)}, u32[]{:S(2)}) collective-permute-start(bf16[96,768]{1,0:T(8,128)(2,1)S(1)} %constant_dynamic-update-slice_fusion.slices_ref.refs_0_), channel_id=1, source_target_pairs={{0,6},{2,4},{4,2},{6,0},{1,7},{3,5},{5,3},{7,1},{8,14},{10,12},{12... | collective-permute-start | bytes 442376 | tf_op jit(solution)/shard_map/ppermute | solution.py:518
  14.3 6.4 %collective-permute-start.4 = (bf16[96,768]{1,0:T(8,128)(2,1)S(1)}, bf16[96,768]{1,0:T(8,128)(2,1)S(1)}, u32[]{:S(2)}, u32[]{:S(2)}) collective-permute-start(bf16[96,768]{1,0:T(8,128)(2,1)S(1)} %constant_dynamic-update-slice_fusion.slices_ref.refs_0_), channel_id=1, source_target_pairs={{0,4},{2,6},{4,0},{6,2},{1,5},{3,7},{5,1},{7,3},{8,12},{10,14},{12... | collective-permute-start | bytes 442376 | tf_op jit(solution)/shard_map/ppermute | solution.py:518
  14.8 6.0 %collective-permute-start.3 = (bf16[96,768]{1,0:T(8,128)(2,1)S(1)}, bf16[96,768]{1,0:T(8,128)(2,1)S(1)}, u32[]{:S(2)}, u32[]{:S(2)}) collective-permute-start(bf16[96,768]{1,0:T(8,128)(2,1)S(1)} %constant_dynamic-update-slice_fusion.slices_ref.refs_0_), channel_id=1, source_target_pairs={{0,2},{2,0},{4,6},{6,4},{1,3},{3,1},{5,7},{7,5},{8,10},{10,8},{12,... | collective-permute-start | bytes 442376 | tf_op jit(solution)/shard_map/ppermute | solution.py:518
  20.8 1.5 %collective-permute-start.6 = (bf16[96,768]{1,0:T(8,128)(2,1)S(1)}, bf16[96,768]{1,0:T(8,128)(2,1)S(1)}, u32[]{:S(2)}, u32[]{:S(2)}) collective-permute-start(bf16[96,768]{1,0:T(8,128)(2,1)S(1)} %constant_dynamic-update-slice_fusion.slices_ref.refs_0_), channel_id=1, source_target_pairs={{0,1},{1,0},{2,3},{3,2},{4,5},{5,4},{6,7},{7,6},{8,9},{9,8},{10,11... | collective-permute-start | bytes 442376 | tf_op jit(solution)/shard_map/ppermute | solution.py:518
  20.8 1.7 %collective-permute-start.7 = (bf16[96,768]{1,0:T(8,128)(2,1)S(1)}, bf16[96,768]{1,0:T(8,128)(2,1)}, u32[]{:S(2)}, u32[]{:S(2)}) collective-permute-start(bf16[96,768]{1,0:T(8,128)(2,1)S(1)} %collective-permute-done.3.refs_1_), channel_id=1, source_target_pairs={{0,1},{1,0},{2,3},{3,2},{4,5},{5,4},{6,7},{7,6},{8,9},{9,8},{10,11... | collective-permute-start | bytes 442376 | tf_op jit(solution)/shard_map/ppermute | solution.py:518
  21.3 1.5 %collective-permute-start.8 = (bf16[96,768]{1,0:T(8,128)(2,1)S(1)}, bf16[96,768]{1,0:T(8,128)(2,1)}, u32[]{:S(2)}, u32[]{:S(2)}) collective-permute-start(bf16[96,768]{1,0:T(8,128)(2,1)S(1)} %collective-permute-done.4.refs_2_), channel_id=1, source_target_pairs={{0,1},{1,0},{2,3},{3,2},{4,5},{5,4},{6,7},{7,6},{8,9},{9,8},{10,11... | collective-permute-start | bytes 442376 | tf_op jit(solution)/shard_map/ppermute | solution.py:518
  21.3 1.7 %collective-permute-start.9 = (bf16[96,768]{1,0:T(8,128)(2,1)S(1)}, bf16[96,768]{1,0:T(8,128)(2,1)}, u32[]{:S(2)}, u32[]{:S(2)}) collective-permute-start(bf16[96,768]{1,0:T(8,128)(2,1)S(1)} %collective-permute-done.5.refs_3_), channel_id=1, source_target_pairs={{0,1},{1,0},{2,3},{3,2},{4,5},{5,4},{6,7},{7,6},{8,9},{9,8},{10,11... | collective-permute-start | bytes 442376 | tf_op jit(solution)/shard_map/ppermute | solution.py:518
  38.8 2.9 %collective-permute-start.10 = (f32[2304,128]{1,0:T(8,128)S(1)}, f32[2304,128]{1,0:T(8,128)S(1)}, u32[]{:S(2)}, u32[]{:S(2)}) collective-permute-start(f32[2304,128]{1,0:T(8,128)S(1)} %get-tuple-element.65), channel_id=1, source_target_pairs={{0,1},{1,0},{2,3},{3,2},{4,5},{5,4},{6,7},{7,6},{8,9},{9,8},{10,11... | collective-permute-start | bytes 3538952 | tf_op jit(solution)/shard_map/ppermute | solution.py:518
  42.4 10.8 %collective-permute-start.11 = (f32[576,128]{1,0:T(8,128)S(1)}, f32[576,128]{1,0:T(8,128)S(1)}, u32[]{:S(2)}, u32[]{:S(2)}) collective-permute-start(f32[576,128]{1,0:T(8,128)S(1)} %get-tuple-element.67), channel_id=1, source_target_pairs={{0,6},{2,4},{4,2},{6,0},{1,7},{3,5},{5,3},{7,1},{8,14},{10,12},{12... | collective-permute-start | bytes 884744 | tf_op jit(solution)/shard_map/ppermute | solution.py:518
  44.1 14.7 %collective-permute-start.12 = (f32[576,128]{1,0:T(8,128)S(1)}, f32[576,128]{1,0:T(8,128)S(1)}, u32[]{:S(2)}, u32[]{:S(2)}) collective-permute-start(f32[576,128]{1,0:T(8,128)S(1)} %get-tuple-element.68), channel_id=1, source_target_pairs={{0,4},{2,6},{4,0},{6,2},{1,5},{3,7},{5,1},{7,3},{8,12},{10,14},{12... | collective-permute-start | bytes 884744 | tf_op jit(solution)/shard_map/ppermute | solution.py:518
  45.4 13.5 %collective-permute-start.13 = (f32[576,128]{1,0:T(8,128)S(1)}, f32[576,128]{1,0:T(8,128)S(1)}, u32[]{:S(2)}, u32[]{:S(2)}) collective-permute-start(f32[576,128]{1,0:T(8,128)S(1)} %get-tuple-element.69), channel_id=1, source_target_pairs={{0,2},{2,0},{4,6},{6,4},{1,3},{3,1},{5,7},{7,5},{8,10},{10,8},{12,... | collective-permute-start | bytes 884744 | tf_op jit(solution)/shard_map/ppermute | solution.py:518
  59.5 6.9 %collective-permute-start.14 = (f32[144,128]{1,0:T(8,128)S(1)}, f32[144,128]{1,0:T(8,128)S(1)}, u32[]{:S(2)}, u32[]{:S(2)}) collective-permute-start(f32[144,128]{1,0:T(8,128)S(1)} %get-tuple-element.71), channel_id=1, source_target_pairs={{0,24},{8,16},{16,8},{24,0},{1,25},{9,17},{17,9},{25,1},{2,26},{10... | collective-permute-start | bytes 221192 | tf_op jit(solution)/shard_map/ppermute | solution.py:518
  63.1 6.4 %collective-permute-start.15 = (f32[144,128]{1,0:T(8,128)S(1)}, f32[144,128]{1,0:T(8,128)S(1)}, u32[]{:S(2)}, u32[]{:S(2)}) collective-permute-start(f32[144,128]{1,0:T(8,128)S(1)} %get-tuple-element.72), channel_id=1, source_target_pairs={{0,16},{8,24},{16,0},{24,8},{1,17},{9,25},{17,1},{25,9},{2,18},{10... | collective-permute-start | bytes 221192 | tf_op jit(solution)/shard_map/ppermute | solution.py:518
  63.1 6.4 %collective-permute-start.16 = (f32[144,128]{1,0:T(8,128)S(1)}, f32[144,128]{1,0:T(8,128)S(1)}, u32[]{:S(2)}, u32[]{:S(2)}) collective-permute-start(f32[144,128]{1,0:T(8,128)S(1)} %get-tuple-element.73), channel_id=1, source_target_pairs={{0,8},{8,0},{16,24},{24,16},{1,9},{9,1},{17,25},{25,17},{2,10},{10... | collective-permute-start | bytes 221192 | tf_op jit(solution)/shard_map/ppermute | solution.py:518
  70.1 6.7 %collective-permute-start.19 = (f32[144,128]{1,0:T(8,128)S(1)}, f32[144,128]{1,0:T(8,128)S(1)}, u32[]{:S(2)}, u32[]{:S(2)}) collective-permute-start(f32[144,128]{1,0:T(8,128)S(1)} %add_cut.5.refs_0_), channel_id=1, source_target_pairs={{0,24},{8,16},{16,8},{24,0},{1,25},{9,17},{17,9},{25,1},{2,26},{10... | collective-permute-start | bytes 221192 | tf_op jit(solution)/shard_map/ppermute | solution.py:518
  72.6 7.0 %collective-permute-start.18 = (f32[144,128]{1,0:T(8,128)S(1)}, f32[144,128]{1,0:T(8,128)S(1)}, u32[]{:S(2)}, u32[]{:S(2)}) collective-permute-start(f32[144,128]{1,0:T(8,128)S(1)} %add_cut.5.refs_0_), channel_id=1, source_target_pairs={{0,16},{8,24},{16,0},{24,8},{1,17},{9,25},{17,1},{25,9},{2,18},{10... | collective-permute-start | bytes 221192 | tf_op jit(solution)/shard_map/ppermute | solution.py:518
  72.6 7.0 %collective-permute-start.17 = (f32[144,128]{1,0:T(8,128)S(1)}, f32[144,128]{1,0:T(8,128)S(1)}, u32[]{:S(2)}, u32[]{:S(2)}) collective-permute-start(f32[144,128]{1,0:T(8,128)S(1)} %add_cut.5.refs_0_), channel_id=1, source_target_pairs={{0,8},{8,0},{16,24},{24,16},{1,9},{9,1},{17,25},{25,17},{2,10},{10... | collective-permute-start | bytes 221192 | tf_op jit(solution)/shard_map/ppermute | solution.py:518
  80.2 6.2 %collective-permute-start.22 = (f32[160,128]{1,0:T(8,128)S(1)}, f32[160,128]{1,0:T(8,128)S(1)}, u32[]{:S(2)}, u32[]{:S(2)}) collective-permute-start(f32[160,128]{1,0:T(8,128)S(1)} %get-tuple-element.77.refs_0_), channel_id=1, source_target_pairs={{0,6},{2,4},{4,2},{6,0},{1,7},{3,5},{5,3},{7,1},{8,14},{10,12},{12... | collective-permute-start | bytes 245768 | tf_op jit(solution)/shard_map/ppermute | solution.py:518
  81.9 4.9 %collective-permute-start.21 = (f32[160,128]{1,0:T(8,128)S(1)}, f32[160,128]{1,0:T(8,128)S(1)}, u32[]{:S(2)}, u32[]{:S(2)}) collective-permute-start(f32[160,128]{1,0:T(8,128)S(1)} %get-tuple-element.77.refs_0_), channel_id=1, source_target_pairs={{0,4},{2,6},{4,0},{6,2},{1,5},{3,7},{5,1},{7,3},{8,12},{10,14},{12... | collective-permute-start | bytes 245768 | tf_op jit(solution)/shard_map/ppermute | solution.py:518
  83.2 4.4 %collective-permute-start.20 = (f32[160,128]{1,0:T(8,128)S(1)}, f32[160,128]{1,0:T(8,128)S(1)}, u32[]{:S(2)}, u32[]{:S(2)}) collective-permute-start(f32[160,128]{1,0:T(8,128)S(1)} %get-tuple-element.77.refs_0_), channel_id=1, source_target_pairs={{0,2},{2,0},{4,6},{6,4},{1,3},{3,1},{5,7},{7,5},{8,10},{10,8},{12,... | collective-permute-start | bytes 245768 | tf_op jit(solution)/shard_map/ppermute | solution.py:518
  83.8 3.9 %collective-permute-start.23 = (f32[160,128]{1,0:T(8,128)S(1)}, f32[160,128]{1,0:T(8,128)S(1)}, u32[]{:S(2)}, u32[]{:S(2)}) collective-permute-start(f32[160,128]{1,0:T(8,128)S(1)} %get-tuple-element.77.refs_0_), channel_id=1, source_target_pairs={{0,1},{1,0},{2,3},{3,2},{4,5},{5,4},{6,7},{7,6},{8,9},{9,8},{10,11... | collective-permute-start | bytes 245768 | tf_op jit(solution)/shard_map/ppermute | solution.py:518
  86.4 1.3 %collective-permute-start.26 = (f32[160,128]{1,0:T(8,128)S(1)}, f32[160,128]{1,0:T(8,128)S(1)}, u32[]{:S(2)}, u32[]{:S(2)}) collective-permute-start(f32[160,128]{1,0:T(8,128)S(1)} %collective-permute-done.22.refs_3_), channel_id=1, source_target_pairs={{0,1},{1,0},{2,3},{3,2},{4,5},{5,4},{6,7},{7,6},{8,9},{9,8},{10,11... | collective-permute-start | bytes 245768 | tf_op jit(solution)/shard_map/ppermute | solution.py:518
  86.8 1.3 %collective-permute-start.25 = (f32[160,128]{1,0:T(8,128)S(1)}, f32[160,128]{1,0:T(8,128)S(1)}, u32[]{:S(2)}, u32[]{:S(2)}) collective-permute-start(f32[160,128]{1,0:T(8,128)S(1)} %collective-permute-done.21.refs_2_), channel_id=1, source_target_pairs={{0,1},{1,0},{2,3},{3,2},{4,5},{5,4},{6,7},{7,6},{8,9},{9,8},{10,11... | collective-permute-start | bytes 245768 | tf_op jit(solution)/shard_map/ppermute | solution.py:518
  87.7 1.3 %collective-permute-start.24 = (f32[160,128]{1,0:T(8,128)S(1)}, f32[160,128]{1,0:T(8,128)S(1)}, u32[]{:S(2)}, u32[]{:S(2)}) collective-permute-start(f32[160,128]{1,0:T(8,128)S(1)} %collective-permute-done.20.refs_1_), channel_id=1, source_target_pairs={{0,1},{1,0},{2,3},{3,2},{4,5},{5,4},{6,7},{7,6},{8,9},{9,8},{10,11... | collective-permute-start | bytes 245768 | tf_op jit(solution)/shard_map/ppermute | solution.py:518
  88.9 15.8 %collective-permute-start.29 = (f32[416,128]{1,0:T(8,128)S(1)}, f32[416,128]{1,0:T(8,128)S(1)}, u32[]{:S(2)}, u32[]{:S(2)}) collective-permute-start(f32[416,128]{1,0:T(8,128)S(1)} %get-tuple-element.89.refs_0_), channel_id=1, source_target_pairs={{0,6},{2,4},{4,2},{6,0},{1,7},{3,5},{5,3},{7,1},{8,14},{10,12},{12... | collective-permute-start | bytes 638984 | tf_op jit(solution)/shard_map/ppermute | solution.py:518
  90.3 14.4 %collective-permute-start.28 = (f32[416,128]{1,0:T(8,128)S(1)}, f32[416,128]{1,0:T(8,128)S(1)}, u32[]{:S(2)}, u32[]{:S(2)}) collective-permute-start(f32[416,128]{1,0:T(8,128)S(1)} %get-tuple-element.89.refs_0_), channel_id=1, source_target_pairs={{0,4},{2,6},{4,0},{6,2},{1,5},{3,7},{5,1},{7,3},{8,12},{10,14},{12... | collective-permute-start | bytes 638984 | tf_op jit(solution)/shard_map/ppermute | solution.py:518
  91.2 13.6 %collective-permute-start.27 = (f32[416,128]{1,0:T(8,128)S(1)}, f32[416,128]{1,0:T(8,128)S(1)}, u32[]{:S(2)}, u32[]{:S(2)}) collective-permute-start(f32[416,128]{1,0:T(8,128)S(1)} %get-tuple-element.89.refs_0_), channel_id=1, source_target_pairs={{0,2},{2,0},{4,6},{6,4},{1,3},{3,1},{5,7},{7,5},{8,10},{10,8},{12,... | collective-permute-start | bytes 638984 | tf_op jit(solution)/shard_map/ppermute | solution.py:518
  104.8 1.5 %collective-permute-start.30 = (f32[416,128]{1,0:T(8,128)S(1)}, f32[416,128]{1,0:T(8,128)S(1)}, u32[]{:S(2)}, u32[]{:S(2)}) collective-permute-start(f32[416,128]{1,0:T(8,128)S(1)} %get-tuple-element.89.refs_0_), channel_id=1, source_target_pairs={{0,1},{1,0},{2,3},{3,2},{4,5},{5,4},{6,7},{7,6},{8,9},{9,8},{10,11... | collective-permute-start | bytes 638984 | tf_op jit(solution)/shard_map/ppermute | solution.py:518
  104.9 1.8 %collective-permute-start.31 = (f32[416,128]{1,0:T(8,128)S(1)}, f32[416,128]{1,0:T(8,128)S(1)}, u32[]{:S(2)}, u32[]{:S(2)}) collective-permute-start(f32[416,128]{1,0:T(8,128)S(1)} %collective-permute-done.27.refs_1_), channel_id=1, source_target_pairs={{0,1},{1,0},{2,3},{3,2},{4,5},{5,4},{6,7},{7,6},{8,9},{9,8},{10,11... | collective-permute-start | bytes 638984 | tf_op jit(solution)/shard_map/ppermute | solution.py:518
  105.4 1.6 %collective-permute-start.32 = (f32[416,128]{1,0:T(8,128)S(1)}, f32[416,128]{1,0:T(8,128)S(1)}, u32[]{:S(2)}, u32[]{:S(2)}) collective-permute-start(f32[416,128]{1,0:T(8,128)S(1)} %collective-permute-done.28.refs_2_), channel_id=1, source_target_pairs={{0,1},{1,0},{2,3},{3,2},{4,5},{5,4},{6,7},{7,6},{8,9},{9,8},{10,11... | collective-permute-start | bytes 638984 | tf_op jit(solution)/shard_map/ppermute | solution.py:518
  105.5 1.8 %collective-permute-start.33 = (f32[416,128]{1,0:T(8,128)S(1)}, f32[416,128]{1,0:T(8,128)S(1)}, u32[]{:S(2)}, u32[]{:S(2)}) collective-permute-start(f32[416,128]{1,0:T(8,128)S(1)} %collective-permute-done.29.refs_3_), channel_id=1, source_target_pairs={{0,1},{1,0},{2,3},{3,2},{4,5},{5,4},{6,7},{7,6},{8,9},{9,8},{10,11... | collective-permute-start | bytes 638984 | tf_op jit(solution)/shard_map/ppermute | solution.py:518

commit v9 on v8

--- a/solution.py
+++ b/solution.py
@@ -329,10 +329,10 @@
 
 def factor_block(d):
     row8 = lax.broadcasted_iota(jnp.int32, (8, B), 0)
-    eye = (lax.broadcasted_iota(jnp.int32, (B, B), 0) == lax.broadcasted_iota(jnp.int32, (B, B), 1)).astype(jnp.float32)
-    left = [d[i : i + 8] for i in range(0, B, 8)]
-    right = [eye[i : i + 8] for i in range(0, B, 8)]
-    zero = left[0] * 0.0
+    lane8 = lax.broadcasted_iota(jnp.int32, (8, B), 1)
+    rows = [d[i : i + 8] for i in range(0, B, 8)]
+    factor, inverse = [None] * (B // 8), [None] * (B // 8)
+    zero = rows[0] * 0.0
     half = HALF // 8
 
     def spread_columns(x, lane):
@@ -344,23 +344,28 @@
 
     for start in range(0, B // 8, half):
         end = start + half
-        diag = spread_columns(left[start], 8 * start)
+        diag = spread_columns(rows[start], 8 * start)
         for p in range(start, end):
-            col = {r: spread_columns(left[r], 8 * p) for r in range(p + 1, end)}
-            after = spread_columns(left[p + 1], 8 * p + 8) if p + 1 < end else None
+            col = {r: spread_columns(rows[r], 8 * p) for r in range(p + 1, end)}
+            after = spread_columns(rows[p + 1], 8 * p + 8) if p + 1 < end else None
+            panel = (lane8 >= 8 * p) & (lane8 < 8 * p + 8)
+            unit = jnp.where(lane8 == row8 + 8 * p, 1.0, 0.0)
+            for r in col:
+                rows[r] = jnp.where(panel, 0.0, rows[r])
             pivots = jnp.ones((8, B), jnp.float32)
             for j in range(8):
                 pivot = splat(diag[j], j)
                 pivots = jnp.where(row8 == j, pivot, pivots)
                 inv = 1.0 / pivot
                 coef = {i: splat(diag[j], i) for i in range(j + 1, 8)}
+                row, unit_row = splat(rows[p], j), splat(unit, j)
+                both = jnp.where(panel, unit_row, row)
+                if j < 7:
+                    c = jnp.where(row8 > j, diag[j] * inv, 0.0)
+                    rows[p] = rows[p] - c * row
+                    unit = unit - c * unit_row
                 for i in coef:
                     diag[i] = diag[i] - (diag[j] * coef[i]) * inv
-                rl, rr = splat(left[p], j), splat(right[p], j)
-                if j < 7:
-                    c = jnp.where(row8 > j, diag[j] * inv, 0.0)
-                    left[p] = left[p] - c * rl
-                    right[p] = right[p] - c * rr
                 for r in col:
                     c = col[r][j] * inv
                     if r == p + 1:
@@ -368,42 +373,46 @@
                             after[i] = after[i] - c * splat(col[r][j], i)
                     for i in coef:
                         col[r][i] = col[r][i] - c * coef[i]
-                    left[r] = left[r] - c * rl
-                    right[r] = right[r] - c * rr
+                    rows[r] = rows[r] - c * both
             s = lax.rsqrt(pivots)
-            left[p] = left[p] * s
-            right[p] = right[p] * s
+            factor[p] = rows[p] * s
+            inverse[p] = jnp.where(panel, unit * s, jnp.where(lane8 < 8 * p, factor[p], 0.0))
             diag = after
         if end < B // 8:
-            ul = jnp.concatenate(left[start:end], 0)
-            u = jnp.concatenate([ul, jnp.concatenate(right[start:end], 0)], 1)
-            upd = dot32_t(ul, u)
+            u = jnp.concatenate(factor[start:end], 0)
+            w = jnp.concatenate(inverse[start:end], 0)
+            lanes = lax.broadcasted_iota(jnp.int32, w.shape, 1)
+            upd = lax.dot_general(
+                left_terms(u, 0),
+                right_terms(jnp.where(lanes < 8 * end, w, u), 0),
+                (((0,), (0,)), ((), ())),
+                preferred_element_type=jnp.float32,
+            )
             for r in range(end, B // 8):
-                left[r] = left[r] - upd[8 * r : 8 * r + 8, :B]
-                right[r] = right[r] - upd[8 * r : 8 * r + 8, B:]
+                rows[r] = jnp.where(lane8 < 8 * end, 0.0, rows[r]) - upd[8 * r : 8 * r + 8]
     tri = lax.broadcasted_iota(jnp.int32, (B, B), 0) <= lax.broadcasted_iota(jnp.int32, (B, B), 1)
-    return jnp.where(tri, jnp.concatenate(left, 0), 0.0), jnp.concatenate(right, 0)
-
-
-def eliminate(nb, m_ref, d_ref, r_ref, store):
-    lane_block = lax.broadcasted_iota(jnp.int32, (B, nb * B), 1) // B
-    d_ref[...] = m_ref[:B, :B]
-    r_ref[...] = jnp.zeros_like(r_ref)
-
-    def step(k, _):
-        u, w = factor_block(d_ref[...])
-        prev = r_ref[...]
-        m_ref[...] = m_ref[...] - dot32_t(prev, prev)
-        row = dot32(w, m_ref[pl.ds(pl.multiple_of(k * B, B), B), :])
-        row = jnp.where(lane_block > k, row, 0.0)
-        r_ref[...] = row
-        nxt = pl.multiple_of(jnp.minimum(k + 1, nb - 1) * B, B)
-        rn = r_ref[:, pl.ds(nxt, B)]
-        d_ref[...] = m_ref[pl.ds(nxt, B), pl.ds(nxt, B)] - dot32_t(rn, rn)
-        store(k, row, u, w)
-        return 0
-
-    lax.fori_loop(0, nb, step, 0)
+    return jnp.where(tri, jnp.concatenate(factor, 0), 0.0), jnp.concatenate(inverse, 0)
+
+
+def product(a_terms, b_terms):
+    return lax.dot_general(a_terms, b_terms, (((1,), (0,)), ((), ())), preferred_element_type=jnp.float32)
+
+
+def update_upper(m_ref, row, first):
+    turned, terms = left_terms(row.T, 1), right_terms(row, 0)
+    for i in range(row.shape[1] // B):
+        at = (first + i) * B
+        m_ref[at : at + B, at:] = m_ref[at : at + B, at:] - product(turned[i * B : (i + 1) * B], terms[:, i * B :])
+
+
+def eliminate(nb, m_ref, store):
+    for k in range(nb):
+        at, on = k * B, (k + 1) * B
+        u, w = factor_block(m_ref[at:on, at:on])
+        row = dot32(w, m_ref[at:on, on:]) if k < nb - 1 else None
+        store(k, u, w, row)
+        if row is not None:
+            update_upper(m_ref, row, k + 1)
 
 
 def place_parts(plan, at_ref, parts, a_ref):
@@ -416,19 +425,22 @@
 
 def first_factor_kernel(plan, at_ref, *refs):
     count = plan.chips * plan.cores
-    f_ref, w_ref, a_ref, m_ref, d_ref, r_ref = refs[count:]
+    f_ref, w_ref, a_ref, m_ref = refs[count:]
     na = f_ref.shape[0] // B
     place_parts(plan, at_ref, refs[:count], a_ref)
     for j in range(na):
         m_ref[: (j + 1) * B, j * B : (j + 1) * B] = a_ref[packed_start(j) : packed_start(j) + (j + 1) * B, :]
 
-    def store(k, row, u, w):
-        at = pl.multiple_of(k * B, B)
-        f_ref[pl.ds(at, B), :] = row
-        f_ref[pl.ds(at, B), pl.ds(at, B)] = u
-        w_ref[pl.ds(at, B), :] = w
-
-    eliminate(na, m_ref, d_ref, r_ref, store)
+    f_ref[...] = jnp.zeros_like(f_ref)
+
+    def store(k, u, w, row):
+        at, on = k * B, (k + 1) * B
+        f_ref[at:on, at:on] = u
+        w_ref[at:on, :] = w
+        if row is not None:
+            f_ref[at:on, on:] = row
+
+    eliminate(na, m_ref, store)
 
 
 def first_factor(at, plan, na, parts):
@@ -444,8 +456,6 @@
         scratch_shapes=[
             pltpu.VMEM((parts[0].shape[0] * len(parts), B), jnp.float32),
             pltpu.VMEM((na * B, na * B), jnp.float32),
-            pltpu.VMEM((B, B), jnp.float32),
-            pltpu.VMEM((B, na * B), jnp.float32),
         ],
         compiler_params=pltpu.CompilerParams(vmem_limit_bytes=16 << 20),
         name="chol_first",
@@ -454,7 +464,7 @@
 
 def last_factor_kernel(plan, at_ref, f_ref, w_ref, *refs):
     count = plan.chips * plan.cores
-    out_ref, o_ref, a_ref, t_ref, m_ref, d_ref, r_ref, sem = refs[count:]
+    out_ref, o_ref, a_ref, t_ref, m_ref, sem = refs[count:]
     n, top = o_ref.shape[0] // B, f_ref.shape[0]
     na = top // B
     place_parts(plan, at_ref, refs[:count], a_ref)
@@ -464,32 +474,31 @@
         t_ref[:, lanes] = a_ref[start : start + top, :]
         m_ref[: (j - na + 1) * B, lanes] = a_ref[start + top : start + (j + 1) * B, :]
     o_ref[:top, :top] = f_ref[...]
-    o_ref[top:, :top] = jnp.zeros((n * B - top, top), jnp.float32)
+    o_ref[top:, :] = jnp.zeros((n * B - top, n * B), jnp.float32)
     for k in range(na):
         rows = slice(k * B, (k + 1) * B)
         row = dot32(w_ref[rows, :], t_ref[rows, :])
         o_ref[rows, top:] = row
         if k < na - 1:
             t_ref[(k + 1) * B :, :] = t_ref[(k + 1) * B :, :] - dot32_t(f_ref[rows, (k + 1) * B :], row)
-        m_ref[...] = m_ref[...] - dot32_t(row, row)
+        update_upper(m_ref, row, 0)
 
     head = pltpu.make_async_copy(o_ref.at[pl.ds(0, top), :], out_ref.at[pl.ds(0, top), :], sem.at[n - na])
     head.start()
 
-    def block_row(k):
-        rows = pl.ds(pl.multiple_of(top + k * B, B), B)
-        return pltpu.make_async_copy(o_ref.at[rows, :], out_ref.at[rows, :], sem.at[k])
-
-    def store(k, row, u, w):
-        down = pl.multiple_of(top + k * B, B)
-        o_ref[pl.ds(down, B), top:] = row
-        o_ref[pl.ds(down, B), pl.ds(down, B)] = u
-        block_row(k).start()
-
-    eliminate(n - na, m_ref, d_ref, r_ref, store)
-    for k in range(n - na):
-        block_row(k).wait()
-    head.wait()
+    copies = [head]
+
+    def store(k, u, w, row):
+        at, on = top + k * B, top + (k + 1) * B
+        o_ref[at:on, at:on] = u
+        if row is not None:
+            o_ref[at:on, on:] = row
+        copies.append(pltpu.make_async_copy(o_ref.at[pl.ds(at, B), :], out_ref.at[pl.ds(at, B), :], sem.at[k]))
+        copies[-1].start()
+
+    eliminate(n - na, m_ref, store)
+    for copy in copies:
+        copy.wait()
 
 
 def last_factor(at, plan, n, f, w, parts):
@@ -505,8 +514,6 @@
             pltpu.VMEM((parts[0].shape[0] * len(parts), B), jnp.float32),
             pltpu.VMEM((top, n - top), jnp.float32),
             pltpu.VMEM((n - top, n - top), jnp.float32),
-            pltpu.VMEM((B, B), jnp.float32),
-            pltpu.VMEM((B, n - top), jnp.float32),
             pltpu.SemaphoreType.DMA(((n - top) // B + 1,)),
         ],
         compiler_params=pltpu.CompilerParams(vmem_limit_bytes=24 << 20),

time: 124 us -> 120 us (0.968)
  Pallas kernels: 54.2 us -> 50.2 us
    pallas_call x1, Pallas kernels: 12.3 us -> 10.3 us  [first_factor(): pl.pallas_call(functools.partial(first_factor_kernel, plan), out_shape=(j...]
    pallas_call x1, Pallas kernels: 16.6 us -> 14.6 us  [last_factor(): pl.pallas_call(functools.partial(last_factor_kernel, plan), out_shape=jax...]
  transfers between devices with their start and end apart: 34 -> 34, of which waited for: 22 -> 22; matrix products, arithmetic and copies ran while one was open for 1% -> 1% of each run, Pallas kernels for 16% -> 15%
where the time goes in v9:
time: 120 us
  Pallas kernels  50.2 us (42%)
  waiting for transfers between devices  34.9 us (29%)
  starting transfers between devices  31.2 us (26%)
  local copies, waits for them, and re-layouts  3.28 us (3%)
    ppermute x34, waiting for transfers between devices, swap(): lax.ppermute(x, axis, [(i, i ^ s) for i in range(lax.axis_size(axis))])  34.9 us
    ppermute x34, starting transfers between devices, swap(): lax.ppermute(x, axis, [(i, i ^ s) for i in range(lax.axis_size(axis))])  31.2 us
    pallas_call x1, Pallas kernels, local_normal(): pl.pallas_call(functools.partial(gram_kernel, plan, na), out_shape=(half,...  15.8 us
    pallas_call x1, Pallas kernels, last_factor(): pl.pallas_call(functools.partial(last_factor_kernel, plan), out_shape=jax...  14.6 us
    pallas_call x1, Pallas kernels, first_factor(): pl.pallas_call(functools.partial(first_factor_kernel, plan), out_shape=(j...  10.3 us
    pallas_call x1, Pallas kernels, next_cross(): pl.pallas_call(next_kernel, out_shape=tuple((jax.ShapeDtypeStruct((x.shap...  4.49 us
    pallas_call x1, Pallas kernels, own_cross(): pl.pallas_call(own_kernel, out_shape=(jax.ShapeDtypeStruct((rows, m), jnp...  2.61 us
  transfers between devices with their start and end apart: 34, of which 22 were waited for; matrix products, arithmetic and copies ran while one was open for 1% of the time, Pallas kernels for 15%

profile of v9, /device:TPU:0, one launch (start us, length us, event | category | flops | bytes accessed | tf_op | source)
XLA Modules:
  0.0 120.0 jit_solution(9462447525005931030)
XLA Ops:
  0.0 0.8 constant_dynamic-slice_fusion.own_ref
  0.8 5.0 %collective-permute-start.2 = (bf16[32,768]{1,0:T(8,128)(2,1)S(1)}, bf16[32,768]{1,0:T(8,128)(2,1)S(1)}, u32[]{:S(2)}, u32[]{:S(2)}) collective-permute-start(bf16[32,768]{1,0:T(8,128)(2,1)S(1)} %constant_dynamic-slice_fusion.own_ref), channel_id=1, source_target_pairs={{0,24},{8,16},{16,8},{24,0},{1,25},{9,17},{17,9},{25,1},{2,26},{10... | collective-permute-start | bytes 147464 | tf_op jit(solution)/shard_map/ppermute | solution.py:525
  5.9 0.6 collective-permute-start
  6.4 1.0 fusion
  7.5 1.4 %copy-done = bf16[1024,768]{1,0:T(8,128)(2,1)S(1)} copy-done((bf16[1024,768]{1,0:T(8,128)(2,1)S(1)}, bf16[1024,768]{1,0:T(8,128)(2,1)}, u32[]{:S(2)}) %copy-start) | copy-done | bytes 1572888
  8.9 2.6 %own_cross.1 = (bf16[128,1024]{1,0:T(8,128)(2,1)S(1)}, f32[16,1024]{1,0:T(8,128)S(1)}) custom-call(bf16[128,768]{1,0:T(8,128)(2,1)S(1)} %get-tuple-element.94.marks_ref, bf16[1024,768]{1,0:T(8,128)(2,1)S(1)} %copy-done), custom_call_target="tpu_custom_call" | custom-call | tf_op jit(solution)/shard_map/own_cross/pallas_call | solution.py:106
  11.6 2.7 %collective-permute-start.5 = (bf16[96,768]{1,0:T(8,128)(2,1)S(1)}, bf16[96,768]{1,0:T(8,128)(2,1)S(1)}, u32[]{:S(2)}, u32[]{:S(2)}) collective-permute-start(bf16[96,768]{1,0:T(8,128)(2,1)S(1)} %constant_dynamic-update-slice_fusion.slices_ref.refs_0_), channel_id=1, source_target_pairs={{0,6},{2,4},{4,2},{6,0},{1,7},{3,5},{5,3},{7,1},{8,14},{10,12},{12... | collective-permute-start | bytes 442376 | tf_op jit(solution)/shard_map/ppermute | solution.py:525
  14.3 0.5 collective-permute-start.4
  15.1 4.5 %next_cross.1 = (bf16[128,1024]{1,0:T(8,128)(2,1)S(1)}, bf16[96,1024]{1,0:T(8,128)(2,1)S(1)}) custom-call(bf16[128,768]{1,0:T(8,128)(2,1)S(1)} %get-tuple-element.93.marks_ref, bf16[96,768]{1,0:T(8,128)(2,1)S(1)} %constant_dynamic-update-slice_fusion.slices_ref.refs_0_, bf16[1024,768]{1,0:T(8,128)(2,1)S(1)} %copy-done.1, f32[16,1024]{1,0:T(8,128)S(1)} %get-tuple-element.51.u_ref), custom_call_target="tpu_custom_call" | custom-call | tf_op jit(solution)/shard_map/next_cross/pallas_call | solution.py:126
  19.7 1.1 collective-permute-done.4.refs_2_
  20.8 0.5 collective-permute-start.7
  21.3 0.5 collective-permute-start.9
  21.9 0.4 collective-permute-done.6.refs_4_
  23.0 15.8 %gram.1 = (f32[2304,128]{1,0:T(8,128)S(1)}, f32[2304,128]{1,0:T(8,128)S(1)}) custom-call(s32[3]{0:T(128)S(1)} %pad_add_fusion.at_ref, bf16[1024,768]{1,0:T(8,128)(2,1)S(1)} %copy-done.1, bf16[256,768]{1,0:T(8,128)(2,1)S(1)} %copy-done.2, bf16[32,768]{1,0:T(8,128)(2,1)S(1)} %constant_dynamic-slice_fusion.own_ref, f32[16,1024]{1,0:T(8,128)S(1)} %get-tuple-element.51.u_ref, ...), custom_call_target="tpu_custom_call" | custom-call | tf_op jit(solution)/shard_map/gram/pallas_call | solution.py:243
  39.2 2.5 %collective-permute-done.10.refs_1_ = f32[2304,128]{1,0:T(8,128)S(1)} collective-permute-done((f32[2304,128]{1,0:T(8,128)S(1)}, f32[2304,128]{1,0:T(8,128)S(1)}, u32[]{:S(2)}, u32[]{:S(2)}) %collective-permute-start.10) | collective-permute-done | bytes 1179680 | tf_op jit(solution)/shard_map/ppermute | solution.py:525
  41.7 0.7 add_cut.3
  42.4 1.8 %collective-permute-start.11 = (f32[576,128]{1,0:T(8,128)S(1)}, f32[576,128]{1,0:T(8,128)S(1)}, u32[]{:S(2)}, u32[]{:S(2)}) collective-permute-start(f32[576,128]{1,0:T(8,128)S(1)} %get-tuple-element.67), channel_id=1, source_target_pairs={{0,6},{2,4},{4,2},{6,0},{1,7},{3,5},{5,3},{7,1},{8,14},{10,12},{12... | collective-permute-start | bytes 884744 | tf_op jit(solution)/shard_map/ppermute | solution.py:525
  44.1 1.3 %collective-permute-start.12 = (f32[576,128]{1,0:T(8,128)S(1)}, f32[576,128]{1,0:T(8,128)S(1)}, u32[]{:S(2)}, u32[]{:S(2)}) collective-permute-start(f32[576,128]{1,0:T(8,128)S(1)} %get-tuple-element.68), channel_id=1, source_target_pairs={{0,4},{2,6},{4,0},{6,2},{1,5},{3,7},{5,1},{7,3},{8,12},{10,14},{12... | collective-permute-start | bytes 884744 | tf_op jit(solution)/shard_map/ppermute | solution.py:525
  45.4 0.5 collective-permute-start.13
  45.9 7.3 %collective-permute-done.11.refs_1_ = f32[576,128]{1,0:T(8,128)S(1)} collective-permute-done((f32[576,128]{1,0:T(8,128)S(1)}, f32[576,128]{1,0:T(8,128)S(1)}, u32[]{:S(2)}, u32[]{:S(2)}) %collective-permute-start.11) | collective-permute-done | bytes 294944 | tf_op jit(solution)/shard_map/ppermute | solution.py:525
  53.2 5.7 %collective-permute-done.12.refs_2_ = f32[576,128]{1,0:T(8,128)S(1)} collective-permute-done((f32[576,128]{1,0:T(8,128)S(1)}, f32[576,128]{1,0:T(8,128)S(1)}, u32[]{:S(2)}, u32[]{:S(2)}) %collective-permute-start.12) | collective-permute-done | bytes 294944 | tf_op jit(solution)/shard_map/ppermute | solution.py:525
  58.9 0.6 add_cut.4
  59.5 3.6 %collective-permute-start.14 = (f32[144,128]{1,0:T(8,128)S(1)}, f32[144,128]{1,0:T(8,128)S(1)}, u32[]{:S(2)}, u32[]{:S(2)}) collective-permute-start(f32[144,128]{1,0:T(8,128)S(1)} %get-tuple-element.71), channel_id=1, source_target_pairs={{0,24},{8,16},{16,8},{24,0},{1,25},{9,17},{17,9},{25,1},{2,26},{10... | collective-permute-start | bytes 221192 | tf_op jit(solution)/shard_map/ppermute | solution.py:525
  63.1 0.9 collective-permute-start.16
  64.0 2.4 %collective-permute-done.14.refs_1_ = f32[144,128]{1,0:T(8,128)S(1)} collective-permute-done((f32[144,128]{1,0:T(8,128)S(1)}, f32[144,128]{1,0:T(8,128)S(1)}, u32[]{:S(2)}, u32[]{:S(2)}) %collective-permute-start.14) | collective-permute-done | bytes 73760 | tf_op jit(solution)/shard_map/ppermute | solution.py:525
  66.4 3.1 %collective-permute-done.15.refs_2_ = f32[144,128]{1,0:T(8,128)S(1)} collective-permute-done((f32[144,128]{1,0:T(8,128)S(1)}, f32[144,128]{1,0:T(8,128)S(1)}, u32[]{:S(2)}, u32[]{:S(2)}) %collective-permute-start.15) | collective-permute-done | bytes 73760 | tf_op jit(solution)/shard_map/ppermute | solution.py:525
  69.5 0.6 add_cut.5.refs_0_
  70.1 2.5 %collective-permute-start.19 = (f32[144,128]{1,0:T(8,128)S(1)}, f32[144,128]{1,0:T(8,128)S(1)}, u32[]{:S(2)}, u32[]{:S(2)}) collective-permute-start(f32[144,128]{1,0:T(8,128)S(1)} %add_cut.5.refs_0_), channel_id=1, source_target_pairs={{0,24},{8,16},{16,8},{24,0},{1,25},{9,17},{17,9},{25,1},{2,26},{10... | collective-permute-start | bytes 221192 | tf_op jit(solution)/shard_map/ppermute | solution.py:525
  72.6 1.9 %collective-permute-start.17 = (f32[144,128]{1,0:T(8,128)S(1)}, f32[144,128]{1,0:T(8,128)S(1)}, u32[]{:S(2)}, u32[]{:S(2)}) collective-permute-start(f32[144,128]{1,0:T(8,128)S(1)} %add_cut.5.refs_0_), channel_id=1, source_target_pairs={{0,8},{8,0},{16,24},{24,16},{1,9},{9,1},{17,25},{25,17},{2,10},{10... | collective-permute-start | bytes 221192 | tf_op jit(solution)/shard_map/ppermute | solution.py:525
  74.5 2.2 %collective-permute-done.19.refs_3_ = f32[144,128]{1,0:T(8,128)S(1)} collective-permute-done((f32[144,128]{1,0:T(8,128)S(1)}, f32[144,128]{1,0:T(8,128)S(1)}, u32[]{:S(2)}, u32[]{:S(2)}) %collective-permute-start.19) | collective-permute-done | bytes 73760 | tf_op jit(solution)/shard_map/ppermute | solution.py:525
  76.8 2.9 %collective-permute-done.18.refs_2_ = f32[144,128]{1,0:T(8,128)S(1)} collective-permute-done((f32[144,128]{1,0:T(8,128)S(1)}, f32[144,128]{1,0:T(8,128)S(1)}, u32[]{:S(2)}, u32[]{:S(2)}) %collective-permute-start.18) | collective-permute-done | bytes 73760 | tf_op jit(solution)/shard_map/ppermute | solution.py:525
  79.6 0.6 place.1
  80.2 1.7 %collective-permute-start.22 = (f32[160,128]{1,0:T(8,128)S(1)}, f32[160,128]{1,0:T(8,128)S(1)}, u32[]{:S(2)}, u32[]{:S(2)}) collective-permute-start(f32[160,128]{1,0:T(8,128)S(1)} %get-tuple-element.77.refs_0_), channel_id=1, source_target_pairs={{0,6},{2,4},{4,2},{6,0},{1,7},{3,5},{5,3},{7,1},{8,14},{10,12},{12... | collective-permute-start | bytes 245768 | tf_op jit(solution)/shard_map/ppermute | solution.py:525
  81.9 1.3 %collective-permute-start.21 = (f32[160,128]{1,0:T(8,128)S(1)}, f32[160,128]{1,0:T(8,128)S(1)}, u32[]{:S(2)}, u32[]{:S(2)}) collective-permute-start(f32[160,128]{1,0:T(8,128)S(1)} %get-tuple-element.77.refs_0_), channel_id=1, source_target_pairs={{0,4},{2,6},{4,0},{6,2},{1,5},{3,7},{5,1},{7,3},{8,12},{10,14},{12... | collective-permute-start | bytes 245768 | tf_op jit(solution)/shard_map/ppermute | solution.py:525
  83.2 0.5 collective-permute-start.20
  83.8 2.6 %collective-permute-done.22.refs_3_ = f32[160,128]{1,0:T(8,128)S(1)} collective-permute-done((f32[160,128]{1,0:T(8,128)S(1)}, f32[160,128]{1,0:T(8,128)S(1)}, u32[]{:S(2)}, u32[]{:S(2)}) %collective-permute-start.22) | collective-permute-done | bytes 81952 | tf_op jit(solution)/shard_map/ppermute | solution.py:525
  86.4 0.4 collective-permute-done.21.refs_2_
  86.9 0.8 collective-permute-done.20.refs_1_
  87.7 0.4 collective-permute-done.25.refs_6_
  88.1 0.9 collective-permute-done.24.refs_5_
  88.9 1.4 %collective-permute-start.29 = (f32[416,128]{1,0:T(8,128)S(1)}, f32[416,128]{1,0:T(8,128)S(1)}, u32[]{:S(2)}, u32[]{:S(2)}) collective-permute-start(f32[416,128]{1,0:T(8,128)S(1)} %get-tuple-element.89.refs_0_), channel_id=1, source_target_pairs={{0,6},{2,4},{4,2},{6,0},{1,7},{3,5},{5,3},{7,1},{8,14},{10,12},{12... | collective-permute-start | bytes 638984 | tf_op jit(solution)/shard_map/ppermute | solution.py:525
  90.3 0.9 collective-permute-start.28
  91.2 1.2 %collective-permute-start.27 = (f32[416,128]{1,0:T(8,128)S(1)}, f32[416,128]{1,0:T(8,128)S(1)}, u32[]{:S(2)}, u32[]{:S(2)}) collective-permute-start(f32[416,128]{1,0:T(8,128)S(1)} %get-tuple-element.89.refs_0_), channel_id=1, source_target_pairs={{0,2},{2,0},{4,6},{6,4},{1,3},{3,1},{5,7},{7,5},{8,10},{10,8},{12,... | collective-permute-start | bytes 638984 | tf_op jit(solution)/shard_map/ppermute | solution.py:525
  92.4 10.3 %chol_first.1 = (f32[512,512]{1,0:T(8,128)S(1)}, f32[512,128]{1,0:T(8,128)S(1)}) custom-call(s32[3]{0:T(128)S(1)} %pad_add_fusion.at_ref, f32[160,128]{1,0:T(8,128)S(1)} %get-tuple-element.77.refs_0_, f32[160,128]{1,0:T(8,128)S(1)} %collective-permute-done.20.refs_1_, f32[160,128]{1,0:T(8,128)S(1)} %collective-permute-done.21.refs_2_, ...), custom_call_target="tpu_custom_call" | custom-call | tf_op jit(solution)/shard_map/chol_first/pallas_call | solution.py:448
  102.9 0.5 collective-permute-start.31
  103.4 0.4 collective-permute-start.33
  103.9 0.4 collective-permute-done.30.refs_4_
  105.2 14.6 %chol_last.1 = f32[1024,1024]{1,0:T(8,128)} custom-call(s32[3]{0:T(128)S(1)} %pad_add_fusion.at_ref, f32[512,512]{1,0:T(8,128)S(1)} %get-tuple-element.87.f_ref, f32[512,128]{1,0:T(8,128)S(1)} %get-tuple-element.88.w_ref, f32[416,128]{1,0:T(8,128)S(1)} %get-tuple-element.89.refs_0_, f32[416,128]{1,0:T(8,128)S(1)} %collective-permute-done.27.refs_1_, ...), custom_call_target="tpu_custom_call" | custom-call | tf_op jit(solution)/shard_map/chol_last/pallas_call | solution.py:507
  (41 shorter events, 2.8 us)
Async XLA Ops:
  0.8 10.7 %collective-permute-start.2 = (bf16[32,768]{1,0:T(8,128)(2,1)S(1)}, bf16[32,768]{1,0:T(8,128)(2,1)S(1)}, u32[]{:S(2)}, u32[]{:S(2)}) collective-permute-start(bf16[32,768]{1,0:T(8,128)(2,1)S(1)} %constant_dynamic-slice_fusion.own_ref), channel_id=1, source_target_pairs={{0,24},{8,16},{16,8},{24,0},{1,25},{9,17},{17,9},{25,1},{2,26},{10... | collective-permute-start | bytes 147464 | tf_op jit(solution)/shard_map/ppermute | solution.py:525
  5.9 5.7 %collective-permute-start.1 = (bf16[32,768]{1,0:T(8,128)(2,1)S(1)}, bf16[32,768]{1,0:T(8,128)(2,1)S(1)}, u32[]{:S(2)}, u32[]{:S(2)}) collective-permute-start(bf16[32,768]{1,0:T(8,128)(2,1)S(1)} %constant_dynamic-slice_fusion.own_ref), channel_id=1, source_target_pairs={{0,16},{8,24},{16,0},{24,8},{1,17},{9,25},{17,1},{25,9},{2,18},{10... | collective-permute-start | bytes 147464 | tf_op jit(solution)/shard_map/ppermute | solution.py:525
  5.9 5.7 %collective-permute-start = (bf16[32,768]{1,0:T(8,128)(2,1)S(1)}, bf16[32,768]{1,0:T(8,128)(2,1)S(1)}, u32[]{:S(2)}, u32[]{:S(2)}) collective-permute-start(bf16[32,768]{1,0:T(8,128)(2,1)S(1)} %constant_dynamic-slice_fusion.own_ref), channel_id=1, source_target_pairs={{0,8},{8,0},{16,24},{24,16},{1,9},{9,1},{17,25},{25,17},{2,10},{10... | collective-permute-start | bytes 147464 | tf_op jit(solution)/shard_map/ppermute | solution.py:525
  7.5 1.4 %copy-start = (bf16[1024,768]{1,0:T(8,128)(2,1)S(1)}, bf16[1024,768]{1,0:T(8,128)(2,1)}, u32[]{:S(2)}) copy-start(bf16[1024,768]{1,0:T(8,128)(2,1)} %emb_ref.5) | copy-start | bytes 4718596
  8.9 6.3 %copy-start.1 = (bf16[1024,768]{1,0:T(8,128)(2,1)S(1)}, bf16[1024,768]{1,0:T(8,128)(2,1)}, u32[]{:S(2)}) copy-start(bf16[1024,768]{1,0:T(8,128)(2,1)} %emb_ref.5) | copy-start | bytes 4718596
  11.5 11.5 %copy-start.2 = (bf16[256,768]{1,0:T(8,128)(2,1)S(1)}, bf16[256,768]{1,0:T(8,128)(2,1)}, u32[]{:S(2)}) copy-start(bf16[256,768]{1,0:T(8,128)(2,1)} %mine_ref.1) | copy-start | bytes 1179652
  11.6 8.1 %collective-permute-start.5 = (bf16[96,768]{1,0:T(8,128)(2,1)S(1)}, bf16[96,768]{1,0:T(8,128)(2,1)S(1)}, u32[]{:S(2)}, u32[]{:S(2)}) collective-permute-start(bf16[96,768]{1,0:T(8,128)(2,1)S(1)} %constant_dynamic-update-slice_fusion.slices_ref.refs_0_), channel_id=1, source_target_pairs={{0,6},{2,4},{4,2},{6,0},{1,7},{3,5},{5,3},{7,1},{8,14},{10,12},{12... | collective-permute-start | bytes 442376 | tf_op jit(solution)/shard_map/ppermute | solution.py:525
  14.3 6.4 %collective-permute-start.4 = (bf16[96,768]{1,0:T(8,128)(2,1)S(1)}, bf16[96,768]{1,0:T(8,128)(2,1)S(1)}, u32[]{:S(2)}, u32[]{:S(2)}) collective-permute-start(bf16[96,768]{1,0:T(8,128)(2,1)S(1)} %constant_dynamic-update-slice_fusion.slices_ref.refs_0_), channel_id=1, source_target_pairs={{0,4},{2,6},{4,0},{6,2},{1,5},{3,7},{5,1},{7,3},{8,12},{10,14},{12... | collective-permute-start | bytes 442376 | tf_op jit(solution)/shard_map/ppermute | solution.py:525
  14.8 6.0 %collective-permute-start.3 = (bf16[96,768]{1,0:T(8,128)(2,1)S(1)}, bf16[96,768]{1,0:T(8,128)(2,1)S(1)}, u32[]{:S(2)}, u32[]{:S(2)}) collective-permute-start(bf16[96,768]{1,0:T(8,128)(2,1)S(1)} %constant_dynamic-update-slice_fusion.slices_ref.refs_0_), channel_id=1, source_target_pairs={{0,2},{2,0},{4,6},{6,4},{1,3},{3,1},{5,7},{7,5},{8,10},{10,8},{12,... | collective-permute-start | bytes 442376 | tf_op jit(solution)/shard_map/ppermute | solution.py:525
  20.8 1.5 %collective-permute-start.6 = (bf16[96,768]{1,0:T(8,128)(2,1)S(1)}, bf16[96,768]{1,0:T(8,128)(2,1)S(1)}, u32[]{:S(2)}, u32[]{:S(2)}) collective-permute-start(bf16[96,768]{1,0:T(8,128)(2,1)S(1)} %constant_dynamic-update-slice_fusion.slices_ref.refs_0_), channel_id=1, source_target_pairs={{0,1},{1,0},{2,3},{3,2},{4,5},{5,4},{6,7},{7,6},{8,9},{9,8},{10,11... | collective-permute-start | bytes 442376 | tf_op jit(solution)/shard_map/ppermute | solution.py:525
  20.8 1.7 %collective-permute-start.7 = (bf16[96,768]{1,0:T(8,128)(2,1)S(1)}, bf16[96,768]{1,0:T(8,128)(2,1)}, u32[]{:S(2)}, u32[]{:S(2)}) collective-permute-start(bf16[96,768]{1,0:T(8,128)(2,1)S(1)} %collective-permute-done.3.refs_1_), channel_id=1, source_target_pairs={{0,1},{1,0},{2,3},{3,2},{4,5},{5,4},{6,7},{7,6},{8,9},{9,8},{10,11... | collective-permute-start | bytes 442376 | tf_op jit(solution)/shard_map/ppermute | solution.py:525
  21.3 1.5 %collective-permute-start.8 = (bf16[96,768]{1,0:T(8,128)(2,1)S(1)}, bf16[96,768]{1,0:T(8,128)(2,1)}, u32[]{:S(2)}, u32[]{:S(2)}) collective-permute-start(bf16[96,768]{1,0:T(8,128)(2,1)S(1)} %collective-permute-done.4.refs_2_), channel_id=1, source_target_pairs={{0,1},{1,0},{2,3},{3,2},{4,5},{5,4},{6,7},{7,6},{8,9},{9,8},{10,11... | collective-permute-start | bytes 442376 | tf_op jit(solution)/shard_map/ppermute | solution.py:525
  21.3 1.7 %collective-permute-start.9 = (bf16[96,768]{1,0:T(8,128)(2,1)S(1)}, bf16[96,768]{1,0:T(8,128)(2,1)}, u32[]{:S(2)}, u32[]{:S(2)}) collective-permute-start(bf16[96,768]{1,0:T(8,128)(2,1)S(1)} %collective-permute-done.5.refs_3_), channel_id=1, source_target_pairs={{0,1},{1,0},{2,3},{3,2},{4,5},{5,4},{6,7},{7,6},{8,9},{9,8},{10,11... | collective-permute-start | bytes 442376 | tf_op jit(solution)/shard_map/ppermute | solution.py:525
  38.8 2.9 %collective-permute-start.10 = (f32[2304,128]{1,0:T(8,128)S(1)}, f32[2304,128]{1,0:T(8,128)S(1)}, u32[]{:S(2)}, u32[]{:S(2)}) collective-permute-start(f32[2304,128]{1,0:T(8,128)S(1)} %get-tuple-element.65), channel_id=1, source_target_pairs={{0,1},{1,0},{2,3},{3,2},{4,5},{5,4},{6,7},{7,6},{8,9},{9,8},{10,11... | collective-permute-start | bytes 3538952 | tf_op jit(solution)/shard_map/ppermute | solution.py:525
  42.4 10.8 %collective-permute-start.11 = (f32[576,128]{1,0:T(8,128)S(1)}, f32[576,128]{1,0:T(8,128)S(1)}, u32[]{:S(2)}, u32[]{:S(2)}) collective-permute-start(f32[576,128]{1,0:T(8,128)S(1)} %get-tuple-element.67), channel_id=1, source_target_pairs={{0,6},{2,4},{4,2},{6,0},{1,7},{3,5},{5,3},{7,1},{8,14},{10,12},{12... | collective-permute-start | bytes 884744 | tf_op jit(solution)/shard_map/ppermute | solution.py:525
  44.1 14.7 %collective-permute-start.12 = (f32[576,128]{1,0:T(8,128)S(1)}, f32[576,128]{1,0:T(8,128)S(1)}, u32[]{:S(2)}, u32[]{:S(2)}) collective-permute-start(f32[576,128]{1,0:T(8,128)S(1)} %get-tuple-element.68), channel_id=1, source_target_pairs={{0,4},{2,6},{4,0},{6,2},{1,5},{3,7},{5,1},{7,3},{8,12},{10,14},{12... | collective-permute-start | bytes 884744 | tf_op jit(solution)/shard_map/ppermute | solution.py:525
  45.4 13.5 %collective-permute-start.13 = (f32[576,128]{1,0:T(8,128)S(1)}, f32[576,128]{1,0:T(8,128)S(1)}, u32[]{:S(2)}, u32[]{:S(2)}) collective-permute-start(f32[576,128]{1,0:T(8,128)S(1)} %get-tuple-element.69), channel_id=1, source_target_pairs={{0,2},{2,0},{4,6},{6,4},{1,3},{3,1},{5,7},{7,5},{8,10},{10,8},{12,... | collective-permute-start | bytes 884744 | tf_op jit(solution)/shard_map/ppermute | solution.py:525
  59.5 6.9 %collective-permute-start.14 = (f32[144,128]{1,0:T(8,128)S(1)}, f32[144,128]{1,0:T(8,128)S(1)}, u32[]{:S(2)}, u32[]{:S(2)}) collective-permute-start(f32[144,128]{1,0:T(8,128)S(1)} %get-tuple-element.71), channel_id=1, source_target_pairs={{0,24},{8,16},{16,8},{24,0},{1,25},{9,17},{17,9},{25,1},{2,26},{10... | collective-permute-start | bytes 221192 | tf_op jit(solution)/shard_map/ppermute | solution.py:525
  63.1 6.4 %collective-permute-start.15 = (f32[144,128]{1,0:T(8,128)S(1)}, f32[144,128]{1,0:T(8,128)S(1)}, u32[]{:S(2)}, u32[]{:S(2)}) collective-permute-start(f32[144,128]{1,0:T(8,128)S(1)} %get-tuple-element.72), channel_id=1, source_target_pairs={{0,16},{8,24},{16,0},{24,8},{1,17},{9,25},{17,1},{25,9},{2,18},{10... | collective-permute-start | bytes 221192 | tf_op jit(solution)/shard_map/ppermute | solution.py:525
  63.1 6.4 %collective-permute-start.16 = (f32[144,128]{1,0:T(8,128)S(1)}, f32[144,128]{1,0:T(8,128)S(1)}, u32[]{:S(2)}, u32[]{:S(2)}) collective-permute-start(f32[144,128]{1,0:T(8,128)S(1)} %get-tuple-element.73), channel_id=1, source_target_pairs={{0,8},{8,0},{16,24},{24,16},{1,9},{9,1},{17,25},{25,17},{2,10},{10... | collective-permute-start | bytes 221192 | tf_op jit(solution)/shard_map/ppermute | solution.py:525
  70.1 6.7 %collective-permute-start.19 = (f32[144,128]{1,0:T(8,128)S(1)}, f32[144,128]{1,0:T(8,128)S(1)}, u32[]{:S(2)}, u32[]{:S(2)}) collective-permute-start(f32[144,128]{1,0:T(8,128)S(1)} %add_cut.5.refs_0_), channel_id=1, source_target_pairs={{0,24},{8,16},{16,8},{24,0},{1,25},{9,17},{17,9},{25,1},{2,26},{10... | collective-permute-start | bytes 221192 | tf_op jit(solution)/shard_map/ppermute | solution.py:525
  72.6 7.0 %collective-permute-start.18 = (f32[144,128]{1,0:T(8,128)S(1)}, f32[144,128]{1,0:T(8,128)S(1)}, u32[]{:S(2)}, u32[]{:S(2)}) collective-permute-start(f32[144,128]{1,0:T(8,128)S(1)} %add_cut.5.refs_0_), channel_id=1, source_target_pairs={{0,16},{8,24},{16,0},{24,8},{1,17},{9,25},{17,1},{25,9},{2,18},{10... | collective-permute-start | bytes 221192 | tf_op jit(solution)/shard_map/ppermute | solution.py:525
  72.6 7.0 %collective-permute-start.17 = (f32[144,128]{1,0:T(8,128)S(1)}, f32[144,128]{1,0:T(8,128)S(1)}, u32[]{:S(2)}, u32[]{:S(2)}) collective-permute-start(f32[144,128]{1,0:T(8,128)S(1)} %add_cut.5.refs_0_), channel_id=1, source_target_pairs={{0,8},{8,0},{16,24},{24,16},{1,9},{9,1},{17,25},{25,17},{2,10},{10... | collective-permute-start | bytes 221192 | tf_op jit(solution)/shard_map/ppermute | solution.py:525
  80.2 6.2 %collective-permute-start.22 = (f32[160,128]{1,0:T(8,128)S(1)}, f32[160,128]{1,0:T(8,128)S(1)}, u32[]{:S(2)}, u32[]{:S(2)}) collective-permute-start(f32[160,128]{1,0:T(8,128)S(1)} %get-tuple-element.77.refs_0_), channel_id=1, source_target_pairs={{0,6},{2,4},{4,2},{6,0},{1,7},{3,5},{5,3},{7,1},{8,14},{10,12},{12... | collective-permute-start | bytes 245768 | tf_op jit(solution)/shard_map/ppermute | solution.py:525
  81.9 4.9 %collective-permute-start.21 = (f32[160,128]{1,0:T(8,128)S(1)}, f32[160,128]{1,0:T(8,128)S(1)}, u32[]{:S(2)}, u32[]{:S(2)}) collective-permute-start(f32[160,128]{1,0:T(8,128)S(1)} %get-tuple-element.77.refs_0_), channel_id=1, source_target_pairs={{0,4},{2,6},{4,0},{6,2},{1,5},{3,7},{5,1},{7,3},{8,12},{10,14},{12... | collective-permute-start | bytes 245768 | tf_op jit(solution)/shard_map/ppermute | solution.py:525
  83.2 4.4 %collective-permute-start.20 = (f32[160,128]{1,0:T(8,128)S(1)}, f32[160,128]{1,0:T(8,128)S(1)}, u32[]{:S(2)}, u32[]{:S(2)}) collective-permute-start(f32[160,128]{1,0:T(8,128)S(1)} %get-tuple-element.77.refs_0_), channel_id=1, source_target_pairs={{0,2},{2,0},{4,6},{6,4},{1,3},{3,1},{5,7},{7,5},{8,10},{10,8},{12,... | collective-permute-start | bytes 245768 | tf_op jit(solution)/shard_map/ppermute | solution.py:525
  83.8 3.9 %collective-permute-start.23 = (f32[160,128]{1,0:T(8,128)S(1)}, f32[160,128]{1,0:T(8,128)S(1)}, u32[]{:S(2)}, u32[]{:S(2)}) collective-permute-start(f32[160,128]{1,0:T(8,128)S(1)} %get-tuple-element.77.refs_0_), channel_id=1, source_target_pairs={{0,1},{1,0},{2,3},{3,2},{4,5},{5,4},{6,7},{7,6},{8,9},{9,8},{10,11... | collective-permute-start | bytes 245768 | tf_op jit(solution)/shard_map/ppermute | solution.py:525
  86.4 1.3 %collective-permute-start.26 = (f32[160,128]{1,0:T(8,128)S(1)}, f32[160,128]{1,0:T(8,128)S(1)}, u32[]{:S(2)}, u32[]{:S(2)}) collective-permute-start(f32[160,128]{1,0:T(8,128)S(1)} %collective-permute-done.22.refs_3_), channel_id=1, source_target_pairs={{0,1},{1,0},{2,3},{3,2},{4,5},{5,4},{6,7},{7,6},{8,9},{9,8},{10,11... | collective-permute-start | bytes 245768 | tf_op jit(solution)/shard_map/ppermute | solution.py:525
  86.8 1.3 %collective-permute-start.25 = (f32[160,128]{1,0:T(8,128)S(1)}, f32[160,128]{1,0:T(8,128)S(1)}, u32[]{:S(2)}, u32[]{:S(2)}) collective-permute-start(f32[160,128]{1,0:T(8,128)S(1)} %collective-permute-done.21.refs_2_), channel_id=1, source_target_pairs={{0,1},{1,0},{2,3},{3,2},{4,5},{5,4},{6,7},{7,6},{8,9},{9,8},{10,11... | collective-permute-start | bytes 245768 | tf_op jit(solution)/shard_map/ppermute | solution.py:525
  87.7 1.3 %collective-permute-start.24 = (f32[160,128]{1,0:T(8,128)S(1)}, f32[160,128]{1,0:T(8,128)S(1)}, u32[]{:S(2)}, u32[]{:S(2)}) collective-permute-start(f32[160,128]{1,0:T(8,128)S(1)} %collective-permute-done.20.refs_1_), channel_id=1, source_target_pairs={{0,1},{1,0},{2,3},{3,2},{4,5},{5,4},{6,7},{7,6},{8,9},{9,8},{10,11... | collective-permute-start | bytes 245768 | tf_op jit(solution)/shard_map/ppermute | solution.py:525
  88.9 13.8 %collective-permute-start.29 = (f32[416,128]{1,0:T(8,128)S(1)}, f32[416,128]{1,0:T(8,128)S(1)}, u32[]{:S(2)}, u32[]{:S(2)}) collective-permute-start(f32[416,128]{1,0:T(8,128)S(1)} %get-tuple-element.89.refs_0_), channel_id=1, source_target_pairs={{0,6},{2,4},{4,2},{6,0},{1,7},{3,5},{5,3},{7,1},{8,14},{10,12},{12... | collective-permute-start | bytes 638984 | tf_op jit(solution)/shard_map/ppermute | solution.py:525
  90.3 12.4 %collective-permute-start.28 = (f32[416,128]{1,0:T(8,128)S(1)}, f32[416,128]{1,0:T(8,128)S(1)}, u32[]{:S(2)}, u32[]{:S(2)}) collective-permute-start(f32[416,128]{1,0:T(8,128)S(1)} %get-tuple-element.89.refs_0_), channel_id=1, source_target_pairs={{0,4},{2,6},{4,0},{6,2},{1,5},{3,7},{5,1},{7,3},{8,12},{10,14},{12... | collective-permute-start | bytes 638984 | tf_op jit(solution)/shard_map/ppermute | solution.py:525
  91.2 11.6 %collective-permute-start.27 = (f32[416,128]{1,0:T(8,128)S(1)}, f32[416,128]{1,0:T(8,128)S(1)}, u32[]{:S(2)}, u32[]{:S(2)}) collective-permute-start(f32[416,128]{1,0:T(8,128)S(1)} %get-tuple-element.89.refs_0_), channel_id=1, source_target_pairs={{0,2},{2,0},{4,6},{6,4},{1,3},{3,1},{5,7},{7,5},{8,10},{10,8},{12,... | collective-permute-start | bytes 638984 | tf_op jit(solution)/shard_map/ppermute | solution.py:525
  102.8 1.5 %collective-permute-start.30 = (f32[416,128]{1,0:T(8,128)S(1)}, f32[416,128]{1,0:T(8,128)S(1)}, u32[]{:S(2)}, u32[]{:S(2)}) collective-permute-start(f32[416,128]{1,0:T(8,128)S(1)} %get-tuple-element.89.refs_0_), channel_id=1, source_target_pairs={{0,1},{1,0},{2,3},{3,2},{4,5},{5,4},{6,7},{7,6},{8,9},{9,8},{10,11... | collective-permute-start | bytes 638984 | tf_op jit(solution)/shard_map/ppermute | solution.py:525
  102.9 1.8 %collective-permute-start.31 = (f32[416,128]{1,0:T(8,128)S(1)}, f32[416,128]{1,0:T(8,128)S(1)}, u32[]{:S(2)}, u32[]{:S(2)}) collective-permute-start(f32[416,128]{1,0:T(8,128)S(1)} %collective-permute-done.27.refs_1_), channel_id=1, source_target_pairs={{0,1},{1,0},{2,3},{3,2},{4,5},{5,4},{6,7},{7,6},{8,9},{9,8},{10,11... | collective-permute-start | bytes 638984 | tf_op jit(solution)/shard_map/ppermute | solution.py:525
  103.3 1.6 %collective-permute-start.32 = (f32[416,128]{1,0:T(8,128)S(1)}, f32[416,128]{1,0:T(8,128)S(1)}, u32[]{:S(2)}, u32[]{:S(2)}) collective-permute-start(f32[416,128]{1,0:T(8,128)S(1)} %collective-permute-done.28.refs_2_), channel_id=1, source_target_pairs={{0,1},{1,0},{2,3},{3,2},{4,5},{5,4},{6,7},{7,6},{8,9},{9,8},{10,11... | collective-permute-start | bytes 638984 | tf_op jit(solution)/shard_map/ppermute | solution.py:525
  103.4 1.8 %collective-permute-start.33 = (f32[416,128]{1,0:T(8,128)S(1)}, f32[416,128]{1,0:T(8,128)S(1)}, u32[]{:S(2)}, u32[]{:S(2)}) collective-permute-start(f32[416,128]{1,0:T(8,128)S(1)} %collective-permute-done.29.refs_3_), channel_id=1, source_target_pairs={{0,1},{1,0},{2,3},{3,2},{4,5},{5,4},{6,7},{7,6},{8,9},{9,8},{10,11... | collective-permute-start | bytes 638984 | tf_op jit(solution)/shard_map/ppermute | solution.py:525

commit v10 on v9

--- a/solution.py
+++ b/solution.py
@@ -65,6 +65,7 @@
 
 
 CHUNK = 16
+LANES = 512
 
 
 def fill_cross(marks_ref, emb_ref, u_ref, k_ref, vq_ref, x_ref, chunks, rows_of):
@@ -73,18 +74,23 @@
     k_ref[:rows, :] = nt(marks_ref[...], emb_ref[...])
     vq_ref[:rows, :] = squares_mean_column(marks_ref[...])
 
+    together = max(d for d in range(1, 9) if chunks % d == 0)
+
     def part(i, _):
-        r, to = (pl.multiple_of(at, CHUNK) for at in rows_of(i))
-        vq = vq_ref[pl.ds(r, CHUNK), :]
-        v_inv = lax.rsqrt(vq)
-        v_root = vq * v_inv
-        up = jnp.concatenate([u_ref[:8, :]] * (CHUNK // 8), axis=0)
-        ur = jnp.concatenate([u_ref[8:, :]] * (CHUNK // 8), axis=0)
-        c = recursion(k_ref[pl.ds(r, CHUNK), :] * up * spread(v_inv * (1.0 / e), m))
-        x_ref[pl.ds(to, CHUNK), :] = (c * ur * spread(v_root * GROWTH, m)).astype(jnp.bfloat16)
+        for q in range(together):
+            r, to = (pl.multiple_of(at, CHUNK) for at in rows_of(i * together + q))
+            vq = vq_ref[pl.ds(r, CHUNK), :]
+            v_inv = lax.rsqrt(vq)
+            v_in, v_out = v_inv * (1.0 / e), vq * v_inv * GROWTH
+            for l in range(0, m, LANES):
+                lanes = slice(l, l + LANES)
+                up = jnp.concatenate([u_ref[:8, lanes]] * (CHUNK // 8), axis=0)
+                ur = jnp.concatenate([u_ref[8:, lanes]] * (CHUNK // 8), axis=0)
+                c = recursion(k_ref[pl.ds(r, CHUNK), lanes] * up * spread(v_in, LANES))
+                x_ref[pl.ds(to, CHUNK), lanes] = (c * ur * spread(v_out, LANES)).astype(jnp.bfloat16)
         return 0
 
-    lax.fori_loop(0, chunks, part, 0)
+    lax.fori_loop(0, chunks // together, part, 0)
 
 
 def in_order(i):

time: 120 us -> 118 us (0.983)
  Pallas kernels: 50.2 us -> 47.4 us
    pallas_call x1, Pallas kernels: 15.8 us -> 14.2 us  [local_normal(): pl.pallas_call(functools.partial(gram_kernel, plan, na), out_shape=(half,...]
  transfers between devices with their start and end apart: 34 -> 34, of which waited for: 22 -> 22; matrix products, arithmetic and copies ran while one was open for 1% -> 1% of each run, Pallas kernels for 15% -> 14%
where the time goes in v10:
time: 118 us
  Pallas kernels  47.4 us (40%)
  waiting for transfers between devices  35.8 us (30%)
  starting transfers between devices  31.2 us (26%)
  local copies, waits for them, and re-layouts  3.28 us (3%)
    ppermute x34, waiting for transfers between devices, swap(): lax.ppermute(x, axis, [(i, i ^ s) for i in range(lax.axis_size(axis))])  35.8 us
    ppermute x34, starting transfers between devices, swap(): lax.ppermute(x, axis, [(i, i ^ s) for i in range(lax.axis_size(axis))])  31.2 us
    pallas_call x1, Pallas kernels, last_factor(): pl.pallas_call(functools.partial(last_factor_kernel, plan), out_shape=jax...  14.6 us
    pallas_call x1, Pallas kernels, local_normal(): pl.pallas_call(functools.partial(gram_kernel, plan, na), out_shape=(half,...  14.2 us
    pallas_call x1, Pallas kernels, first_factor(): pl.pallas_call(functools.partial(first_factor_kernel, plan), out_shape=(j...  10.3 us
    pallas_call x1, Pallas kernels, next_cross(): pl.pallas_call(next_kernel, out_shape=tuple((jax.ShapeDtypeStruct((x.shap...  3.6 us
  transfers between devices with their start and end apart: 34, of which 22 were waited for; matrix products, arithmetic and copies ran while one was open for 1% of the time, Pallas kernels for 14%

profile of v10, /device:TPU:0, one launch (start us, length us, event | category | flops | bytes accessed | tf_op | source)
XLA Modules:
  0.0 118.1 jit_solution(12771715874030122733)
XLA Ops:
  0.0 0.8 constant_dynamic-slice_fusion.own_ref
  0.8 5.0 %collective-permute-start.2 = (bf16[32,768]{1,0:T(8,128)(2,1)S(1)}, bf16[32,768]{1,0:T(8,128)(2,1)S(1)}, u32[]{:S(2)}, u32[]{:S(2)}) collective-permute-start(bf16[32,768]{1,0:T(8,128)(2,1)S(1)} %constant_dynamic-slice_fusion.own_ref), channel_id=1, source_target_pairs={{0,24},{8,16},{16,8},{24,0},{1,25},{9,17},{17,9},{25,1},{2,26},{10... | collective-permute-start | bytes 147464 | tf_op jit(solution)/shard_map/ppermute | solution.py:531
  5.9 0.6 collective-permute-start
  6.4 1.0 fusion
  7.5 1.4 %copy-done = bf16[1024,768]{1,0:T(8,128)(2,1)S(1)} copy-done((bf16[1024,768]{1,0:T(8,128)(2,1)S(1)}, bf16[1024,768]{1,0:T(8,128)(2,1)}, u32[]{:S(2)}) %copy-start) | copy-done | bytes 1572888
  8.9 2.2 %own_cross.1 = (bf16[128,1024]{1,0:T(8,128)(2,1)S(1)}, f32[16,1024]{1,0:T(8,128)S(1)}) custom-call(bf16[128,768]{1,0:T(8,128)(2,1)S(1)} %get-tuple-element.94.marks_ref, bf16[1024,768]{1,0:T(8,128)(2,1)S(1)} %copy-done), custom_call_target="tpu_custom_call" | custom-call | tf_op jit(solution)/shard_map/own_cross/pallas_call | solution.py:112
  11.2 2.7 %collective-permute-start.5 = (bf16[96,768]{1,0:T(8,128)(2,1)S(1)}, bf16[96,768]{1,0:T(8,128)(2,1)S(1)}, u32[]{:S(2)}, u32[]{:S(2)}) collective-permute-start(bf16[96,768]{1,0:T(8,128)(2,1)S(1)} %constant_dynamic-update-slice_fusion.slices_ref.refs_0_), channel_id=1, source_target_pairs={{0,6},{2,4},{4,2},{6,0},{1,7},{3,5},{5,3},{7,1},{8,14},{10,12},{12... | collective-permute-start | bytes 442376 | tf_op jit(solution)/shard_map/ppermute | solution.py:531
  13.9 0.5 collective-permute-start.4
  14.8 3.6 %next_cross.1 = (bf16[128,1024]{1,0:T(8,128)(2,1)S(1)}, bf16[96,1024]{1,0:T(8,128)(2,1)S(1)}) custom-call(bf16[128,768]{1,0:T(8,128)(2,1)S(1)} %get-tuple-element.93.marks_ref, bf16[96,768]{1,0:T(8,128)(2,1)S(1)} %constant_dynamic-update-slice_fusion.slices_ref.refs_0_, bf16[1024,768]{1,0:T(8,128)(2,1)S(1)} %copy-done.1, f32[16,1024]{1,0:T(8,128)S(1)} %get-tuple-element.51.u_ref), custom_call_target="tpu_custom_call" | custom-call | tf_op jit(solution)/shard_map/next_cross/pallas_call | solution.py:132
  18.4 2.0 %collective-permute-done.4.refs_2_ = bf16[96,768]{1,0:T(8,128)(2,1)S(1)} collective-permute-done((bf16[96,768]{1,0:T(8,128)(2,1)S(1)}, bf16[96,768]{1,0:T(8,128)(2,1)S(1)}, u32[]{:S(2)}, u32[]{:S(2)}) %collective-permute-start.4) | collective-permute-done | bytes 147488 | tf_op jit(solution)/shard_map/ppermute | solution.py:531
  20.4 0.5 collective-permute-start.7
  20.9 0.5 collective-permute-start.9
  21.5 0.4 collective-permute-done.6.refs_4_
  22.6 14.2 %gram.1 = (f32[2304,128]{1,0:T(8,128)S(1)}, f32[2304,128]{1,0:T(8,128)S(1)}) custom-call(s32[3]{0:T(128)S(1)} %pad_add_fusion.at_ref, bf16[1024,768]{1,0:T(8,128)(2,1)S(1)} %copy-done.1, bf16[256,768]{1,0:T(8,128)(2,1)S(1)} %copy-done.2, bf16[32,768]{1,0:T(8,128)(2,1)S(1)} %constant_dynamic-slice_fusion.own_ref, f32[16,1024]{1,0:T(8,128)S(1)} %get-tuple-element.51.u_ref, ...), custom_call_target="tpu_custom_call" | custom-call | tf_op jit(solution)/shard_map/gram/pallas_call | solution.py:249
  37.2 2.5 %collective-permute-done.10.refs_1_ = f32[2304,128]{1,0:T(8,128)S(1)} collective-permute-done((f32[2304,128]{1,0:T(8,128)S(1)}, f32[2304,128]{1,0:T(8,128)S(1)}, u32[]{:S(2)}, u32[]{:S(2)}) %collective-permute-start.10) | collective-permute-done | bytes 1179680 | tf_op jit(solution)/shard_map/ppermute | solution.py:531
  39.8 0.7 add_cut.3
  40.4 1.7 %collective-permute-start.11 = (f32[576,128]{1,0:T(8,128)S(1)}, f32[576,128]{1,0:T(8,128)S(1)}, u32[]{:S(2)}, u32[]{:S(2)}) collective-permute-start(f32[576,128]{1,0:T(8,128)S(1)} %get-tuple-element.67), channel_id=1, source_target_pairs={{0,6},{2,4},{4,2},{6,0},{1,7},{3,5},{5,3},{7,1},{8,14},{10,12},{12... | collective-permute-start | bytes 884744 | tf_op jit(solution)/shard_map/ppermute | solution.py:531
  42.2 1.3 %collective-permute-start.12 = (f32[576,128]{1,0:T(8,128)S(1)}, f32[576,128]{1,0:T(8,128)S(1)}, u32[]{:S(2)}, u32[]{:S(2)}) collective-permute-start(f32[576,128]{1,0:T(8,128)S(1)} %get-tuple-element.68), channel_id=1, source_target_pairs={{0,4},{2,6},{4,0},{6,2},{1,5},{3,7},{5,1},{7,3},{8,12},{10,14},{12... | collective-permute-start | bytes 884744 | tf_op jit(solution)/shard_map/ppermute | solution.py:531
  43.5 0.5 collective-permute-start.13
  44.0 7.3 %collective-permute-done.11.refs_1_ = f32[576,128]{1,0:T(8,128)S(1)} collective-permute-done((f32[576,128]{1,0:T(8,128)S(1)}, f32[576,128]{1,0:T(8,128)S(1)}, u32[]{:S(2)}, u32[]{:S(2)}) %collective-permute-start.11) | collective-permute-done | bytes 294944 | tf_op jit(solution)/shard_map/ppermute | solution.py:531
  51.3 5.7 %collective-permute-done.12.refs_2_ = f32[576,128]{1,0:T(8,128)S(1)} collective-permute-done((f32[576,128]{1,0:T(8,128)S(1)}, f32[576,128]{1,0:T(8,128)S(1)}, u32[]{:S(2)}, u32[]{:S(2)}) %collective-permute-start.12) | collective-permute-done | bytes 294944 | tf_op jit(solution)/shard_map/ppermute | solution.py:531
  57.0 0.6 add_cut.4
  57.6 3.6 %collective-permute-start.14 = (f32[144,128]{1,0:T(8,128)S(1)}, f32[144,128]{1,0:T(8,128)S(1)}, u32[]{:S(2)}, u32[]{:S(2)}) collective-permute-start(f32[144,128]{1,0:T(8,128)S(1)} %get-tuple-element.71), channel_id=1, source_target_pairs={{0,24},{8,16},{16,8},{24,0},{1,25},{9,17},{17,9},{25,1},{2,26},{10... | collective-permute-start | bytes 221192 | tf_op jit(solution)/shard_map/ppermute | solution.py:531
  61.2 0.9 collective-permute-start.16
  62.1 2.4 %collective-permute-done.14.refs_1_ = f32[144,128]{1,0:T(8,128)S(1)} collective-permute-done((f32[144,128]{1,0:T(8,128)S(1)}, f32[144,128]{1,0:T(8,128)S(1)}, u32[]{:S(2)}, u32[]{:S(2)}) %collective-permute-start.14) | collective-permute-done | bytes 73760 | tf_op jit(solution)/shard_map/ppermute | solution.py:531
  64.5 3.1 %collective-permute-done.15.refs_2_ = f32[144,128]{1,0:T(8,128)S(1)} collective-permute-done((f32[144,128]{1,0:T(8,128)S(1)}, f32[144,128]{1,0:T(8,128)S(1)}, u32[]{:S(2)}, u32[]{:S(2)}) %collective-permute-start.15) | collective-permute-done | bytes 73760 | tf_op jit(solution)/shard_map/ppermute | solution.py:531
  67.6 0.6 add_cut.5.refs_0_
  68.1 2.5 %collective-permute-start.19 = (f32[144,128]{1,0:T(8,128)S(1)}, f32[144,128]{1,0:T(8,128)S(1)}, u32[]{:S(2)}, u32[]{:S(2)}) collective-permute-start(f32[144,128]{1,0:T(8,128)S(1)} %add_cut.5.refs_0_), channel_id=1, source_target_pairs={{0,24},{8,16},{16,8},{24,0},{1,25},{9,17},{17,9},{25,1},{2,26},{10... | collective-permute-start | bytes 221192 | tf_op jit(solution)/shard_map/ppermute | solution.py:531
  70.6 1.9 %collective-permute-start.17 = (f32[144,128]{1,0:T(8,128)S(1)}, f32[144,128]{1,0:T(8,128)S(1)}, u32[]{:S(2)}, u32[]{:S(2)}) collective-permute-start(f32[144,128]{1,0:T(8,128)S(1)} %add_cut.5.refs_0_), channel_id=1, source_target_pairs={{0,8},{8,0},{16,24},{24,16},{1,9},{9,1},{17,25},{25,17},{2,10},{10... | collective-permute-start | bytes 221192 | tf_op jit(solution)/shard_map/ppermute | solution.py:531
  72.6 2.2 %collective-permute-done.19.refs_3_ = f32[144,128]{1,0:T(8,128)S(1)} collective-permute-done((f32[144,128]{1,0:T(8,128)S(1)}, f32[144,128]{1,0:T(8,128)S(1)}, u32[]{:S(2)}, u32[]{:S(2)}) %collective-permute-start.19) | collective-permute-done | bytes 73760 | tf_op jit(solution)/shard_map/ppermute | solution.py:531
  74.8 2.9 %collective-permute-done.18.refs_2_ = f32[144,128]{1,0:T(8,128)S(1)} collective-permute-done((f32[144,128]{1,0:T(8,128)S(1)}, f32[144,128]{1,0:T(8,128)S(1)}, u32[]{:S(2)}, u32[]{:S(2)}) %collective-permute-start.18) | collective-permute-done | bytes 73760 | tf_op jit(solution)/shard_map/ppermute | solution.py:531
  77.7 0.6 place.1
  78.3 1.7 %collective-permute-start.22 = (f32[160,128]{1,0:T(8,128)S(1)}, f32[160,128]{1,0:T(8,128)S(1)}, u32[]{:S(2)}, u32[]{:S(2)}) collective-permute-start(f32[160,128]{1,0:T(8,128)S(1)} %get-tuple-element.77.refs_0_), channel_id=1, source_target_pairs={{0,6},{2,4},{4,2},{6,0},{1,7},{3,5},{5,3},{7,1},{8,14},{10,12},{12... | collective-permute-start | bytes 245768 | tf_op jit(solution)/shard_map/ppermute | solution.py:531
  80.0 1.3 %collective-permute-start.21 = (f32[160,128]{1,0:T(8,128)S(1)}, f32[160,128]{1,0:T(8,128)S(1)}, u32[]{:S(2)}, u32[]{:S(2)}) collective-permute-start(f32[160,128]{1,0:T(8,128)S(1)} %get-tuple-element.77.refs_0_), channel_id=1, source_target_pairs={{0,4},{2,6},{4,0},{6,2},{1,5},{3,7},{5,1},{7,3},{8,12},{10,14},{12... | collective-permute-start | bytes 245768 | tf_op jit(solution)/shard_map/ppermute | solution.py:531
  81.3 0.5 collective-permute-start.20
  81.8 2.6 %collective-permute-done.22.refs_3_ = f32[160,128]{1,0:T(8,128)S(1)} collective-permute-done((f32[160,128]{1,0:T(8,128)S(1)}, f32[160,128]{1,0:T(8,128)S(1)}, u32[]{:S(2)}, u32[]{:S(2)}) %collective-permute-start.22) | collective-permute-done | bytes 81952 | tf_op jit(solution)/shard_map/ppermute | solution.py:531
  84.4 0.4 collective-permute-done.21.refs_2_
  85.0 0.8 collective-permute-done.20.refs_1_
  85.7 0.4 collective-permute-done.25.refs_6_
  86.2 0.9 collective-permute-done.24.refs_5_
  87.0 1.4 %collective-permute-start.29 = (f32[416,128]{1,0:T(8,128)S(1)}, f32[416,128]{1,0:T(8,128)S(1)}, u32[]{:S(2)}, u32[]{:S(2)}) collective-permute-start(f32[416,128]{1,0:T(8,128)S(1)} %get-tuple-element.89.refs_0_), channel_id=1, source_target_pairs={{0,6},{2,4},{4,2},{6,0},{1,7},{3,5},{5,3},{7,1},{8,14},{10,12},{12... | collective-permute-start | bytes 638984 | tf_op jit(solution)/shard_map/ppermute | solution.py:531
  88.4 0.9 collective-permute-start.28
  89.3 1.2 %collective-permute-start.27 = (f32[416,128]{1,0:T(8,128)S(1)}, f32[416,128]{1,0:T(8,128)S(1)}, u32[]{:S(2)}, u32[]{:S(2)}) collective-permute-start(f32[416,128]{1,0:T(8,128)S(1)} %get-tuple-element.89.refs_0_), channel_id=1, source_target_pairs={{0,2},{2,0},{4,6},{6,4},{1,3},{3,1},{5,7},{7,5},{8,10},{10,8},{12,... | collective-permute-start | bytes 638984 | tf_op jit(solution)/shard_map/ppermute | solution.py:531
  90.5 10.3 %chol_first.1 = (f32[512,512]{1,0:T(8,128)S(1)}, f32[512,128]{1,0:T(8,128)S(1)}) custom-call(s32[3]{0:T(128)S(1)} %pad_add_fusion.at_ref, f32[160,128]{1,0:T(8,128)S(1)} %get-tuple-element.77.refs_0_, f32[160,128]{1,0:T(8,128)S(1)} %collective-permute-done.20.refs_1_, f32[160,128]{1,0:T(8,128)S(1)} %collective-permute-done.21.refs_2_, ...), custom_call_target="tpu_custom_call" | custom-call | tf_op jit(solution)/shard_map/chol_first/pallas_call | solution.py:454
  100.9 0.5 collective-permute-start.31
  101.5 0.4 collective-permute-start.33
  101.9 0.4 collective-permute-done.30.refs_4_
  103.3 14.6 %chol_last.1 = f32[1024,1024]{1,0:T(8,128)} custom-call(s32[3]{0:T(128)S(1)} %pad_add_fusion.at_ref, f32[512,512]{1,0:T(8,128)S(1)} %get-tuple-element.87.f_ref, f32[512,128]{1,0:T(8,128)S(1)} %get-tuple-element.88.w_ref, f32[416,128]{1,0:T(8,128)S(1)} %get-tuple-element.89.refs_0_, f32[416,128]{1,0:T(8,128)S(1)} %collective-permute-done.27.refs_1_, ...), custom_call_target="tpu_custom_call" | custom-call | tf_op jit(solution)/shard_map/chol_last/pallas_call | solution.py:513
  (41 shorter events, 2.8 us)
Async XLA Ops:
  0.8 10.3 %collective-permute-start.2 = (bf16[32,768]{1,0:T(8,128)(2,1)S(1)}, bf16[32,768]{1,0:T(8,128)(2,1)S(1)}, u32[]{:S(2)}, u32[]{:S(2)}) collective-permute-start(bf16[32,768]{1,0:T(8,128)(2,1)S(1)} %constant_dynamic-slice_fusion.own_ref), channel_id=1, source_target_pairs={{0,24},{8,16},{16,8},{24,0},{1,25},{9,17},{17,9},{25,1},{2,26},{10... | collective-permute-start | bytes 147464 | tf_op jit(solution)/shard_map/ppermute | solution.py:531
  5.9 5.3 %collective-permute-start.1 = (bf16[32,768]{1,0:T(8,128)(2,1)S(1)}, bf16[32,768]{1,0:T(8,128)(2,1)S(1)}, u32[]{:S(2)}, u32[]{:S(2)}) collective-permute-start(bf16[32,768]{1,0:T(8,128)(2,1)S(1)} %constant_dynamic-slice_fusion.own_ref), channel_id=1, source_target_pairs={{0,16},{8,24},{16,0},{24,8},{1,17},{9,25},{17,1},{25,9},{2,18},{10... | collective-permute-start | bytes 147464 | tf_op jit(solution)/shard_map/ppermute | solution.py:531
  5.9 5.3 %collective-permute-start = (bf16[32,768]{1,0:T(8,128)(2,1)S(1)}, bf16[32,768]{1,0:T(8,128)(2,1)S(1)}, u32[]{:S(2)}, u32[]{:S(2)}) collective-permute-start(bf16[32,768]{1,0:T(8,128)(2,1)S(1)} %constant_dynamic-slice_fusion.own_ref), channel_id=1, source_target_pairs={{0,8},{8,0},{16,24},{24,16},{1,9},{9,1},{17,25},{25,17},{2,10},{10... | collective-permute-start | bytes 147464 | tf_op jit(solution)/shard_map/ppermute | solution.py:531
  7.5 1.4 %copy-start = (bf16[1024,768]{1,0:T(8,128)(2,1)S(1)}, bf16[1024,768]{1,0:T(8,128)(2,1)}, u32[]{:S(2)}) copy-start(bf16[1024,768]{1,0:T(8,128)(2,1)} %emb_ref.5) | copy-start | bytes 4718596
  8.9 5.9 %copy-start.1 = (bf16[1024,768]{1,0:T(8,128)(2,1)S(1)}, bf16[1024,768]{1,0:T(8,128)(2,1)}, u32[]{:S(2)}) copy-start(bf16[1024,768]{1,0:T(8,128)(2,1)} %emb_ref.5) | copy-start | bytes 4718596
  11.1 11.5 %copy-start.2 = (bf16[256,768]{1,0:T(8,128)(2,1)S(1)}, bf16[256,768]{1,0:T(8,128)(2,1)}, u32[]{:S(2)}) copy-start(bf16[256,768]{1,0:T(8,128)(2,1)} %mine_ref.1) | copy-start | bytes 1179652
  11.2 7.2 %collective-permute-start.5 = (bf16[96,768]{1,0:T(8,128)(2,1)S(1)}, bf16[96,768]{1,0:T(8,128)(2,1)S(1)}, u32[]{:S(2)}, u32[]{:S(2)}) collective-permute-start(bf16[96,768]{1,0:T(8,128)(2,1)S(1)} %constant_dynamic-update-slice_fusion.slices_ref.refs_0_), channel_id=1, source_target_pairs={{0,6},{2,4},{4,2},{6,0},{1,7},{3,5},{5,3},{7,1},{8,14},{10,12},{12... | collective-permute-start | bytes 442376 | tf_op jit(solution)/shard_map/ppermute | solution.py:531
  13.9 6.4 %collective-permute-start.4 = (bf16[96,768]{1,0:T(8,128)(2,1)S(1)}, bf16[96,768]{1,0:T(8,128)(2,1)S(1)}, u32[]{:S(2)}, u32[]{:S(2)}) collective-permute-start(bf16[96,768]{1,0:T(8,128)(2,1)S(1)} %constant_dynamic-update-slice_fusion.slices_ref.refs_0_), channel_id=1, source_target_pairs={{0,4},{2,6},{4,0},{6,2},{1,5},{3,7},{5,1},{7,3},{8,12},{10,14},{12... | collective-permute-start | bytes 442376 | tf_op jit(solution)/shard_map/ppermute | solution.py:531
  14.4 6.0 %collective-permute-start.3 = (bf16[96,768]{1,0:T(8,128)(2,1)S(1)}, bf16[96,768]{1,0:T(8,128)(2,1)S(1)}, u32[]{:S(2)}, u32[]{:S(2)}) collective-permute-start(bf16[96,768]{1,0:T(8,128)(2,1)S(1)} %constant_dynamic-update-slice_fusion.slices_ref.refs_0_), channel_id=1, source_target_pairs={{0,2},{2,0},{4,6},{6,4},{1,3},{3,1},{5,7},{7,5},{8,10},{10,8},{12,... | collective-permute-start | bytes 442376 | tf_op jit(solution)/shard_map/ppermute | solution.py:531
  20.4 1.5 %collective-permute-start.6 = (bf16[96,768]{1,0:T(8,128)(2,1)S(1)}, bf16[96,768]{1,0:T(8,128)(2,1)S(1)}, u32[]{:S(2)}, u32[]{:S(2)}) collective-permute-start(bf16[96,768]{1,0:T(8,128)(2,1)S(1)} %constant_dynamic-update-slice_fusion.slices_ref.refs_0_), channel_id=1, source_target_pairs={{0,1},{1,0},{2,3},{3,2},{4,5},{5,4},{6,7},{7,6},{8,9},{9,8},{10,11... | collective-permute-start | bytes 442376 | tf_op jit(solution)/shard_map/ppermute | solution.py:531
  20.4 1.7 %collective-permute-start.7 = (bf16[96,768]{1,0:T(8,128)(2,1)S(1)}, bf16[96,768]{1,0:T(8,128)(2,1)}, u32[]{:S(2)}, u32[]{:S(2)}) collective-permute-start(bf16[96,768]{1,0:T(8,128)(2,1)S(1)} %collective-permute-done.3.refs_1_), channel_id=1, source_target_pairs={{0,1},{1,0},{2,3},{3,2},{4,5},{5,4},{6,7},{7,6},{8,9},{9,8},{10,11... | collective-permute-start | bytes 442376 | tf_op jit(solution)/shard_map/ppermute | solution.py:531
  20.9 1.5 %collective-permute-start.8 = (bf16[96,768]{1,0:T(8,128)(2,1)S(1)}, bf16[96,768]{1,0:T(8,128)(2,1)}, u32[]{:S(2)}, u32[]{:S(2)}) collective-permute-start(bf16[96,768]{1,0:T(8,128)(2,1)S(1)} %collective-permute-done.4.refs_2_), channel_id=1, source_target_pairs={{0,1},{1,0},{2,3},{3,2},{4,5},{5,4},{6,7},{7,6},{8,9},{9,8},{10,11... | collective-permute-start | bytes 442376 | tf_op jit(solution)/shard_map/ppermute | solution.py:531
  20.9 1.7 %collective-permute-start.9 = (bf16[96,768]{1,0:T(8,128)(2,1)S(1)}, bf16[96,768]{1,0:T(8,128)(2,1)}, u32[]{:S(2)}, u32[]{:S(2)}) collective-permute-start(bf16[96,768]{1,0:T(8,128)(2,1)S(1)} %collective-permute-done.5.refs_3_), channel_id=1, source_target_pairs={{0,1},{1,0},{2,3},{3,2},{4,5},{5,4},{6,7},{7,6},{8,9},{9,8},{10,11... | collective-permute-start | bytes 442376 | tf_op jit(solution)/shard_map/ppermute | solution.py:531
  36.9 2.9 %collective-permute-start.10 = (f32[2304,128]{1,0:T(8,128)S(1)}, f32[2304,128]{1,0:T(8,128)S(1)}, u32[]{:S(2)}, u32[]{:S(2)}) collective-permute-start(f32[2304,128]{1,0:T(8,128)S(1)} %get-tuple-element.65), channel_id=1, source_target_pairs={{0,1},{1,0},{2,3},{3,2},{4,5},{5,4},{6,7},{7,6},{8,9},{9,8},{10,11... | collective-permute-start | bytes 3538952 | tf_op jit(solution)/shard_map/ppermute | solution.py:531
  40.4 10.8 %collective-permute-start.11 = (f32[576,128]{1,0:T(8,128)S(1)}, f32[576,128]{1,0:T(8,128)S(1)}, u32[]{:S(2)}, u32[]{:S(2)}) collective-permute-start(f32[576,128]{1,0:T(8,128)S(1)} %get-tuple-element.67), channel_id=1, source_target_pairs={{0,6},{2,4},{4,2},{6,0},{1,7},{3,5},{5,3},{7,1},{8,14},{10,12},{12... | collective-permute-start | bytes 884744 | tf_op jit(solution)/shard_map/ppermute | solution.py:531
  42.2 14.7 %collective-permute-start.12 = (f32[576,128]{1,0:T(8,128)S(1)}, f32[576,128]{1,0:T(8,128)S(1)}, u32[]{:S(2)}, u32[]{:S(2)}) collective-permute-start(f32[576,128]{1,0:T(8,128)S(1)} %get-tuple-element.68), channel_id=1, source_target_pairs={{0,4},{2,6},{4,0},{6,2},{1,5},{3,7},{5,1},{7,3},{8,12},{10,14},{12... | collective-permute-start | bytes 884744 | tf_op jit(solution)/shard_map/ppermute | solution.py:531
  43.5 13.5 %collective-permute-start.13 = (f32[576,128]{1,0:T(8,128)S(1)}, f32[576,128]{1,0:T(8,128)S(1)}, u32[]{:S(2)}, u32[]{:S(2)}) collective-permute-start(f32[576,128]{1,0:T(8,128)S(1)} %get-tuple-element.69), channel_id=1, source_target_pairs={{0,2},{2,0},{4,6},{6,4},{1,3},{3,1},{5,7},{7,5},{8,10},{10,8},{12,... | collective-permute-start | bytes 884744 | tf_op jit(solution)/shard_map/ppermute | solution.py:531
  57.6 6.9 %collective-permute-start.14 = (f32[144,128]{1,0:T(8,128)S(1)}, f32[144,128]{1,0:T(8,128)S(1)}, u32[]{:S(2)}, u32[]{:S(2)}) collective-permute-start(f32[144,128]{1,0:T(8,128)S(1)} %get-tuple-element.71), channel_id=1, source_target_pairs={{0,24},{8,16},{16,8},{24,0},{1,25},{9,17},{17,9},{25,1},{2,26},{10... | collective-permute-start | bytes 221192 | tf_op jit(solution)/shard_map/ppermute | solution.py:531
  61.2 6.4 %collective-permute-start.15 = (f32[144,128]{1,0:T(8,128)S(1)}, f32[144,128]{1,0:T(8,128)S(1)}, u32[]{:S(2)}, u32[]{:S(2)}) collective-permute-start(f32[144,128]{1,0:T(8,128)S(1)} %get-tuple-element.72), channel_id=1, source_target_pairs={{0,16},{8,24},{16,0},{24,8},{1,17},{9,25},{17,1},{25,9},{2,18},{10... | collective-permute-start | bytes 221192 | tf_op jit(solution)/shard_map/ppermute | solution.py:531
  61.2 6.4 %collective-permute-start.16 = (f32[144,128]{1,0:T(8,128)S(1)}, f32[144,128]{1,0:T(8,128)S(1)}, u32[]{:S(2)}, u32[]{:S(2)}) collective-permute-start(f32[144,128]{1,0:T(8,128)S(1)} %get-tuple-element.73), channel_id=1, source_target_pairs={{0,8},{8,0},{16,24},{24,16},{1,9},{9,1},{17,25},{25,17},{2,10},{10... | collective-permute-start | bytes 221192 | tf_op jit(solution)/shard_map/ppermute | solution.py:531
  68.1 6.7 %collective-permute-start.19 = (f32[144,128]{1,0:T(8,128)S(1)}, f32[144,128]{1,0:T(8,128)S(1)}, u32[]{:S(2)}, u32[]{:S(2)}) collective-permute-start(f32[144,128]{1,0:T(8,128)S(1)} %add_cut.5.refs_0_), channel_id=1, source_target_pairs={{0,24},{8,16},{16,8},{24,0},{1,25},{9,17},{17,9},{25,1},{2,26},{10... | collective-permute-start | bytes 221192 | tf_op jit(solution)/shard_map/ppermute | solution.py:531
  70.6 7.0 %collective-permute-start.18 = (f32[144,128]{1,0:T(8,128)S(1)}, f32[144,128]{1,0:T(8,128)S(1)}, u32[]{:S(2)}, u32[]{:S(2)}) collective-permute-start(f32[144,128]{1,0:T(8,128)S(1)} %add_cut.5.refs_0_), channel_id=1, source_target_pairs={{0,16},{8,24},{16,0},{24,8},{1,17},{9,25},{17,1},{25,9},{2,18},{10... | collective-permute-start | bytes 221192 | tf_op jit(solution)/shard_map/ppermute | solution.py:531
  70.6 7.0 %collective-permute-start.17 = (f32[144,128]{1,0:T(8,128)S(1)}, f32[144,128]{1,0:T(8,128)S(1)}, u32[]{:S(2)}, u32[]{:S(2)}) collective-permute-start(f32[144,128]{1,0:T(8,128)S(1)} %add_cut.5.refs_0_), channel_id=1, source_target_pairs={{0,8},{8,0},{16,24},{24,16},{1,9},{9,1},{17,25},{25,17},{2,10},{10... | collective-permute-start | bytes 221192 | tf_op jit(solution)/shard_map/ppermute | solution.py:531
  78.3 6.2 %collective-permute-start.22 = (f32[160,128]{1,0:T(8,128)S(1)}, f32[160,128]{1,0:T(8,128)S(1)}, u32[]{:S(2)}, u32[]{:S(2)}) collective-permute-start(f32[160,128]{1,0:T(8,128)S(1)} %get-tuple-element.77.refs_0_), channel_id=1, source_target_pairs={{0,6},{2,4},{4,2},{6,0},{1,7},{3,5},{5,3},{7,1},{8,14},{10,12},{12... | collective-permute-start | bytes 245768 | tf_op jit(solution)/shard_map/ppermute | solution.py:531
  80.0 4.9 %collective-permute-start.21 = (f32[160,128]{1,0:T(8,128)S(1)}, f32[160,128]{1,0:T(8,128)S(1)}, u32[]{:S(2)}, u32[]{:S(2)}) collective-permute-start(f32[160,128]{1,0:T(8,128)S(1)} %get-tuple-element.77.refs_0_), channel_id=1, source_target_pairs={{0,4},{2,6},{4,0},{6,2},{1,5},{3,7},{5,1},{7,3},{8,12},{10,14},{12... | collective-permute-start | bytes 245768 | tf_op jit(solution)/shard_map/ppermute | solution.py:531
  81.3 4.4 %collective-permute-start.20 = (f32[160,128]{1,0:T(8,128)S(1)}, f32[160,128]{1,0:T(8,128)S(1)}, u32[]{:S(2)}, u32[]{:S(2)}) collective-permute-start(f32[160,128]{1,0:T(8,128)S(1)} %get-tuple-element.77.refs_0_), channel_id=1, source_target_pairs={{0,2},{2,0},{4,6},{6,4},{1,3},{3,1},{5,7},{7,5},{8,10},{10,8},{12,... | collective-permute-start | bytes 245768 | tf_op jit(solution)/shard_map/ppermute | solution.py:531
  81.8 3.9 %collective-permute-start.23 = (f32[160,128]{1,0:T(8,128)S(1)}, f32[160,128]{1,0:T(8,128)S(1)}, u32[]{:S(2)}, u32[]{:S(2)}) collective-permute-start(f32[160,128]{1,0:T(8,128)S(1)} %get-tuple-element.77.refs_0_), channel_id=1, source_target_pairs={{0,1},{1,0},{2,3},{3,2},{4,5},{5,4},{6,7},{7,6},{8,9},{9,8},{10,11... | collective-permute-start | bytes 245768 | tf_op jit(solution)/shard_map/ppermute | solution.py:531
  84.4 1.3 %collective-permute-start.26 = (f32[160,128]{1,0:T(8,128)S(1)}, f32[160,128]{1,0:T(8,128)S(1)}, u32[]{:S(2)}, u32[]{:S(2)}) collective-permute-start(f32[160,128]{1,0:T(8,128)S(1)} %collective-permute-done.22.refs_3_), channel_id=1, source_target_pairs={{0,1},{1,0},{2,3},{3,2},{4,5},{5,4},{6,7},{7,6},{8,9},{9,8},{10,11... | collective-permute-start | bytes 245768 | tf_op jit(solution)/shard_map/ppermute | solution.py:531
  84.9 1.3 %collective-permute-start.25 = (f32[160,128]{1,0:T(8,128)S(1)}, f32[160,128]{1,0:T(8,128)S(1)}, u32[]{:S(2)}, u32[]{:S(2)}) collective-permute-start(f32[160,128]{1,0:T(8,128)S(1)} %collective-permute-done.21.refs_2_), channel_id=1, source_target_pairs={{0,1},{1,0},{2,3},{3,2},{4,5},{5,4},{6,7},{7,6},{8,9},{9,8},{10,11... | collective-permute-start | bytes 245768 | tf_op jit(solution)/shard_map/ppermute | solution.py:531
  85.7 1.3 %collective-permute-start.24 = (f32[160,128]{1,0:T(8,128)S(1)}, f32[160,128]{1,0:T(8,128)S(1)}, u32[]{:S(2)}, u32[]{:S(2)}) collective-permute-start(f32[160,128]{1,0:T(8,128)S(1)} %collective-permute-done.20.refs_1_), channel_id=1, source_target_pairs={{0,1},{1,0},{2,3},{3,2},{4,5},{5,4},{6,7},{7,6},{8,9},{9,8},{10,11... | collective-permute-start | bytes 245768 | tf_op jit(solution)/shard_map/ppermute | solution.py:531
  87.0 13.8 %collective-permute-start.29 = (f32[416,128]{1,0:T(8,128)S(1)}, f32[416,128]{1,0:T(8,128)S(1)}, u32[]{:S(2)}, u32[]{:S(2)}) collective-permute-start(f32[416,128]{1,0:T(8,128)S(1)} %get-tuple-element.89.refs_0_), channel_id=1, source_target_pairs={{0,6},{2,4},{4,2},{6,0},{1,7},{3,5},{5,3},{7,1},{8,14},{10,12},{12... | collective-permute-start | bytes 638984 | tf_op jit(solution)/shard_map/ppermute | solution.py:531
  88.4 12.4 %collective-permute-start.28 = (f32[416,128]{1,0:T(8,128)S(1)}, f32[416,128]{1,0:T(8,128)S(1)}, u32[]{:S(2)}, u32[]{:S(2)}) collective-permute-start(f32[416,128]{1,0:T(8,128)S(1)} %get-tuple-element.89.refs_0_), channel_id=1, source_target_pairs={{0,4},{2,6},{4,0},{6,2},{1,5},{3,7},{5,1},{7,3},{8,12},{10,14},{12... | collective-permute-start | bytes 638984 | tf_op jit(solution)/shard_map/ppermute | solution.py:531
  89.3 11.6 %collective-permute-start.27 = (f32[416,128]{1,0:T(8,128)S(1)}, f32[416,128]{1,0:T(8,128)S(1)}, u32[]{:S(2)}, u32[]{:S(2)}) collective-permute-start(f32[416,128]{1,0:T(8,128)S(1)} %get-tuple-element.89.refs_0_), channel_id=1, source_target_pairs={{0,2},{2,0},{4,6},{6,4},{1,3},{3,1},{5,7},{7,5},{8,10},{10,8},{12,... | collective-permute-start | bytes 638984 | tf_op jit(solution)/shard_map/ppermute | solution.py:531
  100.8 1.5 %collective-permute-start.30 = (f32[416,128]{1,0:T(8,128)S(1)}, f32[416,128]{1,0:T(8,128)S(1)}, u32[]{:S(2)}, u32[]{:S(2)}) collective-permute-start(f32[416,128]{1,0:T(8,128)S(1)} %get-tuple-element.89.refs_0_), channel_id=1, source_target_pairs={{0,1},{1,0},{2,3},{3,2},{4,5},{5,4},{6,7},{7,6},{8,9},{9,8},{10,11... | collective-permute-start | bytes 638984 | tf_op jit(solution)/shard_map/ppermute | solution.py:531
  100.9 1.8 %collective-permute-start.31 = (f32[416,128]{1,0:T(8,128)S(1)}, f32[416,128]{1,0:T(8,128)S(1)}, u32[]{:S(2)}, u32[]{:S(2)}) collective-permute-start(f32[416,128]{1,0:T(8,128)S(1)} %collective-permute-done.27.refs_1_), channel_id=1, source_target_pairs={{0,1},{1,0},{2,3},{3,2},{4,5},{5,4},{6,7},{7,6},{8,9},{9,8},{10,11... | collective-permute-start | bytes 638984 | tf_op jit(solution)/shard_map/ppermute | solution.py:531
  101.4 1.6 %collective-permute-start.32 = (f32[416,128]{1,0:T(8,128)S(1)}, f32[416,128]{1,0:T(8,128)S(1)}, u32[]{:S(2)}, u32[]{:S(2)}) collective-permute-start(f32[416,128]{1,0:T(8,128)S(1)} %collective-permute-done.28.refs_2_), channel_id=1, source_target_pairs={{0,1},{1,0},{2,3},{3,2},{4,5},{5,4},{6,7},{7,6},{8,9},{9,8},{10,11... | collective-permute-start | bytes 638984 | tf_op jit(solution)/shard_map/ppermute | solution.py:531
  101.5 1.8 %collective-permute-start.33 = (f32[416,128]{1,0:T(8,128)S(1)}, f32[416,128]{1,0:T(8,128)S(1)}, u32[]{:S(2)}, u32[]{:S(2)}) collective-permute-start(f32[416,128]{1,0:T(8,128)S(1)} %collective-permute-done.29.refs_3_), channel_id=1, source_target_pairs={{0,1},{1,0},{2,3},{3,2},{4,5},{5,4},{6,7},{7,6},{8,9},{9,8},{10,11... | collective-permute-start | bytes 638984 | tf_op jit(solution)/shard_map/ppermute | solution.py:531

commit v11 on v10

--- a/solution.py
+++ b/solution.py
@@ -68,33 +68,64 @@
 LANES = 512
 
 
-def fill_cross(marks_ref, emb_ref, u_ref, k_ref, vq_ref, x_ref, chunks, rows_of):
-    m, e = emb_ref.shape
-    rows = marks_ref.shape[0]
+def fill_chunk(k_ref, r, vq, u_ref, x_ref, to, e):
+    v_inv = lax.rsqrt(vq)
+    v_in, v_out = v_inv * (1.0 / e), vq * v_inv * GROWTH
+    for l in range(0, k_ref.shape[1], LANES):
+        lanes = slice(l, l + LANES)
+        up = jnp.concatenate([u_ref[:8, lanes]] * (CHUNK // 8), axis=0)
+        ur = jnp.concatenate([u_ref[8:, lanes]] * (CHUNK // 8), axis=0)
+        c = recursion(k_ref[pl.ds(r, CHUNK), lanes] * up * spread(v_in, LANES))
+        x_ref[pl.ds(to, CHUNK), lanes] = (c * ur * spread(v_out, LANES)).astype(jnp.bfloat16)
+
+
+def loop_chunks(chunks, most, chunk, beside=None):
+    together = max(d for d in range(1, most + 1) if chunks % d == 0)
+
+    def part(i, _):
+        for q in range(together):
+            chunk(i * together + q)
+        if beside is not None:
+            beside(i, chunks // together)
+        return 0
+
+    lax.fori_loop(0, chunks // together, part, 0)
+
+
+def fill_cross(marks_ref, emb_ref, u_ref, k_ref, vq_ref, x_ref, most):
+    rows, e = marks_ref.shape
     k_ref[:rows, :] = nt(marks_ref[...], emb_ref[...])
     vq_ref[:rows, :] = squares_mean_column(marks_ref[...])
 
-    together = max(d for d in range(1, 9) if chunks % d == 0)
-
-    def part(i, _):
-        for q in range(together):
-            r, to = (pl.multiple_of(at, CHUNK) for at in rows_of(i * together + q))
-            vq = vq_ref[pl.ds(r, CHUNK), :]
-            v_inv = lax.rsqrt(vq)
-            v_in, v_out = v_inv * (1.0 / e), vq * v_inv * GROWTH
-            for l in range(0, m, LANES):
-                lanes = slice(l, l + LANES)
-                up = jnp.concatenate([u_ref[:8, lanes]] * (CHUNK // 8), axis=0)
-                ur = jnp.concatenate([u_ref[8:, lanes]] * (CHUNK // 8), axis=0)
-                c = recursion(k_ref[pl.ds(r, CHUNK), lanes] * up * spread(v_in, LANES))
-                x_ref[pl.ds(to, CHUNK), lanes] = (c * ur * spread(v_out, LANES)).astype(jnp.bfloat16)
-        return 0
-
-    lax.fori_loop(0, chunks // together, part, 0)
-
-
-def in_order(i):
-    return i * CHUNK, i * CHUNK
+    def chunk(i):
+        r = pl.multiple_of(i * CHUNK, CHUNK)
+        fill_chunk(k_ref, r, vq_ref[pl.ds(r, CHUNK), :], u_ref, x_ref, r, e)
+
+    loop_chunks(rows // CHUNK, most, chunk)
+
+
+def fill_shards(marks_ref, emb_ref, u_ref, k_refs, vq_ref, x_ref, chunks, rows_of):
+    m, e = emb_ref.shape
+    shard = marks_ref.shape[0] // len(k_refs)
+    vq_ref[...] = squares_mean_column(marks_ref[...])
+    k_refs[0][...] = nt(marks_ref[:shard, :], emb_ref[...])
+    for s, k_ref in enumerate(k_refs):
+
+        def chunk(i):
+            r, to = (pl.multiple_of(at, CHUNK) for at in rows_of(s, i))
+            fill_chunk(k_ref, r, vq_ref[pl.ds(s * shard + r, CHUNK), :], u_ref, x_ref, to, e)
+
+        def beside(step, steps):
+            span = m // steps
+            at = pl.ds(pl.multiple_of(step * span, B), span)
+            k_refs[s + 1][:, at] = nt(marks_ref[(s + 1) * shard : (s + 2) * shard, :], emb_ref[at, :])
+
+        steps = chunks // max(d for d in range(1, 8) if chunks % d == 0)
+        if s + 1 < len(k_refs) and m % (steps * B):
+            k_refs[s + 1][...] = nt(marks_ref[(s + 1) * shard : (s + 2) * shard, :], emb_ref[...])
+            loop_chunks(chunks, 7, chunk)
+        else:
+            loop_chunks(chunks, 7, chunk, beside if s + 1 < len(k_refs) else None)
 
 
 def own_kernel(marks_ref, emb_ref, x_ref, u_ref, k_ref, vq_ref):
@@ -102,7 +133,7 @@
     inv = lax.rsqrt(uq)
     u_ref[:8, :] = inv
     u_ref[8:, :] = uq * inv
-    fill_cross(marks_ref, emb_ref, u_ref, k_ref, vq_ref, x_ref, x_ref.shape[0] // CHUNK, in_order)
+    fill_cross(marks_ref, emb_ref, u_ref, k_ref, vq_ref, x_ref, 8)
 
 
 def own_cross(landmarks, embeddings):
@@ -122,7 +153,7 @@
 
 def next_kernel(marks_ref, slices_ref, emb_ref, u_ref, x_ref, x_slices_ref, k_ref, vq_ref):
     for m_ref, to_ref in ((marks_ref, x_ref), (slices_ref, x_slices_ref)):
-        fill_cross(m_ref, emb_ref, u_ref, k_ref, vq_ref, to_ref, to_ref.shape[0] // CHUNK, in_order)
+        fill_cross(m_ref, emb_ref, u_ref, k_ref, vq_ref, to_ref, 2)
 
 
 def next_cross(landmarks, slices, embeddings, u):
@@ -152,7 +183,7 @@
     lands, chips, cores, split, all_points = plan
     count = chips * (cores if split else 1)
     far = refs[:count]
-    keep_ref, send_ref, x_ref, ridge_ref, marks_ref, k_ref, vq_ref, out_ref = refs[count:]
+    keep_ref, send_ref, x_ref, ridge_ref, marks_ref, vq_ref, out_ref, *k_refs = refs[count:]
     shard, e = mine_ref.shape
     n = shard * lands
     land, chip, core = at_ref[0], at_ref[1], at_ref[2]
@@ -174,12 +205,11 @@
         x_ref[pl.ds(to, piece), :] = x_slices_ref[(s - 1) * piece : s * piece, :]
     steps = piece // CHUNK
 
-    def rows_of(i):
-        s, rest = i // ((slots - 1) * steps), i % ((slots - 1) * steps)
-        at = (mine ^ (rest // steps + 1)) * piece + rest % steps * CHUNK
-        return s * shard + at, (land ^ (s + 1)) * shard + at
-
-    fill_cross(marks_ref, emb_ref, u_ref, k_ref, vq_ref, x_ref, (lands - 1) * (slots - 1) * steps, rows_of)
+    def rows_of(s, i):
+        at = (mine ^ (i // steps + 1)) * piece + i % steps * CHUNK
+        return at, (land ^ (s + 1)) * shard + at
+
+    fill_shards(marks_ref, emb_ref, u_ref, k_refs, vq_ref, x_ref, (slots - 1) * steps, rows_of)
 
     share = own_ref.shape[0]
     oq = squares_mean_column(own_ref[...])
@@ -255,10 +285,10 @@
             pltpu.VMEM((n, m), jnp.bfloat16),
             pltpu.VMEM((own.shape[0], n), jnp.float32),
             pltpu.VMEM((away, landmarks.shape[1]), jnp.bfloat16),
-            pltpu.VMEM((away, m), jnp.float32),
             pltpu.VMEM((away, B), jnp.float32),
             pltpu.VMEM((rows, B), jnp.float32),
-        ],
+        ]
+        + [pltpu.VMEM((landmarks.shape[0], m), jnp.float32)] * (plan.lands - 1),
         compiler_params=pltpu.CompilerParams(vmem_limit_bytes=24 << 20),
         name="gram",
     )(at, embeddings, landmarks, own, u, x_upper, x_lower, x_slices, *far)

time: 118 us -> 117 us (level)
  no operation moved by 1% of the time
where the time goes in v11:
time: 117 us
  Pallas kernels  47.2 us (40%)
  waiting for transfers between devices  35.1 us (30%)
  starting transfers between devices  31.2 us (27%)
  local copies, waits for them, and re-layouts  3.28 us (3%)
    ppermute x34, waiting for transfers between devices, swap(): lax.ppermute(x, axis, [(i, i ^ s) for i in range(lax.axis_size(axis))])  35.1 us
    ppermute x34, starting transfers between devices, swap(): lax.ppermute(x, axis, [(i, i ^ s) for i in range(lax.axis_size(axis))])  31.2 us
    pallas_call x1, Pallas kernels, last_factor(): pl.pallas_call(functools.partial(last_factor_kernel, plan), out_shape=jax...  14.6 us
    pallas_call x1, Pallas kernels, local_normal(): pl.pallas_call(functools.partial(gram_kernel, plan, na), out_shape=(half,...  13.4 us
    pallas_call x1, Pallas kernels, first_factor(): pl.pallas_call(functools.partial(first_factor_kernel, plan), out_shape=(j...  10.3 us
    pallas_call x1, Pallas kernels, next_cross(): pl.pallas_call(next_kernel, out_shape=tuple((jax.ShapeDtypeStruct((x.shap...  4.27 us
  transfers between devices with their start and end apart: 34, of which 22 were waited for; matrix products, arithmetic and copies ran while one was open for 1% of the time, Pallas kernels for 14%

profile of v11, /device:TPU:0, one launch (start us, length us, event | category | flops | bytes accessed | tf_op | source)
XLA Modules:
  0.0 117.2 jit_solution(7724314062003518252)
XLA Ops:
  0.0 0.8 constant_dynamic-slice_fusion.own_ref
  0.8 5.0 %collective-permute-start.2 = (bf16[32,768]{1,0:T(8,128)(2,1)S(1)}, bf16[32,768]{1,0:T(8,128)(2,1)S(1)}, u32[]{:S(2)}, u32[]{:S(2)}) collective-permute-start(bf16[32,768]{1,0:T(8,128)(2,1)S(1)} %constant_dynamic-slice_fusion.own_ref), channel_id=1, source_target_pairs={{0,24},{8,16},{16,8},{24,0},{1,25},{9,17},{17,9},{25,1},{2,26},{10... | collective-permute-start | bytes 147464 | tf_op jit(solution)/shard_map/ppermute | solution.py:561
  5.9 0.6 collective-permute-start
  6.4 1.0 fusion
  7.5 1.4 %copy-done = bf16[1024,768]{1,0:T(8,128)(2,1)S(1)} copy-done((bf16[1024,768]{1,0:T(8,128)(2,1)S(1)}, bf16[1024,768]{1,0:T(8,128)(2,1)}, u32[]{:S(2)}) %copy-start) | copy-done | bytes 1572888
  8.9 2.2 %own_cross.1 = (bf16[128,1024]{1,0:T(8,128)(2,1)S(1)}, f32[16,1024]{1,0:T(8,128)S(1)}) custom-call(bf16[128,768]{1,0:T(8,128)(2,1)S(1)} %get-tuple-element.94.marks_ref, bf16[1024,768]{1,0:T(8,128)(2,1)S(1)} %copy-done), custom_call_target="tpu_custom_call" | custom-call | tf_op jit(solution)/shard_map/own_cross/pallas_call | solution.py:143
  11.2 2.7 %collective-permute-start.5 = (bf16[96,768]{1,0:T(8,128)(2,1)S(1)}, bf16[96,768]{1,0:T(8,128)(2,1)S(1)}, u32[]{:S(2)}, u32[]{:S(2)}) collective-permute-start(bf16[96,768]{1,0:T(8,128)(2,1)S(1)} %constant_dynamic-update-slice_fusion.slices_ref.refs_0_), channel_id=1, source_target_pairs={{0,6},{2,4},{4,2},{6,0},{1,7},{3,5},{5,3},{7,1},{8,14},{10,12},{12... | collective-permute-start | bytes 442376 | tf_op jit(solution)/shard_map/ppermute | solution.py:561
  13.9 0.5 collective-permute-start.4
  14.8 4.3 %next_cross.1 = (bf16[128,1024]{1,0:T(8,128)(2,1)S(1)}, bf16[96,1024]{1,0:T(8,128)(2,1)S(1)}) custom-call(bf16[128,768]{1,0:T(8,128)(2,1)S(1)} %get-tuple-element.93.marks_ref, bf16[96,768]{1,0:T(8,128)(2,1)S(1)} %constant_dynamic-update-slice_fusion.slices_ref.refs_0_, bf16[1024,768]{1,0:T(8,128)(2,1)S(1)} %copy-done.1, f32[16,1024]{1,0:T(8,128)S(1)} %get-tuple-element.51.u_ref), custom_call_target="tpu_custom_call" | custom-call | tf_op jit(solution)/shard_map/next_cross/pallas_call | solution.py:163
  19.1 1.3 %collective-permute-done.4.refs_2_ = bf16[96,768]{1,0:T(8,128)(2,1)S(1)} collective-permute-done((bf16[96,768]{1,0:T(8,128)(2,1)S(1)}, bf16[96,768]{1,0:T(8,128)(2,1)S(1)}, u32[]{:S(2)}, u32[]{:S(2)}) %collective-permute-start.4) | collective-permute-done | bytes 147488 | tf_op jit(solution)/shard_map/ppermute | solution.py:561
  20.4 0.5 collective-permute-start.7
  20.9 0.5 collective-permute-start.9
  21.5 0.4 collective-permute-done.6.refs_4_
  22.6 13.4 %gram.1 = (f32[2304,128]{1,0:T(8,128)S(1)}, f32[2304,128]{1,0:T(8,128)S(1)}) custom-call(s32[3]{0:T(128)S(1)} %pad_add_fusion.at_ref, bf16[1024,768]{1,0:T(8,128)(2,1)S(1)} %copy-done.1, bf16[256,768]{1,0:T(8,128)(2,1)S(1)} %copy-done.2, bf16[32,768]{1,0:T(8,128)(2,1)S(1)} %constant_dynamic-slice_fusion.own_ref, f32[16,1024]{1,0:T(8,128)S(1)} %get-tuple-element.51.u_ref, ...), custom_call_target="tpu_custom_call" | custom-call | tf_op jit(solution)/shard_map/gram/pallas_call | solution.py:279
  36.4 2.5 %collective-permute-done.10.refs_1_ = f32[2304,128]{1,0:T(8,128)S(1)} collective-permute-done((f32[2304,128]{1,0:T(8,128)S(1)}, f32[2304,128]{1,0:T(8,128)S(1)}, u32[]{:S(2)}, u32[]{:S(2)}) %collective-permute-start.10) | collective-permute-done | bytes 1179680 | tf_op jit(solution)/shard_map/ppermute | solution.py:561
  38.9 0.7 add_cut.3
  39.6 1.8 %collective-permute-start.11 = (f32[576,128]{1,0:T(8,128)S(1)}, f32[576,128]{1,0:T(8,128)S(1)}, u32[]{:S(2)}, u32[]{:S(2)}) collective-permute-start(f32[576,128]{1,0:T(8,128)S(1)} %get-tuple-element.67), channel_id=1, source_target_pairs={{0,6},{2,4},{4,2},{6,0},{1,7},{3,5},{5,3},{7,1},{8,14},{10,12},{12... | collective-permute-start | bytes 884744 | tf_op jit(solution)/shard_map/ppermute | solution.py:561
  41.3 1.3 %collective-permute-start.12 = (f32[576,128]{1,0:T(8,128)S(1)}, f32[576,128]{1,0:T(8,128)S(1)}, u32[]{:S(2)}, u32[]{:S(2)}) collective-permute-start(f32[576,128]{1,0:T(8,128)S(1)} %get-tuple-element.68), channel_id=1, source_target_pairs={{0,4},{2,6},{4,0},{6,2},{1,5},{3,7},{5,1},{7,3},{8,12},{10,14},{12... | collective-permute-start | bytes 884744 | tf_op jit(solution)/shard_map/ppermute | solution.py:561
  42.6 0.5 collective-permute-start.13
  43.1 7.3 %collective-permute-done.11.refs_1_ = f32[576,128]{1,0:T(8,128)S(1)} collective-permute-done((f32[576,128]{1,0:T(8,128)S(1)}, f32[576,128]{1,0:T(8,128)S(1)}, u32[]{:S(2)}, u32[]{:S(2)}) %collective-permute-start.11) | collective-permute-done | bytes 294944 | tf_op jit(solution)/shard_map/ppermute | solution.py:561
  50.4 5.7 %collective-permute-done.12.refs_2_ = f32[576,128]{1,0:T(8,128)S(1)} collective-permute-done((f32[576,128]{1,0:T(8,128)S(1)}, f32[576,128]{1,0:T(8,128)S(1)}, u32[]{:S(2)}, u32[]{:S(2)}) %collective-permute-start.12) | collective-permute-done | bytes 294944 | tf_op jit(solution)/shard_map/ppermute | solution.py:561
  56.1 0.6 add_cut.4
  56.7 3.6 %collective-permute-start.14 = (f32[144,128]{1,0:T(8,128)S(1)}, f32[144,128]{1,0:T(8,128)S(1)}, u32[]{:S(2)}, u32[]{:S(2)}) collective-permute-start(f32[144,128]{1,0:T(8,128)S(1)} %get-tuple-element.71), channel_id=1, source_target_pairs={{0,24},{8,16},{16,8},{24,0},{1,25},{9,17},{17,9},{25,1},{2,26},{10... | collective-permute-start | bytes 221192 | tf_op jit(solution)/shard_map/ppermute | solution.py:561
  60.3 0.9 collective-permute-start.16
  61.2 2.4 %collective-permute-done.14.refs_1_ = f32[144,128]{1,0:T(8,128)S(1)} collective-permute-done((f32[144,128]{1,0:T(8,128)S(1)}, f32[144,128]{1,0:T(8,128)S(1)}, u32[]{:S(2)}, u32[]{:S(2)}) %collective-permute-start.14) | collective-permute-done | bytes 73760 | tf_op jit(solution)/shard_map/ppermute | solution.py:561
  63.6 3.1 %collective-permute-done.15.refs_2_ = f32[144,128]{1,0:T(8,128)S(1)} collective-permute-done((f32[144,128]{1,0:T(8,128)S(1)}, f32[144,128]{1,0:T(8,128)S(1)}, u32[]{:S(2)}, u32[]{:S(2)}) %collective-permute-start.15) | collective-permute-done | bytes 73760 | tf_op jit(solution)/shard_map/ppermute | solution.py:561
  66.7 0.6 add_cut.5.refs_0_
  67.3 2.5 %collective-permute-start.19 = (f32[144,128]{1,0:T(8,128)S(1)}, f32[144,128]{1,0:T(8,128)S(1)}, u32[]{:S(2)}, u32[]{:S(2)}) collective-permute-start(f32[144,128]{1,0:T(8,128)S(1)} %add_cut.5.refs_0_), channel_id=1, source_target_pairs={{0,24},{8,16},{16,8},{24,0},{1,25},{9,17},{17,9},{25,1},{2,26},{10... | collective-permute-start | bytes 221192 | tf_op jit(solution)/shard_map/ppermute | solution.py:561
  69.8 1.9 %collective-permute-start.17 = (f32[144,128]{1,0:T(8,128)S(1)}, f32[144,128]{1,0:T(8,128)S(1)}, u32[]{:S(2)}, u32[]{:S(2)}) collective-permute-start(f32[144,128]{1,0:T(8,128)S(1)} %add_cut.5.refs_0_), channel_id=1, source_target_pairs={{0,8},{8,0},{16,24},{24,16},{1,9},{9,1},{17,25},{25,17},{2,10},{10... | collective-permute-start | bytes 221192 | tf_op jit(solution)/shard_map/ppermute | solution.py:561
  71.7 2.2 %collective-permute-done.19.refs_3_ = f32[144,128]{1,0:T(8,128)S(1)} collective-permute-done((f32[144,128]{1,0:T(8,128)S(1)}, f32[144,128]{1,0:T(8,128)S(1)}, u32[]{:S(2)}, u32[]{:S(2)}) %collective-permute-start.19) | collective-permute-done | bytes 73760 | tf_op jit(solution)/shard_map/ppermute | solution.py:561
  74.0 2.9 %collective-permute-done.18.refs_2_ = f32[144,128]{1,0:T(8,128)S(1)} collective-permute-done((f32[144,128]{1,0:T(8,128)S(1)}, f32[144,128]{1,0:T(8,128)S(1)}, u32[]{:S(2)}, u32[]{:S(2)}) %collective-permute-start.18) | collective-permute-done | bytes 73760 | tf_op jit(solution)/shard_map/ppermute | solution.py:561
  76.8 0.6 place.1
  77.4 1.7 %collective-permute-start.22 = (f32[160,128]{1,0:T(8,128)S(1)}, f32[160,128]{1,0:T(8,128)S(1)}, u32[]{:S(2)}, u32[]{:S(2)}) collective-permute-start(f32[160,128]{1,0:T(8,128)S(1)} %get-tuple-element.77.refs_0_), channel_id=1, source_target_pairs={{0,6},{2,4},{4,2},{6,0},{1,7},{3,5},{5,3},{7,1},{8,14},{10,12},{12... | collective-permute-start | bytes 245768 | tf_op jit(solution)/shard_map/ppermute | solution.py:561
  79.1 1.3 %collective-permute-start.21 = (f32[160,128]{1,0:T(8,128)S(1)}, f32[160,128]{1,0:T(8,128)S(1)}, u32[]{:S(2)}, u32[]{:S(2)}) collective-permute-start(f32[160,128]{1,0:T(8,128)S(1)} %get-tuple-element.77.refs_0_), channel_id=1, source_target_pairs={{0,4},{2,6},{4,0},{6,2},{1,5},{3,7},{5,1},{7,3},{8,12},{10,14},{12... | collective-permute-start | bytes 245768 | tf_op jit(solution)/shard_map/ppermute | solution.py:561
  80.4 0.5 collective-permute-start.20
  81.0 2.6 %collective-permute-done.22.refs_3_ = f32[160,128]{1,0:T(8,128)S(1)} collective-permute-done((f32[160,128]{1,0:T(8,128)S(1)}, f32[160,128]{1,0:T(8,128)S(1)}, u32[]{:S(2)}, u32[]{:S(2)}) %collective-permute-start.22) | collective-permute-done | bytes 81952 | tf_op jit(solution)/shard_map/ppermute | solution.py:561
  83.6 0.4 collective-permute-done.21.refs_2_
  84.1 0.8 collective-permute-done.20.refs_1_
  84.9 0.4 collective-permute-done.25.refs_6_
  85.3 0.8 collective-permute-done.24.refs_5_
  86.2 1.4 %collective-permute-start.29 = (f32[416,128]{1,0:T(8,128)S(1)}, f32[416,128]{1,0:T(8,128)S(1)}, u32[]{:S(2)}, u32[]{:S(2)}) collective-permute-start(f32[416,128]{1,0:T(8,128)S(1)} %get-tuple-element.89.refs_0_), channel_id=1, source_target_pairs={{0,6},{2,4},{4,2},{6,0},{1,7},{3,5},{5,3},{7,1},{8,14},{10,12},{12... | collective-permute-start | bytes 638984 | tf_op jit(solution)/shard_map/ppermute | solution.py:561
  87.6 0.9 collective-permute-start.28
  88.4 1.2 %collective-permute-start.27 = (f32[416,128]{1,0:T(8,128)S(1)}, f32[416,128]{1,0:T(8,128)S(1)}, u32[]{:S(2)}, u32[]{:S(2)}) collective-permute-start(f32[416,128]{1,0:T(8,128)S(1)} %get-tuple-element.89.refs_0_), channel_id=1, source_target_pairs={{0,2},{2,0},{4,6},{6,4},{1,3},{3,1},{5,7},{7,5},{8,10},{10,8},{12,... | collective-permute-start | bytes 638984 | tf_op jit(solution)/shard_map/ppermute | solution.py:561
  89.6 10.3 %chol_first.1 = (f32[512,512]{1,0:T(8,128)S(1)}, f32[512,128]{1,0:T(8,128)S(1)}) custom-call(s32[3]{0:T(128)S(1)} %pad_add_fusion.at_ref, f32[160,128]{1,0:T(8,128)S(1)} %get-tuple-element.77.refs_0_, f32[160,128]{1,0:T(8,128)S(1)} %collective-permute-done.20.refs_1_, f32[160,128]{1,0:T(8,128)S(1)} %collective-permute-done.21.refs_2_, ...), custom_call_target="tpu_custom_call" | custom-call | tf_op jit(solution)/shard_map/chol_first/pallas_call | solution.py:484
  100.1 0.5 collective-permute-start.31
  100.6 0.4 collective-permute-start.33
  101.1 0.4 collective-permute-done.30.refs_4_
  102.4 14.6 %chol_last.1 = f32[1024,1024]{1,0:T(8,128)} custom-call(s32[3]{0:T(128)S(1)} %pad_add_fusion.at_ref, f32[512,512]{1,0:T(8,128)S(1)} %get-tuple-element.87.f_ref, f32[512,128]{1,0:T(8,128)S(1)} %get-tuple-element.88.w_ref, f32[416,128]{1,0:T(8,128)S(1)} %get-tuple-element.89.refs_0_, f32[416,128]{1,0:T(8,128)S(1)} %collective-permute-done.27.refs_1_, ...), custom_call_target="tpu_custom_call" | custom-call | tf_op jit(solution)/shard_map/chol_last/pallas_call | solution.py:543
  (41 shorter events, 2.8 us)
Async XLA Ops:
  0.8 10.3 %collective-permute-start.2 = (bf16[32,768]{1,0:T(8,128)(2,1)S(1)}, bf16[32,768]{1,0:T(8,128)(2,1)S(1)}, u32[]{:S(2)}, u32[]{:S(2)}) collective-permute-start(bf16[32,768]{1,0:T(8,128)(2,1)S(1)} %constant_dynamic-slice_fusion.own_ref), channel_id=1, source_target_pairs={{0,24},{8,16},{16,8},{24,0},{1,25},{9,17},{17,9},{25,1},{2,26},{10... | collective-permute-start | bytes 147464 | tf_op jit(solution)/shard_map/ppermute | solution.py:561
  5.9 5.3 %collective-permute-start.1 = (bf16[32,768]{1,0:T(8,128)(2,1)S(1)}, bf16[32,768]{1,0:T(8,128)(2,1)S(1)}, u32[]{:S(2)}, u32[]{:S(2)}) collective-permute-start(bf16[32,768]{1,0:T(8,128)(2,1)S(1)} %constant_dynamic-slice_fusion.own_ref), channel_id=1, source_target_pairs={{0,16},{8,24},{16,0},{24,8},{1,17},{9,25},{17,1},{25,9},{2,18},{10... | collective-permute-start | bytes 147464 | tf_op jit(solution)/shard_map/ppermute | solution.py:561
  5.9 5.3 %collective-permute-start = (bf16[32,768]{1,0:T(8,128)(2,1)S(1)}, bf16[32,768]{1,0:T(8,128)(2,1)S(1)}, u32[]{:S(2)}, u32[]{:S(2)}) collective-permute-start(bf16[32,768]{1,0:T(8,128)(2,1)S(1)} %constant_dynamic-slice_fusion.own_ref), channel_id=1, source_target_pairs={{0,8},{8,0},{16,24},{24,16},{1,9},{9,1},{17,25},{25,17},{2,10},{10... | collective-permute-start | bytes 147464 | tf_op jit(solution)/shard_map/ppermute | solution.py:561
  7.5 1.4 %copy-start = (bf16[1024,768]{1,0:T(8,128)(2,1)S(1)}, bf16[1024,768]{1,0:T(8,128)(2,1)}, u32[]{:S(2)}) copy-start(bf16[1024,768]{1,0:T(8,128)(2,1)} %emb_ref.5) | copy-start | bytes 4718596
  8.9 5.9 %copy-start.1 = (bf16[1024,768]{1,0:T(8,128)(2,1)S(1)}, bf16[1024,768]{1,0:T(8,128)(2,1)}, u32[]{:S(2)}) copy-start(bf16[1024,768]{1,0:T(8,128)(2,1)} %emb_ref.5) | copy-start | bytes 4718596
  11.1 11.5 %copy-start.2 = (bf16[256,768]{1,0:T(8,128)(2,1)S(1)}, bf16[256,768]{1,0:T(8,128)(2,1)}, u32[]{:S(2)}) copy-start(bf16[256,768]{1,0:T(8,128)(2,1)} %mine_ref.1) | copy-start | bytes 1179652
  11.2 7.8 %collective-permute-start.5 = (bf16[96,768]{1,0:T(8,128)(2,1)S(1)}, bf16[96,768]{1,0:T(8,128)(2,1)S(1)}, u32[]{:S(2)}, u32[]{:S(2)}) collective-permute-start(bf16[96,768]{1,0:T(8,128)(2,1)S(1)} %constant_dynamic-update-slice_fusion.slices_ref.refs_0_), channel_id=1, source_target_pairs={{0,6},{2,4},{4,2},{6,0},{1,7},{3,5},{5,3},{7,1},{8,14},{10,12},{12... | collective-permute-start | bytes 442376 | tf_op jit(solution)/shard_map/ppermute | solution.py:561
  13.9 6.4 %collective-permute-start.4 = (bf16[96,768]{1,0:T(8,128)(2,1)S(1)}, bf16[96,768]{1,0:T(8,128)(2,1)S(1)}, u32[]{:S(2)}, u32[]{:S(2)}) collective-permute-start(bf16[96,768]{1,0:T(8,128)(2,1)S(1)} %constant_dynamic-update-slice_fusion.slices_ref.refs_0_), channel_id=1, source_target_pairs={{0,4},{2,6},{4,0},{6,2},{1,5},{3,7},{5,1},{7,3},{8,12},{10,14},{12... | collective-permute-start | bytes 442376 | tf_op jit(solution)/shard_map/ppermute | solution.py:561
  14.4 6.0 %collective-permute-start.3 = (bf16[96,768]{1,0:T(8,128)(2,1)S(1)}, bf16[96,768]{1,0:T(8,128)(2,1)S(1)}, u32[]{:S(2)}, u32[]{:S(2)}) collective-permute-start(bf16[96,768]{1,0:T(8,128)(2,1)S(1)} %constant_dynamic-update-slice_fusion.slices_ref.refs_0_), channel_id=1, source_target_pairs={{0,2},{2,0},{4,6},{6,4},{1,3},{3,1},{5,7},{7,5},{8,10},{10,8},{12,... | collective-permute-start | bytes 442376 | tf_op jit(solution)/shard_map/ppermute | solution.py:561
  20.4 1.5 %collective-permute-start.6 = (bf16[96,768]{1,0:T(8,128)(2,1)S(1)}, bf16[96,768]{1,0:T(8,128)(2,1)S(1)}, u32[]{:S(2)}, u32[]{:S(2)}) collective-permute-start(bf16[96,768]{1,0:T(8,128)(2,1)S(1)} %constant_dynamic-update-slice_fusion.slices_ref.refs_0_), channel_id=1, source_target_pairs={{0,1},{1,0},{2,3},{3,2},{4,5},{5,4},{6,7},{7,6},{8,9},{9,8},{10,11... | collective-permute-start | bytes 442376 | tf_op jit(solution)/shard_map/ppermute | solution.py:561
  20.4 1.7 %collective-permute-start.7 = (bf16[96,768]{1,0:T(8,128)(2,1)S(1)}, bf16[96,768]{1,0:T(8,128)(2,1)}, u32[]{:S(2)}, u32[]{:S(2)}) collective-permute-start(bf16[96,768]{1,0:T(8,128)(2,1)S(1)} %collective-permute-done.3.refs_1_), channel_id=1, source_target_pairs={{0,1},{1,0},{2,3},{3,2},{4,5},{5,4},{6,7},{7,6},{8,9},{9,8},{10,11... | collective-permute-start | bytes 442376 | tf_op jit(solution)/shard_map/ppermute | solution.py:561
  20.9 1.5 %collective-permute-start.8 = (bf16[96,768]{1,0:T(8,128)(2,1)S(1)}, bf16[96,768]{1,0:T(8,128)(2,1)}, u32[]{:S(2)}, u32[]{:S(2)}) collective-permute-start(bf16[96,768]{1,0:T(8,128)(2,1)S(1)} %collective-permute-done.4.refs_2_), channel_id=1, source_target_pairs={{0,1},{1,0},{2,3},{3,2},{4,5},{5,4},{6,7},{7,6},{8,9},{9,8},{10,11... | collective-permute-start | bytes 442376 | tf_op jit(solution)/shard_map/ppermute | solution.py:561
  20.9 1.7 %collective-permute-start.9 = (bf16[96,768]{1,0:T(8,128)(2,1)S(1)}, bf16[96,768]{1,0:T(8,128)(2,1)}, u32[]{:S(2)}, u32[]{:S(2)}) collective-permute-start(bf16[96,768]{1,0:T(8,128)(2,1)S(1)} %collective-permute-done.5.refs_3_), channel_id=1, source_target_pairs={{0,1},{1,0},{2,3},{3,2},{4,5},{5,4},{6,7},{7,6},{8,9},{9,8},{10,11... | collective-permute-start | bytes 442376 | tf_op jit(solution)/shard_map/ppermute | solution.py:561
  36.0 2.9 %collective-permute-start.10 = (f32[2304,128]{1,0:T(8,128)S(1)}, f32[2304,128]{1,0:T(8,128)S(1)}, u32[]{:S(2)}, u32[]{:S(2)}) collective-permute-start(f32[2304,128]{1,0:T(8,128)S(1)} %get-tuple-element.65), channel_id=1, source_target_pairs={{0,1},{1,0},{2,3},{3,2},{4,5},{5,4},{6,7},{7,6},{8,9},{9,8},{10,11... | collective-permute-start | bytes 3538952 | tf_op jit(solution)/shard_map/ppermute | solution.py:561
  39.6 10.8 %collective-permute-start.11 = (f32[576,128]{1,0:T(8,128)S(1)}, f32[576,128]{1,0:T(8,128)S(1)}, u32[]{:S(2)}, u32[]{:S(2)}) collective-permute-start(f32[576,128]{1,0:T(8,128)S(1)} %get-tuple-element.67), channel_id=1, source_target_pairs={{0,6},{2,4},{4,2},{6,0},{1,7},{3,5},{5,3},{7,1},{8,14},{10,12},{12... | collective-permute-start | bytes 884744 | tf_op jit(solution)/shard_map/ppermute | solution.py:561
  41.3 14.7 %collective-permute-start.12 = (f32[576,128]{1,0:T(8,128)S(1)}, f32[576,128]{1,0:T(8,128)S(1)}, u32[]{:S(2)}, u32[]{:S(2)}) collective-permute-start(f32[576,128]{1,0:T(8,128)S(1)} %get-tuple-element.68), channel_id=1, source_target_pairs={{0,4},{2,6},{4,0},{6,2},{1,5},{3,7},{5,1},{7,3},{8,12},{10,14},{12... | collective-permute-start | bytes 884744 | tf_op jit(solution)/shard_map/ppermute | solution.py:561
  42.6 13.5 %collective-permute-start.13 = (f32[576,128]{1,0:T(8,128)S(1)}, f32[576,128]{1,0:T(8,128)S(1)}, u32[]{:S(2)}, u32[]{:S(2)}) collective-permute-start(f32[576,128]{1,0:T(8,128)S(1)} %get-tuple-element.69), channel_id=1, source_target_pairs={{0,2},{2,0},{4,6},{6,4},{1,3},{3,1},{5,7},{7,5},{8,10},{10,8},{12,... | collective-permute-start | bytes 884744 | tf_op jit(solution)/shard_map/ppermute | solution.py:561
  56.7 6.9 %collective-permute-start.14 = (f32[144,128]{1,0:T(8,128)S(1)}, f32[144,128]{1,0:T(8,128)S(1)}, u32[]{:S(2)}, u32[]{:S(2)}) collective-permute-start(f32[144,128]{1,0:T(8,128)S(1)} %get-tuple-element.71), channel_id=1, source_target_pairs={{0,24},{8,16},{16,8},{24,0},{1,25},{9,17},{17,9},{25,1},{2,26},{10... | collective-permute-start | bytes 221192 | tf_op jit(solution)/shard_map/ppermute | solution.py:561
  60.3 6.4 %collective-permute-start.15 = (f32[144,128]{1,0:T(8,128)S(1)}, f32[144,128]{1,0:T(8,128)S(1)}, u32[]{:S(2)}, u32[]{:S(2)}) collective-permute-start(f32[144,128]{1,0:T(8,128)S(1)} %get-tuple-element.72), channel_id=1, source_target_pairs={{0,16},{8,24},{16,0},{24,8},{1,17},{9,25},{17,1},{25,9},{2,18},{10... | collective-permute-start | bytes 221192 | tf_op jit(solution)/shard_map/ppermute | solution.py:561
  60.3 6.4 %collective-permute-start.16 = (f32[144,128]{1,0:T(8,128)S(1)}, f32[144,128]{1,0:T(8,128)S(1)}, u32[]{:S(2)}, u32[]{:S(2)}) collective-permute-start(f32[144,128]{1,0:T(8,128)S(1)} %get-tuple-element.73), channel_id=1, source_target_pairs={{0,8},{8,0},{16,24},{24,16},{1,9},{9,1},{17,25},{25,17},{2,10},{10... | collective-permute-start | bytes 221192 | tf_op jit(solution)/shard_map/ppermute | solution.py:561
  67.3 6.7 %collective-permute-start.19 = (f32[144,128]{1,0:T(8,128)S(1)}, f32[144,128]{1,0:T(8,128)S(1)}, u32[]{:S(2)}, u32[]{:S(2)}) collective-permute-start(f32[144,128]{1,0:T(8,128)S(1)} %add_cut.5.refs_0_), channel_id=1, source_target_pairs={{0,24},{8,16},{16,8},{24,0},{1,25},{9,17},{17,9},{25,1},{2,26},{10... | collective-permute-start | bytes 221192 | tf_op jit(solution)/shard_map/ppermute | solution.py:561
  69.8 7.1 %collective-permute-start.18 = (f32[144,128]{1,0:T(8,128)S(1)}, f32[144,128]{1,0:T(8,128)S(1)}, u32[]{:S(2)}, u32[]{:S(2)}) collective-permute-start(f32[144,128]{1,0:T(8,128)S(1)} %add_cut.5.refs_0_), channel_id=1, source_target_pairs={{0,16},{8,24},{16,0},{24,8},{1,17},{9,25},{17,1},{25,9},{2,18},{10... | collective-permute-start | bytes 221192 | tf_op jit(solution)/shard_map/ppermute | solution.py:561
  69.8 7.1 %collective-permute-start.17 = (f32[144,128]{1,0:T(8,128)S(1)}, f32[144,128]{1,0:T(8,128)S(1)}, u32[]{:S(2)}, u32[]{:S(2)}) collective-permute-start(f32[144,128]{1,0:T(8,128)S(1)} %add_cut.5.refs_0_), channel_id=1, source_target_pairs={{0,8},{8,0},{16,24},{24,16},{1,9},{9,1},{17,25},{25,17},{2,10},{10... | collective-permute-start | bytes 221192 | tf_op jit(solution)/shard_map/ppermute | solution.py:561
  77.4 6.2 %collective-permute-start.22 = (f32[160,128]{1,0:T(8,128)S(1)}, f32[160,128]{1,0:T(8,128)S(1)}, u32[]{:S(2)}, u32[]{:S(2)}) collective-permute-start(f32[160,128]{1,0:T(8,128)S(1)} %get-tuple-element.77.refs_0_), channel_id=1, source_target_pairs={{0,6},{2,4},{4,2},{6,0},{1,7},{3,5},{5,3},{7,1},{8,14},{10,12},{12... | collective-permute-start | bytes 245768 | tf_op jit(solution)/shard_map/ppermute | solution.py:561
  79.1 4.9 %collective-permute-start.21 = (f32[160,128]{1,0:T(8,128)S(1)}, f32[160,128]{1,0:T(8,128)S(1)}, u32[]{:S(2)}, u32[]{:S(2)}) collective-permute-start(f32[160,128]{1,0:T(8,128)S(1)} %get-tuple-element.77.refs_0_), channel_id=1, source_target_pairs={{0,4},{2,6},{4,0},{6,2},{1,5},{3,7},{5,1},{7,3},{8,12},{10,14},{12... | collective-permute-start | bytes 245768 | tf_op jit(solution)/shard_map/ppermute | solution.py:561
  80.4 4.4 %collective-permute-start.20 = (f32[160,128]{1,0:T(8,128)S(1)}, f32[160,128]{1,0:T(8,128)S(1)}, u32[]{:S(2)}, u32[]{:S(2)}) collective-permute-start(f32[160,128]{1,0:T(8,128)S(1)} %get-tuple-element.77.refs_0_), channel_id=1, source_target_pairs={{0,2},{2,0},{4,6},{6,4},{1,3},{3,1},{5,7},{7,5},{8,10},{10,8},{12,... | collective-permute-start | bytes 245768 | tf_op jit(solution)/shard_map/ppermute | solution.py:561
  81.0 3.9 %collective-permute-start.23 = (f32[160,128]{1,0:T(8,128)S(1)}, f32[160,128]{1,0:T(8,128)S(1)}, u32[]{:S(2)}, u32[]{:S(2)}) collective-permute-start(f32[160,128]{1,0:T(8,128)S(1)} %get-tuple-element.77.refs_0_), channel_id=1, source_target_pairs={{0,1},{1,0},{2,3},{3,2},{4,5},{5,4},{6,7},{7,6},{8,9},{9,8},{10,11... | collective-permute-start | bytes 245768 | tf_op jit(solution)/shard_map/ppermute | solution.py:561
  83.6 1.3 %collective-permute-start.26 = (f32[160,128]{1,0:T(8,128)S(1)}, f32[160,128]{1,0:T(8,128)S(1)}, u32[]{:S(2)}, u32[]{:S(2)}) collective-permute-start(f32[160,128]{1,0:T(8,128)S(1)} %collective-permute-done.22.refs_3_), channel_id=1, source_target_pairs={{0,1},{1,0},{2,3},{3,2},{4,5},{5,4},{6,7},{7,6},{8,9},{9,8},{10,11... | collective-permute-start | bytes 245768 | tf_op jit(solution)/shard_map/ppermute | solution.py:561
  84.0 1.3 %collective-permute-start.25 = (f32[160,128]{1,0:T(8,128)S(1)}, f32[160,128]{1,0:T(8,128)S(1)}, u32[]{:S(2)}, u32[]{:S(2)}) collective-permute-start(f32[160,128]{1,0:T(8,128)S(1)} %collective-permute-done.21.refs_2_), channel_id=1, source_target_pairs={{0,1},{1,0},{2,3},{3,2},{4,5},{5,4},{6,7},{7,6},{8,9},{9,8},{10,11... | collective-permute-start | bytes 245768 | tf_op jit(solution)/shard_map/ppermute | solution.py:561
  84.9 1.3 %collective-permute-start.24 = (f32[160,128]{1,0:T(8,128)S(1)}, f32[160,128]{1,0:T(8,128)S(1)}, u32[]{:S(2)}, u32[]{:S(2)}) collective-permute-start(f32[160,128]{1,0:T(8,128)S(1)} %collective-permute-done.20.refs_1_), channel_id=1, source_target_pairs={{0,1},{1,0},{2,3},{3,2},{4,5},{5,4},{6,7},{7,6},{8,9},{9,8},{10,11... | collective-permute-start | bytes 245768 | tf_op jit(solution)/shard_map/ppermute | solution.py:561
  86.2 13.8 %collective-permute-start.29 = (f32[416,128]{1,0:T(8,128)S(1)}, f32[416,128]{1,0:T(8,128)S(1)}, u32[]{:S(2)}, u32[]{:S(2)}) collective-permute-start(f32[416,128]{1,0:T(8,128)S(1)} %get-tuple-element.89.refs_0_), channel_id=1, source_target_pairs={{0,6},{2,4},{4,2},{6,0},{1,7},{3,5},{5,3},{7,1},{8,14},{10,12},{12... | collective-permute-start | bytes 638984 | tf_op jit(solution)/shard_map/ppermute | solution.py:561
  87.6 12.4 %collective-permute-start.28 = (f32[416,128]{1,0:T(8,128)S(1)}, f32[416,128]{1,0:T(8,128)S(1)}, u32[]{:S(2)}, u32[]{:S(2)}) collective-permute-start(f32[416,128]{1,0:T(8,128)S(1)} %get-tuple-element.89.refs_0_), channel_id=1, source_target_pairs={{0,4},{2,6},{4,0},{6,2},{1,5},{3,7},{5,1},{7,3},{8,12},{10,14},{12... | collective-permute-start | bytes 638984 | tf_op jit(solution)/shard_map/ppermute | solution.py:561
  88.4 11.6 %collective-permute-start.27 = (f32[416,128]{1,0:T(8,128)S(1)}, f32[416,128]{1,0:T(8,128)S(1)}, u32[]{:S(2)}, u32[]{:S(2)}) collective-permute-start(f32[416,128]{1,0:T(8,128)S(1)} %get-tuple-element.89.refs_0_), channel_id=1, source_target_pairs={{0,2},{2,0},{4,6},{6,4},{1,3},{3,1},{5,7},{7,5},{8,10},{10,8},{12,... | collective-permute-start | bytes 638984 | tf_op jit(solution)/shard_map/ppermute | solution.py:561
  100.0 1.5 %collective-permute-start.30 = (f32[416,128]{1,0:T(8,128)S(1)}, f32[416,128]{1,0:T(8,128)S(1)}, u32[]{:S(2)}, u32[]{:S(2)}) collective-permute-start(f32[416,128]{1,0:T(8,128)S(1)} %get-tuple-element.89.refs_0_), channel_id=1, source_target_pairs={{0,1},{1,0},{2,3},{3,2},{4,5},{5,4},{6,7},{7,6},{8,9},{9,8},{10,11... | collective-permute-start | bytes 638984 | tf_op jit(solution)/shard_map/ppermute | solution.py:561
  100.1 1.8 %collective-permute-start.31 = (f32[416,128]{1,0:T(8,128)S(1)}, f32[416,128]{1,0:T(8,128)S(1)}, u32[]{:S(2)}, u32[]{:S(2)}) collective-permute-start(f32[416,128]{1,0:T(8,128)S(1)} %collective-permute-done.27.refs_1_), channel_id=1, source_target_pairs={{0,1},{1,0},{2,3},{3,2},{4,5},{5,4},{6,7},{7,6},{8,9},{9,8},{10,11... | collective-permute-start | bytes 638984 | tf_op jit(solution)/shard_map/ppermute | solution.py:561
  100.6 1.6 %collective-permute-start.32 = (f32[416,128]{1,0:T(8,128)S(1)}, f32[416,128]{1,0:T(8,128)S(1)}, u32[]{:S(2)}, u32[]{:S(2)}) collective-permute-start(f32[416,128]{1,0:T(8,128)S(1)} %collective-permute-done.28.refs_2_), channel_id=1, source_target_pairs={{0,1},{1,0},{2,3},{3,2},{4,5},{5,4},{6,7},{7,6},{8,9},{9,8},{10,11... | collective-permute-start | bytes 638984 | tf_op jit(solution)/shard_map/ppermute | solution.py:561
  100.6 1.8 %collective-permute-start.33 = (f32[416,128]{1,0:T(8,128)S(1)}, f32[416,128]{1,0:T(8,128)S(1)}, u32[]{:S(2)}, u32[]{:S(2)}) collective-permute-start(f32[416,128]{1,0:T(8,128)S(1)} %collective-permute-done.29.refs_3_), channel_id=1, source_target_pairs={{0,1},{1,0},{2,3},{3,2},{4,5},{5,4},{6,7},{7,6},{8,9},{9,8},{10,11... | collective-permute-start | bytes 638984 | tf_op jit(solution)/shard_map/ppermute | solution.py:561

commit v12 on v11

--- a/solution.py
+++ b/solution.py
@@ -593,7 +593,7 @@
         for a in range(1, cores):
             far = far + [swap(f, "core", a) for f in far[:chips]]
 
-    na = n // B // 2
+    na = max(1, n // B * 3 // 8)
     keep, send = local_normal(at, plan, na, embeddings, landmarks, own, u, x_upper, x_lower, x_slices, far)
     rows = [r // cores for r in segments(plan, na, n // B)]
     parts = scatter(add_cut(at, 1, chips, rows, [keep, swap(send, "core", 1)]), "chip")

time: 117 us -> 120 us (1.026)
  waiting for transfers between devices: 35.1 us -> 37.9 us
    ppermute x34, waiting for transfers between devices: 35.1 us -> 37.9 us  [swap(): lax.ppermute(x, axis, [(i, i ^ s) for i in range(lax.axis_size(axis))])]
    pallas_call x1, Pallas kernels: 10.3 us -> 7.66 us  [first_factor(): pl.pallas_call(functools.partial(first_factor_kernel, plan), out_shape=(j...]
    pallas_call x1, Pallas kernels: 14.6 us -> 16.9 us  [last_factor(): pl.pallas_call(functools.partial(last_factor_kernel, plan), out_shape=jax...]
  transfers between devices with their start and end apart: 34 -> 34, of which waited for: 22 -> 22; matrix products, arithmetic and copies ran while one was open for 1% -> 1% of each run, Pallas kernels for 14% -> 12%
where the time goes in v12:
time: 120 us
  Pallas kernels  46.8 us (39%)
  waiting for transfers between devices  37.9 us (32%)
  starting transfers between devices  31.2 us (26%)
  local copies, waits for them, and re-layouts  3.28 us (3%)
    ppermute x34, waiting for transfers between devices, swap(): lax.ppermute(x, axis, [(i, i ^ s) for i in range(lax.axis_size(axis))])  37.9 us
    ppermute x34, starting transfers between devices, swap(): lax.ppermute(x, axis, [(i, i ^ s) for i in range(lax.axis_size(axis))])  31.2 us
    pallas_call x1, Pallas kernels, last_factor(): pl.pallas_call(functools.partial(last_factor_kernel, plan), out_shape=jax...  16.9 us
    pallas_call x1, Pallas kernels, local_normal(): pl.pallas_call(functools.partial(gram_kernel, plan, na), out_shape=(half,...  13.4 us
    pallas_call x1, Pallas kernels, first_factor(): pl.pallas_call(functools.partial(first_factor_kernel, plan), out_shape=(j...  7.66 us
    pallas_call x1, Pallas kernels, next_cross(): pl.pallas_call(next_kernel, out_shape=tuple((jax.ShapeDtypeStruct((x.shap...  4.27 us
  transfers between devices with their start and end apart: 34, of which 22 were waited for; matrix products, arithmetic and copies ran while one was open for 1% of the time, Pallas kernels for 12%

profile of v12, /device:TPU:0, one launch (start us, length us, event | category | flops | bytes accessed | tf_op | source)
XLA Modules:
  0.0 119.6 jit_solution(5610391391427342932)
XLA Ops:
  0.0 0.8 constant_dynamic-slice_fusion.own_ref
  0.8 5.0 %collective-permute-start.2 = (bf16[32,768]{1,0:T(8,128)(2,1)S(1)}, bf16[32,768]{1,0:T(8,128)(2,1)S(1)}, u32[]{:S(2)}, u32[]{:S(2)}) collective-permute-start(bf16[32,768]{1,0:T(8,128)(2,1)S(1)} %constant_dynamic-slice_fusion.own_ref), channel_id=1, source_target_pairs={{0,24},{8,16},{16,8},{24,0},{1,25},{9,17},{17,9},{25,1},{2,26},{10... | collective-permute-start | bytes 147464 | tf_op jit(solution)/shard_map/ppermute | solution.py:561
  5.9 0.6 collective-permute-start
  6.4 1.0 fusion
  7.5 1.4 %copy-done = bf16[1024,768]{1,0:T(8,128)(2,1)S(1)} copy-done((bf16[1024,768]{1,0:T(8,128)(2,1)S(1)}, bf16[1024,768]{1,0:T(8,128)(2,1)}, u32[]{:S(2)}) %copy-start) | copy-done | bytes 1572888
  8.9 2.2 %own_cross.1 = (bf16[128,1024]{1,0:T(8,128)(2,1)S(1)}, f32[16,1024]{1,0:T(8,128)S(1)}) custom-call(bf16[128,768]{1,0:T(8,128)(2,1)S(1)} %get-tuple-element.94.marks_ref, bf16[1024,768]{1,0:T(8,128)(2,1)S(1)} %copy-done), custom_call_target="tpu_custom_call" | custom-call | tf_op jit(solution)/shard_map/own_cross/pallas_call | solution.py:143
  11.2 2.7 %collective-permute-start.5 = (bf16[96,768]{1,0:T(8,128)(2,1)S(1)}, bf16[96,768]{1,0:T(8,128)(2,1)S(1)}, u32[]{:S(2)}, u32[]{:S(2)}) collective-permute-start(bf16[96,768]{1,0:T(8,128)(2,1)S(1)} %constant_dynamic-update-slice_fusion.slices_ref.refs_0_), channel_id=1, source_target_pairs={{0,6},{2,4},{4,2},{6,0},{1,7},{3,5},{5,3},{7,1},{8,14},{10,12},{12... | collective-permute-start | bytes 442376 | tf_op jit(solution)/shard_map/ppermute | solution.py:561
  13.9 0.5 collective-permute-start.4
  14.8 4.3 %next_cross.1 = (bf16[128,1024]{1,0:T(8,128)(2,1)S(1)}, bf16[96,1024]{1,0:T(8,128)(2,1)S(1)}) custom-call(bf16[128,768]{1,0:T(8,128)(2,1)S(1)} %get-tuple-element.93.marks_ref, bf16[96,768]{1,0:T(8,128)(2,1)S(1)} %constant_dynamic-update-slice_fusion.slices_ref.refs_0_, bf16[1024,768]{1,0:T(8,128)(2,1)S(1)} %copy-done.1, f32[16,1024]{1,0:T(8,128)S(1)} %get-tuple-element.51.u_ref), custom_call_target="tpu_custom_call" | custom-call | tf_op jit(solution)/shard_map/next_cross/pallas_call | solution.py:163
  19.1 1.3 %collective-permute-done.4.refs_2_ = bf16[96,768]{1,0:T(8,128)(2,1)S(1)} collective-permute-done((bf16[96,768]{1,0:T(8,128)(2,1)S(1)}, bf16[96,768]{1,0:T(8,128)(2,1)S(1)}, u32[]{:S(2)}, u32[]{:S(2)}) %collective-permute-start.4) | collective-permute-done | bytes 147488 | tf_op jit(solution)/shard_map/ppermute | solution.py:561
  20.4 0.5 collective-permute-start.7
  20.9 0.5 collective-permute-start.9
  21.5 0.4 collective-permute-done.6.refs_4_
  22.6 13.4 %gram.1 = (f32[2304,128]{1,0:T(8,128)S(1)}, f32[2304,128]{1,0:T(8,128)S(1)}) custom-call(s32[3]{0:T(128)S(1)} %pad_add_fusion.at_ref, bf16[1024,768]{1,0:T(8,128)(2,1)S(1)} %copy-done.1, bf16[256,768]{1,0:T(8,128)(2,1)S(1)} %copy-done.2, bf16[32,768]{1,0:T(8,128)(2,1)S(1)} %constant_dynamic-slice_fusion.own_ref, f32[16,1024]{1,0:T(8,128)S(1)} %get-tuple-element.51.u_ref, ...), custom_call_target="tpu_custom_call" | custom-call | tf_op jit(solution)/shard_map/gram/pallas_call | solution.py:279
  36.4 2.5 %collective-permute-done.10.refs_1_ = f32[2304,128]{1,0:T(8,128)S(1)} collective-permute-done((f32[2304,128]{1,0:T(8,128)S(1)}, f32[2304,128]{1,0:T(8,128)S(1)}, u32[]{:S(2)}, u32[]{:S(2)}) %collective-permute-start.10) | collective-permute-done | bytes 1179680 | tf_op jit(solution)/shard_map/ppermute | solution.py:561
  38.9 0.7 add_cut.3
  39.6 1.8 %collective-permute-start.11 = (f32[576,128]{1,0:T(8,128)S(1)}, f32[576,128]{1,0:T(8,128)S(1)}, u32[]{:S(2)}, u32[]{:S(2)}) collective-permute-start(f32[576,128]{1,0:T(8,128)S(1)} %get-tuple-element.67), channel_id=1, source_target_pairs={{0,6},{2,4},{4,2},{6,0},{1,7},{3,5},{5,3},{7,1},{8,14},{10,12},{12... | collective-permute-start | bytes 884744 | tf_op jit(solution)/shard_map/ppermute | solution.py:561
  41.3 1.3 %collective-permute-start.12 = (f32[576,128]{1,0:T(8,128)S(1)}, f32[576,128]{1,0:T(8,128)S(1)}, u32[]{:S(2)}, u32[]{:S(2)}) collective-permute-start(f32[576,128]{1,0:T(8,128)S(1)} %get-tuple-element.68), channel_id=1, source_target_pairs={{0,4},{2,6},{4,0},{6,2},{1,5},{3,7},{5,1},{7,3},{8,12},{10,14},{12... | collective-permute-start | bytes 884744 | tf_op jit(solution)/shard_map/ppermute | solution.py:561
  42.6 0.5 collective-permute-start.13
  43.1 7.3 %collective-permute-done.11.refs_1_ = f32[576,128]{1,0:T(8,128)S(1)} collective-permute-done((f32[576,128]{1,0:T(8,128)S(1)}, f32[576,128]{1,0:T(8,128)S(1)}, u32[]{:S(2)}, u32[]{:S(2)}) %collective-permute-start.11) | collective-permute-done | bytes 294944 | tf_op jit(solution)/shard_map/ppermute | solution.py:561
  50.4 5.7 %collective-permute-done.12.refs_2_ = f32[576,128]{1,0:T(8,128)S(1)} collective-permute-done((f32[576,128]{1,0:T(8,128)S(1)}, f32[576,128]{1,0:T(8,128)S(1)}, u32[]{:S(2)}, u32[]{:S(2)}) %collective-permute-start.12) | collective-permute-done | bytes 294944 | tf_op jit(solution)/shard_map/ppermute | solution.py:561
  56.1 0.6 add_cut.4
  56.7 3.6 %collective-permute-start.14 = (f32[144,128]{1,0:T(8,128)S(1)}, f32[144,128]{1,0:T(8,128)S(1)}, u32[]{:S(2)}, u32[]{:S(2)}) collective-permute-start(f32[144,128]{1,0:T(8,128)S(1)} %get-tuple-element.71), channel_id=1, source_target_pairs={{0,24},{8,16},{16,8},{24,0},{1,25},{9,17},{17,9},{25,1},{2,26},{10... | collective-permute-start | bytes 221192 | tf_op jit(solution)/shard_map/ppermute | solution.py:561
  60.3 0.9 collective-permute-start.16
  61.2 2.4 %collective-permute-done.14.refs_1_ = f32[144,128]{1,0:T(8,128)S(1)} collective-permute-done((f32[144,128]{1,0:T(8,128)S(1)}, f32[144,128]{1,0:T(8,128)S(1)}, u32[]{:S(2)}, u32[]{:S(2)}) %collective-permute-start.14) | collective-permute-done | bytes 73760 | tf_op jit(solution)/shard_map/ppermute | solution.py:561
  63.6 3.1 %collective-permute-done.15.refs_2_ = f32[144,128]{1,0:T(8,128)S(1)} collective-permute-done((f32[144,128]{1,0:T(8,128)S(1)}, f32[144,128]{1,0:T(8,128)S(1)}, u32[]{:S(2)}, u32[]{:S(2)}) %collective-permute-start.15) | collective-permute-done | bytes 73760 | tf_op jit(solution)/shard_map/ppermute | solution.py:561
  66.7 0.6 add_cut.5.refs_0_
  67.3 2.5 %collective-permute-start.19 = (f32[144,128]{1,0:T(8,128)S(1)}, f32[144,128]{1,0:T(8,128)S(1)}, u32[]{:S(2)}, u32[]{:S(2)}) collective-permute-start(f32[144,128]{1,0:T(8,128)S(1)} %add_cut.5.refs_0_), channel_id=1, source_target_pairs={{0,24},{8,16},{16,8},{24,0},{1,25},{9,17},{17,9},{25,1},{2,26},{10... | collective-permute-start | bytes 221192 | tf_op jit(solution)/shard_map/ppermute | solution.py:561
  69.8 1.9 %collective-permute-start.17 = (f32[144,128]{1,0:T(8,128)S(1)}, f32[144,128]{1,0:T(8,128)S(1)}, u32[]{:S(2)}, u32[]{:S(2)}) collective-permute-start(f32[144,128]{1,0:T(8,128)S(1)} %add_cut.5.refs_0_), channel_id=1, source_target_pairs={{0,8},{8,0},{16,24},{24,16},{1,9},{9,1},{17,25},{25,17},{2,10},{10... | collective-permute-start | bytes 221192 | tf_op jit(solution)/shard_map/ppermute | solution.py:561
  71.7 2.2 %collective-permute-done.19.refs_3_ = f32[144,128]{1,0:T(8,128)S(1)} collective-permute-done((f32[144,128]{1,0:T(8,128)S(1)}, f32[144,128]{1,0:T(8,128)S(1)}, u32[]{:S(2)}, u32[]{:S(2)}) %collective-permute-start.19) | collective-permute-done | bytes 73760 | tf_op jit(solution)/shard_map/ppermute | solution.py:561
  73.9 2.9 %collective-permute-done.18.refs_2_ = f32[144,128]{1,0:T(8,128)S(1)} collective-permute-done((f32[144,128]{1,0:T(8,128)S(1)}, f32[144,128]{1,0:T(8,128)S(1)}, u32[]{:S(2)}, u32[]{:S(2)}) %collective-permute-start.18) | collective-permute-done | bytes 73760 | tf_op jit(solution)/shard_map/ppermute | solution.py:561
  76.8 0.6 place.1
  77.4 1.7 %collective-permute-start.22 = (f32[96,128]{1,0:T(8,128)S(1)}, f32[96,128]{1,0:T(8,128)S(1)}, u32[]{:S(2)}, u32[]{:S(2)}) collective-permute-start(f32[96,128]{1,0:T(8,128)S(1)} %get-tuple-element.77.refs_0_), channel_id=1, source_target_pairs={{0,6},{2,4},{4,2},{6,0},{1,7},{3,5},{5,3},{7,1},{8,14},{10,12},{12... | collective-permute-start | bytes 147464 | tf_op jit(solution)/shard_map/ppermute | solution.py:561
  79.1 1.3 %collective-permute-start.21 = (f32[96,128]{1,0:T(8,128)S(1)}, f32[96,128]{1,0:T(8,128)S(1)}, u32[]{:S(2)}, u32[]{:S(2)}) collective-permute-start(f32[96,128]{1,0:T(8,128)S(1)} %get-tuple-element.77.refs_0_), channel_id=1, source_target_pairs={{0,4},{2,6},{4,0},{6,2},{1,5},{3,7},{5,1},{7,3},{8,12},{10,14},{12... | collective-permute-start | bytes 147464 | tf_op jit(solution)/shard_map/ppermute | solution.py:561
  80.4 0.5 collective-permute-start.20
  81.0 1.9 %collective-permute-done.22.refs_3_ = f32[96,128]{1,0:T(8,128)S(1)} collective-permute-done((f32[96,128]{1,0:T(8,128)S(1)}, f32[96,128]{1,0:T(8,128)S(1)}, u32[]{:S(2)}, u32[]{:S(2)}) %collective-permute-start.22) | collective-permute-done | bytes 49184 | tf_op jit(solution)/shard_map/ppermute | solution.py:561
  82.9 0.4 collective-permute-done.21.refs_2_
  83.4 1.1 collective-permute-done.20.refs_1_
  84.5 1.2 %collective-permute-done.24.refs_5_ = f32[96,128]{1,0:T(8,128)S(1)} collective-permute-done((f32[96,128]{1,0:T(8,128)S(1)}, f32[96,128]{1,0:T(8,128)S(1)}, u32[]{:S(2)}, u32[]{:S(2)}) %collective-permute-start.24) | collective-permute-done | bytes 49184 | tf_op jit(solution)/shard_map/ppermute | solution.py:561
  85.7 1.4 %collective-permute-start.29 = (f32[480,128]{1,0:T(8,128)S(1)}, f32[480,128]{1,0:T(8,128)S(1)}, u32[]{:S(2)}, u32[]{:S(2)}) collective-permute-start(f32[480,128]{1,0:T(8,128)S(1)} %get-tuple-element.89.refs_0_), channel_id=1, source_target_pairs={{0,6},{2,4},{4,2},{6,0},{1,7},{3,5},{5,3},{7,1},{8,14},{10,12},{12... | collective-permute-start | bytes 737288 | tf_op jit(solution)/shard_map/ppermute | solution.py:561
  87.1 0.6 collective-permute-start.28
  87.7 1.5 %collective-permute-start.27 = (f32[480,128]{1,0:T(8,128)S(1)}, f32[480,128]{1,0:T(8,128)S(1)}, u32[]{:S(2)}, u32[]{:S(2)}) collective-permute-start(f32[480,128]{1,0:T(8,128)S(1)} %get-tuple-element.89.refs_0_), channel_id=1, source_target_pairs={{0,2},{2,0},{4,6},{6,4},{1,3},{3,1},{5,7},{7,5},{8,10},{10,8},{12,... | collective-permute-start | bytes 737288 | tf_op jit(solution)/shard_map/ppermute | solution.py:561
  89.2 7.7 %chol_first.1 = (f32[384,384]{1,0:T(8,128)S(1)}, f32[384,128]{1,0:T(8,128)S(1)}) custom-call(s32[3]{0:T(128)S(1)} %pad_add_fusion.at_ref, f32[96,128]{1,0:T(8,128)S(1)} %get-tuple-element.77.refs_0_, f32[96,128]{1,0:T(8,128)S(1)} %collective-permute-done.20.refs_1_, f32[96,128]{1,0:T(8,128)S(1)} %collective-permute-done.21.refs_2_, ...), custom_call_target="tpu_custom_call" | custom-call | tf_op jit(solution)/shard_map/chol_first/pallas_call | solution.py:484
  96.9 3.0 %collective-permute-done.28.refs_2_ = f32[480,128]{1,0:T(8,128)S(1)} collective-permute-done((f32[480,128]{1,0:T(8,128)S(1)}, f32[480,128]{1,0:T(8,128)S(1)}, u32[]{:S(2)}, u32[]{:S(2)}) %collective-permute-start.28) | collective-permute-done | bytes 245792 | tf_op jit(solution)/shard_map/ppermute | solution.py:561
  100.0 0.5 collective-permute-start.31
  100.5 0.5 collective-permute-start.33
  101.0 0.5 collective-permute-done.30.refs_4_
  102.5 16.9 %chol_last.1 = f32[1024,1024]{1,0:T(8,128)} custom-call(s32[3]{0:T(128)S(1)} %pad_add_fusion.at_ref, f32[384,384]{1,0:T(8,128)S(1)} %get-tuple-element.87.f_ref, f32[384,128]{1,0:T(8,128)S(1)} %get-tuple-element.88.w_ref, f32[480,128]{1,0:T(8,128)S(1)} %get-tuple-element.89.refs_0_, f32[480,128]{1,0:T(8,128)S(1)} %collective-permute-done.27.refs_1_, ...), custom_call_target="tpu_custom_call" | custom-call | tf_op jit(solution)/shard_map/chol_last/pallas_call | solution.py:543
  (41 shorter events, 2.8 us)
Async XLA Ops:
  0.8 10.3 %collective-permute-start.2 = (bf16[32,768]{1,0:T(8,128)(2,1)S(1)}, bf16[32,768]{1,0:T(8,128)(2,1)S(1)}, u32[]{:S(2)}, u32[]{:S(2)}) collective-permute-start(bf16[32,768]{1,0:T(8,128)(2,1)S(1)} %constant_dynamic-slice_fusion.own_ref), channel_id=1, source_target_pairs={{0,24},{8,16},{16,8},{24,0},{1,25},{9,17},{17,9},{25,1},{2,26},{10... | collective-permute-start | bytes 147464 | tf_op jit(solution)/shard_map/ppermute | solution.py:561
  5.9 5.3 %collective-permute-start.1 = (bf16[32,768]{1,0:T(8,128)(2,1)S(1)}, bf16[32,768]{1,0:T(8,128)(2,1)S(1)}, u32[]{:S(2)}, u32[]{:S(2)}) collective-permute-start(bf16[32,768]{1,0:T(8,128)(2,1)S(1)} %constant_dynamic-slice_fusion.own_ref), channel_id=1, source_target_pairs={{0,16},{8,24},{16,0},{24,8},{1,17},{9,25},{17,1},{25,9},{2,18},{10... | collective-permute-start | bytes 147464 | tf_op jit(solution)/shard_map/ppermute | solution.py:561
  5.9 5.3 %collective-permute-start = (bf16[32,768]{1,0:T(8,128)(2,1)S(1)}, bf16[32,768]{1,0:T(8,128)(2,1)S(1)}, u32[]{:S(2)}, u32[]{:S(2)}) collective-permute-start(bf16[32,768]{1,0:T(8,128)(2,1)S(1)} %constant_dynamic-slice_fusion.own_ref), channel_id=1, source_target_pairs={{0,8},{8,0},{16,24},{24,16},{1,9},{9,1},{17,25},{25,17},{2,10},{10... | collective-permute-start | bytes 147464 | tf_op jit(solution)/shard_map/ppermute | solution.py:561
  7.5 1.4 %copy-start = (bf16[1024,768]{1,0:T(8,128)(2,1)S(1)}, bf16[1024,768]{1,0:T(8,128)(2,1)}, u32[]{:S(2)}) copy-start(bf16[1024,768]{1,0:T(8,128)(2,1)} %emb_ref.5) | copy-start | bytes 4718596
  8.9 5.9 %copy-start.1 = (bf16[1024,768]{1,0:T(8,128)(2,1)S(1)}, bf16[1024,768]{1,0:T(8,128)(2,1)}, u32[]{:S(2)}) copy-start(bf16[1024,768]{1,0:T(8,128)(2,1)} %emb_ref.5) | copy-start | bytes 4718596
  11.1 11.5 %copy-start.2 = (bf16[256,768]{1,0:T(8,128)(2,1)S(1)}, bf16[256,768]{1,0:T(8,128)(2,1)}, u32[]{:S(2)}) copy-start(bf16[256,768]{1,0:T(8,128)(2,1)} %mine_ref.1) | copy-start | bytes 1179652
  11.2 7.8 %collective-permute-start.5 = (bf16[96,768]{1,0:T(8,128)(2,1)S(1)}, bf16[96,768]{1,0:T(8,128)(2,1)S(1)}, u32[]{:S(2)}, u32[]{:S(2)}) collective-permute-start(bf16[96,768]{1,0:T(8,128)(2,1)S(1)} %constant_dynamic-update-slice_fusion.slices_ref.refs_0_), channel_id=1, source_target_pairs={{0,6},{2,4},{4,2},{6,0},{1,7},{3,5},{5,3},{7,1},{8,14},{10,12},{12... | collective-permute-start | bytes 442376 | tf_op jit(solution)/shard_map/ppermute | solution.py:561
  13.9 6.4 %collective-permute-start.4 = (bf16[96,768]{1,0:T(8,128)(2,1)S(1)}, bf16[96,768]{1,0:T(8,128)(2,1)S(1)}, u32[]{:S(2)}, u32[]{:S(2)}) collective-permute-start(bf16[96,768]{1,0:T(8,128)(2,1)S(1)} %constant_dynamic-update-slice_fusion.slices_ref.refs_0_), channel_id=1, source_target_pairs={{0,4},{2,6},{4,0},{6,2},{1,5},{3,7},{5,1},{7,3},{8,12},{10,14},{12... | collective-permute-start | bytes 442376 | tf_op jit(solution)/shard_map/ppermute | solution.py:561
  14.4 6.0 %collective-permute-start.3 = (bf16[96,768]{1,0:T(8,128)(2,1)S(1)}, bf16[96,768]{1,0:T(8,128)(2,1)S(1)}, u32[]{:S(2)}, u32[]{:S(2)}) collective-permute-start(bf16[96,768]{1,0:T(8,128)(2,1)S(1)} %constant_dynamic-update-slice_fusion.slices_ref.refs_0_), channel_id=1, source_target_pairs={{0,2},{2,0},{4,6},{6,4},{1,3},{3,1},{5,7},{7,5},{8,10},{10,8},{12,... | collective-permute-start | bytes 442376 | tf_op jit(solution)/shard_map/ppermute | solution.py:561
  20.4 1.5 %collective-permute-start.6 = (bf16[96,768]{1,0:T(8,128)(2,1)S(1)}, bf16[96,768]{1,0:T(8,128)(2,1)S(1)}, u32[]{:S(2)}, u32[]{:S(2)}) collective-permute-start(bf16[96,768]{1,0:T(8,128)(2,1)S(1)} %constant_dynamic-update-slice_fusion.slices_ref.refs_0_), channel_id=1, source_target_pairs={{0,1},{1,0},{2,3},{3,2},{4,5},{5,4},{6,7},{7,6},{8,9},{9,8},{10,11... | collective-permute-start | bytes 442376 | tf_op jit(solution)/shard_map/ppermute | solution.py:561
  20.4 1.7 %collective-permute-start.7 = (bf16[96,768]{1,0:T(8,128)(2,1)S(1)}, bf16[96,768]{1,0:T(8,128)(2,1)}, u32[]{:S(2)}, u32[]{:S(2)}) collective-permute-start(bf16[96,768]{1,0:T(8,128)(2,1)S(1)} %collective-permute-done.3.refs_1_), channel_id=1, source_target_pairs={{0,1},{1,0},{2,3},{3,2},{4,5},{5,4},{6,7},{7,6},{8,9},{9,8},{10,11... | collective-permute-start | bytes 442376 | tf_op jit(solution)/shard_map/ppermute | solution.py:561
  20.9 1.5 %collective-permute-start.8 = (bf16[96,768]{1,0:T(8,128)(2,1)S(1)}, bf16[96,768]{1,0:T(8,128)(2,1)}, u32[]{:S(2)}, u32[]{:S(2)}) collective-permute-start(bf16[96,768]{1,0:T(8,128)(2,1)S(1)} %collective-permute-done.4.refs_2_), channel_id=1, source_target_pairs={{0,1},{1,0},{2,3},{3,2},{4,5},{5,4},{6,7},{7,6},{8,9},{9,8},{10,11... | collective-permute-start | bytes 442376 | tf_op jit(solution)/shard_map/ppermute | solution.py:561
  20.9 1.7 %collective-permute-start.9 = (bf16[96,768]{1,0:T(8,128)(2,1)S(1)}, bf16[96,768]{1,0:T(8,128)(2,1)}, u32[]{:S(2)}, u32[]{:S(2)}) collective-permute-start(bf16[96,768]{1,0:T(8,128)(2,1)S(1)} %collective-permute-done.5.refs_3_), channel_id=1, source_target_pairs={{0,1},{1,0},{2,3},{3,2},{4,5},{5,4},{6,7},{7,6},{8,9},{9,8},{10,11... | collective-permute-start | bytes 442376 | tf_op jit(solution)/shard_map/ppermute | solution.py:561
  36.0 2.9 %collective-permute-start.10 = (f32[2304,128]{1,0:T(8,128)S(1)}, f32[2304,128]{1,0:T(8,128)S(1)}, u32[]{:S(2)}, u32[]{:S(2)}) collective-permute-start(f32[2304,128]{1,0:T(8,128)S(1)} %get-tuple-element.65), channel_id=1, source_target_pairs={{0,1},{1,0},{2,3},{3,2},{4,5},{5,4},{6,7},{7,6},{8,9},{9,8},{10,11... | collective-permute-start | bytes 3538952 | tf_op jit(solution)/shard_map/ppermute | solution.py:561
  39.6 10.8 %collective-permute-start.11 = (f32[576,128]{1,0:T(8,128)S(1)}, f32[576,128]{1,0:T(8,128)S(1)}, u32[]{:S(2)}, u32[]{:S(2)}) collective-permute-start(f32[576,128]{1,0:T(8,128)S(1)} %get-tuple-element.67), channel_id=1, source_target_pairs={{0,6},{2,4},{4,2},{6,0},{1,7},{3,5},{5,3},{7,1},{8,14},{10,12},{12... | collective-permute-start | bytes 884744 | tf_op jit(solution)/shard_map/ppermute | solution.py:561
  41.3 14.7 %collective-permute-start.12 = (f32[576,128]{1,0:T(8,128)S(1)}, f32[576,128]{1,0:T(8,128)S(1)}, u32[]{:S(2)}, u32[]{:S(2)}) collective-permute-start(f32[576,128]{1,0:T(8,128)S(1)} %get-tuple-element.68), channel_id=1, source_target_pairs={{0,4},{2,6},{4,0},{6,2},{1,5},{3,7},{5,1},{7,3},{8,12},{10,14},{12... | collective-permute-start | bytes 884744 | tf_op jit(solution)/shard_map/ppermute | solution.py:561
  42.6 13.5 %collective-permute-start.13 = (f32[576,128]{1,0:T(8,128)S(1)}, f32[576,128]{1,0:T(8,128)S(1)}, u32[]{:S(2)}, u32[]{:S(2)}) collective-permute-start(f32[576,128]{1,0:T(8,128)S(1)} %get-tuple-element.69), channel_id=1, source_target_pairs={{0,2},{2,0},{4,6},{6,4},{1,3},{3,1},{5,7},{7,5},{8,10},{10,8},{12,... | collective-permute-start | bytes 884744 | tf_op jit(solution)/shard_map/ppermute | solution.py:561
  56.7 6.9 %collective-permute-start.14 = (f32[144,128]{1,0:T(8,128)S(1)}, f32[144,128]{1,0:T(8,128)S(1)}, u32[]{:S(2)}, u32[]{:S(2)}) collective-permute-start(f32[144,128]{1,0:T(8,128)S(1)} %get-tuple-element.71), channel_id=1, source_target_pairs={{0,24},{8,16},{16,8},{24,0},{1,25},{9,17},{17,9},{25,1},{2,26},{10... | collective-permute-start | bytes 221192 | tf_op jit(solution)/shard_map/ppermute | solution.py:561
  60.3 6.4 %collective-permute-start.15 = (f32[144,128]{1,0:T(8,128)S(1)}, f32[144,128]{1,0:T(8,128)S(1)}, u32[]{:S(2)}, u32[]{:S(2)}) collective-permute-start(f32[144,128]{1,0:T(8,128)S(1)} %get-tuple-element.72), channel_id=1, source_target_pairs={{0,16},{8,24},{16,0},{24,8},{1,17},{9,25},{17,1},{25,9},{2,18},{10... | collective-permute-start | bytes 221192 | tf_op jit(solution)/shard_map/ppermute | solution.py:561
  60.3 6.4 %collective-permute-start.16 = (f32[144,128]{1,0:T(8,128)S(1)}, f32[144,128]{1,0:T(8,128)S(1)}, u32[]{:S(2)}, u32[]{:S(2)}) collective-permute-start(f32[144,128]{1,0:T(8,128)S(1)} %get-tuple-element.73), channel_id=1, source_target_pairs={{0,8},{8,0},{16,24},{24,16},{1,9},{9,1},{17,25},{25,17},{2,10},{10... | collective-permute-start | bytes 221192 | tf_op jit(solution)/shard_map/ppermute | solution.py:561
  67.3 6.7 %collective-permute-start.19 = (f32[144,128]{1,0:T(8,128)S(1)}, f32[144,128]{1,0:T(8,128)S(1)}, u32[]{:S(2)}, u32[]{:S(2)}) collective-permute-start(f32[144,128]{1,0:T(8,128)S(1)} %add_cut.5.refs_0_), channel_id=1, source_target_pairs={{0,24},{8,16},{16,8},{24,0},{1,25},{9,17},{17,9},{25,1},{2,26},{10... | collective-permute-start | bytes 221192 | tf_op jit(solution)/shard_map/ppermute | solution.py:561
  69.8 7.1 %collective-permute-start.18 = (f32[144,128]{1,0:T(8,128)S(1)}, f32[144,128]{1,0:T(8,128)S(1)}, u32[]{:S(2)}, u32[]{:S(2)}) collective-permute-start(f32[144,128]{1,0:T(8,128)S(1)} %add_cut.5.refs_0_), channel_id=1, source_target_pairs={{0,16},{8,24},{16,0},{24,8},{1,17},{9,25},{17,1},{25,9},{2,18},{10... | collective-permute-start | bytes 221192 | tf_op jit(solution)/shard_map/ppermute | solution.py:561
  69.8 7.0 %collective-permute-start.17 = (f32[144,128]{1,0:T(8,128)S(1)}, f32[144,128]{1,0:T(8,128)S(1)}, u32[]{:S(2)}, u32[]{:S(2)}) collective-permute-start(f32[144,128]{1,0:T(8,128)S(1)} %add_cut.5.refs_0_), channel_id=1, source_target_pairs={{0,8},{8,0},{16,24},{24,16},{1,9},{9,1},{17,25},{25,17},{2,10},{10... | collective-permute-start | bytes 221192 | tf_op jit(solution)/shard_map/ppermute | solution.py:561
  77.4 5.5 %collective-permute-start.22 = (f32[96,128]{1,0:T(8,128)S(1)}, f32[96,128]{1,0:T(8,128)S(1)}, u32[]{:S(2)}, u32[]{:S(2)}) collective-permute-start(f32[96,128]{1,0:T(8,128)S(1)} %get-tuple-element.77.refs_0_), channel_id=1, source_target_pairs={{0,6},{2,4},{4,2},{6,0},{1,7},{3,5},{5,3},{7,1},{8,14},{10,12},{12... | collective-permute-start | bytes 147464 | tf_op jit(solution)/shard_map/ppermute | solution.py:561
  79.1 4.2 %collective-permute-start.21 = (f32[96,128]{1,0:T(8,128)S(1)}, f32[96,128]{1,0:T(8,128)S(1)}, u32[]{:S(2)}, u32[]{:S(2)}) collective-permute-start(f32[96,128]{1,0:T(8,128)S(1)} %get-tuple-element.77.refs_0_), channel_id=1, source_target_pairs={{0,4},{2,6},{4,0},{6,2},{1,5},{3,7},{5,1},{7,3},{8,12},{10,14},{12... | collective-permute-start | bytes 147464 | tf_op jit(solution)/shard_map/ppermute | solution.py:561
  80.4 4.1 %collective-permute-start.20 = (f32[96,128]{1,0:T(8,128)S(1)}, f32[96,128]{1,0:T(8,128)S(1)}, u32[]{:S(2)}, u32[]{:S(2)}) collective-permute-start(f32[96,128]{1,0:T(8,128)S(1)} %get-tuple-element.77.refs_0_), channel_id=1, source_target_pairs={{0,2},{2,0},{4,6},{6,4},{1,3},{3,1},{5,7},{7,5},{8,10},{10,8},{12,... | collective-permute-start | bytes 147464 | tf_op jit(solution)/shard_map/ppermute | solution.py:561
  81.0 3.6 %collective-permute-start.23 = (f32[96,128]{1,0:T(8,128)S(1)}, f32[96,128]{1,0:T(8,128)S(1)}, u32[]{:S(2)}, u32[]{:S(2)}) collective-permute-start(f32[96,128]{1,0:T(8,128)S(1)} %get-tuple-element.77.refs_0_), channel_id=1, source_target_pairs={{0,1},{1,0},{2,3},{3,2},{4,5},{5,4},{6,7},{7,6},{8,9},{9,8},{10,11... | collective-permute-start | bytes 147464 | tf_op jit(solution)/shard_map/ppermute | solution.py:561
  82.9 1.6 %collective-permute-start.26 = (f32[96,128]{1,0:T(8,128)S(1)}, f32[96,128]{1,0:T(8,128)S(1)}, u32[]{:S(2)}, u32[]{:S(2)}) collective-permute-start(f32[96,128]{1,0:T(8,128)S(1)} %collective-permute-done.22.refs_3_), channel_id=1, source_target_pairs={{0,1},{1,0},{2,3},{3,2},{4,5},{5,4},{6,7},{7,6},{8,9},{9,8},{10,11... | collective-permute-start | bytes 147464 | tf_op jit(solution)/shard_map/ppermute | solution.py:561
  83.3 1.2 %collective-permute-start.25 = (f32[96,128]{1,0:T(8,128)S(1)}, f32[96,128]{1,0:T(8,128)S(1)}, u32[]{:S(2)}, u32[]{:S(2)}) collective-permute-start(f32[96,128]{1,0:T(8,128)S(1)} %collective-permute-done.21.refs_2_), channel_id=1, source_target_pairs={{0,1},{1,0},{2,3},{3,2},{4,5},{5,4},{6,7},{7,6},{8,9},{9,8},{10,11... | collective-permute-start | bytes 147464 | tf_op jit(solution)/shard_map/ppermute | solution.py:561
  84.5 1.2 %collective-permute-start.24 = (f32[96,128]{1,0:T(8,128)S(1)}, f32[96,128]{1,0:T(8,128)S(1)}, u32[]{:S(2)}, u32[]{:S(2)}) collective-permute-start(f32[96,128]{1,0:T(8,128)S(1)} %collective-permute-done.20.refs_1_), channel_id=1, source_target_pairs={{0,1},{1,0},{2,3},{3,2},{4,5},{5,4},{6,7},{7,6},{8,9},{9,8},{10,11... | collective-permute-start | bytes 147464 | tf_op jit(solution)/shard_map/ppermute | solution.py:561
  85.7 11.2 %collective-permute-start.29 = (f32[480,128]{1,0:T(8,128)S(1)}, f32[480,128]{1,0:T(8,128)S(1)}, u32[]{:S(2)}, u32[]{:S(2)}) collective-permute-start(f32[480,128]{1,0:T(8,128)S(1)} %get-tuple-element.89.refs_0_), channel_id=1, source_target_pairs={{0,6},{2,4},{4,2},{6,0},{1,7},{3,5},{5,3},{7,1},{8,14},{10,12},{12... | collective-permute-start | bytes 737288 | tf_op jit(solution)/shard_map/ppermute | solution.py:561
  87.1 12.8 %collective-permute-start.28 = (f32[480,128]{1,0:T(8,128)S(1)}, f32[480,128]{1,0:T(8,128)S(1)}, u32[]{:S(2)}, u32[]{:S(2)}) collective-permute-start(f32[480,128]{1,0:T(8,128)S(1)} %get-tuple-element.89.refs_0_), channel_id=1, source_target_pairs={{0,4},{2,6},{4,0},{6,2},{1,5},{3,7},{5,1},{7,3},{8,12},{10,14},{12... | collective-permute-start | bytes 737288 | tf_op jit(solution)/shard_map/ppermute | solution.py:561
  87.7 12.2 %collective-permute-start.27 = (f32[480,128]{1,0:T(8,128)S(1)}, f32[480,128]{1,0:T(8,128)S(1)}, u32[]{:S(2)}, u32[]{:S(2)}) collective-permute-start(f32[480,128]{1,0:T(8,128)S(1)} %get-tuple-element.89.refs_0_), channel_id=1, source_target_pairs={{0,2},{2,0},{4,6},{6,4},{1,3},{3,1},{5,7},{7,5},{8,10},{10,8},{12,... | collective-permute-start | bytes 737288 | tf_op jit(solution)/shard_map/ppermute | solution.py:561
  99.9 1.5 %collective-permute-start.30 = (f32[480,128]{1,0:T(8,128)S(1)}, f32[480,128]{1,0:T(8,128)S(1)}, u32[]{:S(2)}, u32[]{:S(2)}) collective-permute-start(f32[480,128]{1,0:T(8,128)S(1)} %get-tuple-element.89.refs_0_), channel_id=1, source_target_pairs={{0,1},{1,0},{2,3},{3,2},{4,5},{5,4},{6,7},{7,6},{8,9},{9,8},{10,11... | collective-permute-start | bytes 737288 | tf_op jit(solution)/shard_map/ppermute | solution.py:561
  100.0 1.8 %collective-permute-start.31 = (f32[480,128]{1,0:T(8,128)S(1)}, f32[480,128]{1,0:T(8,128)S(1)}, u32[]{:S(2)}, u32[]{:S(2)}) collective-permute-start(f32[480,128]{1,0:T(8,128)S(1)} %collective-permute-done.27.refs_1_), channel_id=1, source_target_pairs={{0,1},{1,0},{2,3},{3,2},{4,5},{5,4},{6,7},{7,6},{8,9},{9,8},{10,11... | collective-permute-start | bytes 737288 | tf_op jit(solution)/shard_map/ppermute | solution.py:561
  100.4 1.7 %collective-permute-start.32 = (f32[480,128]{1,0:T(8,128)S(1)}, f32[480,128]{1,0:T(8,128)S(1)}, u32[]{:S(2)}, u32[]{:S(2)}) collective-permute-start(f32[480,128]{1,0:T(8,128)S(1)} %collective-permute-done.28.refs_2_), channel_id=1, source_target_pairs={{0,1},{1,0},{2,3},{3,2},{4,5},{5,4},{6,7},{7,6},{8,9},{9,8},{10,11... | collective-permute-start | bytes 737288 | tf_op jit(solution)/shard_map/ppermute | solution.py:561
  100.5 2.0 %collective-permute-start.33 = (f32[480,128]{1,0:T(8,128)S(1)}, f32[480,128]{1,0:T(8,128)S(1)}, u32[]{:S(2)}, u32[]{:S(2)}) collective-permute-start(f32[480,128]{1,0:T(8,128)S(1)} %collective-permute-done.29.refs_3_), channel_id=1, source_target_pairs={{0,1},{1,0},{2,3},{3,2},{4,5},{5,4},{6,7},{7,6},{8,9},{9,8},{10,11... | collective-permute-start | bytes 737288 | tf_op jit(solution)/shard_map/ppermute | solution.py:561
